TPU v7x, 32 devices: a whole 2x2x4 slice. The times are simulated.
32 devices in a mesh: groups: 2 (over y), var: 4 (over z), probe: 2 (over x), rep: 2 (over core).
Axes of the slice: x: 2, y: 2, z: 4, core: 2. Of those that a mesh axis runs over, the one named last changes fastest.
Arguments:
- block_values: bfloat16 [512, 6, 128, 128], P(('groups', 'var'), 'rep'), parts along dimension 0, may hold values from -6 to 6
- columns: int32 [512, 6], P(('groups', 'var'), 'rep'), parts along dimension 0, may hold values from 0 to 255, as said below
- probe_signs: int32 [512, 24, 128], P('groups', 'probe'), parts along dimension 0, may hold values from -1 to 1, as said below
Outputs:
- gradient: bfloat16 [512, 6, 128, 128], P(('groups', 'var'), 'rep'), parts along dimension 0
There are 2 independent parts, one for each index of `groups`. A program takes and returns all parts, laid end to end along the dimension named above; each array names one. Nothing has to cross between parts.
Inputs may be any that keep to these rules, and one draw needn't show every extreme that they name: The 6 block columns of each block row are distinct. `probe_signs`: every entry is -1 or 1.
All inputs are finite; a program needn't handle non-finite values.
Results may differ from a plain program's by a relative error of at most 0.015.
Values may be sent and summed in bfloat16 or wider, within the bound.
No kernel may reach another device: no remote copies, remote signals or barrier semaphores. Data moves between devices by JAX's collectives and lax.ppermute only.
A program may use at most 128 MiB of HBM per device.

v0:
```python
import math

import jax
import jax.numpy as jnp
from jax import lax
from jax.sharding import PartitionSpec as P

BLK = 128
KS = 6


def local(block_values, columns, probe_signs):
    rows_here = block_values.shape[0]
    slots_here = block_values.shape[1]
    block_width = block_values.shape[3]
    blocks_all = probe_signs.shape[0]
    probes_here = probe_signs.shape[1]
    inverse = 1.0 / math.sqrt(KS * BLK)
    column_list = columns.reshape(-1)
    total_probes = probes_here * lax.axis_size("probe")
    signs_all = probe_signs.astype(jnp.bfloat16)
    own_rows = lax.dynamic_slice_in_dim(signs_all, lax.axis_index("var") * rows_here, rows_here, 0)

    def select_local(panel_all):
        return jnp.take(panel_all, column_list, axis=0)

    forward_blocks = [select_local(signs_all)]
    back_panels = [own_rows]
    forward_own = own_rows
    for step_index in range(3):
        shaped = forward_blocks[step_index].reshape(rows_here, slots_here, probes_here, block_width)
        product = jnp.einsum(
            "rkij,rksj->rsi", block_values, shaped, preferred_element_type=jnp.float32
        )
        product = lax.psum(product.astype(jnp.bfloat16), "rep").astype(jnp.float32)
        forward_own = (forward_own.astype(jnp.float32) + inverse * product).astype(jnp.bfloat16)
        forward_blocks.append(select_local(lax.all_gather(forward_own, "var", axis=0, tiled=True)))
    for step_index in range(3):
        panel_own = back_panels[step_index]
        weighted = jnp.einsum(
            "rkij,rsi->rksj", block_values, panel_own, preferred_element_type=jnp.float32
        )
        weighted = weighted.reshape(-1, probes_here, block_width)
        contrib = jax.ops.segment_sum(weighted, column_list, num_segments=blocks_all)
        share_rows = blocks_all // (lax.axis_size("var") * lax.axis_size("rep"))
        summed = lax.psum_scatter(
            contrib.astype(jnp.bfloat16), ("var", "rep"), scatter_dimension=0, tiled=True
        ).astype(jnp.float32)
        previous = lax.dynamic_slice_in_dim(
            panel_own, lax.axis_index("rep") * share_rows, share_rows, 0
        )
        updated = (previous.astype(jnp.float32) + inverse * summed).astype(jnp.bfloat16)
        back_panels.append(lax.all_gather(updated, "rep", axis=0, tiled=True))
    left_panels = jnp.stack(back_panels)
    right_blocks = jnp.stack(forward_blocks[::-1]).reshape(
        4, rows_here, slots_here, probes_here, block_width
    )
    estimate = jnp.einsum(
        "trsi,trksj->rkij", left_panels, right_blocks, preferred_element_type=jnp.float32
    )
    estimate = lax.psum(estimate.astype(jnp.bfloat16), "probe").astype(jnp.float32)
    return (estimate / total_probes).astype(jnp.bfloat16)


def solution(mesh):
    return jax.shard_map(
        local,
        mesh=mesh,
        in_specs=(
            P(("groups", "var"), "rep", None, None),
            P(("groups", "var"), "rep"),
            P("groups", "probe", None),
        ),
        out_specs=P(("groups", "var"), "rep", None, None),
        check_vma=False,
    )
```

profile of v0, /device:TPU:0, one launch (start us, length us, event | category | flops | bytes accessed | tf_op | source)
XLA Modules:
  0.0 377.2 jit_solution(8192982231538396565)
XLA Ops:
  7.4 0.8 copy.88
  8.1 0.1 reshape.35
  8.3 1.6 convert_element_type.87
  9.9 0.5 copy.89
  10.4 0.8 gather_fusion
  11.2 0.3 broadcast_select_fusion.2
  11.5 5.4 %convolution_bitcast_fusion.2 = bf16[64,12,128]{2,1,0:T(8,128)(2,1)S(1)} fusion(bf16[64,3,12,128]{3,2,1,0:T(8,128)(2,1)S(1)} %bitcast.66, bf16[64,3,128,128]{3,2,1,0:T(8,128)(2,1)} %param.5), kind=kOutput, calls=%fused_computation.22 | convolution fusion | flops 75497472 | bytes 7077888 | tf_op jit(solution)/shard_map/rkij,rksj->rsi/dot_general | solution.py:32
  16.9 0.7 copy.163
  17.6 0.0 reduce-scatter.4.cloned.1.call-start
  17.7 0.7 dynamic-slice_bitcast_fusion.1
  18.4 5.1 %fusion.18 = f32[64,12,3,128]{3,1,2,0:T(8,128)} fusion(bf16[64,3,128,128]{3,2,1,0:T(8,128)(2,1)} %param.5, bf16[64,12,128,1]{2,0,1,3:T(8,128)(2,1)S(1)} %get-tuple-element.7), kind=kOutput, calls=%fused_computation.44 | convolution fusion | flops 75497472 | bytes 7667712 | tf_op jit(solution)/shard_map/rkij,rsi->rksj/dot_general | solution.py:40
  23.6 0.1 broadcast.14.clone.1
  23.7 15.5 %scatter_fusion = f32[256,12,128]{2,1,0:T(8,128)S(1)} fusion(f32[256,12,128]{2,1,0:T(8,128)S(1)} %broadcast.14.clone.1, s32[192]{0:T(256)S(1)} %reshape.35, f32[192,12,128]{2,1,0:T(8,128)} %bitcast.64), kind=kCustom, calls=%fused_computation.4 | custom fusion | flops 294912 | bytes 3539712 | tf_op jit(solution)/shard_map/scatter-add | solution.py:44
  39.2 1.4 copy.160
  40.6 0.0 all-reduce.7.cloned.1.call-start
  40.7 0.0 all-reduce.5.cloned.1.call-done
  40.7 1.0 add_convert_fusion.2
  41.7 25.0 %all_gather.18 = bf16[256,12,128]{2,0,1:T(8,128)(2,1)S(1)} all-gather(bf16[64,12,128]{2,0,1:T(8,128)(2,1)S(1)} %add_convert_fusion.2), channel_id=1, replica_groups=mesh['groups'=2,'var'=4,'probe'=2,'rep'=2] {'var'}, dimensions={0}, use_global_device_ids=true | all-gather | bytes 983040 | tf_op jit(solution)/shard_map/all_gather | solution.py:37
  66.7 0.5 copy.93
  67.3 0.8 gather_fusion.1
  68.1 0.3 broadcast_select_fusion.1
  68.3 5.4 %convolution_bitcast_fusion.1 = bf16[64,12,128]{2,1,0:T(8,128)(2,1)S(1)} fusion(bf16[64,3,12,128]{3,2,1,0:T(8,128)(2,1)S(1)} %bitcast.68, bf16[64,3,128,128]{3,2,1,0:T(8,128)(2,1)} %param.5), kind=kOutput, calls=%fused_computation.21 | convolution fusion | flops 75497472 | bytes 7077888 | tf_op jit(solution)/shard_map/rkij,rksj->rsi/dot_general | solution.py:32
  73.7 0.7 copy.162
  74.5 0.0 reduce-scatter.6.cloned.1.call-start
  74.6 2.2 reduce-scatter.4.cloned.1.call-done
  76.8 0.9 add_convert_fusion.5
  77.7 1.9 all_gather.21
  79.7 5.3 %fusion.16 = f32[64,12,3,128]{3,1,2,0:T(8,128)} fusion(bf16[64,3,128,128]{3,2,1,0:T(8,128)(2,1)} %param.5, bf16[64,12,128,1]{2,0,1,3:T(8,128)(2,1)S(1)} %bitcast.72), kind=kOutput, calls=%fused_computation.42 | convolution fusion | flops 75497472 | bytes 7667712 | tf_op jit(solution)/shard_map/rkij,rsi->rksj/dot_general | solution.py:40
  84.9 0.1 broadcast.14.clone
  85.1 15.5 %scatter_fusion.1 = f32[256,12,128]{2,1,0:T(8,128)S(1)} fusion(f32[256,12,128]{2,1,0:T(8,128)S(1)} %broadcast.14.clone, s32[192]{0:T(256)S(1)} %reshape.35, f32[192,12,128]{2,1,0:T(8,128)} %bitcast.65), kind=kCustom, calls=%fused_computation.5 | custom fusion | flops 294912 | bytes 3539712 | tf_op jit(solution)/shard_map/scatter-add | solution.py:44
  100.6 1.4 copy.159
  102.0 0.0 all-reduce.9.cloned.1.call-start
  102.1 1.0 add_convert_fusion.1
  103.1 22.7 %all_gather.19 = bf16[256,12,128]{2,0,1:T(8,128)(2,1)S(1)} all-gather(bf16[64,12,128]{2,0,1:T(8,128)(2,1)S(1)} %add_convert_fusion.1), channel_id=1, replica_groups=mesh['groups'=2,'var'=4,'probe'=2,'rep'=2] {'var'}, dimensions={0}, use_global_device_ids=true | all-gather | bytes 983040 | tf_op jit(solution)/shard_map/all_gather | solution.py:37
  125.8 0.5 copy.97
  126.3 0.8 gather_fusion.2
  127.1 0.3 broadcast_select_fusion
  127.4 5.1 %convolution_bitcast_fusion = bf16[64,12,128]{2,1,0:T(8,128)(2,1)S(1)} fusion(bf16[64,3,12,128]{3,2,1,0:T(8,128)(2,1)S(1)} %bitcast.70, bf16[64,3,128,128]{3,2,1,0:T(8,128)(2,1)} %param.5), kind=kOutput, calls=%fused_computation.20 | convolution fusion | flops 75497472 | bytes 7077888 | tf_op jit(solution)/shard_map/rkij,rksj->rsi/dot_general | solution.py:32
  132.5 0.7 copy.161
  133.3 0.0 reduce-scatter.8.cloned.1.call-start
  133.3 0.8 reduce-scatter.6.cloned.1.call-done
  134.1 0.9 add_convert_fusion.4
  135.1 1.9 all_gather.22
  137.0 5.3 %fusion.14 = f32[64,12,3,128]{3,1,2,0:T(8,128)} fusion(bf16[64,3,128,128]{3,2,1,0:T(8,128)(2,1)} %param.5, bf16[64,12,128,1]{2,0,1,3:T(8,128)(2,1)S(1)} %bitcast.73), kind=kOutput, calls=%fused_computation.40 | convolution fusion | flops 75497472 | bytes 7667712 | tf_op jit(solution)/shard_map/rkij,rsi->rksj/dot_general | solution.py:40
  142.3 0.1 broadcast.14
  142.5 15.5 %scatter_fusion.2 = f32[256,12,128]{2,1,0:T(8,128)S(1)} fusion(f32[256,12,128]{2,1,0:T(8,128)S(1)} %broadcast.14, s32[192]{0:T(256)S(1)} %reshape.35, f32[192,12,128]{2,1,0:T(8,128)} %bitcast.63), kind=kCustom, calls=%fused_computation.6 | custom fusion | flops 294912 | bytes 3539712 | tf_op jit(solution)/shard_map/scatter-add | solution.py:44
  157.9 1.4 copy.158
  159.4 0.0 all-reduce.11.cloned.1.call-start
  159.4 0.8 copy.119
  160.3 1.0 add_convert_fusion
  161.3 22.9 %all_gather.20 = bf16[256,12,128]{2,0,1:T(8,128)(2,1)S(1)} all-gather(bf16[64,12,128]{2,0,1:T(8,128)(2,1)S(1)} %add_convert_fusion), channel_id=1, replica_groups=mesh['groups'=2,'var'=4,'probe'=2,'rep'=2] {'var'}, dimensions={0}, use_global_device_ids=true | all-gather | bytes 983040 | tf_op jit(solution)/shard_map/all_gather | solution.py:37
  184.1 0.5 copy.101
  184.7 1.6 gather_fusion.3
  186.3 1.4 broadcast_select_fusion.3
  187.7 1.8 copy.166
  189.5 1.8 copy.165
  191.3 0.5 reduce-scatter.8.cloned.1.call-done
  191.8 1.0 add_convert_fusion.3
  192.8 1.9 all_gather.23
  194.7 0.1 copy.164
  194.9 6.1 %fusion = bf16[64,3,128,128]{2,3,1,0:T(8,128)(2,1)} fusion(bf16[1,64,3,12,128]{4,3,0,2,1:T(8,128)(2,1)S(1)} %bitcast.67, bf16[1,64,3,12,128]{4,3,0,2,1:T(8,128)(2,1)S(1)} %bitcast.69, bf16[1,64,3,12,128]{4,3,0,2,1:T(8,128)(2,1)S(1)} %bitcast.71, bf16[1,64,3,12,128]{4,3,0,2,1:T(8,128)(2,1)S(1)} %bitcast.74, bf16[1,64,12,128]{3,2,0,1:T(8,128)(2,1)S(1)} %bitcast.77, ...), kind=kOutput, calls=%fused_computation.9 | convolution fusion | flops 309854208 | bytes 9437184 | tf_op jit(solution)/shard_map/trsi,trksj->rkij/dot_general | solution.py:58
  201.0 152.0 %all-reduce.11.cloned.1.call-done = bf16[64,3,128,128]{2,3,1,0:T(8,128)(2,1)} async-done(((bf16[64,3,128,128]{2,3,1,0:T(8,128)(2,1)}), bf16[64,3,128,128]{2,3,1,0:T(8,128)(2,1)}) %all-reduce.11.cloned.1.call-update) | async-done | bytes 6291472 | tf_op jit(solution)/shard_map/psum | solution.py:61
  353.0 8.3 %multiply_convert_fusion = bf16[64,3,128,128]{2,3,1,0:T(8,128)(2,1)} fusion(bf16[64,3,128,128]{2,3,1,0:T(8,128)(2,1)} %all-reduce.11.cloned.1.call-done), kind=kLoop, calls=%fused_computation.8 | loop fusion | flops 9437184 | bytes 12582912 | tf_op jit(solution)/shard_map/convert_element_type | solution.py:62
  361.2 8.6 %copy.120 = bf16[64,3,128,128]{3,2,1,0:T(8,128)(2,1)} copy(bf16[64,3,128,128]{2,3,1,0:T(8,128)(2,1)} %multiply_convert_fusion) | data formatting | bytes 12582912 | tf_op jit(solution)/shard_map/convert_element_type | solution.py:62
  (27 shorter events, 0.2 us)
Async XLA Ops:
  7.4 33.3 %all-reduce.5.cloned.1.call-start = ((), (), s32[]{:S(2)}) async-start(), calls=%async_computation.3 | async-start | bytes 393216 | tf_op jit(solution)/shard_map/psum | solution.py:35
  11.5 5.4 %copy-start = (bf16[192,12,128]{2,1,0:T(8,128)(2,1)}, bf16[192,12,128]{2,1,0:T(8,128)(2,1)S(1)}, u32[]{:S(2)}) copy-start(bf16[192,12,128]{2,1,0:T(8,128)(2,1)S(1)} %broadcast_select_fusion.2) | copy-start | bytes 1769476
  17.6 59.1 %reduce-scatter.4.cloned.1.call-start = ((), (), s32[]{:S(2)}) async-start(), calls=%async_computation.6 | async-start | bytes 884736 | tf_op jit(solution)/shard_map/reduce_scatter | solution.py:46
  40.6 61.5 %all-reduce.7.cloned.1.call-start = ((), (), s32[]{:S(2)}) async-start(), calls=%async_computation.4 | async-start | bytes 393216 | tf_op jit(solution)/shard_map/psum | solution.py:35
  68.3 5.4 %copy-start.2 = (bf16[192,12,128]{2,1,0:T(8,128)(2,1)}, bf16[192,12,128]{2,1,0:T(8,128)(2,1)S(1)}, u32[]{:S(2)}) copy-start(bf16[192,12,128]{2,1,0:T(8,128)(2,1)S(1)} %broadcast_select_fusion.1) | copy-start | bytes 1769476
  74.5 59.6 %reduce-scatter.6.cloned.1.call-start = ((), (), s32[]{:S(2)}) async-start(), calls=%async_computation.7 | async-start | bytes 884736 | tf_op jit(solution)/shard_map/reduce_scatter | solution.py:46
  79.7 54.5 %copy-start.4 = (bf16[64,12,128]{2,0,1:T(8,128)(2,1)}, bf16[64,12,128]{2,0,1:T(8,128)(2,1)S(1)}, u32[]{:S(2)}) copy-start(bf16[64,12,128]{2,0,1:T(8,128)(2,1)S(1)} %all_gather.21) | copy-start | bytes 589828
  102.0 58.3 %all-reduce.9.cloned.1.call-start = ((), (), s32[]{:S(2)}) async-start(), calls=%async_computation.5 | async-start | bytes 393216 | tf_op jit(solution)/shard_map/psum | solution.py:35
  133.3 58.5 %reduce-scatter.8.cloned.1.call-start = ((), (), s32[]{:S(2)}) async-start(), calls=%async_computation.8 | async-start | bytes 884736 | tf_op jit(solution)/shard_map/reduce_scatter | solution.py:46
  137.0 5.3 %copy-start.5 = (bf16[64,12,128]{2,0,1:T(8,128)(2,1)}, bf16[64,12,128]{2,0,1:T(8,128)(2,1)S(1)}, u32[]{:S(2)}) copy-start(bf16[64,12,128]{2,0,1:T(8,128)(2,1)S(1)} %all_gather.22) | copy-start | bytes 589828
  142.4 17.0 %copy-start.6 = (bf16[1,64,12,128]{3,1,2,0:T(8,128)(2,1)S(1)}, bf16[1,64,12,128]{3,1,2,0:T(8,128)(2,1)}, u32[]{:S(2)}) copy-start(bf16[1,64,12,128]{3,1,2,0:T(8,128)(2,1)} %get-tuple-element.6) | copy-start | bytes 589828
  159.4 193.6 %all-reduce.11.cloned.1.call-start = ((), (), s32[]{:S(2)}) async-start(), calls=%async_computation.9 | async-start | bytes 12582912 | tf_op jit(solution)/shard_map/psum | solution.py:61
  184.1 10.7 %copy-start.1 = (bf16[192,12,128]{2,1,0:T(8,128)(2,1)S(1)}, bf16[192,12,128]{2,1,0:T(8,128)(2,1)}, u32[]{:S(2)}) copy-start(bf16[192,12,128]{2,1,0:T(8,128)(2,1)} %copy-done) | copy-start | bytes 1769476
  184.1 10.7 %copy-start.3 = (bf16[192,12,128]{2,1,0:T(8,128)(2,1)S(1)}, bf16[192,12,128]{2,1,0:T(8,128)(2,1)}, u32[]{:S(2)}) copy-start(bf16[192,12,128]{2,1,0:T(8,128)(2,1)} %copy-done.2) | copy-start | bytes 1769476
Sparse Core Ops, SparseCore 0:
  17.8 20.7 all-reduce.4
  74.6 18.4 all-reduce.6
  133.4 17.4 all-reduce.8
  201.1 151.8 all-reduce.10
Sparse Core Ops, SparseCore 1:
  40.7 36.0 reduce-scatter.3
  102.1 32.0 reduce-scatter.5
  159.5 32.3 reduce-scatter.7
where the time goes:
time: 379 us; the launch traced here: 377 us
  waiting for transfers between devices  156 us (41%)
  blocking collectives  76.5 us (20%)
  other arithmetic  64.4 us (17%)
  matrix products  37.7 us (10%)
  local copies, waits for them, and re-layouts  27.7 us (7%)
  between operations  15.1 us (4%)
    psum x1, waiting for transfers between devices, local(): lax.psum(estimate.astype(jnp.bfloat16), 'probe').astype(jnp.float32)  152 us
    all_gather x3, blocking collectives, local(): lax.all_gather(forward_own, 'var', axis=0, tiled=True)  70.6 us
    scatter-add x3, other arithmetic, local(): jax.ops.segment_sum(weighted, column_list, num_segments=blocks_all)  46.5 us
    dot_general x3, matrix products, local(): jnp.einsum('rkij,rksj->rsi', block_values, shaped, preferred_element_type...  15.9 us
    dot_general x3, matrix products, local(): jnp.einsum('rkij,rsi->rksj', block_values, panel_own, preferred_element_t...  15.7 us
    convert_element_type x1, local copies, waits for them, and re-layouts, local(): return (estimate / total_probes).astype(jnp.bfloat16)  8.61 us
    convert_element_type x1, other arithmetic, local(): return (estimate / total_probes).astype(jnp.bfloat16)  8.26 us
  transfers between devices with their start and end apart: 7, of which 4 were waited for; matrix products, arithmetic and copies ran while one was open for 25% of the time, Pallas kernels for 0%

commit v1 on v0

v1 whole, which is shorter than its diff:
```python
import functools
import math

import jax
import jax.numpy as jnp
from jax import lax
from jax.experimental import pallas as pl
from jax.experimental.pallas import tpu as pltpu
from jax.sharding import PartitionSpec as P

KS = 6
PAD = 16
VMEM_LIMIT = 40 * 1024 * 1024


def whole():
    return pl.BlockSpec(memory_space=pltpu.VMEM)


def params():
    return pltpu.CompilerParams(
        dimension_semantics=("arbitrary",), vmem_limit_bytes=VMEM_LIMIT
    )


def split_pair(pair, count):
    wide = pair.astype(jnp.float32)
    keep = lax.broadcasted_iota(jnp.int32, (PAD, wide.shape[1]), 0) < count
    first = jnp.where(keep, wide[:PAD], 0.0)
    second = jnp.where(keep, pltpu.roll(wide, count, 0)[:PAD], 0.0)
    return first, second


def join_pair(first, second, count):
    tail = jnp.zeros((2 * count - PAD, first.shape[1]), jnp.float32)
    low = jnp.concatenate([first, tail], axis=0)
    high = pltpu.roll(jnp.concatenate([second, tail], axis=0), count, 0)
    return low + high


def init_kernel(count, half_pairs, meta, signs, panel, send):
    blocks = signs.shape[0]
    width = signs.shape[2]
    pad = jnp.zeros((PAD - count, width), jnp.float32)

    def body(b, carry):
        value = jnp.concatenate([signs[b].astype(jnp.float32), pad], axis=0)
        panel[b] = value.astype(jnp.bfloat16)
        return carry

    lax.fori_loop(0, blocks, body, 0, unroll=8)
    base = meta[1] * (2 * half_pairs)

    def pack(i, carry):
        b = base + 2 * i
        send[i] = join_pair(
            panel[b].astype(jnp.float32), panel[b + 1].astype(jnp.float32), count
        ).astype(jnp.bfloat16)
        return carry

    lax.fori_loop(0, half_pairs, pack, 0, unroll=8)


def init_panel(meta, signs):
    blocks, count, width = signs.shape
    half_pairs = blocks // 4
    return pl.pallas_call(
        functools.partial(init_kernel, count, half_pairs),
        out_shape=(
            jax.ShapeDtypeStruct((blocks, PAD, width), jnp.bfloat16),
            jax.ShapeDtypeStruct((half_pairs, 2 * count, width), jnp.bfloat16),
        ),
        grid_spec=pltpu.PrefetchScalarGridSpec(
            num_scalar_prefetch=1, grid=(1,), in_specs=[whole()], out_specs=(whole(), whole())
        ),
        compiler_params=params(),
        name="init_panel",
    )(meta, signs)


def unpack_kernel(count, where, meta, *refs):
    panel = refs[-1]
    for ref, base_of in zip(refs[:-1], where):
        pairs = ref.shape[0]
        base = base_of(meta[0], meta[1])

        def body(i, carry, ref=ref, base=base):
            first, second = split_pair(ref[i], count)
            panel[base + 2 * i] = first.astype(jnp.bfloat16)
            panel[base + 2 * i + 1] = second.astype(jnp.bfloat16)
            return carry

        lax.fori_loop(0, pairs, body, 0, unroll=8 if pairs % 8 == 0 else 4)


def unpack(meta, pieces, where, blocks):
    count = pieces[0].shape[1] // 2
    width = pieces[0].shape[2]
    return pl.pallas_call(
        functools.partial(unpack_kernel, count, where),
        out_shape=jax.ShapeDtypeStruct((blocks, PAD, width), jnp.bfloat16),
        grid_spec=pltpu.PrefetchScalarGridSpec(
            num_scalar_prefetch=1,
            grid=(1,),
            in_specs=[whole()] * len(pieces),
            out_specs=whole(),
        ),
        compiler_params=params(),
        name="unpack_panel",
    )(meta, *pieces)


def forward_kernel(
    count, chunk, rows, inverse, meta, cols_own, cols_other, own, other, panel, out
):
    half = rows // 2
    step = pl.program_id(0)
    first_own = meta[1] * half + step * chunk
    first_other = step * chunk
    first_block = meta[0] * rows + first_own
    slots = own.shape[1]
    contract = (((1,), (1,)), ((), ()))
    for i in range(0, chunk, 2):
        results = []
        for r in (i, i + 1):
            total = panel[first_block + r].astype(jnp.float32)
            product = None
            for ref, cols, base in ((own, cols_own, first_own), (other, cols_other, first_other)):
                for k in range(slots):
                    term = lax.dot_general(
                        panel[cols[base + r, k]],
                        ref[r, k],
                        contract,
                        preferred_element_type=jnp.float32,
                    )
                    product = term if product is None else product + term
            results.append(total + inverse * product)
        out[i // 2] = join_pair(results[0], results[1], count).astype(jnp.bfloat16)


def forward(meta, cols_own, cols_other, own, other, panel, count, inverse):
    rows, slots, width = own.shape[0], own.shape[1], own.shape[3]
    half = rows // 2
    chunk = min(8, half)
    steps = half // chunk
    block = (chunk, slots, width, width)
    flops = 2 * half * 2 * slots * PAD * width * width
    return pl.pallas_call(
        functools.partial(forward_kernel, count, chunk, rows, inverse),
        out_shape=jax.ShapeDtypeStruct((half // 2, 2 * count, width), jnp.bfloat16),
        grid_spec=pltpu.PrefetchScalarGridSpec(
            num_scalar_prefetch=3,
            grid=(steps,),
            in_specs=[
                pl.BlockSpec(block, lambda g, meta, *_: (meta[1] * steps + g, 0, 0, 0)),
                pl.BlockSpec(block, lambda g, *_: (g, 0, 0, 0)),
                whole(),
            ],
            out_specs=pl.BlockSpec((chunk // 2, 2 * count, width), lambda g, *_: (g, 0, 0)),
        ),
        compiler_params=params(),
        cost_estimate=pl.CostEstimate(
            flops=flops, transcendentals=0, bytes_accessed=2 * half * slots * 2 * width * width
        ),
        name="forward_step",
    )(meta, cols_own, cols_other, own, other, panel)


def backward_kernel(
    count, chunk, rows, meta, cols_own, cols_other, own, other, left, keep, send, total
):
    half = rows // 2
    step = pl.program_id(0)

    @pl.when(step == 0)
    def _():
        total[...] = jnp.zeros_like(total)

    first_own = meta[1] * half + step * chunk
    first_other = step * chunk
    slots = own.shape[1]
    contract = (((1,), (0,)), ((), ()))
    for i in range(0, chunk, 2):
        pair = split_pair(left[step * (chunk // 2) + i // 2], count)
        for r, value in zip((i, i + 1), pair):
            value = value.astype(jnp.bfloat16)
            for ref, cols, base in ((own, cols_own, first_own), (other, cols_other, first_other)):
                for k in range(slots):
                    term = lax.dot_general(
                        value, ref[r, k], contract, preferred_element_type=jnp.float32
                    )
                    target = cols[base + r, k]
                    total[target] = total[target] + term

    @pl.when(step == pl.num_programs(0) - 1)
    def _():
        parts = keep.shape[0]
        for d in range(parts):
            for out, h in ((send, 1), (keep, 0)):
                base = (meta[0] ^ d) * rows + (meta[1] ^ h) * half

                def body(i, carry, out=out, base=base, d=d):
                    out[d, i] = join_pair(
                        total[base + 2 * i], total[base + 2 * i + 1], count
                    ).astype(jnp.bfloat16)
                    return carry

                pairs = half // 2
                lax.fori_loop(0, pairs, body, 0, unroll=8 if pairs % 8 == 0 else 4)


def backward(meta, cols_own, cols_other, own, other, left, blocks):
    rows, slots, width = own.shape[0], own.shape[1], own.shape[3]
    count = left.shape[1] // 2
    half = rows // 2
    chunk = min(8, half)
    steps = half // chunk
    block = (chunk, slots, width, width)
    flops = 2 * half * 2 * slots * PAD * width * width
    result = jax.ShapeDtypeStruct((blocks // rows, half // 2, 2 * count, width), jnp.bfloat16)
    return pl.pallas_call(
        functools.partial(backward_kernel, count, chunk, rows),
        out_shape=(result, result),
        grid_spec=pltpu.PrefetchScalarGridSpec(
            num_scalar_prefetch=3,
            grid=(steps,),
            in_specs=[
                pl.BlockSpec(block, lambda g, meta, *_: (meta[1] * steps + g, 0, 0, 0)),
                pl.BlockSpec(block, lambda g, *_: (g, 0, 0, 0)),
                whole(),
            ],
            out_specs=(whole(), whole()),
            scratch_shapes=[pltpu.VMEM((blocks, PAD, width), jnp.float32)],
        ),
        compiler_params=params(),
        cost_estimate=pl.CostEstimate(
            flops=flops, transcendentals=0, bytes_accessed=2 * half * slots * 2 * width * width
        ),
        name="backward_step",
    )(meta, cols_own, cols_other, own, other, left)


def gradient_kernel(scale, chunk, rows, terms, meta, cols, *refs):
    out = refs[-1]
    lefts = refs[: 4 * terms]
    rights = refs[4 * terms : 8 * terms]
    step = pl.program_id(0)
    slots = out.shape[1]
    contract = (((0,), (0,)), ((), ()))
    for r in range(chunk):
        row = step * chunk + r
        left = []
        for position, ref in enumerate(lefts):
            start = meta[0] * rows if position < terms else 0
            left.append(ref[start + row])
        left = jnp.concatenate(left, axis=0)
        right = []
        for k in range(slots):
            target = cols[row, k]
            right.append(jnp.concatenate([ref[target] for ref in rights], axis=0))
        product = lax.dot_general(
            left, jnp.concatenate(right, axis=1), contract, preferred_element_type=jnp.float32
        )
        width = out.shape[3]
        for k in range(slots):
            out[r, k] = (product[:, k * width : (k + 1) * width] * scale).astype(jnp.bfloat16)


def gradient(meta, cols, lefts, rights, rows, slots, scale):
    width = lefts[0].shape[2]
    chunk = min(8, rows)
    operands = list(lefts) + list(rights)
    return pl.pallas_call(
        functools.partial(gradient_kernel, scale, chunk, rows, len(lefts) // 4),
        out_shape=jax.ShapeDtypeStruct((rows, slots, width, width), jnp.bfloat16),
        grid_spec=pltpu.PrefetchScalarGridSpec(
            num_scalar_prefetch=2,
            grid=(rows // chunk,),
            in_specs=[whole()] * len(operands),
            out_specs=pl.BlockSpec((chunk, slots, width, width), lambda g, *_: (g, 0, 0, 0)),
        ),
        compiler_params=params(),
        name="gradient",
    )(meta, cols, *operands)


def local(block_values, columns, probe_signs):
    rows, slots, width = block_values.shape[0], block_values.shape[1], block_values.shape[3]
    blocks, count = probe_signs.shape[0], probe_signs.shape[1]
    half = rows // 2
    n_var = lax.axis_size("var")
    n_probe = lax.axis_size("probe")
    inverse = 1.0 / math.sqrt(KS * width)
    rep_index = lax.axis_index("rep")
    meta = jnp.stack([lax.axis_index("var"), rep_index]).astype(jnp.int32)

    def swap_rep(x):
        return lax.ppermute(x, "rep", [(0, 1), (1, 0)])

    def shift_var(x, bit):
        return lax.ppermute(x, "var", [(i, i ^ bit) for i in range(n_var)])

    def from_probes(x):
        return [
            lax.ppermute(x, "probe", [(i, (i + d) % n_probe) for i in range(n_probe)])
            for d in range(1, n_probe)
        ]

    bits = [1 << i for i in range(n_var.bit_length() - 1)]

    def gather_var(x):
        held = {0: x}
        for bit in reversed(bits):
            for d in list(held):
                held[d | bit] = shift_var(held[d], bit)
        return [held[d] for d in range(n_var)]

    def scatter_var(parts):
        held = {d: part.astype(jnp.float32) for d, part in enumerate(parts)}
        for bit in bits:
            for d in sorted(held, reverse=True):
                if d & bit:
                    held[d ^ bit] = held[d ^ bit] + shift_var(
                        held.pop(d).astype(jnp.bfloat16), bit
                    ).astype(jnp.float32)
        return held[0]

    start = (1 - rep_index) * half
    other_blocks = swap_rep(lax.dynamic_slice_in_dim(block_values, start, half, 0))
    other_columns = swap_rep(lax.dynamic_slice_in_dim(columns, start, half, 0))

    def home(d, h):
        return lambda v, r: (v ^ d) * rows + (r ^ h) * half

    panel_where = [home(d, 0) for d in range(n_var)] + [home(d, 1) for d in range(n_var)]
    row_where = [lambda v, r: r * half, lambda v, r: (1 - r) * half]

    panel, sent = init_panel(meta, probe_signs)
    right = [[panel]]
    start_where = [lambda v, r: r * (blocks // 2), lambda v, r: (1 - r) * (blocks // 2)]
    for arrived in from_probes(sent):
        right.append([unpack(meta, [arrived, swap_rep(arrived)], start_where, blocks)])
    left = [[group[0]] for group in right]

    def first_rows():
        base = lax.axis_index("var") * rows + rep_index * half
        mine = lax.dynamic_slice_in_dim(probe_signs, base, half, 0)
        return mine.astype(jnp.bfloat16).reshape(half // 2, 2 * count, width)

    left_own = first_rows()
    for step in range(3):
        updated = forward(
            meta, columns, other_columns, block_values, other_blocks, panel, count, inverse
        )
        keep, send = backward(
            meta, columns, other_columns, block_values, other_blocks, left_own, blocks
        )
        pieces = gather_var(updated)
        partner = [swap_rep(x) for x in pieces]
        panel = unpack(meta, pieces + partner, panel_where, blocks)
        right[0].append(panel)
        joined = jnp.concatenate(pieces, axis=0)
        joined_where = panel_where
        for index, arrived in enumerate(from_probes(joined)):
            swapped = swap_rep(arrived)
            size = half // 2
            cut = [arrived[d * size : (d + 1) * size] for d in range(n_var)]
            cut += [swapped[d * size : (d + 1) * size] for d in range(n_var)]
            right[1 + index].append(unpack(meta, cut, joined_where, blocks))

        received = swap_rep(send)
        sums = [
            keep[d].astype(jnp.float32) + received[d].astype(jnp.float32) for d in range(n_var)
        ]
        summed = scatter_var(sums)
        left_own = (left_own.astype(jnp.float32) + inverse * summed).astype(jnp.bfloat16)
        left[0].append(unpack(meta, [left_own, swap_rep(left_own)], row_where, rows))
        for index, arrived in enumerate(from_probes(left_own)):
            left[1 + index].append(
                unpack(meta, [arrived, swap_rep(arrived)], row_where, rows)
            )

    lefts = [group[t] for t in range(4) for group in left]
    rights = [group[3 - t] for t in range(4) for group in right]
    scale = 1.0 / (count * n_probe)
    return gradient(meta, columns, lefts, rights, rows, slots, scale)


def solution(mesh):
    return jax.shard_map(
        local,
        mesh=mesh,
        in_specs=(
            P(("groups", "var"), "rep", None, None),
            P(("groups", "var"), "rep"),
            P("groups", "probe", None),
        ),
        out_specs=P(("groups", "var"), "rep", None, None),
        check_vma=False,
    )
```

time: 379 us -> 134 us (0.35)
  waiting for transfers between devices: 156 us -> 43.9 us
  blocking collectives: 76.5 us -> 0 us
  other arithmetic: 64.4 us -> 1.72 us
  Pallas kernels: 0 us -> 44.2 us
  matrix products: 37.7 us -> 0 us
  starting transfers between devices: 0.26 us -> 34.9 us
  local copies, waits for them, and re-layouts: 27.7 us -> 8.14 us
  between operations: 15.1 us -> 0.43 us
    psum x4 -> x0, waiting for transfers between devices: 152 us -> none  [the longest x1 152 us: local(): lax.psum(estimate.astype(jnp.bfloat16), 'probe').astype(jnp.float32)]
    all_gather x6 -> x0, blocking collectives: 76.5 us -> none  [the longest x3 70.6 us: local(): lax.all_gather(forward_own, 'var', axis=0, tiled=True)]
    scatter-add x3 -> x0, other arithmetic: 46.5 us -> none  [local(): jax.ops.segment_sum(weighted, column_list, num_segments=blocks_all)]
    pallas_call x0 -> x21, Pallas kernels: none -> 44.2 us  [the longest x3 15.3 us: forward(): pl.pallas_call(functools.partial(forward_kernel, count, chunk, rows, inve...]
    ppermute x0 -> x52, waiting for transfers between devices: none -> 43.9 us  [the longest x18 26 us: shift_var(): return lax.ppermute(x, 'var', [(i, i ^ bit) for i in range(n_var)])]
    dot_general x7 -> x0, matrix products: 37.7 us -> none  [the longest x3 15.9 us: local(): jnp.einsum('rkij,rksj->rsi', block_values, shaped, preferred_element_type...]
    ppermute x0 -> x52, starting transfers between devices: none -> 34.9 us  [the longest x18 21.3 us: shift_var(): return lax.ppermute(x, 'var', [(i, i ^ bit) for i in range(n_var)])]
    convert_element_type x8 -> x10, other arithmetic: 15.7 us -> 1.49 us  [the longest x1 0.94 us: first_rows(): return mine.astype(jnp.bfloat16).reshape(half // 2, 2 * count, width)]
  transfers between devices with their start and end apart: 7 -> 52, of which waited for: 4 -> 18; matrix products, arithmetic and copies ran while one was open for 25% -> 2% of each run, Pallas kernels for 0% -> 25%
where the time goes in v1:
time: 134 us; the launch traced here: 133 us
  Pallas kernels  44.2 us (33%)
  waiting for transfers between devices  43.9 us (33%)
  starting transfers between devices  34.9 us (26%)
  local copies, waits for them, and re-layouts  8.14 us (6%)
  other arithmetic  1.72 us (1%)
    ppermute x18, waiting for transfers between devices, shift_var(): return lax.ppermute(x, 'var', [(i, i ^ bit) for i in range(n_var)])  26 us
    ppermute x18, starting transfers between devices, shift_var(): return lax.ppermute(x, 'var', [(i, i ^ bit) for i in range(n_var)])  21.3 us
    pallas_call x3, Pallas kernels, forward(): pl.pallas_call(functools.partial(forward_kernel, count, chunk, rows, inve...  15.3 us
    pallas_call x3, Pallas kernels, backward(): pl.pallas_call(functools.partial(backward_kernel, count, chunk, rows), ou...  11.6 us
    ppermute x7, waiting for transfers between devices, from_probes(): lax.ppermute(x, 'probe', [(i, (i + d) % n_probe) for i in range(n_probe)])  11 us
    pallas_call x13, Pallas kernels, unpack(): pl.pallas_call(functools.partial(unpack_kernel, count, where), out_shape=...  9.51 us
    ppermute x7, starting transfers between devices, from_probes(): lax.ppermute(x, 'probe', [(i, (i + d) % n_probe) for i in range(n_probe)])  9.03 us
    ppermute x27, waiting for transfers between devices, swap_rep(): return lax.ppermute(x, 'rep', [(0, 1), (1, 0)])  6.89 us
  transfers between devices with their start and end apart: 52, of which 18 were waited for; matrix products, arithmetic and copies ran while one was open for 2% of the time, Pallas kernels for 25%

profile of v1, /device:TPU:0, one launch (start us, length us, event | category | flops | bytes accessed | tf_op | source)
XLA Modules:
  0.0 133.3 jit_solution(14430582664712474611)
XLA Ops:
  0.0 4.0 %constant_dynamic-slice_fusion = bf16[32,3,128,128]{3,2,1,0:T(8,128)(2,1)} fusion(bf16[64,3,128,128]{3,2,1,0:T(8,128)(2,1)} %own.11, s32[]{:T(128)S(6)} %select_n.8), kind=kLoop, calls=%fused_computation.37 | loop fusion | bytes 6291460 | tf_op jit(solution)/shard_map/dynamic_slice | solution.py:329
  4.0 0.5 collective-permute-start.3
  4.7 0.9 dynamic-slice_convert_fusion
  5.8 3.9 %collective-permute-done.2.cols_other = s32[32,3]{1,0:T(8,128)S(1)} collective-permute-done((s32[32,3]{1,0:T(8,128)S(1)}, s32[32,3]{1,0:T(8,128)S(1)}, u32[]{:S(2)}, u32[]{:S(2)}) %collective-permute-start.2) | collective-permute-done | bytes 416 | tf_op jit(solution)/shard_map/ppermute | solution.py:298
  10.0 2.8 %copy-done = bf16[64,3,128,128]{3,2,1,0:T(8,128)(2,1)S(1)} copy-done((bf16[64,3,128,128]{3,2,1,0:T(8,128)(2,1)S(1)}, bf16[64,3,128,128]{3,2,1,0:T(8,128)(2,1)}, u32[]{:S(2)}) %copy-start) | copy-done | bytes 6291480
  12.7 3.9 %backward_step.3 = (bf16[4,16,24,128]{3,2,1,0:T(8,128)(2,1)S(1)}, bf16[4,16,24,128]{3,2,1,0:T(8,128)(2,1)S(1)}) custom-call(s32[2]{0:T(128)S(1)} %pad_add_fusion.meta, s32[64,3]{1,0:T(8,128)S(1)} %copy.23.cols_own.cols, s32[32,3]{1,0:T(8,128)S(1)} %collective-permute-done.2.cols_other, bf16[64,3,128,128]{3,2,1,0:T(8,128)(2,1)S(1)} %copy-done, ...), custom_call_target="tpu_custom_call" | custom-call | flops 100663296 | bytes 6291456 | tf_op jit(solution)/shard_map/backward_step/pallas_call | solution.py:221
  17.1 1.4 %collective-permute-done.4 = bf16[4,16,24,128]{3,2,1,0:T(8,128)(2,1)S(1)} collective-permute-done((bf16[4,16,24,128]{3,2,1,0:T(8,128)(2,1)S(1)}, bf16[4,16,24,128]{3,2,1,0:T(8,128)(2,1)S(1)}, u32[]{:S(2)}, u32[]{:S(2)}) %collective-permute-start.4) | collective-permute-done | bytes 393248 | tf_op jit(solution)/shard_map/ppermute | solution.py:298
  18.5 3.0 %collective-permute-start.6 = (bf16[16,24,128]{2,1,0:T(8,128)(2,1)S(1)}, bf16[16,24,128]{2,1,0:T(8,128)(2,1)S(1)}, u32[]{:S(2)}, u32[]{:S(2)}) collective-permute-start(bf16[16,24,128]{2,1,0:T(8,128)(2,1)S(1)} %get-tuple-element.26), channel_id=1, source_target_pairs={{0,4},{4,0},{8,12},{12,8},{1,5},{5,1},{9,13},{13,9},{2,6},{6,2},{1... | collective-permute-start | bytes 294920 | tf_op jit(solution)/shard_map/ppermute | solution.py:301
  21.5 0.9 copy.14.signs
  22.4 1.0 init_panel.1
  23.4 1.6 %collective-permute-start = (bf16[64,24,128]{2,1,0:T(8,128)(2,1)S(1)}, bf16[64,24,128]{2,1,0:T(8,128)(2,1)S(1)}, u32[]{:S(2)}, u32[]{:S(2)}) collective-permute-start(bf16[64,24,128]{2,1,0:T(8,128)(2,1)S(1)} %get-tuple-element.14), channel_id=1, source_target_pairs={{0,2},{2,0},{1,3},{3,1},{4,6},{6,4},{5,7},{7,5},{8,10},{10,8},{9,1... | collective-permute-start | bytes 1179656 | tf_op jit(solution)/shard_map/ppermute | solution.py:305
  25.5 2.7 %collective-permute-start.7 = (bf16[16,24,128]{2,1,0:T(8,128)(2,1)S(1)}, bf16[16,24,128]{2,1,0:T(8,128)(2,1)S(1)}, u32[]{:S(2)}, u32[]{:S(2)}) collective-permute-start(bf16[16,24,128]{2,1,0:T(8,128)(2,1)S(1)} %fusion.10), channel_id=1, source_target_pairs={{0,8},{4,12},{8,0},{12,4},{1,9},{5,13},{9,1},{13,5},{2,10},{6,14},... | collective-permute-start | bytes 294920 | tf_op jit(solution)/shard_map/ppermute | solution.py:301
  28.1 6.2 %collective-permute-done.refs_0_ = bf16[64,24,128]{2,1,0:T(8,128)(2,1)S(1)} collective-permute-done((bf16[64,24,128]{2,1,0:T(8,128)(2,1)S(1)}, bf16[64,24,128]{2,1,0:T(8,128)(2,1)S(1)}, u32[]{:S(2)}, u32[]{:S(2)}) %collective-permute-start) | collective-permute-done | bytes 393248 | tf_op jit(solution)/shard_map/ppermute | solution.py:305
  34.4 5.1 %forward_step.3.refs_0_ = bf16[16,24,128]{2,1,0:T(8,128)(2,1)S(1)} custom-call(s32[2]{0:T(128)S(1)} %pad_add_fusion.meta, s32[64,3]{1,0:T(8,128)S(1)} %copy.23.cols_own.cols, s32[32,3]{1,0:T(8,128)S(1)} %collective-permute-done.2.cols_other, bf16[64,3,128,128]{3,2,1,0:T(8,128)(2,1)S(1)} %copy-done.1, ...), custom_call_target="tpu_custom_call" | custom-call | flops 100663296 | bytes 6291456 | tf_op jit(solution)/shard_map/forward_step/pallas_call | solution.py:148
  39.5 2.6 %collective-permute-start.26 = (bf16[16,24,128]{2,1,0:T(8,128)(2,1)S(1)}, bf16[16,24,128]{2,1,0:T(8,128)(2,1)S(1)}, u32[]{:S(2)}, u32[]{:S(2)}) collective-permute-start(bf16[16,24,128]{2,1,0:T(8,128)(2,1)S(1)} %forward_step.3.refs_0_), channel_id=1, source_target_pairs={{0,8},{4,12},{8,0},{12,4},{1,9},{5,13},{9,1},{13,5},{2,10},{6,14},... | collective-permute-start | bytes 294920 | tf_op jit(solution)/shard_map/ppermute | solution.py:301
  42.2 3.9 %backward_step.4 = (bf16[4,16,24,128]{3,2,1,0:T(8,128)(2,1)S(1)}, bf16[4,16,24,128]{3,2,1,0:T(8,128)(2,1)S(1)}) custom-call(s32[2]{0:T(128)S(1)} %pad_add_fusion.meta, s32[64,3]{1,0:T(8,128)S(1)} %copy.23.cols_own.cols, s32[32,3]{1,0:T(8,128)S(1)} %collective-permute-done.2.cols_other, bf16[64,3,128,128]{3,2,1,0:T(8,128)(2,1)S(1)} %copy-done.1, ...), custom_call_target="tpu_custom_call" | custom-call | flops 100663296 | bytes 6291456 | tf_op jit(solution)/shard_map/backward_step/pallas_call | solution.py:221
  46.6 0.5 collective-permute-start.25
  47.5 1.1 collective-permute-start.27
  48.7 3.6 %collective-permute-done.25.refs_1_ = bf16[16,24,128]{2,1,0:T(8,128)(2,1)S(1)} collective-permute-done((bf16[16,24,128]{2,1,0:T(8,128)(2,1)S(1)}, bf16[16,24,128]{2,1,0:T(8,128)(2,1)S(1)}, u32[]{:S(2)}, u32[]{:S(2)}) %collective-permute-start.25) | collective-permute-done | bytes 98336 | tf_op jit(solution)/shard_map/ppermute | solution.py:301
  52.3 1.4 %collective-permute-done.27.refs_3_ = bf16[16,24,128]{2,1,0:T(8,128)(2,1)S(1)} collective-permute-done((bf16[16,24,128]{2,1,0:T(8,128)(2,1)S(1)}, bf16[16,24,128]{2,1,0:T(8,128)(2,1)S(1)}, u32[]{:S(2)}, u32[]{:S(2)}) %collective-permute-start.27) | collective-permute-done | bytes 98336 | tf_op jit(solution)/shard_map/ppermute | solution.py:301
  53.7 1.3 collective-permute-done.31.refs_7_
  55.0 0.8 unpack_panel.20.panel.refs_12_
  55.8 5.1 %forward_step.4.refs_0_ = bf16[16,24,128]{2,1,0:T(8,128)(2,1)S(1)} custom-call(s32[2]{0:T(128)S(1)} %pad_add_fusion.meta, s32[64,3]{1,0:T(8,128)S(1)} %copy.23.cols_own.cols, s32[32,3]{1,0:T(8,128)S(1)} %collective-permute-done.2.cols_other, bf16[64,3,128,128]{3,2,1,0:T(8,128)(2,1)S(1)} %copy-done.1, ...), custom_call_target="tpu_custom_call" | custom-call | flops 100663296 | bytes 6291456 | tf_op jit(solution)/shard_map/forward_step/pallas_call | solution.py:148
  61.3 0.8 unpack_panel.13.refs_1_.refs_15_
  62.1 1.5 %collective-permute-start.32 = (bf16[16,24,128]{2,1,0:T(8,128)(2,1)S(1)}, bf16[16,24,128]{2,1,0:T(8,128)(2,1)S(1)}, u32[]{:S(2)}, u32[]{:S(2)}) collective-permute-start(bf16[16,24,128]{2,1,0:T(8,128)(2,1)S(1)} %forward_step.4.refs_0_), channel_id=1, source_target_pairs={{0,4},{4,0},{8,12},{12,8},{1,5},{5,1},{9,13},{13,9},{2,6},{6,2},{1... | collective-permute-start | bytes 294920 | tf_op jit(solution)/shard_map/ppermute | solution.py:301
  63.6 5.2 %collective-permute-done.33.refs_2_ = bf16[16,24,128]{2,1,0:T(8,128)(2,1)S(1)} collective-permute-done((bf16[16,24,128]{2,1,0:T(8,128)(2,1)S(1)}, bf16[16,24,128]{2,1,0:T(8,128)(2,1)S(1)}, u32[]{:S(2)}, u32[]{:S(2)}) %collective-permute-start.33) | collective-permute-done | bytes 98336 | tf_op jit(solution)/shard_map/ppermute | solution.py:301
  68.8 2.1 %collective-permute-start.13 = (bf16[16,24,128]{2,1,0:T(8,128)(2,1)S(1)}, bf16[16,24,128]{2,1,0:T(8,128)(2,1)S(1)}, u32[]{:S(2)}, u32[]{:S(2)}) collective-permute-start(bf16[16,24,128]{2,1,0:T(8,128)(2,1)S(1)} %get-tuple-element.24), channel_id=1, source_target_pairs={{0,4},{4,0},{8,12},{12,8},{1,5},{5,1},{9,13},{13,9},{2,6},{6,2},{1... | collective-permute-start | bytes 294920 | tf_op jit(solution)/shard_map/ppermute | solution.py:301
  71.0 1.6 %collective-permute-start.50 = (bf16[64,24,128]{2,1,0:T(8,128)(2,1)S(1)}, bf16[64,24,128]{2,1,0:T(8,128)(2,1)S(1)}, u32[]{:S(2)}, u32[]{:S(2)}) collective-permute-start(bf16[64,24,128]{2,1,0:T(8,128)(2,1)S(1)} %pad_maximum_fusion.2), channel_id=1, source_target_pairs={{0,2},{2,0},{1,3},{3,1},{4,6},{6,4},{5,7},{7,5},{8,10},{10,8},{9,1... | collective-permute-start | bytes 1179656 | tf_op jit(solution)/shard_map/ppermute | solution.py:305
  72.6 0.5 collective-permute-start.37
  73.1 1.4 %collective-permute-done.34.refs_3_ = bf16[16,24,128]{2,1,0:T(8,128)(2,1)S(1)} collective-permute-done((bf16[16,24,128]{2,1,0:T(8,128)(2,1)S(1)}, bf16[16,24,128]{2,1,0:T(8,128)(2,1)S(1)}, u32[]{:S(2)}, u32[]{:S(2)}) %collective-permute-start.34) | collective-permute-done | bytes 98336 | tf_op jit(solution)/shard_map/ppermute | solution.py:301
  74.4 1.1 collective-permute-done.13
  75.6 1.6 %collective-permute-start.9 = (bf16[16,24,128]{2,1,0:T(8,128)(2,1)S(1)}, bf16[16,24,128]{2,1,0:T(8,128)(2,1)S(1)}, u32[]{:S(2)}, u32[]{:S(2)}) collective-permute-start(bf16[16,24,128]{2,1,0:T(8,128)(2,1)S(1)} %fusion.14.refs_0_.left), channel_id=1, source_target_pairs={{0,2},{2,0},{1,3},{3,1},{4,6},{6,4},{5,7},{7,5},{8,10},{10,8},{9,1... | collective-permute-start | bytes 294920 | tf_op jit(solution)/shard_map/ppermute | solution.py:305
  77.5 1.5 %collective-permute-start.14 = (bf16[16,24,128]{2,1,0:T(8,128)(2,1)S(1)}, bf16[16,24,128]{2,1,0:T(8,128)(2,1)S(1)}, u32[]{:S(2)}, u32[]{:S(2)}) collective-permute-start(bf16[16,24,128]{2,1,0:T(8,128)(2,1)S(1)} %fusion.5), channel_id=1, source_target_pairs={{0,8},{4,12},{8,0},{12,4},{1,9},{5,13},{9,1},{13,5},{2,10},{6,14},... | collective-permute-start | bytes 294920 | tf_op jit(solution)/shard_map/ppermute | solution.py:301
  79.0 0.6 collective-permute-start.48
  79.6 0.8 unpack_panel.21.panel.refs_10_
  80.5 5.1 %forward_step.5.refs_0_ = bf16[16,24,128]{2,1,0:T(8,128)(2,1)S(1)} custom-call(s32[2]{0:T(128)S(1)} %pad_add_fusion.meta, s32[64,3]{1,0:T(8,128)S(1)} %copy.23.cols_own.cols, s32[32,3]{1,0:T(8,128)S(1)} %collective-permute-done.2.cols_other, bf16[64,3,128,128]{3,2,1,0:T(8,128)(2,1)S(1)} %copy-done.1, ...), custom_call_target="tpu_custom_call" | custom-call | flops 100663296 | bytes 6291456 | tf_op jit(solution)/shard_map/forward_step/pallas_call | solution.py:148
  85.7 1.5 %collective-permute-start.40 = (bf16[16,24,128]{2,1,0:T(8,128)(2,1)S(1)}, bf16[16,24,128]{2,1,0:T(8,128)(2,1)S(1)}, u32[]{:S(2)}, u32[]{:S(2)}) collective-permute-start(bf16[16,24,128]{2,1,0:T(8,128)(2,1)S(1)} %forward_step.5.refs_0_), channel_id=1, source_target_pairs={{0,8},{4,12},{8,0},{12,4},{1,9},{5,13},{9,1},{13,5},{2,10},{6,14},... | collective-permute-start | bytes 294920 | tf_op jit(solution)/shard_map/ppermute | solution.py:301
  87.4 3.9 %backward_step.5 = (bf16[4,16,24,128]{3,2,1,0:T(8,128)(2,1)S(1)}, bf16[4,16,24,128]{3,2,1,0:T(8,128)(2,1)S(1)}) custom-call(s32[2]{0:T(128)S(1)} %pad_add_fusion.meta, s32[64,3]{1,0:T(8,128)S(1)} %copy.23.cols_own.cols, s32[32,3]{1,0:T(8,128)S(1)} %collective-permute-done.2.cols_other, bf16[64,3,128,128]{3,2,1,0:T(8,128)(2,1)S(1)} %copy-done.1, ...), custom_call_target="tpu_custom_call" | custom-call | flops 100663296 | bytes 6291456 | tf_op jit(solution)/shard_map/backward_step/pallas_call | solution.py:221
  91.8 2.1 %collective-permute-done.40.refs_2_ = bf16[16,24,128]{2,1,0:T(8,128)(2,1)S(1)} collective-permute-done((bf16[16,24,128]{2,1,0:T(8,128)(2,1)S(1)}, bf16[16,24,128]{2,1,0:T(8,128)(2,1)S(1)}, u32[]{:S(2)}, u32[]{:S(2)}) %collective-permute-start.40) | collective-permute-done | bytes 98336 | tf_op jit(solution)/shard_map/ppermute | solution.py:301
  93.9 2.0 %collective-permute-start.41 = (bf16[16,24,128]{2,1,0:T(8,128)(2,1)S(1)}, bf16[16,24,128]{2,1,0:T(8,128)(2,1)S(1)}, u32[]{:S(2)}, u32[]{:S(2)}) collective-permute-start(bf16[16,24,128]{2,1,0:T(8,128)(2,1)S(1)} %collective-permute-done.40.refs_2_), channel_id=1, source_target_pairs={{0,4},{4,0},{8,12},{12,8},{1,5},{5,1},{9,13},{13,9},{2,6},{6,2},{1... | collective-permute-start | bytes 294920 | tf_op jit(solution)/shard_map/ppermute | solution.py:301
  95.9 0.6 unpack_panel.14.refs_2_
  96.6 0.6 unpack_panel.15.refs_3_
  97.2 0.6 collective-permute-start.44
  97.8 1.7 %collective-permute-done.39.refs_1_ = bf16[16,24,128]{2,1,0:T(8,128)(2,1)S(1)} collective-permute-done((bf16[16,24,128]{2,1,0:T(8,128)(2,1)S(1)}, bf16[16,24,128]{2,1,0:T(8,128)(2,1)S(1)}, u32[]{:S(2)}, u32[]{:S(2)}) %collective-permute-start.39) | collective-permute-done | bytes 98336 | tf_op jit(solution)/shard_map/ppermute | solution.py:301
  99.5 1.2 collective-permute-done.41.refs_3_
  100.8 0.6 collective-permute-start.51
  101.4 1.5 %collective-permute-start.46 = (bf16[64,24,128]{2,1,0:T(8,128)(2,1)S(1)}, bf16[64,24,128]{2,1,0:T(8,128)(2,1)S(1)}, u32[]{:S(2)}, u32[]{:S(2)}) collective-permute-start(bf16[64,24,128]{2,1,0:T(8,128)(2,1)S(1)} %pad_maximum_fusion), channel_id=1, source_target_pairs={{0,2},{2,0},{1,3},{3,1},{4,6},{6,4},{5,7},{7,5},{8,10},{10,8},{9,1... | collective-permute-start | bytes 1179656 | tf_op jit(solution)/shard_map/ppermute | solution.py:305
  102.9 0.8 unpack_panel.22.refs_8_
  104.2 0.8 unpack_panel.25.refs_13_
  105.1 0.7 collective-permute-start.16
  105.8 3.3 %collective-permute-done.20 = bf16[16,24,128]{2,1,0:T(8,128)(2,1)S(1)} collective-permute-done((bf16[16,24,128]{2,1,0:T(8,128)(2,1)S(1)}, bf16[16,24,128]{2,1,0:T(8,128)(2,1)S(1)}, u32[]{:S(2)}, u32[]{:S(2)}) %collective-permute-start.20) | collective-permute-done | bytes 98336 | tf_op jit(solution)/shard_map/ppermute | solution.py:301
  109.4 3.9 %collective-permute-done.46 = bf16[64,24,128]{2,1,0:T(8,128)(2,1)S(1)} collective-permute-done((bf16[64,24,128]{2,1,0:T(8,128)(2,1)S(1)}, bf16[64,24,128]{2,1,0:T(8,128)(2,1)S(1)}, u32[]{:S(2)}, u32[]{:S(2)}) %collective-permute-start.46) | collective-permute-done | bytes 393248 | tf_op jit(solution)/shard_map/ppermute | solution.py:305
  113.3 1.2 collective-permute-start.21
  114.7 0.5 collective-permute-start.17
  115.2 4.5 %collective-permute-done.21 = bf16[16,24,128]{2,1,0:T(8,128)(2,1)S(1)} collective-permute-done((bf16[16,24,128]{2,1,0:T(8,128)(2,1)S(1)}, bf16[16,24,128]{2,1,0:T(8,128)(2,1)S(1)}, u32[]{:S(2)}, u32[]{:S(2)}) %collective-permute-start.21) | collective-permute-done | bytes 98336 | tf_op jit(solution)/shard_map/ppermute | solution.py:301
  119.7 1.6 %collective-permute-start.23 = (bf16[16,24,128]{2,1,0:T(8,128)(2,1)S(1)}, bf16[16,24,128]{2,1,0:T(8,128)(2,1)S(1)}, u32[]{:S(2)}, u32[]{:S(2)}) collective-permute-start(bf16[16,24,128]{2,1,0:T(8,128)(2,1)S(1)} %fusion.4.refs_0_), channel_id=1, source_target_pairs={{0,2},{2,0},{1,3},{3,1},{4,6},{6,4},{5,7},{7,5},{8,10},{10,8},{9,1... | collective-permute-start | bytes 294920 | tf_op jit(solution)/shard_map/ppermute | solution.py:305
  121.3 0.8 unpack_panel.24.refs_11_
  122.2 0.6 unpack_panel.16.refs_4_
  122.8 0.6 unpack_panel.17.refs_5_
  123.5 0.9 collective-permute-done.23.refs_0_
  124.5 0.8 unpack_panel.23.refs_9_
  125.3 0.6 unpack_panel.18.refs_6_
  125.9 0.6 unpack_panel.19.refs_7_
  126.6 6.7 %gradient.1 = bf16[64,3,128,128]{3,2,1,0:T(8,128)(2,1)} custom-call(s32[2]{0:T(128)S(1)} %pad_add_fusion.meta, s32[64,3]{1,0:T(8,128)S(1)} %copy.23.cols_own.cols, bf16[256,16,128]{2,1,0:T(8,128)(2,1)S(1)} %get-tuple-element.13.panel.refs_0_.refs_14_, bf16[256,16,128]{2,1,0:T(8,128)(2,1)S(1)} %unpack_panel.13.refs_1_.refs_15_, ...), custom_call_target="tpu_custom_call" | custom-call | tf_op jit(solution)/shard_map/gradient/pallas_call | solution.py:273
  (95 shorter events, 5.7 us)
Async XLA Ops:
  0.0 4.4 %copy-start.3 = (s32[64,3]{0,1:T(4,128)S(1)}, s32[64,3]{0,1:T(4,128)}, u32[]{:S(2)}) copy-start(s32[64,3]{0,1:T(4,128)} %param.4) | copy-start | bytes 2308
  4.0 6.0 %collective-permute-start.3 = (bf16[32,3,128,128]{3,2,1,0:T(8,128)(2,1)}, bf16[32,3,128,128]{3,2,1,0:T(8,128)(2,1)S(1)}, u32[]{:S(2)}, u32[]{:S(2)}) collective-permute-start(bf16[32,3,128,128]{3,2,1,0:T(8,128)(2,1)} %constant_dynamic-slice_fusion), channel_id=1, source_target_pairs={{0,1},{1,0},{2,3},{3,2},{4,5},{5,4},{6,7},{7,6},{8,9},{9,8},{10,11... | collective-permute-start | bytes 9437192 | tf_op jit(solution)/shard_map/ppermute | solution.py:298
  4.5 5.1 %collective-permute-start.2 = (s32[32,3]{1,0:T(8,128)S(1)}, s32[32,3]{1,0:T(8,128)S(1)}, u32[]{:S(2)}, u32[]{:S(2)}) collective-permute-start(s32[32,3]{1,0:T(8,128)S(1)} %constant_dynamic-slice_fusion.1), channel_id=1, source_target_pairs={{0,1},{1,0},{2,3},{3,2},{4,5},{5,4},{6,7},{7,6},{8,9},{9,8},{10,11... | collective-permute-start | bytes 1160 | tf_op jit(solution)/shard_map/ppermute | solution.py:298
  10.0 2.8 %copy-start = (bf16[64,3,128,128]{3,2,1,0:T(8,128)(2,1)S(1)}, bf16[64,3,128,128]{3,2,1,0:T(8,128)(2,1)}, u32[]{:S(2)}) copy-start(bf16[64,3,128,128]{3,2,1,0:T(8,128)(2,1)} %own.11) | copy-start | bytes 18874372
  12.7 8.7 %copy-start.2 = (s32[256,12,128]{2,0,1:T(8,128)S(1)}, s32[256,12,128]{2,0,1:T(8,128)}, u32[]{:S(2)}) copy-start(s32[256,12,128]{2,0,1:T(8,128)} %param.5) | copy-start | bytes 4718596
  16.6 1.8 %collective-permute-start.4 = (bf16[4,16,24,128]{3,2,1,0:T(8,128)(2,1)S(1)}, bf16[4,16,24,128]{3,2,1,0:T(8,128)(2,1)S(1)}, u32[]{:S(2)}, u32[]{:S(2)}) collective-permute-start(bf16[4,16,24,128]{3,2,1,0:T(8,128)(2,1)S(1)} %get-tuple-element.16), channel_id=1, source_target_pairs={{0,1},{1,0},{2,3},{3,2},{4,5},{5,4},{6,7},{7,6},{8,9},{9,8},{10,11... | collective-permute-start | bytes 1179656 | tf_op jit(solution)/shard_map/ppermute | solution.py:298
  18.4 15.9 %copy-start.1 = (bf16[64,3,128,128]{3,2,1,0:T(8,128)(2,1)S(1)}, bf16[64,3,128,128]{3,2,1,0:T(8,128)(2,1)}, u32[]{:S(2)}) copy-start(bf16[64,3,128,128]{3,2,1,0:T(8,128)(2,1)} %own.11) | copy-start | bytes 18874372
  18.5 6.9 %collective-permute-start.6 = (bf16[16,24,128]{2,1,0:T(8,128)(2,1)S(1)}, bf16[16,24,128]{2,1,0:T(8,128)(2,1)S(1)}, u32[]{:S(2)}, u32[]{:S(2)}) collective-permute-start(bf16[16,24,128]{2,1,0:T(8,128)(2,1)S(1)} %get-tuple-element.26), channel_id=1, source_target_pairs={{0,4},{4,0},{8,12},{12,8},{1,5},{5,1},{9,13},{13,9},{2,6},{6,2},{1... | collective-permute-start | bytes 294920 | tf_op jit(solution)/shard_map/ppermute | solution.py:301
  23.4 10.9 %collective-permute-start = (bf16[64,24,128]{2,1,0:T(8,128)(2,1)S(1)}, bf16[64,24,128]{2,1,0:T(8,128)(2,1)S(1)}, u32[]{:S(2)}, u32[]{:S(2)}) collective-permute-start(bf16[64,24,128]{2,1,0:T(8,128)(2,1)S(1)} %get-tuple-element.14), channel_id=1, source_target_pairs={{0,2},{2,0},{1,3},{3,1},{4,6},{6,4},{5,7},{7,5},{8,10},{10,8},{9,1... | collective-permute-start | bytes 1179656 | tf_op jit(solution)/shard_map/ppermute | solution.py:305
  25.0 17.1 %collective-permute-start.5 = (bf16[16,24,128]{2,1,0:T(8,128)(2,1)S(1)}, bf16[16,24,128]{2,1,0:T(8,128)(2,1)S(1)}, u32[]{:S(2)}, u32[]{:S(2)}) collective-permute-start(bf16[16,24,128]{2,1,0:T(8,128)(2,1)S(1)} %get-tuple-element.25), channel_id=1, source_target_pairs={{0,4},{4,0},{8,12},{12,8},{1,5},{5,1},{9,13},{13,9},{2,6},{6,2},{1... | collective-permute-start | bytes 294920 | tf_op jit(solution)/shard_map/ppermute | solution.py:301
  25.5 16.6 %collective-permute-start.7 = (bf16[16,24,128]{2,1,0:T(8,128)(2,1)S(1)}, bf16[16,24,128]{2,1,0:T(8,128)(2,1)S(1)}, u32[]{:S(2)}, u32[]{:S(2)}) collective-permute-start(bf16[16,24,128]{2,1,0:T(8,128)(2,1)S(1)} %fusion.10), channel_id=1, source_target_pairs={{0,8},{4,12},{8,0},{12,4},{1,9},{5,13},{9,1},{13,5},{2,10},{6,14},... | collective-permute-start | bytes 294920 | tf_op jit(solution)/shard_map/ppermute | solution.py:301
  34.4 26.9 %collective-permute-start.1 = (bf16[64,24,128]{2,1,0:T(8,128)(2,1)S(1)}, bf16[64,24,128]{2,1,0:T(8,128)(2,1)S(1)}, u32[]{:S(2)}, u32[]{:S(2)}) collective-permute-start(bf16[64,24,128]{2,1,0:T(8,128)(2,1)S(1)} %collective-permute-done.refs_0_), channel_id=1, source_target_pairs={{0,1},{1,0},{2,3},{3,2},{4,5},{5,4},{6,7},{7,6},{8,9},{9,8},{10,11... | collective-permute-start | bytes 1179656 | tf_op jit(solution)/shard_map/ppermute | solution.py:298
  39.5 8.1 %collective-permute-start.26 = (bf16[16,24,128]{2,1,0:T(8,128)(2,1)S(1)}, bf16[16,24,128]{2,1,0:T(8,128)(2,1)S(1)}, u32[]{:S(2)}, u32[]{:S(2)}) collective-permute-start(bf16[16,24,128]{2,1,0:T(8,128)(2,1)S(1)} %forward_step.3.refs_0_), channel_id=1, source_target_pairs={{0,8},{4,12},{8,0},{12,4},{1,9},{5,13},{9,1},{13,5},{2,10},{6,14},... | collective-permute-start | bytes 294920 | tf_op jit(solution)/shard_map/ppermute | solution.py:301
  46.1 22.7 %collective-permute-start.11 = (bf16[4,16,24,128]{3,2,1,0:T(8,128)(2,1)S(1)}, bf16[4,16,24,128]{3,2,1,0:T(8,128)(2,1)S(1)}, u32[]{:S(2)}, u32[]{:S(2)}) collective-permute-start(bf16[4,16,24,128]{3,2,1,0:T(8,128)(2,1)S(1)} %get-tuple-element.18), channel_id=1, source_target_pairs={{0,1},{1,0},{2,3},{3,2},{4,5},{5,4},{6,7},{7,6},{8,9},{9,8},{10,11... | collective-permute-start | bytes 1179656 | tf_op jit(solution)/shard_map/ppermute | solution.py:298
  46.4 2.3 %collective-permute-start.28 = (bf16[16,24,128]{2,1,0:T(8,128)(2,1)S(1)}, bf16[16,24,128]{2,1,0:T(8,128)(2,1)S(1)}, u32[]{:S(2)}, u32[]{:S(2)}) collective-permute-start(bf16[16,24,128]{2,1,0:T(8,128)(2,1)S(1)} %forward_step.3.refs_0_), channel_id=1, source_target_pairs={{0,1},{1,0},{2,3},{3,2},{4,5},{5,4},{6,7},{7,6},{8,9},{9,8},{10,11... | collective-permute-start | bytes 294920 | tf_op jit(solution)/shard_map/ppermute | solution.py:298
  46.6 5.6 %collective-permute-start.25 = (bf16[16,24,128]{2,1,0:T(8,128)(2,1)S(1)}, bf16[16,24,128]{2,1,0:T(8,128)(2,1)S(1)}, u32[]{:S(2)}, u32[]{:S(2)}) collective-permute-start(bf16[16,24,128]{2,1,0:T(8,128)(2,1)S(1)} %forward_step.3.refs_0_), channel_id=1, source_target_pairs={{0,4},{4,0},{8,12},{12,8},{1,5},{5,1},{9,13},{13,9},{2,6},{6,2},{1... | collective-permute-start | bytes 294920 | tf_op jit(solution)/shard_map/ppermute | solution.py:301
  47.5 6.1 %collective-permute-start.27 = (bf16[16,24,128]{2,1,0:T(8,128)(2,1)S(1)}, bf16[16,24,128]{2,1,0:T(8,128)(2,1)S(1)}, u32[]{:S(2)}, u32[]{:S(2)}) collective-permute-start(bf16[16,24,128]{2,1,0:T(8,128)(2,1)S(1)} %collective-permute-done.26.refs_2_), channel_id=1, source_target_pairs={{0,4},{4,0},{8,12},{12,8},{1,5},{5,1},{9,13},{13,9},{2,6},{6,2},{1... | collective-permute-start | bytes 294920 | tf_op jit(solution)/shard_map/ppermute | solution.py:301
  48.7 5.0 %collective-permute-start.30 = (bf16[16,24,128]{2,1,0:T(8,128)(2,1)S(1)}, bf16[16,24,128]{2,1,0:T(8,128)(2,1)S(1)}, u32[]{:S(2)}, u32[]{:S(2)}) collective-permute-start(bf16[16,24,128]{2,1,0:T(8,128)(2,1)S(1)} %collective-permute-done.26.refs_2_), channel_id=1, source_target_pairs={{0,1},{1,0},{2,3},{3,2},{4,5},{5,4},{6,7},{7,6},{8,9},{9,8},{10,11... | collective-permute-start | bytes 294920 | tf_op jit(solution)/shard_map/ppermute | solution.py:298
  52.3 1.4 %collective-permute-start.29 = (bf16[16,24,128]{2,1,0:T(8,128)(2,1)S(1)}, bf16[16,24,128]{2,1,0:T(8,128)(2,1)S(1)}, u32[]{:S(2)}, u32[]{:S(2)}) collective-permute-start(bf16[16,24,128]{2,1,0:T(8,128)(2,1)S(1)} %collective-permute-done.25.refs_1_), channel_id=1, source_target_pairs={{0,1},{1,0},{2,3},{3,2},{4,5},{5,4},{6,7},{7,6},{8,9},{9,8},{10,11... | collective-permute-start | bytes 294920 | tf_op jit(solution)/shard_map/ppermute | solution.py:298
  53.7 1.3 collective-permute-start.31
  60.9 7.9 %collective-permute-start.33 = (bf16[16,24,128]{2,1,0:T(8,128)(2,1)S(1)}, bf16[16,24,128]{2,1,0:T(8,128)(2,1)S(1)}, u32[]{:S(2)}, u32[]{:S(2)}) collective-permute-start(bf16[16,24,128]{2,1,0:T(8,128)(2,1)S(1)} %forward_step.4.refs_0_), channel_id=1, source_target_pairs={{0,8},{4,12},{8,0},{12,4},{1,9},{5,13},{9,1},{13,5},{2,10},{6,14},... | collective-permute-start | bytes 294920 | tf_op jit(solution)/shard_map/ppermute | solution.py:301
  62.1 10.5 %collective-permute-start.32 = (bf16[16,24,128]{2,1,0:T(8,128)(2,1)S(1)}, bf16[16,24,128]{2,1,0:T(8,128)(2,1)S(1)}, u32[]{:S(2)}, u32[]{:S(2)}) collective-permute-start(bf16[16,24,128]{2,1,0:T(8,128)(2,1)S(1)} %forward_step.4.refs_0_), channel_id=1, source_target_pairs={{0,4},{4,0},{8,12},{12,8},{1,5},{5,1},{9,13},{13,9},{2,6},{6,2},{1... | collective-permute-start | bytes 294920 | tf_op jit(solution)/shard_map/ppermute | solution.py:301
  68.8 5.7 %collective-permute-start.34 = (bf16[16,24,128]{2,1,0:T(8,128)(2,1)S(1)}, bf16[16,24,128]{2,1,0:T(8,128)(2,1)S(1)}, u32[]{:S(2)}, u32[]{:S(2)}) collective-permute-start(bf16[16,24,128]{2,1,0:T(8,128)(2,1)S(1)} %collective-permute-done.33.refs_2_), channel_id=1, source_target_pairs={{0,4},{4,0},{8,12},{12,8},{1,5},{5,1},{9,13},{13,9},{2,6},{6,2},{1... | collective-permute-start | bytes 294920 | tf_op jit(solution)/shard_map/ppermute | solution.py:301
  68.8 6.7 %collective-permute-start.13 = (bf16[16,24,128]{2,1,0:T(8,128)(2,1)S(1)}, bf16[16,24,128]{2,1,0:T(8,128)(2,1)S(1)}, u32[]{:S(2)}, u32[]{:S(2)}) collective-permute-start(bf16[16,24,128]{2,1,0:T(8,128)(2,1)S(1)} %get-tuple-element.24), channel_id=1, source_target_pairs={{0,4},{4,0},{8,12},{12,8},{1,5},{5,1},{9,13},{13,9},{2,6},{6,2},{1... | collective-permute-start | bytes 294920 | tf_op jit(solution)/shard_map/ppermute | solution.py:301
  71.0 20.3 %collective-permute-start.50 = (bf16[64,24,128]{2,1,0:T(8,128)(2,1)S(1)}, bf16[64,24,128]{2,1,0:T(8,128)(2,1)S(1)}, u32[]{:S(2)}, u32[]{:S(2)}) collective-permute-start(bf16[64,24,128]{2,1,0:T(8,128)(2,1)S(1)} %pad_maximum_fusion.2), channel_id=1, source_target_pairs={{0,2},{2,0},{1,3},{3,1},{4,6},{6,4},{5,7},{7,5},{8,10},{10,8},{9,1... | collective-permute-start | bytes 1179656 | tf_op jit(solution)/shard_map/ppermute | solution.py:305
  72.5 3.1 %collective-permute-start.35 = (bf16[16,24,128]{2,1,0:T(8,128)(2,1)S(1)}, bf16[16,24,128]{2,1,0:T(8,128)(2,1)S(1)}, u32[]{:S(2)}, u32[]{:S(2)}) collective-permute-start(bf16[16,24,128]{2,1,0:T(8,128)(2,1)S(1)} %forward_step.4.refs_0_), channel_id=1, source_target_pairs={{0,1},{1,0},{2,3},{3,2},{4,5},{5,4},{6,7},{7,6},{8,9},{9,8},{10,11... | collective-permute-start | bytes 294920 | tf_op jit(solution)/shard_map/ppermute | solution.py:298
  72.6 4.6 %collective-permute-start.37 = (bf16[16,24,128]{2,1,0:T(8,128)(2,1)S(1)}, bf16[16,24,128]{2,1,0:T(8,128)(2,1)S(1)}, u32[]{:S(2)}, u32[]{:S(2)}) collective-permute-start(bf16[16,24,128]{2,1,0:T(8,128)(2,1)S(1)} %collective-permute-done.33.refs_2_), channel_id=1, source_target_pairs={{0,1},{1,0},{2,3},{3,2},{4,5},{5,4},{6,7},{7,6},{8,9},{9,8},{10,11... | collective-permute-start | bytes 294920 | tf_op jit(solution)/shard_map/ppermute | solution.py:298
  74.4 3.0 %collective-permute-start.36 = (bf16[16,24,128]{2,1,0:T(8,128)(2,1)S(1)}, bf16[16,24,128]{2,1,0:T(8,128)(2,1)S(1)}, u32[]{:S(2)}, u32[]{:S(2)}) collective-permute-start(bf16[16,24,128]{2,1,0:T(8,128)(2,1)S(1)} %collective-permute-done.32.refs_1_), channel_id=1, source_target_pairs={{0,1},{1,0},{2,3},{3,2},{4,5},{5,4},{6,7},{7,6},{8,9},{9,8},{10,11... | collective-permute-start | bytes 294920 | tf_op jit(solution)/shard_map/ppermute | solution.py:298
  75.6 3.4 %collective-permute-start.38 = (bf16[16,24,128]{2,1,0:T(8,128)(2,1)S(1)}, bf16[16,24,128]{2,1,0:T(8,128)(2,1)S(1)}, u32[]{:S(2)}, u32[]{:S(2)}) collective-permute-start(bf16[16,24,128]{2,1,0:T(8,128)(2,1)S(1)} %collective-permute-done.34.refs_3_), channel_id=1, source_target_pairs={{0,1},{1,0},{2,3},{3,2},{4,5},{5,4},{6,7},{7,6},{8,9},{9,8},{10,11... | collective-permute-start | bytes 294920 | tf_op jit(solution)/shard_map/ppermute | solution.py:298
  75.6 9.9 %collective-permute-start.9 = (bf16[16,24,128]{2,1,0:T(8,128)(2,1)S(1)}, bf16[16,24,128]{2,1,0:T(8,128)(2,1)S(1)}, u32[]{:S(2)}, u32[]{:S(2)}) collective-permute-start(bf16[16,24,128]{2,1,0:T(8,128)(2,1)S(1)} %fusion.14.refs_0_.left), channel_id=1, source_target_pairs={{0,2},{2,0},{1,3},{3,1},{4,6},{6,4},{5,7},{7,5},{8,10},{10,8},{9,1... | collective-permute-start | bytes 294920 | tf_op jit(solution)/shard_map/ppermute | solution.py:305
  77.2 8.5 %collective-permute-start.12 = (bf16[16,24,128]{2,1,0:T(8,128)(2,1)S(1)}, bf16[16,24,128]{2,1,0:T(8,128)(2,1)S(1)}, u32[]{:S(2)}, u32[]{:S(2)}) collective-permute-start(bf16[16,24,128]{2,1,0:T(8,128)(2,1)S(1)} %get-tuple-element.23), channel_id=1, source_target_pairs={{0,4},{4,0},{8,12},{12,8},{1,5},{5,1},{9,13},{13,9},{2,6},{6,2},{1... | collective-permute-start | bytes 294920 | tf_op jit(solution)/shard_map/ppermute | solution.py:301
  77.5 9.7 %collective-permute-start.14 = (bf16[16,24,128]{2,1,0:T(8,128)(2,1)S(1)}, bf16[16,24,128]{2,1,0:T(8,128)(2,1)S(1)}, u32[]{:S(2)}, u32[]{:S(2)}) collective-permute-start(bf16[16,24,128]{2,1,0:T(8,128)(2,1)S(1)} %fusion.5), channel_id=1, source_target_pairs={{0,8},{4,12},{8,0},{12,4},{1,9},{5,13},{9,1},{13,5},{2,10},{6,14},... | collective-permute-start | bytes 294920 | tf_op jit(solution)/shard_map/ppermute | solution.py:301
  79.0 23.9 %collective-permute-start.48 = (bf16[64,24,128]{2,1,0:T(8,128)(2,1)S(1)}, bf16[64,24,128]{2,1,0:T(8,128)(2,1)S(1)}, u32[]{:S(2)}, u32[]{:S(2)}) collective-permute-start(bf16[64,24,128]{2,1,0:T(8,128)(2,1)S(1)} %pad_maximum_fusion.1), channel_id=1, source_target_pairs={{0,2},{2,0},{1,3},{3,1},{4,6},{6,4},{5,7},{7,5},{8,10},{10,8},{9,1... | collective-permute-start | bytes 1179656 | tf_op jit(solution)/shard_map/ppermute | solution.py:305
  85.6 8.3 %collective-permute-start.8 = (bf16[16,24,128]{2,1,0:T(8,128)(2,1)S(1)}, bf16[16,24,128]{2,1,0:T(8,128)(2,1)S(1)}, u32[]{:S(2)}, u32[]{:S(2)}) collective-permute-start(bf16[16,24,128]{2,1,0:T(8,128)(2,1)S(1)} %fusion.14.refs_0_.left), channel_id=1, source_target_pairs={{0,1},{1,0},{2,3},{3,2},{4,5},{5,4},{6,7},{7,6},{8,9},{9,8},{10,11... | collective-permute-start | bytes 294920 | tf_op jit(solution)/shard_map/ppermute | solution.py:298
  85.7 8.2 %collective-permute-start.40 = (bf16[16,24,128]{2,1,0:T(8,128)(2,1)S(1)}, bf16[16,24,128]{2,1,0:T(8,128)(2,1)S(1)}, u32[]{:S(2)}, u32[]{:S(2)}) collective-permute-start(bf16[16,24,128]{2,1,0:T(8,128)(2,1)S(1)} %forward_step.5.refs_0_), channel_id=1, source_target_pairs={{0,8},{4,12},{8,0},{12,4},{1,9},{5,13},{9,1},{13,5},{2,10},{6,14},... | collective-permute-start | bytes 294920 | tf_op jit(solution)/shard_map/ppermute | solution.py:301
  87.2 8.7 %collective-permute-start.10 = (bf16[16,24,128]{2,1,0:T(8,128)(2,1)S(1)}, bf16[16,24,128]{2,1,0:T(8,128)(2,1)S(1)}, u32[]{:S(2)}, u32[]{:S(2)}) collective-permute-start(bf16[16,24,128]{2,1,0:T(8,128)(2,1)S(1)} %collective-permute-done.9.refs_0_), channel_id=1, source_target_pairs={{0,1},{1,0},{2,3},{3,2},{4,5},{5,4},{6,7},{7,6},{8,9},{9,8},{10,11... | collective-permute-start | bytes 294920 | tf_op jit(solution)/shard_map/ppermute | solution.py:298
  91.3 5.9 %collective-permute-start.42 = (bf16[16,24,128]{2,1,0:T(8,128)(2,1)S(1)}, bf16[16,24,128]{2,1,0:T(8,128)(2,1)S(1)}, u32[]{:S(2)}, u32[]{:S(2)}) collective-permute-start(bf16[16,24,128]{2,1,0:T(8,128)(2,1)S(1)} %forward_step.5.refs_0_), channel_id=1, source_target_pairs={{0,1},{1,0},{2,3},{3,2},{4,5},{5,4},{6,7},{7,6},{8,9},{9,8},{10,11... | collective-permute-start | bytes 294920 | tf_op jit(solution)/shard_map/ppermute | solution.py:298
  93.9 5.6 %collective-permute-start.39 = (bf16[16,24,128]{2,1,0:T(8,128)(2,1)S(1)}, bf16[16,24,128]{2,1,0:T(8,128)(2,1)S(1)}, u32[]{:S(2)}, u32[]{:S(2)}) collective-permute-start(bf16[16,24,128]{2,1,0:T(8,128)(2,1)S(1)} %forward_step.5.refs_0_), channel_id=1, source_target_pairs={{0,4},{4,0},{8,12},{12,8},{1,5},{5,1},{9,13},{13,9},{2,6},{6,2},{1... | collective-permute-start | bytes 294920 | tf_op jit(solution)/shard_map/ppermute | solution.py:301
  93.9 6.9 %collective-permute-start.41 = (bf16[16,24,128]{2,1,0:T(8,128)(2,1)S(1)}, bf16[16,24,128]{2,1,0:T(8,128)(2,1)S(1)}, u32[]{:S(2)}, u32[]{:S(2)}) collective-permute-start(bf16[16,24,128]{2,1,0:T(8,128)(2,1)S(1)} %collective-permute-done.40.refs_2_), channel_id=1, source_target_pairs={{0,4},{4,0},{8,12},{12,8},{1,5},{5,1},{9,13},{13,9},{2,6},{6,2},{1... | collective-permute-start | bytes 294920 | tf_op jit(solution)/shard_map/ppermute | solution.py:301
  95.9 7.9 %collective-permute-start.18 = (bf16[4,16,24,128]{3,2,1,0:T(8,128)(2,1)S(1)}, bf16[4,16,24,128]{3,2,1,0:T(8,128)(2,1)S(1)}, u32[]{:S(2)}, u32[]{:S(2)}) collective-permute-start(bf16[4,16,24,128]{3,2,1,0:T(8,128)(2,1)S(1)} %get-tuple-element.20), channel_id=1, source_target_pairs={{0,1},{1,0},{2,3},{3,2},{4,5},{5,4},{6,7},{7,6},{8,9},{9,8},{10,11... | collective-permute-start | bytes 1179656 | tf_op jit(solution)/shard_map/ppermute | solution.py:298
  97.2 3.6 %collective-permute-start.44 = (bf16[16,24,128]{2,1,0:T(8,128)(2,1)S(1)}, bf16[16,24,128]{2,1,0:T(8,128)(2,1)S(1)}, u32[]{:S(2)}, u32[]{:S(2)}) collective-permute-start(bf16[16,24,128]{2,1,0:T(8,128)(2,1)S(1)} %collective-permute-done.40.refs_2_), channel_id=1, source_target_pairs={{0,1},{1,0},{2,3},{3,2},{4,5},{5,4},{6,7},{7,6},{8,9},{9,8},{10,11... | collective-permute-start | bytes 294920 | tf_op jit(solution)/shard_map/ppermute | solution.py:298
  99.5 1.9 %collective-permute-start.43 = (bf16[16,24,128]{2,1,0:T(8,128)(2,1)S(1)}, bf16[16,24,128]{2,1,0:T(8,128)(2,1)S(1)}, u32[]{:S(2)}, u32[]{:S(2)}) collective-permute-start(bf16[16,24,128]{2,1,0:T(8,128)(2,1)S(1)} %collective-permute-done.39.refs_1_), channel_id=1, source_target_pairs={{0,1},{1,0},{2,3},{3,2},{4,5},{5,4},{6,7},{7,6},{8,9},{9,8},{10,11... | collective-permute-start | bytes 294920 | tf_op jit(solution)/shard_map/ppermute | solution.py:298
  100.7 2.1 %collective-permute-start.45 = (bf16[16,24,128]{2,1,0:T(8,128)(2,1)S(1)}, bf16[16,24,128]{2,1,0:T(8,128)(2,1)S(1)}, u32[]{:S(2)}, u32[]{:S(2)}) collective-permute-start(bf16[16,24,128]{2,1,0:T(8,128)(2,1)S(1)} %collective-permute-done.41.refs_3_), channel_id=1, source_target_pairs={{0,1},{1,0},{2,3},{3,2},{4,5},{5,4},{6,7},{7,6},{8,9},{9,8},{10,11... | collective-permute-start | bytes 294920 | tf_op jit(solution)/shard_map/ppermute | solution.py:298
  100.8 3.4 %collective-permute-start.51 = (bf16[64,24,128]{2,1,0:T(8,128)(2,1)S(1)}, bf16[64,24,128]{2,1,0:T(8,128)(2,1)S(1)}, u32[]{:S(2)}, u32[]{:S(2)}) collective-permute-start(bf16[64,24,128]{2,1,0:T(8,128)(2,1)S(1)} %collective-permute-done.50), channel_id=1, source_target_pairs={{0,1},{1,0},{2,3},{3,2},{4,5},{5,4},{6,7},{7,6},{8,9},{9,8},{10,11... | collective-permute-start | bytes 1179656 | tf_op jit(solution)/shard_map/ppermute | solution.py:298
  101.4 12.0 %collective-permute-start.46 = (bf16[64,24,128]{2,1,0:T(8,128)(2,1)S(1)}, bf16[64,24,128]{2,1,0:T(8,128)(2,1)S(1)}, u32[]{:S(2)}, u32[]{:S(2)}) collective-permute-start(bf16[64,24,128]{2,1,0:T(8,128)(2,1)S(1)} %pad_maximum_fusion), channel_id=1, source_target_pairs={{0,2},{2,0},{1,3},{3,1},{4,6},{6,4},{5,7},{7,5},{8,10},{10,8},{9,1... | collective-permute-start | bytes 1179656 | tf_op jit(solution)/shard_map/ppermute | solution.py:305
  102.9 18.4 %collective-permute-start.49 = (bf16[64,24,128]{2,1,0:T(8,128)(2,1)S(1)}, bf16[64,24,128]{2,1,0:T(8,128)(2,1)S(1)}, u32[]{:S(2)}, u32[]{:S(2)}) collective-permute-start(bf16[64,24,128]{2,1,0:T(8,128)(2,1)S(1)} %collective-permute-done.48), channel_id=1, source_target_pairs={{0,1},{1,0},{2,3},{3,2},{4,5},{5,4},{6,7},{7,6},{8,9},{9,8},{10,11... | collective-permute-start | bytes 1179656 | tf_op jit(solution)/shard_map/ppermute | solution.py:298
  103.8 5.3 %collective-permute-start.20 = (bf16[16,24,128]{2,1,0:T(8,128)(2,1)S(1)}, bf16[16,24,128]{2,1,0:T(8,128)(2,1)S(1)}, u32[]{:S(2)}, u32[]{:S(2)}) collective-permute-start(bf16[16,24,128]{2,1,0:T(8,128)(2,1)S(1)} %get-tuple-element.22), channel_id=1, source_target_pairs={{0,4},{4,0},{8,12},{12,8},{1,5},{5,1},{9,13},{13,9},{2,6},{6,2},{1... | collective-permute-start | bytes 294920 | tf_op jit(solution)/shard_map/ppermute | solution.py:301
  105.1 9.5 %collective-permute-start.16 = (bf16[16,24,128]{2,1,0:T(8,128)(2,1)S(1)}, bf16[16,24,128]{2,1,0:T(8,128)(2,1)S(1)}, u32[]{:S(2)}, u32[]{:S(2)}) collective-permute-start(bf16[16,24,128]{2,1,0:T(8,128)(2,1)S(1)} %fusion.9.refs_0_.left), channel_id=1, source_target_pairs={{0,2},{2,0},{1,3},{3,1},{4,6},{6,4},{5,7},{7,5},{8,10},{10,8},{9,1... | collective-permute-start | bytes 294920 | tf_op jit(solution)/shard_map/ppermute | solution.py:305
  105.8 16.4 %collective-permute-start.15 = (bf16[16,24,128]{2,1,0:T(8,128)(2,1)S(1)}, bf16[16,24,128]{2,1,0:T(8,128)(2,1)S(1)}, u32[]{:S(2)}, u32[]{:S(2)}) collective-permute-start(bf16[16,24,128]{2,1,0:T(8,128)(2,1)S(1)} %fusion.9.refs_0_.left), channel_id=1, source_target_pairs={{0,1},{1,0},{2,3},{3,2},{4,5},{5,4},{6,7},{7,6},{8,9},{9,8},{10,11... | collective-permute-start | bytes 294920 | tf_op jit(solution)/shard_map/ppermute | solution.py:298
  109.1 5.6 %collective-permute-start.19 = (bf16[16,24,128]{2,1,0:T(8,128)(2,1)S(1)}, bf16[16,24,128]{2,1,0:T(8,128)(2,1)S(1)}, u32[]{:S(2)}, u32[]{:S(2)}) collective-permute-start(bf16[16,24,128]{2,1,0:T(8,128)(2,1)S(1)} %get-tuple-element.21), channel_id=1, source_target_pairs={{0,4},{4,0},{8,12},{12,8},{1,5},{5,1},{9,13},{13,9},{2,6},{6,2},{1... | collective-permute-start | bytes 294920 | tf_op jit(solution)/shard_map/ppermute | solution.py:301
  113.3 6.3 %collective-permute-start.21 = (bf16[16,24,128]{2,1,0:T(8,128)(2,1)S(1)}, bf16[16,24,128]{2,1,0:T(8,128)(2,1)S(1)}, u32[]{:S(2)}, u32[]{:S(2)}) collective-permute-start(bf16[16,24,128]{2,1,0:T(8,128)(2,1)S(1)} %fusion), channel_id=1, source_target_pairs={{0,8},{4,12},{8,0},{12,4},{1,9},{5,13},{9,1},{13,5},{2,10},{6,14},... | collective-permute-start | bytes 294920 | tf_op jit(solution)/shard_map/ppermute | solution.py:301
  114.6 9.8 %collective-permute-start.47 = (bf16[64,24,128]{2,1,0:T(8,128)(2,1)S(1)}, bf16[64,24,128]{2,1,0:T(8,128)(2,1)S(1)}, u32[]{:S(2)}, u32[]{:S(2)}) collective-permute-start(bf16[64,24,128]{2,1,0:T(8,128)(2,1)S(1)} %collective-permute-done.46), channel_id=1, source_target_pairs={{0,1},{1,0},{2,3},{3,2},{4,5},{5,4},{6,7},{7,6},{8,9},{9,8},{10,11... | collective-permute-start | bytes 1179656 | tf_op jit(solution)/shard_map/ppermute | solution.py:298
  114.7 8.1 %collective-permute-start.17 = (bf16[16,24,128]{2,1,0:T(8,128)(2,1)S(1)}, bf16[16,24,128]{2,1,0:T(8,128)(2,1)S(1)}, u32[]{:S(2)}, u32[]{:S(2)}) collective-permute-start(bf16[16,24,128]{2,1,0:T(8,128)(2,1)S(1)} %collective-permute-done.16.refs_0_), channel_id=1, source_target_pairs={{0,1},{1,0},{2,3},{3,2},{4,5},{5,4},{6,7},{7,6},{8,9},{9,8},{10,11... | collective-permute-start | bytes 294920 | tf_op jit(solution)/shard_map/ppermute | solution.py:298
  119.7 4.7 %collective-permute-start.23 = (bf16[16,24,128]{2,1,0:T(8,128)(2,1)S(1)}, bf16[16,24,128]{2,1,0:T(8,128)(2,1)S(1)}, u32[]{:S(2)}, u32[]{:S(2)}) collective-permute-start(bf16[16,24,128]{2,1,0:T(8,128)(2,1)S(1)} %fusion.4.refs_0_), channel_id=1, source_target_pairs={{0,2},{2,0},{1,3},{3,1},{4,6},{6,4},{5,7},{7,5},{8,10},{10,8},{9,1... | collective-permute-start | bytes 294920 | tf_op jit(solution)/shard_map/ppermute | solution.py:305
  123.4 1.9 %collective-permute-start.22 = (bf16[16,24,128]{2,1,0:T(8,128)(2,1)S(1)}, bf16[16,24,128]{2,1,0:T(8,128)(2,1)S(1)}, u32[]{:S(2)}, u32[]{:S(2)}) collective-permute-start(bf16[16,24,128]{2,1,0:T(8,128)(2,1)S(1)} %fusion.4.refs_0_), channel_id=1, source_target_pairs={{0,1},{1,0},{2,3},{3,2},{4,5},{5,4},{6,7},{7,6},{8,9},{9,8},{10,11... | collective-permute-start | bytes 294920 | tf_op jit(solution)/shard_map/ppermute | solution.py:298
  124.4 1.5 %collective-permute-start.24 = (bf16[16,24,128]{2,1,0:T(8,128)(2,1)S(1)}, bf16[16,24,128]{2,1,0:T(8,128)(2,1)S(1)}, u32[]{:S(2)}, u32[]{:S(2)}) collective-permute-start(bf16[16,24,128]{2,1,0:T(8,128)(2,1)S(1)} %collective-permute-done.23.refs_0_), channel_id=1, source_target_pairs={{0,1},{1,0},{2,3},{3,2},{4,5},{5,4},{6,7},{7,6},{8,9},{9,8},{10,11... | collective-permute-start | bytes 294920 | tf_op jit(solution)/shard_map/ppermute | solution.py:298

commit v2 on v1

v2 whole, which is shorter than its diff:
```python
import functools
import math

import jax
import jax.numpy as jnp
from jax import lax
from jax.experimental import pallas as pl
from jax.experimental.pallas import tpu as pltpu
from jax.sharding import PartitionSpec as P

KS = 6
PAD = 16
VMEM_LIMIT = 24 * 1024 * 1024


def whole():
    return pl.BlockSpec(memory_space=pltpu.VMEM)


def params():
    return pltpu.CompilerParams(
        dimension_semantics=("arbitrary",), vmem_limit_bytes=VMEM_LIMIT
    )


def split_pair(pair, count):
    wide = pair.astype(jnp.float32)
    keep = lax.broadcasted_iota(jnp.int32, (PAD, wide.shape[1]), 0) < count
    first = jnp.where(keep, wide[:PAD], 0.0)
    second = jnp.where(keep, pltpu.roll(wide, count, 0)[:PAD], 0.0)
    return first, second


def join_pair(first, second, count):
    tail = jnp.zeros((2 * count - PAD, first.shape[1]), jnp.float32)
    low = jnp.concatenate([first, tail], axis=0)
    high = pltpu.roll(jnp.concatenate([second, tail], axis=0), count, 0)
    return low + high


def unpack_kernel(count, where, meta, *refs):
    panel = refs[-1]
    for ref, base_of in zip(refs[:-1], where):
        pairs = ref.shape[0]
        base = base_of(meta[0], meta[1])

        def body(i, carry, ref=ref, base=base):
            first, second = split_pair(ref[i], count)
            panel[base + 2 * i] = first.astype(jnp.bfloat16)
            panel[base + 2 * i + 1] = second.astype(jnp.bfloat16)
            return carry

        lax.fori_loop(0, pairs, body, 0, unroll=8 if pairs % 8 == 0 else 4)


def unpack(meta, pieces, where, blocks):
    count = pieces[0].shape[1] // 2
    width = pieces[0].shape[2]
    return pl.pallas_call(
        functools.partial(unpack_kernel, count, where),
        out_shape=jax.ShapeDtypeStruct((blocks, PAD, width), jnp.bfloat16),
        grid_spec=pltpu.PrefetchScalarGridSpec(
            num_scalar_prefetch=1,
            grid=(1,),
            in_specs=[whole()] * len(pieces),
            out_specs=whole(),
        ),
        compiler_params=params(),
        name="unpack_panel",
    )(meta, *pieces)


def row_product(refs_and_rows, panel, contract):
    picked = []
    stored = []
    for ref, row, cols, col_row in refs_and_rows:
        for k in range(ref.shape[1]):
            picked.append(panel[cols[col_row, k]])
            stored.append(ref[row, k])
    return lax.dot_general(
        jnp.concatenate(picked, axis=1),
        jnp.concatenate(stored, axis=1),
        contract,
        preferred_element_type=jnp.float32,
    )


LAST = (((1,), (1,)), ((), ()))
FIRST = (((1,), (0,)), ((), ()))


def first_forward_kernel(
    count, chunk, meta, cols, signs, stored, panel, sent, keep, send, near, far
):
    step = pl.program_id(0)
    blocks = signs.shape[0]
    half = near.shape[0]

    @pl.when(step == 0)
    def _():
        pad = jnp.zeros((PAD - count, signs.shape[2]), jnp.float32)

        def body(b, carry):
            value = jnp.concatenate([signs[b].astype(jnp.float32), pad], axis=0)
            panel[b] = value.astype(jnp.bfloat16)
            return carry

        lax.fori_loop(0, blocks, body, 0, unroll=8)

    row = step * chunk
    side = row // half
    base = row - side * half
    results = [
        row_product([(stored, r, cols, row + r)], panel, LAST) for r in range(chunk)
    ]
    pairs = [
        join_pair(results[i], results[i + 1], count) for i in range(0, chunk, 2)
    ]

    @pl.when(side == meta[1])
    def _():
        for i, pair in enumerate(pairs):
            keep[base // 2 + i] = pair
        near[pl.ds(base, chunk)] = stored[...]

    @pl.when(side != meta[1])
    def _():
        for i, pair in enumerate(pairs):
            send[base // 2 + i] = pair.astype(jnp.bfloat16)
        far[pl.ds(base, chunk)] = stored[...]

    @pl.when(step == pl.num_programs(0) - 1)
    def _():
        start = meta[1] * (blocks // 2)

        def pack(i, carry):
            b = start + 2 * i
            sent[i] = join_pair(
                panel[b].astype(jnp.float32), panel[b + 1].astype(jnp.float32), count
            ).astype(jnp.bfloat16)
            return carry

        lax.fori_loop(0, blocks // 4, pack, 0, unroll=8)


def first_forward(meta, cols, signs, stored):
    rows, slots, width = stored.shape[0], stored.shape[1], stored.shape[3]
    blocks, count = signs.shape[0], signs.shape[1]
    half = rows // 2
    chunk = min(16, half)
    split = jax.ShapeDtypeStruct((half, slots, width, width), jnp.bfloat16)
    return pl.pallas_call(
        functools.partial(first_forward_kernel, count, chunk),
        out_shape=(
            jax.ShapeDtypeStruct((blocks, PAD, width), jnp.bfloat16),
            jax.ShapeDtypeStruct((blocks // 4, 2 * count, width), jnp.bfloat16),
            jax.ShapeDtypeStruct((half // 2, 2 * count, width), jnp.float32),
            jax.ShapeDtypeStruct((half // 2, 2 * count, width), jnp.bfloat16),
            split,
            split,
        ),
        grid_spec=pltpu.PrefetchScalarGridSpec(
            num_scalar_prefetch=2,
            grid=(rows // chunk,),
            in_specs=[
                whole(),
                pl.BlockSpec((chunk, slots, width, width), lambda g, *_: (g, 0, 0, 0)),
            ],
            out_specs=(whole(),) * 6,
        ),
        compiler_params=params(),
        cost_estimate=cost(rows * slots, width),
        name="first_forward",
    )(meta, cols, signs, stored)


def cost(stored, width):
    return pl.CostEstimate(
        flops=2 * stored * 128 * width * width,
        transcendentals=0,
        bytes_accessed=8 * stored * width * width,
    )


def forward_kernel(count, chunk, rows, inverse, meta, cols_own, cols_other, own, other, panel, out):
    half = rows // 2
    block = meta[0] * rows + meta[1] * half

    def body(step, carry):
        row = step * chunk
        results = []
        for r in range(chunk):
            product = row_product(
                [
                    (own, row + r, cols_own, meta[1] * half + row + r),
                    (other, row + r, cols_other, row + r),
                ],
                panel,
                LAST,
            )
            results.append(panel[block + row + r].astype(jnp.float32) + inverse * product)
        for i in range(0, chunk, 2):
            out[(row + i) // 2] = join_pair(results[i], results[i + 1], count).astype(
                jnp.bfloat16
            )
        return carry

    lax.fori_loop(0, half // chunk, body, 0)


def forward(meta, cols_own, cols_other, own, other, panel, count, inverse):
    half, slots, width = own.shape[0], own.shape[1], own.shape[3]
    chunk = min(16, half)
    return pl.pallas_call(
        functools.partial(forward_kernel, count, chunk, 2 * half, inverse),
        out_shape=jax.ShapeDtypeStruct((half // 2, 2 * count, width), jnp.bfloat16),
        grid_spec=pltpu.PrefetchScalarGridSpec(
            num_scalar_prefetch=3,
            grid=(1,),
            in_specs=[whole()] * 3,
            out_specs=whole(),
        ),
        compiler_params=params(),
        cost_estimate=cost(2 * half * slots, width),
        name="forward_step",
    )(meta, cols_own, cols_other, own, other, panel)


def scatter_row(value, refs_and_rows, total):
    targets = []
    stored = []
    for ref, row, cols, col_row in refs_and_rows:
        for k in range(ref.shape[1]):
            targets.append(cols[col_row, k])
            stored.append(ref[row, k])
    terms = lax.dot_general(
        value, jnp.concatenate(stored, axis=1), FIRST, preferred_element_type=jnp.float32
    )
    width = stored[0].shape[1]
    for i, target in enumerate(targets):
        total[target] = total[target] + terms[:, i * width : (i + 1) * width]


def give_totals(count, rows, meta, keep, send, total):
    half = rows // 2
    pairs = half // 2
    for out, h in ((send, 1), (keep, 0)):
        for d in range(keep.shape[0]):
            base = (meta[0] ^ d) * rows + (meta[1] ^ h) * half

            def body(i, carry, out=out, base=base, d=d):
                out[d, i] = join_pair(
                    total[base + 2 * i], total[base + 2 * i + 1], count
                ).astype(jnp.bfloat16)
                return carry

            lax.fori_loop(0, pairs, body, 0, unroll=8 if pairs % 8 == 0 else 4)


def first_backward_kernel(count, chunk, meta, cols, near, far, panel, keep, send, total):
    half = near.shape[0]
    total[...] = jnp.zeros_like(total)

    def body(step, carry):
        for r in range(chunk):
            for ref, side in ((near, meta[1]), (far, 1 - meta[1])):
                row = step * chunk + r
                place = side * half + row
                value = panel[meta[0] * 2 * half + place]
                scatter_row(value, [(ref, row, cols, place)], total)
        return carry

    lax.fori_loop(0, half // chunk, body, 0)
    give_totals(count, 2 * half, meta, keep, send, total)


def backward_kernel(
    count, chunk, meta, cols_own, cols_other, own, other, left, keep, send, total
):
    half = own.shape[0]
    total[...] = jnp.zeros_like(total)

    def body(step, carry):
        for i in range(0, chunk, 2):
            pair = split_pair(left[(step * chunk + i) // 2], count)
            for r, value in zip((i, i + 1), pair):
                row = step * chunk + r
                scatter_row(
                    value.astype(jnp.bfloat16),
                    [(own, row, cols_own, meta[1] * half + row), (other, row, cols_other, row)],
                    total,
                )
        return carry

    lax.fori_loop(0, half // chunk, body, 0)
    give_totals(count, 2 * half, meta, keep, send, total)


def backward(kernel, name, scalars, own, other, source, count, blocks):
    half, slots, width = own.shape[0], own.shape[1], own.shape[3]
    chunk = min(16, half)
    result = jax.ShapeDtypeStruct(
        (blocks // (2 * half), half // 2, 2 * count, width), jnp.bfloat16
    )
    return pl.pallas_call(
        functools.partial(kernel, count, chunk),
        out_shape=(result, result),
        grid_spec=pltpu.PrefetchScalarGridSpec(
            num_scalar_prefetch=len(scalars),
            grid=(1,),
            in_specs=[whole()] * 3,
            out_specs=(whole(), whole()),
            scratch_shapes=[pltpu.VMEM((blocks, PAD, width), jnp.float32)],
        ),
        compiler_params=params(),
        cost_estimate=cost(2 * half * slots, width),
        name=name,
    )(*scalars, own, other, source)


def gradient_kernel(scale, chunk, rows, terms, meta, cols, *refs):
    out = refs[-1]
    lefts = refs[: 4 * terms]
    rights = refs[4 * terms : 8 * terms]
    step = pl.program_id(0)
    slots = out.shape[1]
    contract = (((0,), (0,)), ((), ()))
    for r in range(chunk):
        row = step * chunk + r
        left = []
        for position, ref in enumerate(lefts):
            start = meta[0] * rows if position < terms else 0
            left.append(ref[start + row])
        left = jnp.concatenate(left, axis=0)
        right = []
        for k in range(slots):
            target = cols[row, k]
            right.append(jnp.concatenate([ref[target] for ref in rights], axis=0))
        product = lax.dot_general(
            left, jnp.concatenate(right, axis=1), contract, preferred_element_type=jnp.float32
        )
        width = out.shape[3]
        for k in range(slots):
            out[r, k] = (product[:, k * width : (k + 1) * width] * scale).astype(jnp.bfloat16)


def gradient(meta, cols, lefts, rights, rows, slots, scale):
    width = lefts[0].shape[2]
    chunk = min(16, rows)
    operands = list(lefts) + list(rights)
    return pl.pallas_call(
        functools.partial(gradient_kernel, scale, chunk, rows, len(lefts) // 4),
        out_shape=jax.ShapeDtypeStruct((rows, slots, width, width), jnp.bfloat16),
        grid_spec=pltpu.PrefetchScalarGridSpec(
            num_scalar_prefetch=2,
            grid=(rows // chunk,),
            in_specs=[whole()] * len(operands),
            out_specs=pl.BlockSpec((chunk, slots, width, width), lambda g, *_: (g, 0, 0, 0)),
        ),
        compiler_params=params(),
        name="gradient",
    )(meta, cols, *operands)


def after(x, *tokens):
    return lax.optimization_barrier((x,) + tokens)[0]


def local(block_values, columns, probe_signs):
    rows, slots, width = block_values.shape[0], block_values.shape[1], block_values.shape[3]
    blocks, count = probe_signs.shape[0], probe_signs.shape[1]
    half = rows // 2
    n_var = lax.axis_size("var")
    n_probe = lax.axis_size("probe")
    inverse = 1.0 / math.sqrt(KS * width)
    rep_index = lax.axis_index("rep")
    meta = jnp.stack([lax.axis_index("var"), rep_index]).astype(jnp.int32)

    def swap_rep(x):
        return lax.ppermute(x, "rep", [(0, 1), (1, 0)])

    def shift_var(x, bit):
        return lax.ppermute(x, "var", [(i, i ^ bit) for i in range(n_var)])

    def from_probes(x):
        return [
            lax.ppermute(x, "probe", [(i, (i + d) % n_probe) for i in range(n_probe)])
            for d in range(1, n_probe)
        ]

    bits = [1 << i for i in range(n_var.bit_length() - 1)]

    def gather_var(x):
        held = {0: x}
        for bit in reversed(bits):
            for d in list(held):
                held[d | bit] = shift_var(held[d], bit)
        return [held[d] for d in range(n_var)]

    def scatter_var(parts):
        held = {d: part.astype(jnp.float32) for d, part in enumerate(parts)}
        for bit in bits:
            for d in sorted(held, reverse=True):
                if d & bit:
                    held[d ^ bit] = held[d ^ bit] + shift_var(
                        held.pop(d).astype(jnp.bfloat16), bit
                    ).astype(jnp.float32)
        return held[0]

    def home(d, h):
        return lambda v, r: (v ^ d) * rows + (r ^ h) * half

    near_where = [home(d, 0) for d in range(n_var)]
    far_where = [home(d, 1) for d in range(n_var)]
    row_where = [lambda v, r: r * half, lambda v, r: (1 - r) * half]
    start_where = [lambda v, r: r * (blocks // 2), lambda v, r: (1 - r) * (blocks // 2)]

    other_columns = swap_rep(
        lax.dynamic_slice_in_dim(columns, (1 - rep_index) * half, half, 0)
    )
    base = lax.axis_index("var") * rows + rep_index * half
    own_signs = lax.dynamic_slice_in_dim(probe_signs, base, half, 0)
    own_signs = own_signs.astype(jnp.bfloat16).reshape(half // 2, 2 * count, width)

    panel, sent, kept, given, near, far = first_forward(
        meta, columns, probe_signs, block_values
    )
    groups = n_probe
    right = [[panel]] + [[] for _ in range(groups - 1)]
    left = [[panel]] + [[] for _ in range(groups - 1)]
    product = kept + swap_rep(given).astype(jnp.float32)
    updated = (own_signs.astype(jnp.float32) + inverse * product).astype(jnp.bfloat16)

    far = after(far, updated)
    other_blocks = swap_rep(far)
    source = after(panel, updated)
    sent = after(sent, updated)
    waiting = [("start", from_probes(sent))]
    left_own = own_signs

    for step in range(3):
        last = step == 2
        if step == 0:
            keep, send = backward(
                first_backward_kernel, "first_backward", (meta, columns), near, far, source,
                count, blocks,
            )
        else:
            keep, send = backward(
                backward_kernel, "backward_step", (meta, columns, other_columns), near,
                other_blocks, after(left_own, updated), count, blocks,
            )
        pieces = gather_var(updated)
        partner = [swap_rep(x) for x in pieces]
        received = swap_rep(send)
        sums = [
            keep[d].astype(jnp.float32) + received[d].astype(jnp.float32) for d in range(n_var)
        ]
        summed = scatter_var(sums)
        panel = unpack(meta, pieces + partner, near_where + far_where, blocks)
        right[0].append(panel)
        for kind, arrays in waiting:
            for index, arrived in enumerate(arrays):
                arrived = after(arrived, keep)
                swapped = swap_rep(arrived)
                if kind == "start":
                    value = unpack(meta, [arrived, swapped], start_where, blocks)
                    left[1 + index].append(value)
                    right[1 + index].append(value)
                elif kind == "right":
                    size = half // 2
                    cut = [arrived[d * size : (d + 1) * size] for d in range(n_var)]
                    cut += [swapped[d * size : (d + 1) * size] for d in range(n_var)]
                    right[1 + index].append(unpack(meta, cut, near_where + far_where, blocks))
                else:
                    left[1 + index].append(
                        unpack(meta, [arrived, swapped], row_where, rows)
                    )
        if not last:
            updated = forward(
                meta, columns, other_columns, near, other_blocks, panel, count, inverse
            )
            joined = after(jnp.concatenate(pieces, axis=0), updated)
            waiting = [("right", from_probes(joined))]
        left_own = (left_own.astype(jnp.float32) + inverse * summed).astype(jnp.bfloat16)
        left[0].append(unpack(meta, [left_own, swap_rep(left_own)], row_where, rows))
        if not last:
            waiting.append(("left", from_probes(left_own)))

    arrived = [from_probes(piece) for piece in pieces]
    for index in range(groups - 1):
        mine = [arrived[d][index] for d in range(n_var)]
        theirs = [swap_rep(x) for x in mine]
        right[1 + index].append(unpack(meta, mine + theirs, near_where + far_where, blocks))
    for index, mine in enumerate(from_probes(left_own)):
        left[1 + index].append(unpack(meta, [mine, swap_rep(mine)], row_where, rows))

    lefts = [group[t] for t in range(4) for group in left]
    rights = [group[3 - t] for t in range(4) for group in right]
    scale = 1.0 / (count * n_probe)
    return gradient(meta, columns, lefts, rights, rows, slots, scale)


def solution(mesh):
    return jax.shard_map(
        local,
        mesh=mesh,
        in_specs=(
            P(("groups", "var"), "rep", None, None),
            P(("groups", "var"), "rep"),
            P("groups", "probe", None),
        ),
        out_specs=P(("groups", "var"), "rep", None, None),
        check_vma=False,
    )
```

time: 134 us -> 152 us (1.13)
  local copies, waits for them, and re-layouts: 8.14 us -> 15.8 us
  other arithmetic: 1.72 us -> 7.21 us
  starting transfers between devices: 34.9 us -> 40.2 us
    unnamed x10 -> x20, local copies, waits for them, and re-layouts: 3.84 us -> 13.2 us
    ppermute x27 -> x31, waiting for transfers between devices: 6.89 us -> 1.14 us  [swap_rep(): return lax.ppermute(x, 'rep', [(0, 1), (1, 0)])]
    ppermute x7 -> x10, waiting for transfers between devices: 11 us -> 16.6 us  [from_probes(): lax.ppermute(x, 'probe', [(i, (i + d) % n_probe) for i in range(n_probe)])]
    dynamic_slice x2 -> x1, local copies, waits for them, and re-layouts: 3.99 us -> 0.01 us  [local(): lax.dynamic_slice_in_dim(columns, (1 - rep_index) * half, half, 0)]
    ppermute x18, starting transfers between devices: 21.3 us -> 25.3 us  [shift_var(): return lax.ppermute(x, 'var', [(i, i ^ bit) for i in range(n_var)])]
    convert_element_type x6, other arithmetic: 0.3 us -> 2.9 us  [scatter_var(): held.pop(d).astype(jnp.bfloat16)]
    convert_element_type x1 -> x2, local copies, waits for them, and re-layouts: 0.04 us -> 2.5 us  [local(): own_signs.astype(jnp.float32) + inverse * product]
    ppermute x27 -> x31, starting transfers between devices: 4.55 us -> 5.19 us  [swap_rep(): return lax.ppermute(x, 'rep', [(0, 1), (1, 0)])]
  transfers between devices with their start and end apart: 52 -> 59, of which waited for: 18 -> 17; matrix products, arithmetic and copies ran while one was open for 2% -> 6% of each run, Pallas kernels for 25% -> 15%
where the time goes in v2:
time: 152 us
  waiting for transfers between devices  44.1 us (29%)
  Pallas kernels  43.7 us (29%)
  starting transfers between devices  40.2 us (26%)
  local copies, waits for them, and re-layouts  15.8 us (10%)
  other arithmetic  7.21 us (5%)
    ppermute x18, waiting for transfers between devices, shift_var(): return lax.ppermute(x, 'var', [(i, i ^ bit) for i in range(n_var)])  26.4 us
    ppermute x18, starting transfers between devices, shift_var(): return lax.ppermute(x, 'var', [(i, i ^ bit) for i in range(n_var)])  25.3 us
    ppermute x10, waiting for transfers between devices, from_probes(): lax.ppermute(x, 'probe', [(i, (i + d) % n_probe) for i in range(n_probe)])  16.6 us
    pallas_call x3, Pallas kernels, backward(): pl.pallas_call(functools.partial(kernel, count, chunk), out_shape=(result...  13.2 us
    unnamed x20, local copies, waits for them, and re-layouts  13.2 us
    pallas_call x13, Pallas kernels, unpack(): pl.pallas_call(functools.partial(unpack_kernel, count, where), out_shape=...  10.4 us
    pallas_call x2, Pallas kernels, forward(): pl.pallas_call(functools.partial(forward_kernel, count, chunk, 2 * half,...  10.2 us
    ppermute x10, starting transfers between devices, from_probes(): lax.ppermute(x, 'probe', [(i, (i + d) % n_probe) for i in range(n_probe)])  9.67 us
  transfers between devices with their start and end apart: 59, of which 17 were waited for; matrix products, arithmetic and copies ran while one was open for 6% of the time, Pallas kernels for 15%

profile of v2, /device:TPU:0, one launch (start us, length us, event | category | flops | bytes accessed | tf_op | source)
XLA Modules:
  0.0 151.6 jit_solution(16718272495008573901)
XLA Ops:
  0.0 0.8 copy.23.cols.cols_own
  0.8 2.4 %copy.15.signs = s32[256,12,128]{2,1,0:T(8,128)S(1)} copy(s32[256,12,128]{2,0,1:T(8,128)} %param.5) | data formatting | bytes 3145728 | tf_op args[2]
  3.2 2.8 %copy-done.3 = bf16[64,3,128,128]{3,2,1,0:T(8,128)(2,1)S(1)} copy-done((bf16[64,3,128,128]{3,2,1,0:T(8,128)(2,1)S(1)}, bf16[64,3,128,128]{3,2,1,0:T(8,128)(2,1)}, u32[]{:S(2)}) %copy-start.3) | copy-done | bytes 6291480
  6.0 4.6 %first_forward.1 = (bf16[256,16,128]{2,1,0:T(8,128)(2,1)S(1)}, bf16[64,24,128]{2,1,0:T(8,128)(2,1)S(1)}, f32[16,24,128]{2,1,0:T(8,128)S(1)}, bf16[16,24,128]{2,1...) custom-call(s32[2]{0:T(128)S(1)} %pad_add_fusion.meta, ...), custom_call_target="tpu_custom_call" | custom-call | flops 805306368 | bytes 25165824 | tf_op jit(solution)/shard_map/first_forward/pallas_call | solution.py:152
  10.6 1.0 copy-done
  11.6 1.7 %copy-done.4 = bf16[32,3,128,128]{3,2,1,0:T(8,128)(2,1)} copy-done((bf16[32,3,128,128]{3,2,1,0:T(8,128)(2,1)}, bf16[32,3,128,128]{3,2,1,0:T(8,128)(2,1)S(1)}, u32[]{:S(2)}) %copy-start.4) | copy-done | bytes 3145752
  13.3 0.8 copy-done.6
  14.5 0.9 fusion.15
  15.4 0.8 copy.16
  16.3 1.7 %reshape.45 = f32[16,24,128]{2,1,0:T(8,128)} reshape(f32[32,12,128]{2,1,0:T(8,128)} %copy.16) | data formatting | bytes 393216 | tf_op jit(solution)/shard_map/convert_element_type | solution.py:432
  17.9 1.0 add_convert_fusion.6.refs_0_
  19.1 1.2 copy-done.1
  20.3 1.9 %copy-done.5 = bf16[32,3,128,128]{3,2,1,0:T(8,128)(2,1)S(1)} copy-done((bf16[32,3,128,128]{3,2,1,0:T(8,128)(2,1)S(1)}, bf16[32,3,128,128]{3,2,1,0:T(8,128)(2,1)}, u32[]{:S(2)}) %copy-start.5) | copy-done | bytes 3145752
  22.2 3.6 %first_backward.1 = (bf16[4,16,24,128]{3,2,1,0:T(8,128)(2,1)}, bf16[4,16,24,128]{3,2,1,0:T(8,128)(2,1)S(1)}) custom-call(s32[2]{0:T(128)S(1)} %pad_add_fusion.meta, s32[64,3]{1,0:T(8,128)S(1)} %copy.23.cols.cols_own, bf16[32,3,128,128]{3,2,1,0:T(8,128)(2,1)S(1)} %get-tuple-element.34.near.own, bf16[32,3,128,128]{3,2,1,0:T(8,128)(2,1)S(1)} %copy-done.5, ...), custom_call_target="tpu_custom_call" | custom-call | flops 805306368 | bytes 25165824 | tf_op jit(solution)/shard_map/first_backward/pallas_call | solution.py:305
  26.2 3.6 %collective-permute-start.12 = (bf16[16,24,128]{2,1,0:T(8,128)(2,1)S(1)}, bf16[16,24,128]{2,1,0:T(8,128)(2,1)S(1)}, u32[]{:S(2)}, u32[]{:S(2)}) collective-permute-start(bf16[16,24,128]{2,1,0:T(8,128)(2,1)S(1)} %add_convert_fusion.6.refs_0_), channel_id=1, source_target_pairs={{0,8},{4,12},{8,0},{12,4},{1,9},{5,13},{9,1},{13,5},{2,10},{6,14},... | collective-permute-start | bytes 294920 | tf_op jit(solution)/shard_map/ppermute | solution.py:383
  29.8 1.6 %collective-permute-start.11 = (bf16[16,24,128]{2,1,0:T(8,128)(2,1)S(1)}, bf16[16,24,128]{2,1,0:T(8,128)(2,1)S(1)}, u32[]{:S(2)}, u32[]{:S(2)}) collective-permute-start(bf16[16,24,128]{2,1,0:T(8,128)(2,1)S(1)} %add_convert_fusion.6.refs_0_), channel_id=1, source_target_pairs={{0,4},{4,0},{8,12},{12,8},{1,5},{5,1},{9,13},{13,9},{2,6},{6,2},{1... | collective-permute-start | bytes 294920 | tf_op jit(solution)/shard_map/ppermute | solution.py:383
  31.4 4.1 %collective-permute-done.12.refs_2_ = bf16[16,24,128]{2,1,0:T(8,128)(2,1)S(1)} collective-permute-done((bf16[16,24,128]{2,1,0:T(8,128)(2,1)S(1)}, bf16[16,24,128]{2,1,0:T(8,128)(2,1)S(1)}, u32[]{:S(2)}, u32[]{:S(2)}) %collective-permute-start.12) | collective-permute-done | bytes 98336 | tf_op jit(solution)/shard_map/ppermute | solution.py:383
  36.1 0.8 copy-done.8
  36.9 1.7 %fusion.16 = (bf16[16,24,128]{2,1,0:T(8,128)(2,1)}, bf16[16,24,128]{2,1,0:T(8,128)(2,1)}) fusion(bf16[4,16,24,128]{3,2,1,0:T(8,128)(2,1)S(1)} %collective-permute-done.3, bf16[4,16,24,128]{3,2,1,0:T(8,128)(2,1)} %get-tuple-element.38), kind=kLoop, calls=%fused_computation.32 | loop fusion | flops 393216 | bytes 589824 | tf_op jit(solution)/shard_map/convert_element_type | solution.py:406
  38.6 1.4 collective-permute-start.5
  40.5 3.0 %collective-permute-done.5 = bf16[16,24,128]{2,1,0:T(8,128)(2,1)} collective-permute-done((bf16[16,24,128]{2,1,0:T(8,128)(2,1)}, bf16[16,24,128]{2,1,0:T(8,128)(2,1)}, u32[]{:S(2)}, u32[]{:S(2)}) %collective-permute-start.5) | collective-permute-done | bytes 98336 | tf_op jit(solution)/shard_map/ppermute | solution.py:383
  43.5 1.0 fusion.10
  44.5 1.4 collective-permute-start.4
  46.0 2.1 %collective-permute-start.6 = (bf16[16,24,128]{2,1,0:T(8,128)(2,1)S(1)}, bf16[16,24,128]{2,1,0:T(8,128)(2,1)S(1)}, u32[]{:S(2)}, u32[]{:S(2)}) collective-permute-start(bf16[16,24,128]{2,1,0:T(8,128)(2,1)S(1)} %fusion.10), channel_id=1, source_target_pairs={{0,8},{4,12},{8,0},{12,4},{1,9},{5,13},{9,1},{13,5},{2,10},{6,14},... | collective-permute-start | bytes 294920 | tf_op jit(solution)/shard_map/ppermute | solution.py:383
  48.3 1.7 %unpack_panel.15.panel.refs_12_ = bf16[256,16,128]{2,1,0:T(8,128)(2,1)S(1)} custom-call(s32[2]{0:T(128)S(1)} %pad_add_fusion.meta, bf16[16,24,128]{2,1,0:T(8,128)(2,1)S(1)} %add_convert_fusion.6.refs_0_, bf16[16,24,128]{2,1,0:T(8,128)(2,1)S(1)} %collective-permute-done.11.refs_1_, bf16[16,24,128]{2,1,0:T(8,128)(2,1)S(1)} %collective-permute-done.12.refs_2_, ...), custom_call_target="tpu_custom_call" | custom-call | tf_op jit(solution)/shard_map/unpack_panel/pallas_call | solution.py:59
  50.0 2.1 %collective-permute-done.4 = bf16[16,24,128]{2,1,0:T(8,128)(2,1)S(1)} collective-permute-done((bf16[16,24,128]{2,1,0:T(8,128)(2,1)}, bf16[16,24,128]{2,1,0:T(8,128)(2,1)S(1)}, u32[]{:S(2)}, u32[]{:S(2)}) %collective-permute-start.4) | collective-permute-done | bytes 98336 | tf_op jit(solution)/shard_map/ppermute | solution.py:383
  52.1 1.1 fusion.14.refs_0_.left
  53.3 5.1 %forward_step.2.refs_0_ = bf16[16,24,128]{2,1,0:T(8,128)(2,1)S(1)} custom-call(s32[2]{0:T(128)S(1)} %pad_add_fusion.meta, s32[64,3]{1,0:T(8,128)S(1)} %copy.23.cols.cols_own, s32[32,3]{1,0:T(8,128)S(1)} %collective-permute-done.9.cols_other, bf16[32,3,128,128]{3,2,1,0:T(8,128)(2,1)S(1)} %get-tuple-element.34.near.own, ...), custom_call_target="tpu_custom_call" | custom-call | flops 805306368 | bytes 25165824 | tf_op jit(solution)/shard_map/forward_step/pallas_call | solution.py:214
  58.4 4.8 %backward_step.2 = (bf16[4,16,24,128]{3,2,1,0:T(8,128)(2,1)S(1)}, bf16[4,16,24,128]{3,2,1,0:T(8,128)(2,1)S(1)}) custom-call(s32[2]{0:T(128)S(1)} %pad_add_fusion.meta, s32[64,3]{1,0:T(8,128)S(1)} %copy.23.cols.cols_own, s32[32,3]{1,0:T(8,128)S(1)} %collective-permute-done.9.cols_other, bf16[32,3,128,128]{3,2,1,0:T(8,128)(2,1)S(1)} %get-tuple-element.34.near.own, ...), custom_call_target="tpu_custom_call" | custom-call | flops 805306368 | bytes 25165824 | tf_op jit(solution)/shard_map/backward_step/pallas_call | solution.py:305
  63.3 2.4 %collective-permute-start.26 = (bf16[16,24,128]{2,1,0:T(8,128)(2,1)S(1)}, bf16[16,24,128]{2,1,0:T(8,128)(2,1)S(1)}, u32[]{:S(2)}, u32[]{:S(2)}) collective-permute-start(bf16[16,24,128]{2,1,0:T(8,128)(2,1)S(1)} %forward_step.2.refs_0_), channel_id=1, source_target_pairs={{0,8},{4,12},{8,0},{12,4},{1,9},{5,13},{9,1},{13,5},{2,10},{6,14},... | collective-permute-start | bytes 294920 | tf_op jit(solution)/shard_map/ppermute | solution.py:383
  65.7 1.5 %collective-permute-start.1 = (bf16[64,24,128]{2,1,0:T(8,128)(2,1)S(1)}, bf16[64,24,128]{2,1,0:T(8,128)(2,1)S(1)}, u32[]{:S(2)}, u32[]{:S(2)}) collective-permute-start(bf16[64,24,128]{2,1,0:T(8,128)(2,1)S(1)} %copy-done.7), channel_id=1, source_target_pairs={{0,2},{2,0},{1,3},{3,1},{4,6},{6,4},{5,7},{7,5},{8,10},{10,8},{9,1... | collective-permute-start | bytes 1179656 | tf_op jit(solution)/shard_map/ppermute | solution.py:387
  67.3 3.3 %collective-permute-start.25 = (bf16[16,24,128]{2,1,0:T(8,128)(2,1)S(1)}, bf16[16,24,128]{2,1,0:T(8,128)(2,1)S(1)}, u32[]{:S(2)}, u32[]{:S(2)}) collective-permute-start(bf16[16,24,128]{2,1,0:T(8,128)(2,1)S(1)} %forward_step.2.refs_0_), channel_id=1, source_target_pairs={{0,4},{4,0},{8,12},{12,8},{1,5},{5,1},{9,13},{13,9},{2,6},{6,2},{1... | collective-permute-start | bytes 294920 | tf_op jit(solution)/shard_map/ppermute | solution.py:383
  70.6 2.6 %collective-permute-start.27 = (bf16[16,24,128]{2,1,0:T(8,128)(2,1)S(1)}, bf16[16,24,128]{2,1,0:T(8,128)(2,1)S(1)}, u32[]{:S(2)}, u32[]{:S(2)}) collective-permute-start(bf16[16,24,128]{2,1,0:T(8,128)(2,1)S(1)} %collective-permute-done.26.refs_2_), channel_id=1, source_target_pairs={{0,4},{4,0},{8,12},{12,8},{1,5},{5,1},{9,13},{13,9},{2,6},{6,2},{1... | collective-permute-start | bytes 294920 | tf_op jit(solution)/shard_map/ppermute | solution.py:383
  73.9 2.8 %collective-permute-done.27.refs_3_ = bf16[16,24,128]{2,1,0:T(8,128)(2,1)S(1)} collective-permute-done((bf16[16,24,128]{2,1,0:T(8,128)(2,1)S(1)}, bf16[16,24,128]{2,1,0:T(8,128)(2,1)S(1)}, u32[]{:S(2)}, u32[]{:S(2)}) %collective-permute-start.27) | collective-permute-done | bytes 98336 | tf_op jit(solution)/shard_map/ppermute | solution.py:383
  76.7 1.2 collective-permute-done.21
  78.0 2.3 %collective-permute-start.20 = (bf16[16,24,128]{2,1,0:T(8,128)(2,1)S(1)}, bf16[16,24,128]{2,1,0:T(8,128)(2,1)S(1)}, u32[]{:S(2)}, u32[]{:S(2)}) collective-permute-start(bf16[16,24,128]{2,1,0:T(8,128)(2,1)S(1)} %get-tuple-element.55), channel_id=1, source_target_pairs={{0,4},{4,0},{8,12},{12,8},{1,5},{5,1},{9,13},{13,9},{2,6},{6,2},{1... | collective-permute-start | bytes 294920 | tf_op jit(solution)/shard_map/ppermute | solution.py:383
  80.3 1.8 %collective-permute-start.22 = (bf16[16,24,128]{2,1,0:T(8,128)(2,1)S(1)}, bf16[16,24,128]{2,1,0:T(8,128)(2,1)S(1)}, u32[]{:S(2)}, u32[]{:S(2)}) collective-permute-start(bf16[16,24,128]{2,1,0:T(8,128)(2,1)S(1)} %fusion.5), channel_id=1, source_target_pairs={{0,8},{4,12},{8,0},{12,4},{1,9},{5,13},{9,1},{13,5},{2,10},{6,14},... | collective-permute-start | bytes 294920 | tf_op jit(solution)/shard_map/ppermute | solution.py:383
  82.1 0.9 pad_maximum_fusion.1
  83.2 1.7 %collective-permute-start.57 = (bf16[64,24,128]{2,1,0:T(8,128)(2,1)S(1)}, bf16[64,24,128]{2,1,0:T(8,128)(2,1)S(1)}, u32[]{:S(2)}, u32[]{:S(2)}) collective-permute-start(bf16[64,24,128]{2,1,0:T(8,128)(2,1)S(1)} %pad_maximum_fusion.1), channel_id=1, source_target_pairs={{0,2},{2,0},{1,3},{3,1},{4,6},{6,4},{5,7},{7,5},{8,10},{10,8},{9,1... | collective-permute-start | bytes 1179656 | tf_op jit(solution)/shard_map/ppermute | solution.py:387
  84.9 0.8 unpack_panel.18.panel.refs_10_
  85.7 5.1 %forward_step.3.refs_0_ = bf16[16,24,128]{2,1,0:T(8,128)(2,1)S(1)} custom-call(s32[2]{0:T(128)S(1)} %pad_add_fusion.meta, s32[64,3]{1,0:T(8,128)S(1)} %copy.23.cols.cols_own, s32[32,3]{1,0:T(8,128)S(1)} %collective-permute-done.9.cols_other, bf16[32,3,128,128]{3,2,1,0:T(8,128)(2,1)S(1)} %get-tuple-element.34.near.own, ...), custom_call_target="tpu_custom_call" | custom-call | flops 805306368 | bytes 25165824 | tf_op jit(solution)/shard_map/forward_step/pallas_call | solution.py:214
  90.9 4.8 %backward_step.3 = (bf16[4,16,24,128]{3,2,1,0:T(8,128)(2,1)S(1)}, bf16[4,16,24,128]{3,2,1,0:T(8,128)(2,1)S(1)}) custom-call(s32[2]{0:T(128)S(1)} %pad_add_fusion.meta, s32[64,3]{1,0:T(8,128)S(1)} %copy.23.cols.cols_own, s32[32,3]{1,0:T(8,128)S(1)} %collective-permute-done.9.cols_other, bf16[32,3,128,128]{3,2,1,0:T(8,128)(2,1)S(1)} %get-tuple-element.34.near.own, ...), custom_call_target="tpu_custom_call" | custom-call | flops 805306368 | bytes 25165824 | tf_op jit(solution)/shard_map/backward_step/pallas_call | solution.py:305
  96.4 4.6 %collective-permute-done.8.refs_0_ = bf16[16,24,128]{2,1,0:T(8,128)(2,1)S(1)} collective-permute-done((bf16[16,24,128]{2,1,0:T(8,128)(2,1)S(1)}, bf16[16,24,128]{2,1,0:T(8,128)(2,1)S(1)}, u32[]{:S(2)}, u32[]{:S(2)}) %collective-permute-start.8) | collective-permute-done | bytes 98336 | tf_op jit(solution)/shard_map/ppermute | solution.py:387
  101.7 0.8 unpack_panel.13.refs_1_.refs_15_
  103.2 1.0 collective-permute-start.41
  104.8 6.3 %collective-permute-done.41.refs_2_ = bf16[16,24,128]{2,1,0:T(8,128)(2,1)S(1)} collective-permute-done((bf16[16,24,128]{2,1,0:T(8,128)(2,1)S(1)}, bf16[16,24,128]{2,1,0:T(8,128)(2,1)S(1)}, u32[]{:S(2)}, u32[]{:S(2)}) %collective-permute-start.41) | collective-permute-done | bytes 98336 | tf_op jit(solution)/shard_map/ppermute | solution.py:383
  112.3 1.6 %collective-permute-start.48 = (bf16[16,24,128]{2,1,0:T(8,128)(2,1)S(1)}, bf16[16,24,128]{2,1,0:T(8,128)(2,1)S(1)}, u32[]{:S(2)}, u32[]{:S(2)}) collective-permute-start(bf16[16,24,128]{2,1,0:T(8,128)(2,1)S(1)} %collective-permute-done.40.refs_1_), channel_id=1, source_target_pairs={{0,2},{2,0},{1,3},{3,1},{4,6},{6,4},{5,7},{7,5},{8,10},{10,8},{9,1... | collective-permute-start | bytes 294920 | tf_op jit(solution)/shard_map/ppermute | solution.py:387
  113.9 2.3 %collective-permute-done.42.refs_3_ = bf16[16,24,128]{2,1,0:T(8,128)(2,1)S(1)} collective-permute-done((bf16[16,24,128]{2,1,0:T(8,128)(2,1)S(1)}, bf16[16,24,128]{2,1,0:T(8,128)(2,1)S(1)}, u32[]{:S(2)}, u32[]{:S(2)}) %collective-permute-start.42) | collective-permute-done | bytes 98336 | tf_op jit(solution)/shard_map/ppermute | solution.py:383
  116.3 1.6 %collective-permute-start.49 = (bf16[16,24,128]{2,1,0:T(8,128)(2,1)S(1)}, bf16[16,24,128]{2,1,0:T(8,128)(2,1)S(1)}, u32[]{:S(2)}, u32[]{:S(2)}) collective-permute-start(bf16[16,24,128]{2,1,0:T(8,128)(2,1)S(1)} %collective-permute-done.41.refs_2_), channel_id=1, source_target_pairs={{0,2},{2,0},{1,3},{3,1},{4,6},{6,4},{5,7},{7,5},{8,10},{10,8},{9,1... | collective-permute-start | bytes 294920 | tf_op jit(solution)/shard_map/ppermute | solution.py:387
  118.1 1.1 collective-permute-done.46.refs_7_
  119.3 0.8 unpack_panel.22.refs_8_
  120.1 5.1 %collective-permute-done.48.refs_1_ = bf16[16,24,128]{2,1,0:T(8,128)(2,1)S(1)} collective-permute-done((bf16[16,24,128]{2,1,0:T(8,128)(2,1)S(1)}, bf16[16,24,128]{2,1,0:T(8,128)(2,1)S(1)}, u32[]{:S(2)}, u32[]{:S(2)}) %collective-permute-start.48) | collective-permute-done | bytes 98336 | tf_op jit(solution)/shard_map/ppermute | solution.py:387
  125.7 1.0 collective-permute-done.49.refs_2_
  126.7 0.7 collective-permute-start.24
  128.0 2.9 %collective-permute-done.50.refs_3_ = bf16[16,24,128]{2,1,0:T(8,128)(2,1)S(1)} collective-permute-done((bf16[16,24,128]{2,1,0:T(8,128)(2,1)S(1)}, bf16[16,24,128]{2,1,0:T(8,128)(2,1)S(1)}, u32[]{:S(2)}, u32[]{:S(2)}) %collective-permute-start.50) | collective-permute-done | bytes 98336 | tf_op jit(solution)/shard_map/ppermute | solution.py:387
  132.0 0.8 collective-permute-start.36
  134.1 0.8 unpack_panel.23.refs_9_
  134.9 2.6 %collective-permute-done.34 = bf16[16,24,128]{2,1,0:T(8,128)(2,1)S(1)} collective-permute-done((bf16[16,24,128]{2,1,0:T(8,128)(2,1)S(1)}, bf16[16,24,128]{2,1,0:T(8,128)(2,1)S(1)}, u32[]{:S(2)}, u32[]{:S(2)}) %collective-permute-start.34) | collective-permute-done | bytes 98336 | tf_op jit(solution)/shard_map/ppermute | solution.py:383
  137.5 1.9 %collective-permute-done.36 = bf16[16,24,128]{2,1,0:T(8,128)(2,1)S(1)} collective-permute-done((bf16[16,24,128]{2,1,0:T(8,128)(2,1)S(1)}, bf16[16,24,128]{2,1,0:T(8,128)(2,1)S(1)}, u32[]{:S(2)}, u32[]{:S(2)}) %collective-permute-start.36) | collective-permute-done | bytes 98336 | tf_op jit(solution)/shard_map/ppermute | solution.py:383
  139.4 0.7 collective-permute-start.38
  140.2 0.8 unpack_panel.25.refs_13_
  141.8 2.4 %collective-permute-done.38.refs_0_ = bf16[16,24,128]{2,1,0:T(8,128)(2,1)S(1)} collective-permute-done((bf16[16,24,128]{2,1,0:T(8,128)(2,1)S(1)}, bf16[16,24,128]{2,1,0:T(8,128)(2,1)S(1)}, u32[]{:S(2)}, u32[]{:S(2)}) %collective-permute-start.38) | collective-permute-done | bytes 98336 | tf_op jit(solution)/shard_map/ppermute | solution.py:387
  144.2 0.8 unpack_panel.24.refs_11_
  146.3 5.3 %gradient.1 = bf16[64,3,128,128]{3,2,1,0:T(8,128)(2,1)} custom-call(s32[2]{0:T(128)S(1)} %pad_add_fusion.meta, s32[64,3]{1,0:T(8,128)S(1)} %copy.23.cols.cols_own, bf16[256,16,128]{2,1,0:T(8,128)(2,1)S(1)} %copy-done.2, bf16[256,16,128]{2,1,0:T(8,128)(2,1)S(1)} %unpack_panel.13.refs_1_.refs_15_, bf16[64,16,128]{2,1,0:T(8,128)(2,1)S(1)} %unpack_panel.14.refs_2_, ...), custom_call_target="tpu_custom_call" | custom-call | tf_op jit(solution)/shard_map/gradient/pallas_call | solution.py:351
  (115 shorter events, 13.1 us)
Async XLA Ops:
  3.2 2.8 %copy-start.3 = (bf16[64,3,128,128]{3,2,1,0:T(8,128)(2,1)S(1)}, bf16[64,3,128,128]{3,2,1,0:T(8,128)(2,1)}, u32[]{:S(2)}) copy-start(bf16[64,3,128,128]{3,2,1,0:T(8,128)(2,1)} %stored.1) | copy-start | bytes 18874372
  11.6 1.7 %copy-start.4 = (bf16[32,3,128,128]{3,2,1,0:T(8,128)(2,1)}, bf16[32,3,128,128]{3,2,1,0:T(8,128)(2,1)S(1)}, u32[]{:S(2)}) copy-start(bf16[32,3,128,128]{3,2,1,0:T(8,128)(2,1)S(1)} %get-tuple-element.36.far) | copy-start | bytes 9437188
  14.0 3.9 %collective-permute-start = (bf16[16,24,128]{2,1,0:T(8,128)(2,1)S(1)}, bf16[16,24,128]{2,1,0:T(8,128)(2,1)}, u32[]{:S(2)}, u32[]{:S(2)}) collective-permute-start(bf16[16,24,128]{2,1,0:T(8,128)(2,1)S(1)} %get-tuple-element.32), channel_id=1, source_target_pairs={{0,1},{1,0},{2,3},{3,2},{4,5},{5,4},{6,7},{7,6},{8,9},{9,8},{10,11... | collective-permute-start | bytes 294920 | tf_op jit(solution)/shard_map/ppermute | solution.py:380
  19.0 34.3 %collective-permute-start.10 = (bf16[32,3,128,128]{3,2,1,0:T(8,128)(2,1)}, bf16[32,3,128,128]{3,2,1,0:T(8,128)(2,1)}, u32[]{:S(2)}, u32[]{:S(2)}) collective-permute-start(bf16[32,3,128,128]{3,2,1,0:T(8,128)(2,1)} %copy-done.4), channel_id=1, source_target_pairs={{0,1},{1,0},{2,3},{3,2},{4,5},{5,4},{6,7},{7,6},{8,9},{9,8},{10,11... | collective-permute-start | bytes 9437192 | tf_op jit(solution)/shard_map/ppermute | solution.py:380
  20.3 1.9 %copy-start.5 = (bf16[32,3,128,128]{3,2,1,0:T(8,128)(2,1)S(1)}, bf16[32,3,128,128]{3,2,1,0:T(8,128)(2,1)}, u32[]{:S(2)}) copy-start(bf16[32,3,128,128]{3,2,1,0:T(8,128)(2,1)} %copy-done.4) | copy-start | bytes 9437188
  25.8 10.4 %collective-permute-start.3 = (bf16[4,16,24,128]{3,2,1,0:T(8,128)(2,1)S(1)}, bf16[4,16,24,128]{3,2,1,0:T(8,128)(2,1)S(1)}, u32[]{:S(2)}, u32[]{:S(2)}) collective-permute-start(bf16[4,16,24,128]{3,2,1,0:T(8,128)(2,1)S(1)} %get-tuple-element.40), channel_id=1, source_target_pairs={{0,1},{1,0},{2,3},{3,2},{4,5},{5,4},{6,7},{7,6},{8,9},{9,8},{10,11... | collective-permute-start | bytes 1179656 | tf_op jit(solution)/shard_map/ppermute | solution.py:380
  26.2 9.3 %collective-permute-start.12 = (bf16[16,24,128]{2,1,0:T(8,128)(2,1)S(1)}, bf16[16,24,128]{2,1,0:T(8,128)(2,1)S(1)}, u32[]{:S(2)}, u32[]{:S(2)}) collective-permute-start(bf16[16,24,128]{2,1,0:T(8,128)(2,1)S(1)} %add_convert_fusion.6.refs_0_), channel_id=1, source_target_pairs={{0,8},{4,12},{8,0},{12,4},{1,9},{5,13},{9,1},{13,5},{2,10},{6,14},... | collective-permute-start | bytes 294920 | tf_op jit(solution)/shard_map/ppermute | solution.py:383
  29.8 10.1 %collective-permute-start.11 = (bf16[16,24,128]{2,1,0:T(8,128)(2,1)S(1)}, bf16[16,24,128]{2,1,0:T(8,128)(2,1)S(1)}, u32[]{:S(2)}, u32[]{:S(2)}) collective-permute-start(bf16[16,24,128]{2,1,0:T(8,128)(2,1)S(1)} %add_convert_fusion.6.refs_0_), channel_id=1, source_target_pairs={{0,4},{4,0},{8,12},{12,8},{1,5},{5,1},{9,13},{13,9},{2,6},{6,2},{1... | collective-permute-start | bytes 294920 | tf_op jit(solution)/shard_map/ppermute | solution.py:383
  35.5 5.0 %collective-permute-start.13 = (bf16[16,24,128]{2,1,0:T(8,128)(2,1)S(1)}, bf16[16,24,128]{2,1,0:T(8,128)(2,1)}, u32[]{:S(2)}, u32[]{:S(2)}) collective-permute-start(bf16[16,24,128]{2,1,0:T(8,128)(2,1)S(1)} %collective-permute-done.12.refs_2_), channel_id=1, source_target_pairs={{0,4},{4,0},{8,12},{12,8},{1,5},{5,1},{9,13},{13,9},{2,6},{6,2},{1... | collective-permute-start | bytes 294920 | tf_op jit(solution)/shard_map/ppermute | solution.py:383
  38.6 4.9 %collective-permute-start.5 = (bf16[16,24,128]{2,1,0:T(8,128)(2,1)}, bf16[16,24,128]{2,1,0:T(8,128)(2,1)}, u32[]{:S(2)}, u32[]{:S(2)}) collective-permute-start(bf16[16,24,128]{2,1,0:T(8,128)(2,1)} %get-tuple-element.58), channel_id=1, source_target_pairs={{0,4},{4,0},{8,12},{12,8},{1,5},{5,1},{9,13},{13,9},{2,6},{6,2},{1... | collective-permute-start | bytes 294920 | tf_op jit(solution)/shard_map/ppermute | solution.py:383
  40.0 4.6 %collective-permute-start.14 = (bf16[16,24,128]{2,1,0:T(8,128)(2,1)S(1)}, bf16[16,24,128]{2,1,0:T(8,128)(2,1)S(1)}, u32[]{:S(2)}, u32[]{:S(2)}) collective-permute-start(bf16[16,24,128]{2,1,0:T(8,128)(2,1)S(1)} %add_convert_fusion.6.refs_0_), channel_id=1, source_target_pairs={{0,1},{1,0},{2,3},{3,2},{4,5},{5,4},{6,7},{7,6},{8,9},{9,8},{10,11... | collective-permute-start | bytes 294920 | tf_op jit(solution)/shard_map/ppermute | solution.py:380
  40.0 6.0 %collective-permute-start.16 = (bf16[16,24,128]{2,1,0:T(8,128)(2,1)S(1)}, bf16[16,24,128]{2,1,0:T(8,128)(2,1)S(1)}, u32[]{:S(2)}, u32[]{:S(2)}) collective-permute-start(bf16[16,24,128]{2,1,0:T(8,128)(2,1)S(1)} %collective-permute-done.12.refs_2_), channel_id=1, source_target_pairs={{0,1},{1,0},{2,3},{3,2},{4,5},{5,4},{6,7},{7,6},{8,9},{9,8},{10,11... | collective-permute-start | bytes 294920 | tf_op jit(solution)/shard_map/ppermute | solution.py:380
  40.5 7.7 %collective-permute-start.15 = (bf16[16,24,128]{2,1,0:T(8,128)(2,1)S(1)}, bf16[16,24,128]{2,1,0:T(8,128)(2,1)S(1)}, u32[]{:S(2)}, u32[]{:S(2)}) collective-permute-start(bf16[16,24,128]{2,1,0:T(8,128)(2,1)S(1)} %collective-permute-done.11.refs_1_), channel_id=1, source_target_pairs={{0,1},{1,0},{2,3},{3,2},{4,5},{5,4},{6,7},{7,6},{8,9},{9,8},{10,11... | collective-permute-start | bytes 294920 | tf_op jit(solution)/shard_map/ppermute | solution.py:380
  43.5 4.8 %collective-permute-start.17 = (bf16[16,24,128]{2,1,0:T(8,128)(2,1)}, bf16[16,24,128]{2,1,0:T(8,128)(2,1)S(1)}, u32[]{:S(2)}, u32[]{:S(2)}) collective-permute-start(bf16[16,24,128]{2,1,0:T(8,128)(2,1)} %collective-permute-done.13.refs_3_), channel_id=1, source_target_pairs={{0,1},{1,0},{2,3},{3,2},{4,5},{5,4},{6,7},{7,6},{8,9},{9,8},{10,11... | collective-permute-start | bytes 294920 | tf_op jit(solution)/shard_map/ppermute | solution.py:380
  44.5 7.6 %collective-permute-start.4 = (bf16[16,24,128]{2,1,0:T(8,128)(2,1)}, bf16[16,24,128]{2,1,0:T(8,128)(2,1)S(1)}, u32[]{:S(2)}, u32[]{:S(2)}) collective-permute-start(bf16[16,24,128]{2,1,0:T(8,128)(2,1)} %get-tuple-element.57), channel_id=1, source_target_pairs={{0,4},{4,0},{8,12},{12,8},{1,5},{5,1},{9,13},{13,9},{2,6},{6,2},{1... | collective-permute-start | bytes 294920 | tf_op jit(solution)/shard_map/ppermute | solution.py:383
  46.0 6.1 %collective-permute-start.6 = (bf16[16,24,128]{2,1,0:T(8,128)(2,1)S(1)}, bf16[16,24,128]{2,1,0:T(8,128)(2,1)S(1)}, u32[]{:S(2)}, u32[]{:S(2)}) collective-permute-start(bf16[16,24,128]{2,1,0:T(8,128)(2,1)S(1)} %fusion.10), channel_id=1, source_target_pairs={{0,8},{4,12},{8,0},{12,4},{1,9},{5,13},{9,1},{13,5},{2,10},{6,14},... | collective-permute-start | bytes 294920 | tf_op jit(solution)/shard_map/ppermute | solution.py:383
  48.1 5.1 %collective-permute-start.9 = (s32[32,3]{1,0:T(8,128)S(1)}, s32[32,3]{1,0:T(8,128)S(1)}, u32[]{:S(2)}, u32[]{:S(2)}) collective-permute-start(s32[32,3]{1,0:T(8,128)S(1)} %constant_dynamic-slice_fusion), channel_id=1, source_target_pairs={{0,1},{1,0},{2,3},{3,2},{4,5},{5,4},{6,7},{7,6},{8,9},{9,8},{10,11... | collective-permute-start | bytes 1160 | tf_op jit(solution)/shard_map/ppermute | solution.py:380
  58.4 7.4 %copy-start.7 = (bf16[64,24,128]{2,1,0:T(8,128)(2,1)S(1)}, bf16[64,24,128]{2,1,0:T(8,128)(2,1)}, u32[]{:S(2)}) copy-start(bf16[64,24,128]{2,1,0:T(8,128)(2,1)} %copy-done.6) | copy-start | bytes 1179652
  63.2 10.0 %collective-permute-start.19 = (bf16[4,16,24,128]{3,2,1,0:T(8,128)(2,1)S(1)}, bf16[4,16,24,128]{3,2,1,0:T(8,128)(2,1)S(1)}, u32[]{:S(2)}, u32[]{:S(2)}) collective-permute-start(bf16[4,16,24,128]{3,2,1,0:T(8,128)(2,1)S(1)} %get-tuple-element.44), channel_id=1, source_target_pairs={{0,1},{1,0},{2,3},{3,2},{4,5},{5,4},{6,7},{7,6},{8,9},{9,8},{10,11... | collective-permute-start | bytes 1179656 | tf_op jit(solution)/shard_map/ppermute | solution.py:380
  63.3 7.3 %collective-permute-start.26 = (bf16[16,24,128]{2,1,0:T(8,128)(2,1)S(1)}, bf16[16,24,128]{2,1,0:T(8,128)(2,1)S(1)}, u32[]{:S(2)}, u32[]{:S(2)}) collective-permute-start(bf16[16,24,128]{2,1,0:T(8,128)(2,1)S(1)} %forward_step.2.refs_0_), channel_id=1, source_target_pairs={{0,8},{4,12},{8,0},{12,4},{1,9},{5,13},{9,1},{13,5},{2,10},{6,14},... | collective-permute-start | bytes 294920 | tf_op jit(solution)/shard_map/ppermute | solution.py:383
  65.7 12.3 %collective-permute-start.1 = (bf16[64,24,128]{2,1,0:T(8,128)(2,1)S(1)}, bf16[64,24,128]{2,1,0:T(8,128)(2,1)S(1)}, u32[]{:S(2)}, u32[]{:S(2)}) collective-permute-start(bf16[64,24,128]{2,1,0:T(8,128)(2,1)S(1)} %copy-done.7), channel_id=1, source_target_pairs={{0,2},{2,0},{1,3},{3,1},{4,6},{6,4},{5,7},{7,5},{8,10},{10,8},{9,1... | collective-permute-start | bytes 1179656 | tf_op jit(solution)/shard_map/ppermute | solution.py:387
  67.3 6.3 %collective-permute-start.25 = (bf16[16,24,128]{2,1,0:T(8,128)(2,1)S(1)}, bf16[16,24,128]{2,1,0:T(8,128)(2,1)S(1)}, u32[]{:S(2)}, u32[]{:S(2)}) collective-permute-start(bf16[16,24,128]{2,1,0:T(8,128)(2,1)S(1)} %forward_step.2.refs_0_), channel_id=1, source_target_pairs={{0,4},{4,0},{8,12},{12,8},{1,5},{5,1},{9,13},{13,9},{2,6},{6,2},{1... | collective-permute-start | bytes 294920 | tf_op jit(solution)/shard_map/ppermute | solution.py:383
  70.6 6.2 %collective-permute-start.27 = (bf16[16,24,128]{2,1,0:T(8,128)(2,1)S(1)}, bf16[16,24,128]{2,1,0:T(8,128)(2,1)S(1)}, u32[]{:S(2)}, u32[]{:S(2)}) collective-permute-start(bf16[16,24,128]{2,1,0:T(8,128)(2,1)S(1)} %collective-permute-done.26.refs_2_), channel_id=1, source_target_pairs={{0,4},{4,0},{8,12},{12,8},{1,5},{5,1},{9,13},{13,9},{2,6},{6,2},{1... | collective-permute-start | bytes 294920 | tf_op jit(solution)/shard_map/ppermute | solution.py:383
  73.3 4.7 %collective-permute-start.21 = (bf16[16,24,128]{2,1,0:T(8,128)(2,1)S(1)}, bf16[16,24,128]{2,1,0:T(8,128)(2,1)S(1)}, u32[]{:S(2)}, u32[]{:S(2)}) collective-permute-start(bf16[16,24,128]{2,1,0:T(8,128)(2,1)S(1)} %get-tuple-element.56), channel_id=1, source_target_pairs={{0,4},{4,0},{8,12},{12,8},{1,5},{5,1},{9,13},{13,9},{2,6},{6,2},{1... | collective-permute-start | bytes 294920 | tf_op jit(solution)/shard_map/ppermute | solution.py:383
  73.4 6.9 %collective-permute-start.28 = (bf16[16,24,128]{2,1,0:T(8,128)(2,1)S(1)}, bf16[16,24,128]{2,1,0:T(8,128)(2,1)S(1)}, u32[]{:S(2)}, u32[]{:S(2)}) collective-permute-start(bf16[16,24,128]{2,1,0:T(8,128)(2,1)S(1)} %forward_step.2.refs_0_), channel_id=1, source_target_pairs={{0,1},{1,0},{2,3},{3,2},{4,5},{5,4},{6,7},{7,6},{8,9},{9,8},{10,11... | collective-permute-start | bytes 294920 | tf_op jit(solution)/shard_map/ppermute | solution.py:380
  73.6 9.6 %collective-permute-start.30 = (bf16[16,24,128]{2,1,0:T(8,128)(2,1)S(1)}, bf16[16,24,128]{2,1,0:T(8,128)(2,1)S(1)}, u32[]{:S(2)}, u32[]{:S(2)}) collective-permute-start(bf16[16,24,128]{2,1,0:T(8,128)(2,1)S(1)} %collective-permute-done.26.refs_2_), channel_id=1, source_target_pairs={{0,1},{1,0},{2,3},{3,2},{4,5},{5,4},{6,7},{7,6},{8,9},{9,8},{10,11... | collective-permute-start | bytes 294920 | tf_op jit(solution)/shard_map/ppermute | solution.py:380
  76.7 6.3 %collective-permute-start.29 = (bf16[16,24,128]{2,1,0:T(8,128)(2,1)S(1)}, bf16[16,24,128]{2,1,0:T(8,128)(2,1)S(1)}, u32[]{:S(2)}, u32[]{:S(2)}) collective-permute-start(bf16[16,24,128]{2,1,0:T(8,128)(2,1)S(1)} %collective-permute-done.25.refs_1_), channel_id=1, source_target_pairs={{0,1},{1,0},{2,3},{3,2},{4,5},{5,4},{6,7},{7,6},{8,9},{9,8},{10,11... | collective-permute-start | bytes 294920 | tf_op jit(solution)/shard_map/ppermute | solution.py:380
  78.0 6.9 %collective-permute-start.31 = (bf16[16,24,128]{2,1,0:T(8,128)(2,1)S(1)}, bf16[16,24,128]{2,1,0:T(8,128)(2,1)S(1)}, u32[]{:S(2)}, u32[]{:S(2)}) collective-permute-start(bf16[16,24,128]{2,1,0:T(8,128)(2,1)S(1)} %collective-permute-done.27.refs_3_), channel_id=1, source_target_pairs={{0,1},{1,0},{2,3},{3,2},{4,5},{5,4},{6,7},{7,6},{8,9},{9,8},{10,11... | collective-permute-start | bytes 294920 | tf_op jit(solution)/shard_map/ppermute | solution.py:380
  78.0 12.8 %collective-permute-start.20 = (bf16[16,24,128]{2,1,0:T(8,128)(2,1)S(1)}, bf16[16,24,128]{2,1,0:T(8,128)(2,1)S(1)}, u32[]{:S(2)}, u32[]{:S(2)}) collective-permute-start(bf16[16,24,128]{2,1,0:T(8,128)(2,1)S(1)} %get-tuple-element.55), channel_id=1, source_target_pairs={{0,4},{4,0},{8,12},{12,8},{1,5},{5,1},{9,13},{13,9},{2,6},{6,2},{1... | collective-permute-start | bytes 294920 | tf_op jit(solution)/shard_map/ppermute | solution.py:383
  80.3 10.6 %collective-permute-start.22 = (bf16[16,24,128]{2,1,0:T(8,128)(2,1)S(1)}, bf16[16,24,128]{2,1,0:T(8,128)(2,1)S(1)}, u32[]{:S(2)}, u32[]{:S(2)}) collective-permute-start(bf16[16,24,128]{2,1,0:T(8,128)(2,1)S(1)} %fusion.5), channel_id=1, source_target_pairs={{0,8},{4,12},{8,0},{12,4},{1,9},{5,13},{9,1},{13,5},{2,10},{6,14},... | collective-permute-start | bytes 294920 | tf_op jit(solution)/shard_map/ppermute | solution.py:383
  83.1 18.6 %collective-permute-start.2 = (bf16[64,24,128]{2,1,0:T(8,128)(2,1)S(1)}, bf16[64,24,128]{2,1,0:T(8,128)(2,1)S(1)}, u32[]{:S(2)}, u32[]{:S(2)}) collective-permute-start(bf16[64,24,128]{2,1,0:T(8,128)(2,1)S(1)} %collective-permute-done.1.refs_0_), channel_id=1, source_target_pairs={{0,1},{1,0},{2,3},{3,2},{4,5},{5,4},{6,7},{7,6},{8,9},{9,8},{10,11... | collective-permute-start | bytes 1179656 | tf_op jit(solution)/shard_map/ppermute | solution.py:380
  83.2 21.6 %collective-permute-start.57 = (bf16[64,24,128]{2,1,0:T(8,128)(2,1)S(1)}, bf16[64,24,128]{2,1,0:T(8,128)(2,1)S(1)}, u32[]{:S(2)}, u32[]{:S(2)}) collective-permute-start(bf16[64,24,128]{2,1,0:T(8,128)(2,1)S(1)} %pad_maximum_fusion.1), channel_id=1, source_target_pairs={{0,2},{2,0},{1,3},{3,1},{4,6},{6,4},{5,7},{7,5},{8,10},{10,8},{9,1... | collective-permute-start | bytes 1179656 | tf_op jit(solution)/shard_map/ppermute | solution.py:387
  95.8 16.0 %collective-permute-start.33 = (bf16[4,16,24,128]{3,2,1,0:T(8,128)(2,1)S(1)}, bf16[4,16,24,128]{3,2,1,0:T(8,128)(2,1)S(1)}, u32[]{:S(2)}, u32[]{:S(2)}) collective-permute-start(bf16[4,16,24,128]{3,2,1,0:T(8,128)(2,1)S(1)} %get-tuple-element.48), channel_id=1, source_target_pairs={{0,1},{1,0},{2,3},{3,2},{4,5},{5,4},{6,7},{7,6},{8,9},{9,8},{10,11... | collective-permute-start | bytes 1179656 | tf_op jit(solution)/shard_map/ppermute | solution.py:380
  96.0 5.1 %collective-permute-start.8 = (bf16[16,24,128]{2,1,0:T(8,128)(2,1)S(1)}, bf16[16,24,128]{2,1,0:T(8,128)(2,1)S(1)}, u32[]{:S(2)}, u32[]{:S(2)}) collective-permute-start(bf16[16,24,128]{2,1,0:T(8,128)(2,1)S(1)} %fusion.14.refs_0_.left), channel_id=1, source_target_pairs={{0,2},{2,0},{1,3},{3,1},{4,6},{6,4},{5,7},{7,5},{8,10},{10,8},{9,1... | collective-permute-start | bytes 294920 | tf_op jit(solution)/shard_map/ppermute | solution.py:387
  96.4 4.7 %collective-permute-start.7 = (bf16[16,24,128]{2,1,0:T(8,128)(2,1)S(1)}, bf16[16,24,128]{2,1,0:T(8,128)(2,1)S(1)}, u32[]{:S(2)}, u32[]{:S(2)}) collective-permute-start(bf16[16,24,128]{2,1,0:T(8,128)(2,1)S(1)} %fusion.14.refs_0_.left), channel_id=1, source_target_pairs={{0,1},{1,0},{2,3},{3,2},{4,5},{5,4},{6,7},{7,6},{8,9},{9,8},{10,11... | collective-permute-start | bytes 294920 | tf_op jit(solution)/shard_map/ppermute | solution.py:380
  101.0 1.5 collective-permute-start.18
  103.2 8.0 %collective-permute-start.41 = (bf16[16,24,128]{2,1,0:T(8,128)(2,1)S(1)}, bf16[16,24,128]{2,1,0:T(8,128)(2,1)S(1)}, u32[]{:S(2)}, u32[]{:S(2)}) collective-permute-start(bf16[16,24,128]{2,1,0:T(8,128)(2,1)S(1)} %forward_step.3.refs_0_), channel_id=1, source_target_pairs={{0,8},{4,12},{8,0},{12,4},{1,9},{5,13},{9,1},{13,5},{2,10},{6,14},... | collective-permute-start | bytes 294920 | tf_op jit(solution)/shard_map/ppermute | solution.py:383
  104.1 7.5 %collective-permute-start.40 = (bf16[16,24,128]{2,1,0:T(8,128)(2,1)S(1)}, bf16[16,24,128]{2,1,0:T(8,128)(2,1)S(1)}, u32[]{:S(2)}, u32[]{:S(2)}) collective-permute-start(bf16[16,24,128]{2,1,0:T(8,128)(2,1)S(1)} %forward_step.3.refs_0_), channel_id=1, source_target_pairs={{0,4},{4,0},{8,12},{12,8},{1,5},{5,1},{9,13},{13,9},{2,6},{6,2},{1... | collective-permute-start | bytes 294920 | tf_op jit(solution)/shard_map/ppermute | solution.py:383
  104.2 7.5 %collective-permute-start.47 = (bf16[16,24,128]{2,1,0:T(8,128)(2,1)S(1)}, bf16[16,24,128]{2,1,0:T(8,128)(2,1)S(1)}, u32[]{:S(2)}, u32[]{:S(2)}) collective-permute-start(bf16[16,24,128]{2,1,0:T(8,128)(2,1)S(1)} %forward_step.3.refs_0_), channel_id=1, source_target_pairs={{0,2},{2,0},{1,3},{3,1},{4,6},{6,4},{5,7},{7,5},{8,10},{10,8},{9,1... | collective-permute-start | bytes 294920 | tf_op jit(solution)/shard_map/ppermute | solution.py:387
  104.8 7.5 %collective-permute-start.43 = (bf16[16,24,128]{2,1,0:T(8,128)(2,1)S(1)}, bf16[16,24,128]{2,1,0:T(8,128)(2,1)S(1)}, u32[]{:S(2)}, u32[]{:S(2)}) collective-permute-start(bf16[16,24,128]{2,1,0:T(8,128)(2,1)S(1)} %forward_step.3.refs_0_), channel_id=1, source_target_pairs={{0,1},{1,0},{2,3},{3,2},{4,5},{5,4},{6,7},{7,6},{8,9},{9,8},{10,11... | collective-permute-start | bytes 294920 | tf_op jit(solution)/shard_map/ppermute | solution.py:380
  111.2 14.5 %collective-permute-start.55 = (bf16[64,24,128]{2,1,0:T(8,128)(2,1)S(1)}, bf16[64,24,128]{2,1,0:T(8,128)(2,1)S(1)}, u32[]{:S(2)}, u32[]{:S(2)}) collective-permute-start(bf16[64,24,128]{2,1,0:T(8,128)(2,1)S(1)} %pad_maximum_fusion), channel_id=1, source_target_pairs={{0,2},{2,0},{1,3},{3,1},{4,6},{6,4},{5,7},{7,5},{8,10},{10,8},{9,1... | collective-permute-start | bytes 1179656 | tf_op jit(solution)/shard_map/ppermute | solution.py:387
  111.6 4.6 %collective-permute-start.42 = (bf16[16,24,128]{2,1,0:T(8,128)(2,1)S(1)}, bf16[16,24,128]{2,1,0:T(8,128)(2,1)S(1)}, u32[]{:S(2)}, u32[]{:S(2)}) collective-permute-start(bf16[16,24,128]{2,1,0:T(8,128)(2,1)S(1)} %collective-permute-done.41.refs_2_), channel_id=1, source_target_pairs={{0,4},{4,0},{8,12},{12,8},{1,5},{5,1},{9,13},{13,9},{2,6},{6,2},{1... | collective-permute-start | bytes 294920 | tf_op jit(solution)/shard_map/ppermute | solution.py:383
  111.6 6.2 %collective-permute-start.45 = (bf16[16,24,128]{2,1,0:T(8,128)(2,1)S(1)}, bf16[16,24,128]{2,1,0:T(8,128)(2,1)S(1)}, u32[]{:S(2)}, u32[]{:S(2)}) collective-permute-start(bf16[16,24,128]{2,1,0:T(8,128)(2,1)S(1)} %collective-permute-done.41.refs_2_), channel_id=1, source_target_pairs={{0,1},{1,0},{2,3},{3,2},{4,5},{5,4},{6,7},{7,6},{8,9},{9,8},{10,11... | collective-permute-start | bytes 294920 | tf_op jit(solution)/shard_map/ppermute | solution.py:380
  111.7 6.1 %collective-permute-start.44 = (bf16[16,24,128]{2,1,0:T(8,128)(2,1)S(1)}, bf16[16,24,128]{2,1,0:T(8,128)(2,1)S(1)}, u32[]{:S(2)}, u32[]{:S(2)}) collective-permute-start(bf16[16,24,128]{2,1,0:T(8,128)(2,1)S(1)} %collective-permute-done.40.refs_1_), channel_id=1, source_target_pairs={{0,1},{1,0},{2,3},{3,2},{4,5},{5,4},{6,7},{7,6},{8,9},{9,8},{10,11... | collective-permute-start | bytes 294920 | tf_op jit(solution)/shard_map/ppermute | solution.py:380
  112.3 13.0 %collective-permute-start.48 = (bf16[16,24,128]{2,1,0:T(8,128)(2,1)S(1)}, bf16[16,24,128]{2,1,0:T(8,128)(2,1)S(1)}, u32[]{:S(2)}, u32[]{:S(2)}) collective-permute-start(bf16[16,24,128]{2,1,0:T(8,128)(2,1)S(1)} %collective-permute-done.40.refs_1_), channel_id=1, source_target_pairs={{0,2},{2,0},{1,3},{3,1},{4,6},{6,4},{5,7},{7,5},{8,10},{10,8},{9,1... | collective-permute-start | bytes 294920 | tf_op jit(solution)/shard_map/ppermute | solution.py:387
  116.3 10.5 %collective-permute-start.49 = (bf16[16,24,128]{2,1,0:T(8,128)(2,1)S(1)}, bf16[16,24,128]{2,1,0:T(8,128)(2,1)S(1)}, u32[]{:S(2)}, u32[]{:S(2)}) collective-permute-start(bf16[16,24,128]{2,1,0:T(8,128)(2,1)S(1)} %collective-permute-done.41.refs_2_), channel_id=1, source_target_pairs={{0,2},{2,0},{1,3},{3,1},{4,6},{6,4},{5,7},{7,5},{8,10},{10,8},{9,1... | collective-permute-start | bytes 294920 | tf_op jit(solution)/shard_map/ppermute | solution.py:387
  117.8 1.3 collective-permute-start.46
  117.8 9.5 %collective-permute-start.35 = (bf16[16,24,128]{2,1,0:T(8,128)(2,1)S(1)}, bf16[16,24,128]{2,1,0:T(8,128)(2,1)S(1)}, u32[]{:S(2)}, u32[]{:S(2)}) collective-permute-start(bf16[16,24,128]{2,1,0:T(8,128)(2,1)S(1)} %get-tuple-element.54), channel_id=1, source_target_pairs={{0,4},{4,0},{8,12},{12,8},{1,5},{5,1},{9,13},{13,9},{2,6},{6,2},{1... | collective-permute-start | bytes 294920 | tf_op jit(solution)/shard_map/ppermute | solution.py:383
  119.1 8.4 %collective-permute-start.51 = (bf16[16,24,128]{2,1,0:T(8,128)(2,1)S(1)}, bf16[16,24,128]{2,1,0:T(8,128)(2,1)S(1)}, u32[]{:S(2)}, u32[]{:S(2)}) collective-permute-start(bf16[16,24,128]{2,1,0:T(8,128)(2,1)S(1)} %collective-permute-done.47.refs_0_), channel_id=1, source_target_pairs={{0,1},{1,0},{2,3},{3,2},{4,5},{5,4},{6,7},{7,6},{8,9},{9,8},{10,11... | collective-permute-start | bytes 294920 | tf_op jit(solution)/shard_map/ppermute | solution.py:380
  125.3 5.7 %collective-permute-start.50 = (bf16[16,24,128]{2,1,0:T(8,128)(2,1)S(1)}, bf16[16,24,128]{2,1,0:T(8,128)(2,1)S(1)}, u32[]{:S(2)}, u32[]{:S(2)}) collective-permute-start(bf16[16,24,128]{2,1,0:T(8,128)(2,1)S(1)} %collective-permute-done.42.refs_3_), channel_id=1, source_target_pairs={{0,2},{2,0},{1,3},{3,1},{4,6},{6,4},{5,7},{7,5},{8,10},{10,8},{9,1... | collective-permute-start | bytes 294920 | tf_op jit(solution)/shard_map/ppermute | solution.py:387
  125.7 5.2 %collective-permute-start.52 = (bf16[16,24,128]{2,1,0:T(8,128)(2,1)S(1)}, bf16[16,24,128]{2,1,0:T(8,128)(2,1)S(1)}, u32[]{:S(2)}, u32[]{:S(2)}) collective-permute-start(bf16[16,24,128]{2,1,0:T(8,128)(2,1)S(1)} %collective-permute-done.48.refs_1_), channel_id=1, source_target_pairs={{0,1},{1,0},{2,3},{3,2},{4,5},{5,4},{6,7},{7,6},{8,9},{9,8},{10,11... | collective-permute-start | bytes 294920 | tf_op jit(solution)/shard_map/ppermute | solution.py:380
  126.7 5.3 %collective-permute-start.24 = (bf16[16,24,128]{2,1,0:T(8,128)(2,1)S(1)}, bf16[16,24,128]{2,1,0:T(8,128)(2,1)S(1)}, u32[]{:S(2)}, u32[]{:S(2)}) collective-permute-start(bf16[16,24,128]{2,1,0:T(8,128)(2,1)S(1)} %fusion.9.refs_0_.left), channel_id=1, source_target_pairs={{0,2},{2,0},{1,3},{3,1},{4,6},{6,4},{5,7},{7,5},{8,10},{10,8},{9,1... | collective-permute-start | bytes 294920 | tf_op jit(solution)/shard_map/ppermute | solution.py:387
  127.4 4.6 %collective-permute-start.23 = (bf16[16,24,128]{2,1,0:T(8,128)(2,1)S(1)}, bf16[16,24,128]{2,1,0:T(8,128)(2,1)S(1)}, u32[]{:S(2)}, u32[]{:S(2)}) collective-permute-start(bf16[16,24,128]{2,1,0:T(8,128)(2,1)S(1)} %fusion.9.refs_0_.left), channel_id=1, source_target_pairs={{0,1},{1,0},{2,3},{3,2},{4,5},{5,4},{6,7},{7,6},{8,9},{9,8},{10,11... | collective-permute-start | bytes 294920 | tf_op jit(solution)/shard_map/ppermute | solution.py:380
  127.6 12.6 %collective-permute-start.58 = (bf16[64,24,128]{2,1,0:T(8,128)(2,1)S(1)}, bf16[64,24,128]{2,1,0:T(8,128)(2,1)S(1)}, u32[]{:S(2)}, u32[]{:S(2)}) collective-permute-start(bf16[64,24,128]{2,1,0:T(8,128)(2,1)S(1)} %collective-permute-done.57), channel_id=1, source_target_pairs={{0,1},{1,0},{2,3},{3,2},{4,5},{5,4},{6,7},{7,6},{8,9},{9,8},{10,11... | collective-permute-start | bytes 1179656 | tf_op jit(solution)/shard_map/ppermute | solution.py:380
  130.9 2.6 %collective-permute-start.53 = (bf16[16,24,128]{2,1,0:T(8,128)(2,1)S(1)}, bf16[16,24,128]{2,1,0:T(8,128)(2,1)S(1)}, u32[]{:S(2)}, u32[]{:S(2)}) collective-permute-start(bf16[16,24,128]{2,1,0:T(8,128)(2,1)S(1)} %collective-permute-done.49.refs_2_), channel_id=1, source_target_pairs={{0,1},{1,0},{2,3},{3,2},{4,5},{5,4},{6,7},{7,6},{8,9},{9,8},{10,11... | collective-permute-start | bytes 294920 | tf_op jit(solution)/shard_map/ppermute | solution.py:380
  130.9 2.6 %collective-permute-start.54 = (bf16[16,24,128]{2,1,0:T(8,128)(2,1)S(1)}, bf16[16,24,128]{2,1,0:T(8,128)(2,1)S(1)}, u32[]{:S(2)}, u32[]{:S(2)}) collective-permute-start(bf16[16,24,128]{2,1,0:T(8,128)(2,1)S(1)} %collective-permute-done.50.refs_3_), channel_id=1, source_target_pairs={{0,1},{1,0},{2,3},{3,2},{4,5},{5,4},{6,7},{7,6},{8,9},{9,8},{10,11... | collective-permute-start | bytes 294920 | tf_op jit(solution)/shard_map/ppermute | solution.py:380
  132.0 5.5 %collective-permute-start.34 = (bf16[16,24,128]{2,1,0:T(8,128)(2,1)S(1)}, bf16[16,24,128]{2,1,0:T(8,128)(2,1)S(1)}, u32[]{:S(2)}, u32[]{:S(2)}) collective-permute-start(bf16[16,24,128]{2,1,0:T(8,128)(2,1)S(1)} %get-tuple-element.53), channel_id=1, source_target_pairs={{0,4},{4,0},{8,12},{12,8},{1,5},{5,1},{9,13},{13,9},{2,6},{6,2},{1... | collective-permute-start | bytes 294920 | tf_op jit(solution)/shard_map/ppermute | solution.py:383
  132.0 7.4 %collective-permute-start.36 = (bf16[16,24,128]{2,1,0:T(8,128)(2,1)S(1)}, bf16[16,24,128]{2,1,0:T(8,128)(2,1)S(1)}, u32[]{:S(2)}, u32[]{:S(2)}) collective-permute-start(bf16[16,24,128]{2,1,0:T(8,128)(2,1)S(1)} %fusion), channel_id=1, source_target_pairs={{0,8},{4,12},{8,0},{12,4},{1,9},{5,13},{9,1},{13,5},{2,10},{6,14},... | collective-permute-start | bytes 294920 | tf_op jit(solution)/shard_map/ppermute | solution.py:383
  133.5 10.6 %collective-permute-start.56 = (bf16[64,24,128]{2,1,0:T(8,128)(2,1)S(1)}, bf16[64,24,128]{2,1,0:T(8,128)(2,1)S(1)}, u32[]{:S(2)}, u32[]{:S(2)}) collective-permute-start(bf16[64,24,128]{2,1,0:T(8,128)(2,1)S(1)} %collective-permute-done.55), channel_id=1, source_target_pairs={{0,1},{1,0},{2,3},{3,2},{4,5},{5,4},{6,7},{7,6},{8,9},{9,8},{10,11... | collective-permute-start | bytes 1179656 | tf_op jit(solution)/shard_map/ppermute | solution.py:380
  133.6 7.5 %collective-permute-start.32 = (bf16[16,24,128]{2,1,0:T(8,128)(2,1)S(1)}, bf16[16,24,128]{2,1,0:T(8,128)(2,1)S(1)}, u32[]{:S(2)}, u32[]{:S(2)}) collective-permute-start(bf16[16,24,128]{2,1,0:T(8,128)(2,1)S(1)} %collective-permute-done.24.refs_0_), channel_id=1, source_target_pairs={{0,1},{1,0},{2,3},{3,2},{4,5},{5,4},{6,7},{7,6},{8,9},{9,8},{10,11... | collective-permute-start | bytes 294920 | tf_op jit(solution)/shard_map/ppermute | solution.py:380
  139.4 6.9 %copy-start.2 = (bf16[256,16,128]{2,1,0:T(8,128)(2,1)S(1)}, bf16[256,16,128]{2,1,0:T(8,128)(2,1)}, u32[]{:S(2)}) copy-start(bf16[256,16,128]{2,1,0:T(8,128)(2,1)} %copy-done) | copy-start | bytes 3145732
  139.4 4.7 %collective-permute-start.38 = (bf16[16,24,128]{2,1,0:T(8,128)(2,1)S(1)}, bf16[16,24,128]{2,1,0:T(8,128)(2,1)S(1)}, u32[]{:S(2)}, u32[]{:S(2)}) collective-permute-start(bf16[16,24,128]{2,1,0:T(8,128)(2,1)S(1)} %fusion.4.refs_0_), channel_id=1, source_target_pairs={{0,2},{2,0},{1,3},{3,1},{4,6},{6,4},{5,7},{7,5},{8,10},{10,8},{9,1... | collective-permute-start | bytes 294920 | tf_op jit(solution)/shard_map/ppermute | solution.py:387
  141.7 3.3 %collective-permute-start.37 = (bf16[16,24,128]{2,1,0:T(8,128)(2,1)S(1)}, bf16[16,24,128]{2,1,0:T(8,128)(2,1)S(1)}, u32[]{:S(2)}, u32[]{:S(2)}) collective-permute-start(bf16[16,24,128]{2,1,0:T(8,128)(2,1)S(1)} %fusion.4.refs_0_), channel_id=1, source_target_pairs={{0,1},{1,0},{2,3},{3,2},{4,5},{5,4},{6,7},{7,6},{8,9},{9,8},{10,11... | collective-permute-start | bytes 294920 | tf_op jit(solution)/shard_map/ppermute | solution.py:380
  144.1 1.5 %collective-permute-start.39 = (bf16[16,24,128]{2,1,0:T(8,128)(2,1)S(1)}, bf16[16,24,128]{2,1,0:T(8,128)(2,1)S(1)}, u32[]{:S(2)}, u32[]{:S(2)}) collective-permute-start(bf16[16,24,128]{2,1,0:T(8,128)(2,1)S(1)} %collective-permute-done.38.refs_0_), channel_id=1, source_target_pairs={{0,1},{1,0},{2,3},{3,2},{4,5},{5,4},{6,7},{7,6},{8,9},{9,8},{10,11... | collective-permute-start | bytes 294920 | tf_op jit(solution)/shard_map/ppermute | solution.py:380
  (4 other events, 3.7 us)

commit v3 on v2

v3 whole, which is shorter than its diff:
```python
import functools
import math

import jax
import jax.numpy as jnp
from jax import lax
from jax.experimental import pallas as pl
from jax.experimental.pallas import tpu as pltpu
from jax.sharding import PartitionSpec as P

KS = 6
PAD = 16
VMEM_LIMIT = 24 * 1024 * 1024


def whole():
    return pl.BlockSpec(memory_space=pltpu.VMEM)


def params():
    return pltpu.CompilerParams(
        dimension_semantics=("arbitrary",), vmem_limit_bytes=VMEM_LIMIT
    )


def split_pair(pair, count):
    wide = pair.astype(jnp.float32)
    keep = lax.broadcasted_iota(jnp.int32, (PAD, wide.shape[1]), 0) < count
    first = jnp.where(keep, wide[:PAD], 0.0)
    second = jnp.where(keep, pltpu.roll(wide, count, 0)[:PAD], 0.0)
    return first, second


def join_pair(first, second, count):
    tail = jnp.zeros((2 * count - PAD, first.shape[1]), jnp.float32)
    low = jnp.concatenate([first, tail], axis=0)
    high = pltpu.roll(jnp.concatenate([second, tail], axis=0), count, 0)
    return low + high


def unpack_kernel(count, where, meta, *refs):
    panel = refs[-1]
    for ref, places in zip(refs[:-1], where):
        pairs = ref.shape[1]
        for index, base_of in enumerate(places):
            if base_of is None:
                continue
            base = base_of(meta[0], meta[1])

            def body(i, carry, ref=ref, base=base, index=index):
                first, second = split_pair(ref[index, i], count)
                panel[base + 2 * i] = first.astype(jnp.bfloat16)
                panel[base + 2 * i + 1] = second.astype(jnp.bfloat16)
                return carry

            lax.fori_loop(0, pairs, body, 0, unroll=8 if pairs % 8 == 0 else 4)


def unpack(meta, pieces, blocks):
    arrays = [array for array, _ in pieces]
    where = [places for _, places in pieces]
    count = arrays[0].shape[2] // 2
    width = arrays[0].shape[3]
    return pl.pallas_call(
        functools.partial(unpack_kernel, count, where),
        out_shape=jax.ShapeDtypeStruct((blocks, PAD, width), jnp.bfloat16),
        grid_spec=pltpu.PrefetchScalarGridSpec(
            num_scalar_prefetch=1,
            grid=(1,),
            in_specs=[whole()] * len(arrays),
            out_specs=whole(),
        ),
        compiler_params=params(),
        name="unpack_panel",
    )(meta, *arrays)


def row_product(refs_and_rows, panel, contract):
    picked = []
    stored = []
    for ref, row, cols, col_row in refs_and_rows:
        for k in range(ref.shape[1]):
            picked.append(panel[cols[k, col_row]])
            stored.append(ref[row, k])
    return lax.dot_general(
        jnp.concatenate(picked, axis=1),
        jnp.concatenate(stored, axis=1),
        contract,
        preferred_element_type=jnp.float32,
    )


LAST = (((1,), (1,)), ((), ()))
FIRST = (((1,), (0,)), ((), ()))


def first_kernel(
    count, chunk, blocks, meta, cols, signs, stored,
    panel, sent, mine, keep_row, near, far, keep, send, total,
):
    step = pl.program_id(0)
    half = near.shape[0]
    rows = 2 * half

    @pl.when(step == 0)
    def _():
        total[...] = jnp.zeros_like(total)
        pad = jnp.zeros((PAD - count, signs.shape[1]), jnp.float32)

        def body(b, carry):
            value = signs[pl.ds(b, count, stride=blocks), :].astype(jnp.float32)
            panel[b] = jnp.concatenate([value, pad], axis=0).astype(jnp.bfloat16)
            return carry

        lax.fori_loop(0, blocks, body, 0, unroll=8)

    row = step * chunk
    side = row // half
    base = row - side * half
    first_block = meta[0] * rows
    pairs = []
    for i in range(0, chunk, 2):
        results = [
            row_product([(stored, r, cols, row + r)], panel, LAST) for r in (i, i + 1)
        ]
        pairs.append(join_pair(results[0], results[1], count))
    for r in range(chunk):
        scatter_row(panel[first_block + row + r], [(stored, r, cols, row + r)], total)

    @pl.when(side == meta[1])
    def _():
        for i, pair in enumerate(pairs):
            keep_row[base // 2 + i] = pair
        near[pl.ds(base, chunk)] = stored[...]

    @pl.when(side != meta[1])
    def _():
        for i, pair in enumerate(pairs):
            send[send.shape[0] - 1, base // 2 + i] = pair.astype(jnp.bfloat16)
        far[pl.ds(base, chunk)] = stored[...]

    @pl.when(step == pl.num_programs(0) - 1)
    def _():
        parts, pair_rows = sent.shape[0], sent.shape[1]
        for start, out, index in [
            (meta[1] * (blocks // 2) + p * 2 * pair_rows, sent, p) for p in range(parts)
        ] + [(first_block + meta[1] * half, mine, 0)]:

            def pack(i, carry, start=start, out=out, index=index):
                b = start + 2 * i
                out[index, i] = join_pair(
                    panel[b].astype(jnp.float32), panel[b + 1].astype(jnp.float32), count
                ).astype(jnp.bfloat16)
                return carry

            lax.fori_loop(0, pair_rows, pack, 0, unroll=8 if pair_rows % 8 == 0 else 4)
        give_totals(count, rows, meta, keep, send, total)


def first_step(meta, cols, signs, stored, blocks):
    rows, slots, width = stored.shape[0], stored.shape[1], stored.shape[3]
    count = signs.shape[0] // blocks
    half = rows // 2
    chunk = min(16, half)
    parts = blocks // rows
    shape = jax.ShapeDtypeStruct
    piece = (half // 2, 2 * count, width)
    return pl.pallas_call(
        functools.partial(first_kernel, count, chunk, blocks),
        out_shape=(
            shape((blocks, PAD, width), jnp.bfloat16),
            shape((parts,) + piece, jnp.bfloat16),
            shape((1,) + piece, jnp.bfloat16),
            shape(piece, jnp.float32),
            shape((half, slots, width, width), jnp.bfloat16),
            shape((half, slots, width, width), jnp.bfloat16),
            shape((parts,) + piece, jnp.bfloat16),
            shape((parts + 1,) + piece, jnp.bfloat16),
        ),
        grid_spec=pltpu.PrefetchScalarGridSpec(
            num_scalar_prefetch=2,
            grid=(rows // chunk,),
            in_specs=[
                whole(),
                pl.BlockSpec((chunk, slots, width, width), lambda g, *_: (g, 0, 0, 0)),
            ],
            out_specs=(whole(),) * 8,
            scratch_shapes=[pltpu.VMEM((blocks, PAD, width), jnp.float32)],
        ),
        compiler_params=params(),
        cost_estimate=cost(2 * rows * slots, width),
        name="first_step",
    )(meta, cols, signs, stored)


def cost(stored, width):
    return pl.CostEstimate(
        flops=2 * stored * 128 * width * width,
        transcendentals=0,
        bytes_accessed=8 * stored * width * width,
    )


def forward_kernel(
    count, chunk, rows, inverse, meta, cols_own, cols_other, own, other, panel, *rest
):
    out = rest[-1]
    half = rows // 2
    block = meta[0] * rows + meta[1] * half

    def body(step, carry):
        row = step * chunk
        for i in range(0, chunk, 2):
            results = []
            for r in (i, i + 1):
                product = row_product(
                    [
                        (own, row + r, cols_own, meta[1] * half + row + r),
                        (other, row + r, cols_other, row + r),
                    ],
                    panel,
                    LAST,
                )
                results.append(panel[block + row + r].astype(jnp.float32) + inverse * product)
            out[0, (row + i) // 2] = join_pair(results[0], results[1], count).astype(
                jnp.bfloat16
            )
        return carry

    lax.fori_loop(0, half // chunk, body, 0)


def forward(meta, cols_own, cols_other, own, other, panel, count, inverse, tokens):
    half, slots, width = own.shape[0], own.shape[1], own.shape[3]
    chunk = min(16, half)
    return pl.pallas_call(
        functools.partial(forward_kernel, count, chunk, 2 * half, inverse),
        out_shape=jax.ShapeDtypeStruct((1, half // 2, 2 * count, width), jnp.bfloat16),
        grid_spec=pltpu.PrefetchScalarGridSpec(
            num_scalar_prefetch=3,
            grid=(1,),
            in_specs=[whole()] * 3 + [pl.BlockSpec(memory_space=pl.ANY)] * len(tokens),
            out_specs=whole(),
        ),
        compiler_params=params(),
        cost_estimate=cost(2 * half * slots, width),
        name="forward_step",
    )(meta, cols_own, cols_other, own, other, panel, *tokens)


def scatter_row(value, refs_and_rows, total):
    targets = []
    stored = []
    for ref, row, cols, col_row in refs_and_rows:
        for k in range(ref.shape[1]):
            targets.append(cols[k, col_row])
            stored.append(ref[row, k])
    terms = lax.dot_general(
        value, jnp.concatenate(stored, axis=1), FIRST, preferred_element_type=jnp.float32
    )
    width = stored[0].shape[1]
    for i, target in enumerate(targets):
        total[target] = total[target] + terms[:, i * width : (i + 1) * width]


def give_totals(count, rows, meta, keep, send, total):
    half = rows // 2
    pairs = half // 2
    for out, h in ((send, 1), (keep, 0)):
        for d in range(keep.shape[0]):
            base = (meta[0] ^ d) * rows + (meta[1] ^ h) * half

            def body(i, carry, out=out, base=base, d=d):
                out[d, i] = join_pair(
                    total[base + 2 * i], total[base + 2 * i + 1], count
                ).astype(jnp.bfloat16)
                return carry

            lax.fori_loop(0, pairs, body, 0, unroll=8 if pairs % 8 == 0 else 4)


def backward_kernel(
    count, chunk, meta, cols_own, cols_other, own, other, left, keep, send, total
):
    half = own.shape[0]
    total[...] = jnp.zeros_like(total)

    def body(step, carry):
        for i in range(0, chunk, 2):
            pair = split_pair(left[0, (step * chunk + i) // 2], count)
            for r, value in zip((i, i + 1), pair):
                row = step * chunk + r
                scatter_row(
                    value.astype(jnp.bfloat16),
                    [(own, row, cols_own, meta[1] * half + row), (other, row, cols_other, row)],
                    total,
                )
        return carry

    lax.fori_loop(0, half // chunk, body, 0)
    give_totals(count, 2 * half, meta, keep, send, total)


def backward(meta, cols_own, cols_other, own, other, left, blocks):
    half, slots, width = own.shape[0], own.shape[1], own.shape[3]
    count = left.shape[2] // 2
    chunk = min(16, half)
    result = jax.ShapeDtypeStruct(
        (blocks // (2 * half), half // 2, 2 * count, width), jnp.bfloat16
    )
    return pl.pallas_call(
        functools.partial(backward_kernel, count, chunk),
        out_shape=(result, result),
        grid_spec=pltpu.PrefetchScalarGridSpec(
            num_scalar_prefetch=3,
            grid=(1,),
            in_specs=[whole()] * 3,
            out_specs=(whole(), whole()),
            scratch_shapes=[pltpu.VMEM((blocks, PAD, width), jnp.float32)],
        ),
        compiler_params=params(),
        cost_estimate=cost(2 * half * slots, width),
        name="backward_step",
    )(meta, cols_own, cols_other, own, other, left)


def gradient_kernel(scale, chunk, rows, terms, meta, cols, *refs):
    out = refs[-1]
    lefts = refs[: 4 * terms]
    rights = refs[4 * terms : 8 * terms]
    step = pl.program_id(0)
    slots = out.shape[1]
    contract = (((0,), (0,)), ((), ()))
    for r in range(chunk):
        row = step * chunk + r
        left = []
        for position, ref in enumerate(lefts):
            start = meta[0] * rows if position < terms else 0
            left.append(ref[start + row])
        left = jnp.concatenate(left, axis=0)
        right = []
        for k in range(slots):
            target = cols[k, row]
            right.append(jnp.concatenate([ref[target] for ref in rights], axis=0))
        product = lax.dot_general(
            left, jnp.concatenate(right, axis=1), contract, preferred_element_type=jnp.float32
        )
        width = out.shape[3]
        for k in range(slots):
            out[r, k] = (product[:, k * width : (k + 1) * width] * scale).astype(jnp.bfloat16)


def gradient(meta, cols, lefts, rights, rows, slots, scale):
    width = lefts[0].shape[2]
    chunk = min(16, rows)
    operands = list(lefts) + list(rights)
    return pl.pallas_call(
        functools.partial(gradient_kernel, scale, chunk, rows, len(lefts) // 4),
        out_shape=jax.ShapeDtypeStruct((rows, slots, width, width), jnp.bfloat16),
        grid_spec=pltpu.PrefetchScalarGridSpec(
            num_scalar_prefetch=2,
            grid=(rows // chunk,),
            in_specs=[whole()] * len(operands),
            out_specs=pl.BlockSpec((chunk, slots, width, width), lambda g, *_: (g, 0, 0, 0)),
        ),
        compiler_params=params(),
        name="gradient",
    )(meta, cols, *operands)


def local(block_values, columns, probe_signs):
    rows, slots, width = block_values.shape[0], block_values.shape[1], block_values.shape[3]
    blocks, count = probe_signs.shape[0], probe_signs.shape[1]
    half = rows // 2
    n_var = lax.axis_size("var")
    n_probe = lax.axis_size("probe")
    inverse = 1.0 / math.sqrt(KS * width)
    rep_index = lax.axis_index("rep")
    meta = jnp.stack([lax.axis_index("var"), rep_index]).astype(jnp.int32)
    signs = jnp.transpose(probe_signs, (1, 0, 2)).reshape(count * blocks, width)
    cols = columns.T

    def swap_rep(x):
        return lax.ppermute(x, "rep", [(0, 1), (1, 0)])

    def shift_var(x, bit):
        return lax.ppermute(x, "var", [(i, i ^ bit) for i in range(n_var)])

    def from_probes(x):
        return jnp.concatenate(
            [
                lax.ppermute(x, "probe", [(i, (i + d) % n_probe) for i in range(n_probe)])
                for d in range(1, n_probe)
            ],
            axis=0,
        )

    def wide(x):
        return x.astype(jnp.float32)

    def narrow(x):
        return x.astype(jnp.bfloat16)

    def exchange(own, parts, extra):
        size = extra.shape[0]
        if n_var == 4:
            far = shift_var(own, 2)
            near = shift_var(jnp.concatenate([own, narrow(parts[3])], axis=0), 1)
            own_other = swap_rep(own)
            crossed = shift_var(narrow(parts[2] + wide(near[1:])), 2)
            last = shift_var(jnp.concatenate([far, narrow(parts[1])], axis=0), 1)
            swapped = swap_rep(jnp.concatenate([near[:1], far, extra], axis=0))
            summed = parts[0] + wide(last[1:]) + wide(crossed)
            pieces = [
                (own, [0]), (near, [1, None]), (far, [2]), (last, [3, None]),
            ]
            others = [
                (own_other, [0]), (swapped, [1, 2] + [None] * size), (swap_rep(last[:1]), [3]),
            ]
            return pieces, others, summed, swapped[2:]
        bits = [1 << i for i in range(n_var.bit_length() - 1)]
        held = {0: own}
        for bit in reversed(bits):
            for d in list(held):
                held[d | bit] = shift_var(held[d], bit)
        sums = dict(enumerate(parts))
        for bit in bits:
            for d in sorted(sums, reverse=True):
                if d & bit:
                    sums[d ^ bit] = sums[d ^ bit] + wide(shift_var(narrow(sums.pop(d)), bit))
        pieces = [(jnp.concatenate([held[d] for d in range(n_var)], axis=0), list(range(n_var)))]
        swapped = swap_rep(jnp.concatenate([pieces[0][0], extra], axis=0))
        others = [(swapped, list(range(n_var)) + [None] * size)]
        return pieces, others, sums[0], swapped[n_var:]

    def home(d, h):
        if d is None:
            return None
        return lambda v, r: (v ^ d) * rows + (r ^ h) * half

    def place(pieces, h):
        return [(array, [home(d, h) for d in ds]) for array, ds in pieces]

    def joined(pieces):
        found = {}
        for array, ds in pieces:
            for i, d in enumerate(ds):
                if d is not None:
                    found[d] = array if len(ds) == 1 else array[i : i + 1]
        return jnp.concatenate([found[d] for d in range(n_var)], axis=0)

    def row_place(h):
        return lambda v, r: (r ^ h) * half

    def sign_place(p, h):
        return lambda v, r: (r ^ h) * (blocks // 2) + p * half

    other_columns = swap_rep(
        lax.dynamic_slice_in_dim(cols, (1 - rep_index) * half, half, 1)
    )
    panel, sent, left_own, kept, near, far, keep, send = first_step(
        meta, cols, signs, block_values, blocks
    )
    received = swap_rep(send)
    other = swap_rep(far)
    updated = narrow(wide(left_own) + inverse * (kept + wide(received[n_var]))[None])
    groups = n_probe - 1
    right = [[panel]] + [[] for _ in range(groups)]
    left = [[panel]] + [[] for _ in range(groups)]
    travelling = from_probes(sent)

    for step in range(3):
        last = step == 2
        parts = [wide(keep[d : d + 1]) + wide(received[d : d + 1]) for d in range(n_var)]
        extra = travelling if step == 0 else jnp.concatenate([travelling, left_own], axis=0)
        pieces, others, summed, extra_other = exchange(updated, parts, extra)
        size = n_var if step == 0 else n_var + 1
        fresh = []
        for index in range(groups):
            spots = {}
            for h in (0, 1):
                where = [None] * extra.shape[0]
                for p in range(n_var):
                    where[index * size + p] = sign_place(p, h) if step == 0 else home(p, h)
                spots[h] = where
            value = unpack(meta, [(travelling, spots[0][: travelling.shape[0]]), (extra_other, spots[1])], blocks)
            right[1 + index].append(value)
            fresh.append(value)
            if step == 0:
                left[1 + index].append(value)
            else:
                spots = {}
                for h in (0, 1):
                    where = [None] * extra.shape[0]
                    where[index * size + n_var] = row_place(h)
                    spots[h] = where
                value = unpack(meta, [(travelling, spots[0][: travelling.shape[0]]), (extra_other, spots[1])], rows)
                left[1 + index].append(value)
                fresh.append(value)
        if step > 0:
            tail = [None] * (extra.shape[0] - 1)
            value = unpack(
                meta, [(left_own, [row_place(0)]), (extra_other, tail + [row_place(1)])], rows
            )
            left[0].append(value)
            fresh.append(value)
        panel = unpack(meta, place(pieces, 0) + place(others, 1), blocks)
        right[0].append(panel)
        left_own = narrow(wide(left_own) + inverse * summed)
        if not last:
            travelling = from_probes(jnp.concatenate([joined(pieces), left_own], axis=0))
            keep, send = backward(meta, cols, other_columns, near, other, left_own, blocks)
            received = swap_rep(send)
            updated = forward(
                meta, cols, other_columns, near, other, panel, count, inverse, [send] + fresh
            )

    if n_var == 4:
        first = from_probes(jnp.concatenate([pieces[0][0], pieces[1][0][:1], pieces[2][0]], axis=0))
        late = from_probes(jnp.concatenate([pieces[3][0][:1], left_own], axis=0))
        arrays = [(first, [0, 1, 2]), (late, [3, "row"])]
    else:
        arrays = [(from_probes(jnp.concatenate([joined(pieces), left_own], axis=0)), list(range(n_var)) + ["row"])]
    crossed = [swap_rep(array) for array, _ in arrays]
    for index in range(groups):
        blocks_in = []
        rows_in = []
        for h, versions in ((0, [array for array, _ in arrays]), (1, crossed)):
            for array, (_, ds) in zip(versions, arrays):
                lead = [None] * (index * len(ds))
                rest = [None] * (array.shape[0] - (index + 1) * len(ds))
                here = [None if d == "row" else home(d, h) for d in ds]
                blocks_in.append((array, lead + here + rest))
                if "row" in ds:
                    here = [row_place(h) if d == "row" else None for d in ds]
                    rows_in.append((array, lead + here + rest))
        right[1 + index].append(unpack(meta, blocks_in, blocks))
        left[1 + index].append(unpack(meta, rows_in, rows))
    left[0].append(
        unpack(meta, [(left_own, [row_place(0)]), (swap_rep(left_own), [row_place(1)])], rows)
    )

    lefts = [group[t] for t in range(4) for group in left]
    rights = [group[3 - t] for t in range(4) for group in right]
    scale = 1.0 / (count * n_probe)
    return gradient(meta, cols, lefts, rights, rows, slots, scale)


def solution(mesh):
    return jax.shard_map(
        local,
        mesh=mesh,
        in_specs=(
            P(("groups", "var"), "rep", None, None),
            P(("groups", "var"), "rep"),
            P("groups", "probe", None),
        ),
        out_specs=P(("groups", "var"), "rep", None, None),
        check_vma=False,
    )
```

time: 152 us -> 129 us (0.85)
  starting transfers between devices: 40.2 us -> 31.1 us
  local copies, waits for them, and re-layouts: 15.8 us -> 8.24 us
  Pallas kernels: 43.7 us -> 39.4 us
  other arithmetic: 7.21 us -> 5.15 us
    ppermute x31 -> x17, waiting for transfers between devices: 1.14 us -> 8.62 us  [swap_rep(): return lax.ppermute(x, 'rep', [(0, 1), (1, 0)])]
    ppermute x18 -> x12, starting transfers between devices: 25.3 us -> 18.6 us  [shift_var(): return lax.ppermute(x, 'var', [(i, i ^ bit) for i in range(n_var)])]
    unnamed x20 -> x25, local copies, waits for them, and re-layouts: 13.2 us -> 7.27 us
    ppermute x10 -> x5, waiting for transfers between devices: 16.6 us -> 11.4 us  [from_probes(): lax.ppermute(x, 'probe', [(i, (i + d) % n_probe) for i in range(n_probe)])]
    convert_element_type x11 -> x7, other arithmetic: 6.14 us -> 1.4 us  [narrow(): return x.astype(jnp.bfloat16)]
    ppermute x18 -> x12, waiting for transfers between devices: 26.4 us -> 23.9 us  [shift_var(): return lax.ppermute(x, 'var', [(i, i ^ bit) for i in range(n_var)])]
    convert_element_type x2 -> x0, local copies, waits for them, and re-layouts: 2.5 us -> none  [local(): own_signs.astype(jnp.float32) + inverse * product]
    ppermute x31 -> x17, starting transfers between devices: 5.19 us -> 2.84 us  [swap_rep(): return lax.ppermute(x, 'rep', [(0, 1), (1, 0)])]
  transfers between devices with their start and end apart: 59 -> 34, of which waited for: 17 -> 17; matrix products, arithmetic and copies ran while one was open for 6% -> 6% of each run, Pallas kernels for 15% -> 16%
where the time goes in v3:
time: 129 us; the launch traced here: 128 us
  waiting for transfers between devices  43.9 us (34%)
  Pallas kernels  39.4 us (31%)
  starting transfers between devices  31.1 us (24%)
  local copies, waits for them, and re-layouts  8.24 us (6%)
  other arithmetic  5.15 us (4%)
    ppermute x12, waiting for transfers between devices, shift_var(): return lax.ppermute(x, 'var', [(i, i ^ bit) for i in range(n_var)])  23.9 us
    ppermute x12, starting transfers between devices, shift_var(): return lax.ppermute(x, 'var', [(i, i ^ bit) for i in range(n_var)])  18.6 us
    ppermute x5, waiting for transfers between devices, from_probes(): lax.ppermute(x, 'probe', [(i, (i + d) % n_probe) for i in range(n_probe)])  11.4 us
    ppermute x5, starting transfers between devices, from_probes(): lax.ppermute(x, 'probe', [(i, (i + d) % n_probe) for i in range(n_probe)])  9.62 us
    pallas_call x13, Pallas kernels, unpack(): pl.pallas_call(functools.partial(unpack_kernel, count, where), out_shape=...  9.51 us
    pallas_call x2, Pallas kernels, forward(): pl.pallas_call(functools.partial(forward_kernel, count, chunk, 2 * half,...  8.7 us
    ppermute x17, waiting for transfers between devices, swap_rep(): return lax.ppermute(x, 'rep', [(0, 1), (1, 0)])  8.62 us
    pallas_call x1, Pallas kernels, first_step(): pl.pallas_call(functools.partial(first_kernel, count, chunk, blocks), out...  8.3 us
  transfers between devices with their start and end apart: 34, of which 17 were waited for; matrix products, arithmetic and copies ran while one was open for 6% of the time, Pallas kernels for 16%

profile of v3, /device:TPU:0, one launch (start us, length us, event | category | flops | bytes accessed | tf_op | source)
XLA Modules:
  0.0 128.2 jit_solution(4739797006546757059)
XLA Ops:
  0.1 2.8 %copy-done = bf16[64,3,128,128]{3,2,1,0:T(8,128)(2,1)S(1)} copy-done((bf16[64,3,128,128]{3,2,1,0:T(8,128)(2,1)S(1)}, bf16[64,3,128,128]{3,2,1,0:T(8,128)(2,1)}, u32[]{:S(2)}) %copy-start) | copy-done | bytes 6291480
  2.9 1.4 %copy-done.3 = s32[256,12,128]{2,0,1:T(8,128)S(1)} copy-done((s32[256,12,128]{2,0,1:T(8,128)S(1)}, s32[256,12,128]{2,0,1:T(8,128)}, u32[]{:S(2)}) %copy-start.3) | copy-done | bytes 1572888
  4.3 0.7 copy-done.5
  5.0 8.3 %first_step.1 = (bf16[256,16,128]{2,1,0:T(8,128)(2,1)S(1)}, bf16[4,16,24,128]{3,2,1,0:T(8,128)(2,1)S(1)}, bf16[1,16,24,128]{3,2,1,0:T(8,128)(2,1)S(1)}, f32[16,2...) custom-call(s32[2]{0:T(128)S(1)} %pad_add_fusion.meta, ...), custom_call_target="tpu_custom_call" | custom-call | flops 1610612736 | bytes 50331648 | tf_op jit(solution)/shard_map/first_step/pallas_call | solution.py:168
  13.3 1.0 copy-done.1
  14.8 5.9 %collective-permute-done.1 = bf16[5,16,24,128]{3,2,1,0:T(8,128)(2,1)S(1)} collective-permute-done((bf16[5,16,24,128]{3,2,1,0:T(8,128)(2,1)S(1)}, bf16[5,16,24,128]{3,2,1,0:T(8,128)(2,1)S(1)}, u32[]{:S(2)}, u32[]{:S(2)}) %collective-permute-start.1) | collective-permute-done | bytes 491552 | tf_op jit(solution)/shard_map/ppermute | solution.py:384
  20.6 0.8 constant_dynamic-update-slice_fusion.4
  21.4 0.7 pad_maximum_fusion.4
  22.2 2.7 %collective-permute-start.2 = (bf16[2,16,24,128]{3,2,1,0:T(8,128)(2,1)}, bf16[2,16,24,128]{3,2,1,0:T(8,128)(2,1)S(1)}, u32[]{:S(2)}, u32[]{:S(2)}) collective-permute-start(bf16[2,16,24,128]{3,2,1,0:T(8,128)(2,1)} %pad_maximum_fusion.4), channel_id=1, source_target_pairs={{0,4},{4,0},{8,12},{12,8},{1,5},{5,1},{9,13},{13,9},{2,6},{6,2},{1... | collective-permute-start | bytes 589832 | tf_op jit(solution)/shard_map/ppermute | solution.py:387
  25.0 1.5 %collective-permute-start = (bf16[4,16,24,128]{3,2,1,0:T(8,128)(2,1)}, bf16[4,16,24,128]{3,2,1,0:T(8,128)(2,1)S(1)}, u32[]{:S(2)}, u32[]{:S(2)}) collective-permute-start(bf16[4,16,24,128]{3,2,1,0:T(8,128)(2,1)} %copy-done.7), channel_id=1, source_target_pairs={{0,2},{2,0},{1,3},{3,1},{4,6},{6,4},{5,7},{7,5},{8,10},{10,8},{9,1... | collective-permute-start | bytes 1179656 | tf_op jit(solution)/shard_map/ppermute | solution.py:392
  26.5 2.6 %collective-permute-start.3 = (bf16[1,16,24,128]{3,2,1,0:T(8,128)(2,1)S(1)}, bf16[1,16,24,128]{3,2,1,0:T(8,128)(2,1)S(1)}, u32[]{:S(2)}, u32[]{:S(2)}) collective-permute-start(bf16[1,16,24,128]{3,2,1,0:T(8,128)(2,1)S(1)} %get-tuple-element.34.refs_0_), channel_id=1, source_target_pairs={{0,8},{4,12},{8,0},{12,4},{1,9},{5,13},{9,1},{13,5},{2,10},{6,14},... | collective-permute-start | bytes 294920 | tf_op jit(solution)/shard_map/ppermute | solution.py:387
  29.1 3.5 %collective-permute-done.2.refs_1_ = bf16[2,16,24,128]{3,2,1,0:T(8,128)(2,1)S(1)} collective-permute-done((bf16[2,16,24,128]{3,2,1,0:T(8,128)(2,1)}, bf16[2,16,24,128]{3,2,1,0:T(8,128)(2,1)S(1)}, u32[]{:S(2)}, u32[]{:S(2)}) %collective-permute-start.2) | collective-permute-done | bytes 196640 | tf_op jit(solution)/shard_map/ppermute | solution.py:387
  32.6 1.1 add_convert_fusion.8
  33.7 1.4 %collective-permute-start.6 = (bf16[1,16,24,128]{3,2,1,0:T(8,128)(2,1)S(1)}, bf16[1,16,24,128]{3,2,1,0:T(8,128)(2,1)S(1)}, u32[]{:S(2)}, u32[]{:S(2)}) collective-permute-start(bf16[1,16,24,128]{3,2,1,0:T(8,128)(2,1)S(1)} %get-tuple-element.35), channel_id=1, source_target_pairs={{0,8},{4,12},{8,0},{12,4},{1,9},{5,13},{9,1},{13,5},{2,10},{6,14},... | collective-permute-start | bytes 294920 | tf_op jit(solution)/shard_map/ppermute | solution.py:387
  35.1 2.4 %collective-permute-start.5 = (bf16[2,16,24,128]{3,2,1,0:T(8,128)(2,1)S(1)}, bf16[2,16,24,128]{3,2,1,0:T(8,128)(2,1)S(1)}, u32[]{:S(2)}, u32[]{:S(2)}) collective-permute-start(bf16[2,16,24,128]{3,2,1,0:T(8,128)(2,1)S(1)} %pad_maximum_fusion.5), channel_id=1, source_target_pairs={{0,4},{4,0},{8,12},{12,8},{1,5},{5,1},{9,13},{13,9},{2,6},{6,2},{1... | collective-permute-start | bytes 589832 | tf_op jit(solution)/shard_map/ppermute | solution.py:387
  37.5 0.7 constant_dynamic-update-slice_fusion.3
  38.3 0.7 constant_dynamic-update-slice_fusion.2
  39.0 3.9 %collective-permute-done.5.refs_3_ = bf16[2,16,24,128]{3,2,1,0:T(8,128)(2,1)S(1)} collective-permute-done((bf16[2,16,24,128]{3,2,1,0:T(8,128)(2,1)S(1)}, bf16[2,16,24,128]{3,2,1,0:T(8,128)(2,1)S(1)}, u32[]{:S(2)}, u32[]{:S(2)}) %collective-permute-start.5) | collective-permute-done | bytes 196640 | tf_op jit(solution)/shard_map/ppermute | solution.py:387
  42.9 0.7 fusion.7
  43.6 1.7 %constant_dynamic-update-slice_fusion = (bf16[5,16,24,128]{3,2,1,0:T(8,128)(2,1)}, bf16[1,16,24,128]{3,2,1,0:T(8,128)(2,1)S(1)}) fusion(bf16[5,16,24,128]{3,2,1,0:T(8,128)(2,1)} %get-tuple-element.46, bf16[1,16,24,128]{3,2,1,0:T(8,128)(2,1)S(1)} %collective-permute-done.6, bf16[2,16,24,128]{3,2,1,0:T(8,128)(2,1)S(1)} %collective-permute-done.5.refs_3_, ...), kind=kLoop, calls=%fused_computation.30 | loop fusion | flops 540672 | bytes 688128 | tf_op jit(solution)/shard_map/concatenate | solution.py:511
  45.2 4.1 %backward_step.2 = (bf16[4,16,24,128]{3,2,1,0:T(8,128)(2,1)S(1)}, bf16[4,16,24,128]{3,2,1,0:T(8,128)(2,1)S(1)}) custom-call(s32[2]{0:T(128)S(1)} %pad_add_fusion.meta, s32[3,64]{1,0:T(4,128)S(1)} %bitcast.21, s32[3,32]{1,0:T(4,128)S(1)} %collective-permute-done.7.cols_other, bf16[32,3,128,128]{3,2,1,0:T(8,128)(2,1)S(1)} %get-tuple-element.23.own, ...), custom_call_target="tpu_custom_call" | custom-call | flops 805306368 | bytes 25165824 | tf_op jit(solution)/shard_map/backward_step/pallas_call | solution.py:311
  49.4 0.5 collective-permute-start.9
  50.0 0.8 unpack_panel.13.rest_1_.refs_1_.refs_15_
  51.4 0.8 unpack_panel.14.panel.refs_12_
  52.3 4.3 %forward_step.2.refs_0_ = bf16[1,16,24,128]{3,2,1,0:T(8,128)(2,1)S(1)} custom-call(s32[2]{0:T(128)S(1)} %pad_add_fusion.meta, s32[3,64]{1,0:T(4,128)S(1)} %bitcast.22, s32[3,32]{1,0:T(4,128)S(1)} %collective-permute-done.7.cols_other, bf16[32,3,128,128]{3,2,1,0:T(8,128)(2,1)S(1)} %get-tuple-element.23.own, ...), custom_call_target="tpu_custom_call" | custom-call | flops 805306368 | bytes 25165824 | tf_op jit(solution)/shard_map/forward_step/pallas_call | solution.py:236
  56.7 1.0 collective-permute-start.12
  57.7 2.1 %collective-permute-start.14 = (bf16[5,16,24,128]{3,2,1,0:T(8,128)(2,1)S(1)}, bf16[5,16,24,128]{3,2,1,0:T(8,128)(2,1)S(1)}, u32[]{:S(2)}, u32[]{:S(2)}) collective-permute-start(bf16[5,16,24,128]{3,2,1,0:T(8,128)(2,1)S(1)} %copy-done.9), channel_id=1, source_target_pairs={{0,2},{2,0},{1,3},{3,1},{4,6},{6,4},{5,7},{7,5},{8,10},{10,8},{9,1... | collective-permute-start | bytes 1474568 | tf_op jit(solution)/shard_map/ppermute | solution.py:392
  59.9 2.1 %collective-permute-start.13 = (bf16[1,16,24,128]{3,2,1,0:T(8,128)(2,1)S(1)}, bf16[1,16,24,128]{3,2,1,0:T(8,128)(2,1)S(1)}, u32[]{:S(2)}, u32[]{:S(2)}) collective-permute-start(bf16[1,16,24,128]{3,2,1,0:T(8,128)(2,1)S(1)} %forward_step.2.refs_0_), channel_id=1, source_target_pairs={{0,8},{4,12},{8,0},{12,4},{1,9},{5,13},{9,1},{13,5},{2,10},{6,14},... | collective-permute-start | bytes 294920 | tf_op jit(solution)/shard_map/ppermute | solution.py:387
  62.0 3.1 %collective-permute-done.12.refs_1_ = bf16[2,16,24,128]{3,2,1,0:T(8,128)(2,1)S(1)} collective-permute-done((bf16[2,16,24,128]{3,2,1,0:T(8,128)(2,1)S(1)}, bf16[2,16,24,128]{3,2,1,0:T(8,128)(2,1)S(1)}, u32[]{:S(2)}, u32[]{:S(2)}) %collective-permute-start.12) | collective-permute-done | bytes 196640 | tf_op jit(solution)/shard_map/ppermute | solution.py:387
  65.2 0.8 collective-permute-start.17
  66.0 1.7 %collective-permute-done.13.refs_2_ = bf16[1,16,24,128]{3,2,1,0:T(8,128)(2,1)S(1)} collective-permute-done((bf16[1,16,24,128]{3,2,1,0:T(8,128)(2,1)S(1)}, bf16[1,16,24,128]{3,2,1,0:T(8,128)(2,1)S(1)}, u32[]{:S(2)}, u32[]{:S(2)}) %collective-permute-start.13) | collective-permute-done | bytes 98336 | tf_op jit(solution)/shard_map/ppermute | solution.py:387
  67.7 0.8 collective-permute-start.16
  68.6 2.5 %collective-permute-done.14.refs_0_ = bf16[5,16,24,128]{3,2,1,0:T(8,128)(2,1)S(1)} collective-permute-done((bf16[5,16,24,128]{3,2,1,0:T(8,128)(2,1)S(1)}, bf16[5,16,24,128]{3,2,1,0:T(8,128)(2,1)S(1)}, u32[]{:S(2)}, u32[]{:S(2)}) %collective-permute-start.14) | collective-permute-done | bytes 491552 | tf_op jit(solution)/shard_map/ppermute | solution.py:392
  71.3 2.5 %collective-permute-done.16.refs_3_ = bf16[2,16,24,128]{3,2,1,0:T(8,128)(2,1)S(1)} collective-permute-done((bf16[2,16,24,128]{3,2,1,0:T(8,128)(2,1)S(1)}, bf16[2,16,24,128]{3,2,1,0:T(8,128)(2,1)S(1)}, u32[]{:S(2)}, u32[]{:S(2)}) %collective-permute-start.16) | collective-permute-done | bytes 196640 | tf_op jit(solution)/shard_map/ppermute | solution.py:387
  74.0 4.1 %backward_step.3 = (bf16[4,16,24,128]{3,2,1,0:T(8,128)(2,1)S(1)}, bf16[4,16,24,128]{3,2,1,0:T(8,128)(2,1)S(1)}) custom-call(s32[2]{0:T(128)S(1)} %pad_add_fusion.meta, s32[3,64]{1,0:T(4,128)S(1)} %bitcast.23, s32[3,32]{1,0:T(4,128)S(1)} %collective-permute-done.7.cols_other, bf16[32,3,128,128]{3,2,1,0:T(8,128)(2,1)S(1)} %get-tuple-element.23.own, ...), custom_call_target="tpu_custom_call" | custom-call | flops 805306368 | bytes 25165824 | tf_op jit(solution)/shard_map/backward_step/pallas_call | solution.py:311
  78.1 0.5 collective-permute-start.18
  78.7 1.1 collective-permute-done.20
  80.0 0.6 unpack_panel.15.rest_3_.refs_2_
  80.6 0.6 unpack_panel.16.rest_2_.refs_3_
  81.2 0.8 unpack_panel.18.rest_1_.refs_13_
  82.1 0.8 unpack_panel.17.panel.refs_10_
  82.9 4.3 %forward_step.3.refs_0_ = bf16[1,16,24,128]{3,2,1,0:T(8,128)(2,1)S(1)} custom-call(s32[2]{0:T(128)S(1)} %pad_add_fusion.meta, s32[3,64]{1,0:T(4,128)S(1)} %bitcast.24, s32[3,32]{1,0:T(4,128)S(1)} %collective-permute-done.7.cols_other, bf16[32,3,128,128]{3,2,1,0:T(8,128)(2,1)S(1)} %get-tuple-element.23.own, ...), custom_call_target="tpu_custom_call" | custom-call | flops 805306368 | bytes 25165824 | tf_op jit(solution)/shard_map/forward_step/pallas_call | solution.py:236
  87.3 1.1 collective-permute-start.21
  88.4 2.7 %collective-permute-start.23 = (bf16[5,16,24,128]{3,2,1,0:T(8,128)(2,1)S(1)}, bf16[5,16,24,128]{3,2,1,0:T(8,128)(2,1)S(1)}, u32[]{:S(2)}, u32[]{:S(2)}) collective-permute-start(bf16[5,16,24,128]{3,2,1,0:T(8,128)(2,1)S(1)} %get-tuple-element.29), channel_id=1, source_target_pairs={{0,2},{2,0},{1,3},{3,1},{4,6},{6,4},{5,7},{7,5},{8,10},{10,8},{9,1... | collective-permute-start | bytes 1474568 | tf_op jit(solution)/shard_map/ppermute | solution.py:392
  91.1 2.0 %collective-permute-start.22 = (bf16[1,16,24,128]{3,2,1,0:T(8,128)(2,1)S(1)}, bf16[1,16,24,128]{3,2,1,0:T(8,128)(2,1)S(1)}, u32[]{:S(2)}, u32[]{:S(2)}) collective-permute-start(bf16[1,16,24,128]{3,2,1,0:T(8,128)(2,1)S(1)} %forward_step.3.refs_0_), channel_id=1, source_target_pairs={{0,8},{4,12},{8,0},{12,4},{1,9},{5,13},{9,1},{13,5},{2,10},{6,14},... | collective-permute-start | bytes 294920 | tf_op jit(solution)/shard_map/ppermute | solution.py:387
  93.1 1.3 collective-permute-done.21.refs_1_
  94.4 1.7 %collective-permute-start.26 = (bf16[1,16,24,128]{3,2,1,0:T(8,128)(2,1)S(1)}, bf16[1,16,24,128]{3,2,1,0:T(8,128)(2,1)S(1)}, u32[]{:S(2)}, u32[]{:S(2)}) collective-permute-start(bf16[1,16,24,128]{3,2,1,0:T(8,128)(2,1)S(1)} %get-tuple-element.38), channel_id=1, source_target_pairs={{0,8},{4,12},{8,0},{12,4},{1,9},{5,13},{9,1},{13,5},{2,10},{6,14},... | collective-permute-start | bytes 294920 | tf_op jit(solution)/shard_map/ppermute | solution.py:387
  96.1 5.3 %collective-permute-done.22.refs_2_ = bf16[1,16,24,128]{3,2,1,0:T(8,128)(2,1)S(1)} collective-permute-done((bf16[1,16,24,128]{3,2,1,0:T(8,128)(2,1)S(1)}, bf16[1,16,24,128]{3,2,1,0:T(8,128)(2,1)S(1)}, u32[]{:S(2)}, u32[]{:S(2)}) %collective-permute-start.22) | collective-permute-done | bytes 98336 | tf_op jit(solution)/shard_map/ppermute | solution.py:387
  101.5 1.1 collective-permute-done.23.refs_0_
  102.8 1.8 %collective-permute-start.32 = (bf16[3,16,24,128]{3,2,1,0:T(8,128)(2,1)S(1)}, bf16[3,16,24,128]{3,2,1,0:T(8,128)(2,1)S(1)}, u32[]{:S(2)}, u32[]{:S(2)}) collective-permute-start(bf16[3,16,24,128]{3,2,1,0:T(8,128)(2,1)S(1)} %pad_maximum_fusion.3), channel_id=1, source_target_pairs={{0,2},{2,0},{1,3},{3,1},{4,6},{6,4},{5,7},{7,5},{8,10},{10,8},{9,1... | collective-permute-start | bytes 884744 | tf_op jit(solution)/shard_map/ppermute | solution.py:392
  104.6 2.5 %collective-permute-done.25.refs_3_ = bf16[2,16,24,128]{3,2,1,0:T(8,128)(2,1)S(1)} collective-permute-done((bf16[2,16,24,128]{3,2,1,0:T(8,128)(2,1)S(1)}, bf16[2,16,24,128]{3,2,1,0:T(8,128)(2,1)S(1)}, u32[]{:S(2)}, u32[]{:S(2)}) %collective-permute-start.25) | collective-permute-done | bytes 196640 | tf_op jit(solution)/shard_map/ppermute | solution.py:387
  107.3 1.5 %collective-permute-start.28 = (bf16[2,16,24,128]{3,2,1,0:T(8,128)(2,1)S(1)}, bf16[2,16,24,128]{3,2,1,0:T(8,128)(2,1)S(1)}, u32[]{:S(2)}, u32[]{:S(2)}) collective-permute-start(bf16[2,16,24,128]{3,2,1,0:T(8,128)(2,1)S(1)} %pad_maximum_fusion.10), channel_id=1, source_target_pairs={{0,2},{2,0},{1,3},{3,1},{4,6},{6,4},{5,7},{7,5},{8,10},{10,8},{9,1... | collective-permute-start | bytes 589832 | tf_op jit(solution)/shard_map/ppermute | solution.py:392
  108.7 4.0 %collective-permute-done.32.refs_0_ = bf16[3,16,24,128]{3,2,1,0:T(8,128)(2,1)S(1)} collective-permute-done((bf16[3,16,24,128]{3,2,1,0:T(8,128)(2,1)S(1)}, bf16[3,16,24,128]{3,2,1,0:T(8,128)(2,1)S(1)}, u32[]{:S(2)}, u32[]{:S(2)}) %collective-permute-start.32) | collective-permute-done | bytes 294944 | tf_op jit(solution)/shard_map/ppermute | solution.py:392
  112.7 3.8 %collective-permute-done.28.refs_0_.refs_1_ = bf16[2,16,24,128]{3,2,1,0:T(8,128)(2,1)S(1)} collective-permute-done((bf16[2,16,24,128]{3,2,1,0:T(8,128)(2,1)S(1)}, bf16[2,16,24,128]{3,2,1,0:T(8,128)(2,1)S(1)}, u32[]{:S(2)}, u32[]{:S(2)}) %collective-permute-start.28) | collective-permute-done | bytes 196640 | tf_op jit(solution)/shard_map/ppermute | solution.py:392
  116.5 0.5 collective-permute-start.27
  117.0 1.1 collective-permute-done.27.refs_1_
  118.3 0.6 unpack_panel.21.refs_6_
  118.9 0.6 unpack_panel.22.refs_7_
  119.6 0.8 unpack_panel.24.refs_9_
  120.5 0.6 unpack_panel.19.refs_4_
  121.1 0.6 unpack_panel.20.refs_5_
  121.8 0.8 unpack_panel.25.refs_11_
  122.6 0.8 unpack_panel.23.refs_8_
  123.5 4.8 %gradient.1 = bf16[64,3,128,128]{3,2,1,0:T(8,128)(2,1)} custom-call(s32[2]{0:T(128)S(1)} %pad_add_fusion.meta, s32[3,64]{1,0:T(4,128)S(1)} %bitcast.25, bf16[256,16,128]{2,1,0:T(8,128)(2,1)S(1)} %copy-done.2, bf16[256,16,128]{2,1,0:T(8,128)(2,1)S(1)} %unpack_panel.13.rest_1_.refs_1_.refs_15_, bf16[64,16,128]{2,1,0:T(8,128)(2,1)S(1)} %unpack_panel.15.rest_3_.refs_2_, ...), custom_call_target="tpu_custom_call" | custom-call | tf_op jit(solution)/shard_map/gradient/pallas_call | solution.py:357
  (78 shorter events, 3.3 us)
Async XLA Ops:
  0.1 2.8 %copy-start = (bf16[64,3,128,128]{3,2,1,0:T(8,128)(2,1)S(1)}, bf16[64,3,128,128]{3,2,1,0:T(8,128)(2,1)}, u32[]{:S(2)}) copy-start(bf16[64,3,128,128]{3,2,1,0:T(8,128)(2,1)} %stored.1) | copy-start | bytes 18874372
  2.9 1.4 %copy-start.3 = (s32[256,12,128]{2,0,1:T(8,128)S(1)}, s32[256,12,128]{2,0,1:T(8,128)}, u32[]{:S(2)}) copy-start(s32[256,12,128]{2,0,1:T(8,128)} %param.5) | copy-start | bytes 4718596
  4.3 0.7 copy-start.5
  5.0 19.9 %copy-start.6 = (s32[64,3]{0,1:T(4,128)S(1)}, s32[64,3]{0,1:T(4,128)}, u32[]{:S(2)}) copy-start(s32[64,3]{0,1:T(4,128)} %param.4) | copy-start | bytes 2308
  13.3 1.0 copy-start.1
  14.2 7.2 %copy-start.4 = (bf16[4,16,24,128]{3,2,1,0:T(8,128)(2,1)}, bf16[4,16,24,128]{3,2,1,0:T(8,128)(2,1)S(1)}, u32[]{:S(2)}) copy-start(bf16[4,16,24,128]{3,2,1,0:T(8,128)(2,1)S(1)} %get-tuple-element.22) | copy-start | bytes 1179652
  14.2 7.9 %copy-start.7 = (bf16[4,16,24,128]{3,2,1,0:T(8,128)(2,1)}, bf16[4,16,24,128]{3,2,1,0:T(8,128)(2,1)S(1)}, u32[]{:S(2)}) copy-start(bf16[4,16,24,128]{3,2,1,0:T(8,128)(2,1)S(1)} %get-tuple-element.18) | copy-start | bytes 1179652
  14.2 31.0 %collective-permute-start.8 = (bf16[32,3,128,128]{3,2,1,0:T(8,128)(2,1)}, bf16[32,3,128,128]{3,2,1,0:T(8,128)(2,1)}, u32[]{:S(2)}, u32[]{:S(2)}) collective-permute-start(bf16[32,3,128,128]{3,2,1,0:T(8,128)(2,1)} %get-tuple-element.24), channel_id=1, source_target_pairs={{0,1},{1,0},{2,3},{3,2},{4,5},{5,4},{6,7},{7,6},{8,9},{9,8},{10,11... | collective-permute-start | bytes 9437192 | tf_op jit(solution)/shard_map/ppermute | solution.py:384
  14.7 5.9 %collective-permute-start.1 = (bf16[5,16,24,128]{3,2,1,0:T(8,128)(2,1)S(1)}, bf16[5,16,24,128]{3,2,1,0:T(8,128)(2,1)S(1)}, u32[]{:S(2)}, u32[]{:S(2)}) collective-permute-start(bf16[5,16,24,128]{3,2,1,0:T(8,128)(2,1)S(1)} %get-tuple-element.21), channel_id=1, source_target_pairs={{0,1},{1,0},{2,3},{3,2},{4,5},{5,4},{6,7},{7,6},{8,9},{9,8},{10,11... | collective-permute-start | bytes 1474568 | tf_op jit(solution)/shard_map/ppermute | solution.py:384
  20.6 1.6 %copy-start.8 = (bf16[5,16,24,128]{3,2,1,0:T(8,128)(2,1)}, bf16[5,16,24,128]{3,2,1,0:T(8,128)(2,1)S(1)}, u32[]{:S(2)}) copy-start(bf16[5,16,24,128]{3,2,1,0:T(8,128)(2,1)S(1)} %collective-permute-done.1) | copy-start | bytes 1474564
  22.2 10.4 %collective-permute-start.2 = (bf16[2,16,24,128]{3,2,1,0:T(8,128)(2,1)}, bf16[2,16,24,128]{3,2,1,0:T(8,128)(2,1)S(1)}, u32[]{:S(2)}, u32[]{:S(2)}) collective-permute-start(bf16[2,16,24,128]{3,2,1,0:T(8,128)(2,1)} %pad_maximum_fusion.4), channel_id=1, source_target_pairs={{0,4},{4,0},{8,12},{12,8},{1,5},{5,1},{9,13},{13,9},{2,6},{6,2},{1... | collective-permute-start | bytes 589832 | tf_op jit(solution)/shard_map/ppermute | solution.py:387
  24.9 20.3 %collective-permute-start.7 = (s32[3,32]{1,0:T(4,128)S(1)}, s32[3,32]{1,0:T(4,128)S(1)}, u32[]{:S(2)}, u32[]{:S(2)}) collective-permute-start(s32[3,32]{1,0:T(4,128)S(1)} %dynamic-slice_bitcast_fusion), channel_id=1, source_target_pairs={{0,1},{1,0},{2,3},{3,2},{4,5},{5,4},{6,7},{7,6},{8,9},{9,8},{10,11... | collective-permute-start | bytes 1160 | tf_op jit(solution)/shard_map/ppermute | solution.py:384
  25.0 13.2 %collective-permute-start = (bf16[4,16,24,128]{3,2,1,0:T(8,128)(2,1)}, bf16[4,16,24,128]{3,2,1,0:T(8,128)(2,1)S(1)}, u32[]{:S(2)}, u32[]{:S(2)}) collective-permute-start(bf16[4,16,24,128]{3,2,1,0:T(8,128)(2,1)} %copy-done.7), channel_id=1, source_target_pairs={{0,2},{2,0},{1,3},{3,1},{4,6},{6,4},{5,7},{7,5},{8,10},{10,8},{9,1... | collective-permute-start | bytes 1179656 | tf_op jit(solution)/shard_map/ppermute | solution.py:392
  26.5 8.6 %collective-permute-start.3 = (bf16[1,16,24,128]{3,2,1,0:T(8,128)(2,1)S(1)}, bf16[1,16,24,128]{3,2,1,0:T(8,128)(2,1)S(1)}, u32[]{:S(2)}, u32[]{:S(2)}) collective-permute-start(bf16[1,16,24,128]{3,2,1,0:T(8,128)(2,1)S(1)} %get-tuple-element.34.refs_0_), channel_id=1, source_target_pairs={{0,8},{4,12},{8,0},{12,4},{1,9},{5,13},{9,1},{13,5},{2,10},{6,14},... | collective-permute-start | bytes 294920 | tf_op jit(solution)/shard_map/ppermute | solution.py:387
  33.7 9.9 %collective-permute-start.6 = (bf16[1,16,24,128]{3,2,1,0:T(8,128)(2,1)S(1)}, bf16[1,16,24,128]{3,2,1,0:T(8,128)(2,1)S(1)}, u32[]{:S(2)}, u32[]{:S(2)}) collective-permute-start(bf16[1,16,24,128]{3,2,1,0:T(8,128)(2,1)S(1)} %get-tuple-element.35), channel_id=1, source_target_pairs={{0,8},{4,12},{8,0},{12,4},{1,9},{5,13},{9,1},{13,5},{2,10},{6,14},... | collective-permute-start | bytes 294920 | tf_op jit(solution)/shard_map/ppermute | solution.py:387
  35.1 7.8 %collective-permute-start.5 = (bf16[2,16,24,128]{3,2,1,0:T(8,128)(2,1)S(1)}, bf16[2,16,24,128]{3,2,1,0:T(8,128)(2,1)S(1)}, u32[]{:S(2)}, u32[]{:S(2)}) collective-permute-start(bf16[2,16,24,128]{3,2,1,0:T(8,128)(2,1)S(1)} %pad_maximum_fusion.5), channel_id=1, source_target_pairs={{0,4},{4,0},{8,12},{12,8},{1,5},{5,1},{9,13},{13,9},{2,6},{6,2},{1... | collective-permute-start | bytes 589832 | tf_op jit(solution)/shard_map/ppermute | solution.py:387
  38.2 11.8 %collective-permute-start.4 = (bf16[6,16,24,128]{3,2,1,0:T(8,128)(2,1)S(1)}, bf16[6,16,24,128]{3,2,1,0:T(8,128)(2,1)S(1)}, u32[]{:S(2)}, u32[]{:S(2)}) collective-permute-start(bf16[6,16,24,128]{3,2,1,0:T(8,128)(2,1)S(1)} %pad_maximum_fusion.2), channel_id=1, source_target_pairs={{0,1},{1,0},{2,3},{3,2},{4,5},{5,4},{6,7},{7,6},{8,9},{9,8},{10,11... | collective-permute-start | bytes 1769480 | tf_op jit(solution)/shard_map/ppermute | solution.py:384
  49.3 7.3 %collective-permute-start.11 = (bf16[4,16,24,128]{3,2,1,0:T(8,128)(2,1)S(1)}, bf16[4,16,24,128]{3,2,1,0:T(8,128)(2,1)S(1)}, u32[]{:S(2)}, u32[]{:S(2)}) collective-permute-start(bf16[4,16,24,128]{3,2,1,0:T(8,128)(2,1)S(1)} %get-tuple-element.25.rest_0_), channel_id=1, source_target_pairs={{0,1},{1,0},{2,3},{3,2},{4,5},{5,4},{6,7},{7,6},{8,9},{9,8},{10,11... | collective-permute-start | bytes 1179656 | tf_op jit(solution)/shard_map/ppermute | solution.py:384
  49.4 1.9 %collective-permute-start.9 = (bf16[1,16,24,128]{3,2,1,0:T(8,128)(2,1)S(1)}, bf16[1,16,24,128]{3,2,1,0:T(8,128)(2,1)S(1)}, u32[]{:S(2)}, u32[]{:S(2)}) collective-permute-start(bf16[1,16,24,128]{3,2,1,0:T(8,128)(2,1)S(1)} %get-tuple-element.34.refs_0_), channel_id=1, source_target_pairs={{0,1},{1,0},{2,3},{3,2},{4,5},{5,4},{6,7},{7,6},{8,9},{9,8},{10,11... | collective-permute-start | bytes 294920 | tf_op jit(solution)/shard_map/ppermute | solution.py:384
  49.9 1.5 %collective-permute-start.10 = (bf16[1,16,24,128]{3,2,1,0:T(8,128)(2,1)S(1)}, bf16[1,16,24,128]{3,2,1,0:T(8,128)(2,1)S(1)}, u32[]{:S(2)}, u32[]{:S(2)}) collective-permute-start(bf16[1,16,24,128]{3,2,1,0:T(8,128)(2,1)S(1)} %get-tuple-element.45), channel_id=1, source_target_pairs={{0,1},{1,0},{2,3},{3,2},{4,5},{5,4},{6,7},{7,6},{8,9},{9,8},{10,11... | collective-permute-start | bytes 294920 | tf_op jit(solution)/shard_map/ppermute | solution.py:384
  52.2 5.5 %copy-start.9 = (bf16[5,16,24,128]{3,2,1,0:T(8,128)(2,1)S(1)}, bf16[5,16,24,128]{3,2,1,0:T(8,128)(2,1)}, u32[]{:S(2)}) copy-start(bf16[5,16,24,128]{3,2,1,0:T(8,128)(2,1)} %get-tuple-element.31) | copy-start | bytes 1474564
  56.7 8.5 %collective-permute-start.12 = (bf16[2,16,24,128]{3,2,1,0:T(8,128)(2,1)S(1)}, bf16[2,16,24,128]{3,2,1,0:T(8,128)(2,1)S(1)}, u32[]{:S(2)}, u32[]{:S(2)}) collective-permute-start(bf16[2,16,24,128]{3,2,1,0:T(8,128)(2,1)S(1)} %pad_maximum_fusion.6), channel_id=1, source_target_pairs={{0,4},{4,0},{8,12},{12,8},{1,5},{5,1},{9,13},{13,9},{2,6},{6,2},{1... | collective-permute-start | bytes 589832 | tf_op jit(solution)/shard_map/ppermute | solution.py:387
  57.7 13.4 %collective-permute-start.14 = (bf16[5,16,24,128]{3,2,1,0:T(8,128)(2,1)S(1)}, bf16[5,16,24,128]{3,2,1,0:T(8,128)(2,1)S(1)}, u32[]{:S(2)}, u32[]{:S(2)}) collective-permute-start(bf16[5,16,24,128]{3,2,1,0:T(8,128)(2,1)S(1)} %copy-done.9), channel_id=1, source_target_pairs={{0,2},{2,0},{1,3},{3,1},{4,6},{6,4},{5,7},{7,5},{8,10},{10,8},{9,1... | collective-permute-start | bytes 1474568 | tf_op jit(solution)/shard_map/ppermute | solution.py:392
  59.9 7.8 %collective-permute-start.13 = (bf16[1,16,24,128]{3,2,1,0:T(8,128)(2,1)S(1)}, bf16[1,16,24,128]{3,2,1,0:T(8,128)(2,1)S(1)}, u32[]{:S(2)}, u32[]{:S(2)}) collective-permute-start(bf16[1,16,24,128]{3,2,1,0:T(8,128)(2,1)S(1)} %forward_step.2.refs_0_), channel_id=1, source_target_pairs={{0,8},{4,12},{8,0},{12,4},{1,9},{5,13},{9,1},{13,5},{2,10},{6,14},... | collective-permute-start | bytes 294920 | tf_op jit(solution)/shard_map/ppermute | solution.py:387
  65.2 8.6 %collective-permute-start.17 = (bf16[1,16,24,128]{3,2,1,0:T(8,128)(2,1)S(1)}, bf16[1,16,24,128]{3,2,1,0:T(8,128)(2,1)S(1)}, u32[]{:S(2)}, u32[]{:S(2)}) collective-permute-start(bf16[1,16,24,128]{3,2,1,0:T(8,128)(2,1)S(1)} %get-tuple-element.39), channel_id=1, source_target_pairs={{0,8},{4,12},{8,0},{12,4},{1,9},{5,13},{9,1},{13,5},{2,10},{6,14},... | collective-permute-start | bytes 294920 | tf_op jit(solution)/shard_map/ppermute | solution.py:387
  67.7 6.1 %collective-permute-start.16 = (bf16[2,16,24,128]{3,2,1,0:T(8,128)(2,1)S(1)}, bf16[2,16,24,128]{3,2,1,0:T(8,128)(2,1)S(1)}, u32[]{:S(2)}, u32[]{:S(2)}) collective-permute-start(bf16[2,16,24,128]{3,2,1,0:T(8,128)(2,1)S(1)} %pad_maximum_fusion.7), channel_id=1, source_target_pairs={{0,4},{4,0},{8,12},{12,8},{1,5},{5,1},{9,13},{13,9},{2,6},{6,2},{1... | collective-permute-start | bytes 589832 | tf_op jit(solution)/shard_map/ppermute | solution.py:387
  71.2 8.7 %collective-permute-start.15 = (bf16[8,16,24,128]{3,2,1,0:T(8,128)(2,1)S(1)}, bf16[8,16,24,128]{3,2,1,0:T(8,128)(2,1)S(1)}, u32[]{:S(2)}, u32[]{:S(2)}) collective-permute-start(bf16[8,16,24,128]{3,2,1,0:T(8,128)(2,1)S(1)} %pad_maximum_fusion), channel_id=1, source_target_pairs={{0,1},{1,0},{2,3},{3,2},{4,5},{5,4},{6,7},{7,6},{8,9},{9,8},{10,11... | collective-permute-start | bytes 2359304 | tf_op jit(solution)/shard_map/ppermute | solution.py:384
  78.1 1.8 %collective-permute-start.20 = (bf16[4,16,24,128]{3,2,1,0:T(8,128)(2,1)S(1)}, bf16[4,16,24,128]{3,2,1,0:T(8,128)(2,1)S(1)}, u32[]{:S(2)}, u32[]{:S(2)}) collective-permute-start(bf16[4,16,24,128]{3,2,1,0:T(8,128)(2,1)S(1)} %get-tuple-element.27.rest_0_), channel_id=1, source_target_pairs={{0,1},{1,0},{2,3},{3,2},{4,5},{5,4},{6,7},{7,6},{8,9},{9,8},{10,11... | collective-permute-start | bytes 1179656 | tf_op jit(solution)/shard_map/ppermute | solution.py:384
  78.1 3.9 %collective-permute-start.18 = (bf16[1,16,24,128]{3,2,1,0:T(8,128)(2,1)S(1)}, bf16[1,16,24,128]{3,2,1,0:T(8,128)(2,1)S(1)}, u32[]{:S(2)}, u32[]{:S(2)}) collective-permute-start(bf16[1,16,24,128]{3,2,1,0:T(8,128)(2,1)S(1)} %forward_step.2.refs_0_), channel_id=1, source_target_pairs={{0,1},{1,0},{2,3},{3,2},{4,5},{5,4},{6,7},{7,6},{8,9},{9,8},{10,11... | collective-permute-start | bytes 294920 | tf_op jit(solution)/shard_map/ppermute | solution.py:384
  78.6 3.4 %collective-permute-start.19 = (bf16[1,16,24,128]{3,2,1,0:T(8,128)(2,1)S(1)}, bf16[1,16,24,128]{3,2,1,0:T(8,128)(2,1)S(1)}, u32[]{:S(2)}, u32[]{:S(2)}) collective-permute-start(bf16[1,16,24,128]{3,2,1,0:T(8,128)(2,1)S(1)} %get-tuple-element.41), channel_id=1, source_target_pairs={{0,1},{1,0},{2,3},{3,2},{4,5},{5,4},{6,7},{7,6},{8,9},{9,8},{10,11... | collective-permute-start | bytes 294920 | tf_op jit(solution)/shard_map/ppermute | solution.py:384
  87.3 7.0 %collective-permute-start.21 = (bf16[2,16,24,128]{3,2,1,0:T(8,128)(2,1)S(1)}, bf16[2,16,24,128]{3,2,1,0:T(8,128)(2,1)S(1)}, u32[]{:S(2)}, u32[]{:S(2)}) collective-permute-start(bf16[2,16,24,128]{3,2,1,0:T(8,128)(2,1)S(1)} %pad_maximum_fusion.8), channel_id=1, source_target_pairs={{0,4},{4,0},{8,12},{12,8},{1,5},{5,1},{9,13},{13,9},{2,6},{6,2},{1... | collective-permute-start | bytes 589832 | tf_op jit(solution)/shard_map/ppermute | solution.py:387
  88.4 14.2 %collective-permute-start.23 = (bf16[5,16,24,128]{3,2,1,0:T(8,128)(2,1)S(1)}, bf16[5,16,24,128]{3,2,1,0:T(8,128)(2,1)S(1)}, u32[]{:S(2)}, u32[]{:S(2)}) collective-permute-start(bf16[5,16,24,128]{3,2,1,0:T(8,128)(2,1)S(1)} %get-tuple-element.29), channel_id=1, source_target_pairs={{0,2},{2,0},{1,3},{3,1},{4,6},{6,4},{5,7},{7,5},{8,10},{10,8},{9,1... | collective-permute-start | bytes 1474568 | tf_op jit(solution)/shard_map/ppermute | solution.py:392
  91.1 10.3 %collective-permute-start.22 = (bf16[1,16,24,128]{3,2,1,0:T(8,128)(2,1)S(1)}, bf16[1,16,24,128]{3,2,1,0:T(8,128)(2,1)S(1)}, u32[]{:S(2)}, u32[]{:S(2)}) collective-permute-start(bf16[1,16,24,128]{3,2,1,0:T(8,128)(2,1)S(1)} %forward_step.3.refs_0_), channel_id=1, source_target_pairs={{0,8},{4,12},{8,0},{12,4},{1,9},{5,13},{9,1},{13,5},{2,10},{6,14},... | collective-permute-start | bytes 294920 | tf_op jit(solution)/shard_map/ppermute | solution.py:387
  94.4 10.2 %collective-permute-start.26 = (bf16[1,16,24,128]{3,2,1,0:T(8,128)(2,1)S(1)}, bf16[1,16,24,128]{3,2,1,0:T(8,128)(2,1)S(1)}, u32[]{:S(2)}, u32[]{:S(2)}) collective-permute-start(bf16[1,16,24,128]{3,2,1,0:T(8,128)(2,1)S(1)} %get-tuple-element.38), channel_id=1, source_target_pairs={{0,8},{4,12},{8,0},{12,4},{1,9},{5,13},{9,1},{13,5},{2,10},{6,14},... | collective-permute-start | bytes 294920 | tf_op jit(solution)/shard_map/ppermute | solution.py:387
  101.4 5.7 %collective-permute-start.25 = (bf16[2,16,24,128]{3,2,1,0:T(8,128)(2,1)S(1)}, bf16[2,16,24,128]{3,2,1,0:T(8,128)(2,1)S(1)}, u32[]{:S(2)}, u32[]{:S(2)}) collective-permute-start(bf16[2,16,24,128]{3,2,1,0:T(8,128)(2,1)S(1)} %pad_maximum_fusion.9), channel_id=1, source_target_pairs={{0,4},{4,0},{8,12},{12,8},{1,5},{5,1},{9,13},{13,9},{2,6},{6,2},{1... | collective-permute-start | bytes 589832 | tf_op jit(solution)/shard_map/ppermute | solution.py:387
  102.7 17.7 %collective-permute-start.24 = (bf16[8,16,24,128]{3,2,1,0:T(8,128)(2,1)S(1)}, bf16[8,16,24,128]{3,2,1,0:T(8,128)(2,1)S(1)}, u32[]{:S(2)}, u32[]{:S(2)}) collective-permute-start(bf16[8,16,24,128]{3,2,1,0:T(8,128)(2,1)S(1)} %pad_maximum_fusion.1), channel_id=1, source_target_pairs={{0,1},{1,0},{2,3},{3,2},{4,5},{5,4},{6,7},{7,6},{8,9},{9,8},{10,11... | collective-permute-start | bytes 2359304 | tf_op jit(solution)/shard_map/ppermute | solution.py:384
  102.8 9.9 %collective-permute-start.32 = (bf16[3,16,24,128]{3,2,1,0:T(8,128)(2,1)S(1)}, bf16[3,16,24,128]{3,2,1,0:T(8,128)(2,1)S(1)}, u32[]{:S(2)}, u32[]{:S(2)}) collective-permute-start(bf16[3,16,24,128]{3,2,1,0:T(8,128)(2,1)S(1)} %pad_maximum_fusion.3), channel_id=1, source_target_pairs={{0,2},{2,0},{1,3},{3,1},{4,6},{6,4},{5,7},{7,5},{8,10},{10,8},{9,1... | collective-permute-start | bytes 884744 | tf_op jit(solution)/shard_map/ppermute | solution.py:392
  107.3 9.2 %collective-permute-start.28 = (bf16[2,16,24,128]{3,2,1,0:T(8,128)(2,1)S(1)}, bf16[2,16,24,128]{3,2,1,0:T(8,128)(2,1)S(1)}, u32[]{:S(2)}, u32[]{:S(2)}) collective-permute-start(bf16[2,16,24,128]{3,2,1,0:T(8,128)(2,1)S(1)} %pad_maximum_fusion.10), channel_id=1, source_target_pairs={{0,2},{2,0},{1,3},{3,1},{4,6},{6,4},{5,7},{7,5},{8,10},{10,8},{9,1... | collective-permute-start | bytes 589832 | tf_op jit(solution)/shard_map/ppermute | solution.py:392
  112.7 6.9 %collective-permute-start.33 = (bf16[3,16,24,128]{3,2,1,0:T(8,128)(2,1)S(1)}, bf16[3,16,24,128]{3,2,1,0:T(8,128)(2,1)S(1)}, u32[]{:S(2)}, u32[]{:S(2)}) collective-permute-start(bf16[3,16,24,128]{3,2,1,0:T(8,128)(2,1)S(1)} %collective-permute-done.32.refs_0_), channel_id=1, source_target_pairs={{0,1},{1,0},{2,3},{3,2},{4,5},{5,4},{6,7},{7,6},{8,9},{9,8},{10,11... | collective-permute-start | bytes 884744 | tf_op jit(solution)/shard_map/ppermute | solution.py:384
  116.5 2.4 %collective-permute-start.29 = (bf16[2,16,24,128]{3,2,1,0:T(8,128)(2,1)S(1)}, bf16[2,16,24,128]{3,2,1,0:T(8,128)(2,1)S(1)}, u32[]{:S(2)}, u32[]{:S(2)}) collective-permute-start(bf16[2,16,24,128]{3,2,1,0:T(8,128)(2,1)S(1)} %collective-permute-done.28.refs_0_.refs_1_), channel_id=1, source_target_pairs={{0,1},{1,0},{2,3},{3,2},{4,5},{5,4},{6,7},{7,6},{8,9},{9,8},{10,11... | collective-permute-start | bytes 589832 | tf_op jit(solution)/shard_map/ppermute | solution.py:384
  116.5 1.6 %collective-permute-start.27 = (bf16[1,16,24,128]{3,2,1,0:T(8,128)(2,1)S(1)}, bf16[1,16,24,128]{3,2,1,0:T(8,128)(2,1)S(1)}, u32[]{:S(2)}, u32[]{:S(2)}) collective-permute-start(bf16[1,16,24,128]{3,2,1,0:T(8,128)(2,1)S(1)} %add_convert_fusion.refs_0_), channel_id=1, source_target_pairs={{0,1},{1,0},{2,3},{3,2},{4,5},{5,4},{6,7},{7,6},{8,9},{9,8},{10,11... | collective-permute-start | bytes 294920 | tf_op jit(solution)/shard_map/ppermute | solution.py:384
  117.0 5.6 %collective-permute-start.30 = (bf16[1,16,24,128]{3,2,1,0:T(8,128)(2,1)S(1)}, bf16[1,16,24,128]{3,2,1,0:T(8,128)(2,1)S(1)}, u32[]{:S(2)}, u32[]{:S(2)}) collective-permute-start(bf16[1,16,24,128]{3,2,1,0:T(8,128)(2,1)S(1)} %forward_step.3.refs_0_), channel_id=1, source_target_pairs={{0,1},{1,0},{2,3},{3,2},{4,5},{5,4},{6,7},{7,6},{8,9},{9,8},{10,11... | collective-permute-start | bytes 294920 | tf_op jit(solution)/shard_map/ppermute | solution.py:384
  118.1 4.5 %collective-permute-start.31 = (bf16[1,16,24,128]{3,2,1,0:T(8,128)(2,1)S(1)}, bf16[1,16,24,128]{3,2,1,0:T(8,128)(2,1)S(1)}, u32[]{:S(2)}, u32[]{:S(2)}) collective-permute-start(bf16[1,16,24,128]{3,2,1,0:T(8,128)(2,1)S(1)} %slice.193), channel_id=1, source_target_pairs={{0,1},{1,0},{2,3},{3,2},{4,5},{5,4},{6,7},{7,6},{8,9},{9,8},{10,11... | collective-permute-start | bytes 294920 | tf_op jit(solution)/shard_map/ppermute | solution.py:384
  121.1 2.3 %copy-start.2 = (bf16[256,16,128]{2,1,0:T(8,128)(2,1)S(1)}, bf16[256,16,128]{2,1,0:T(8,128)(2,1)}, u32[]{:S(2)}) copy-start(bf16[256,16,128]{2,1,0:T(8,128)(2,1)} %copy-done.1) | copy-start | bytes 3145732

commit v4 on v3

--- a/solution.py
+++ b/solution.py
@@ -10,7 +10,7 @@
 
 KS = 6
 PAD = 16
-VMEM_LIMIT = 24 * 1024 * 1024
+VMEM_LIMIT = 16 * 1024 * 1024
 
 
 def whole():
@@ -38,9 +38,16 @@
     return low + high
 
 
-def unpack_kernel(count, where, meta, *refs):
-    panel = refs[-1]
-    for ref, places in zip(refs[:-1], where):
+def anywhere():
+    return pl.BlockSpec(memory_space=pl.ANY)
+
+
+def in_hbm():
+    return pl.BlockSpec(memory_space=pltpu.HBM)
+
+
+def unpack_into(panel, refs, where, count, meta):
+    for ref, places in zip(refs, where):
         pairs = ref.shape[1]
         for index, base_of in enumerate(places):
             if base_of is None:
@@ -56,23 +63,54 @@
             lax.fori_loop(0, pairs, body, 0, unroll=8 if pairs % 8 == 0 else 4)
 
 
-def unpack(meta, pieces, blocks):
-    arrays = [array for array, _ in pieces]
-    where = [places for _, places in pieces]
+def unpack_kernel(count, wheres, skipped, meta, *refs):
+    panels = refs[len(refs) - len(wheres) :]
+    begin = 0
+    for panel, where in zip(panels, wheres):
+        unpack_into(panel, refs[begin : begin + len(where)], where, count, meta)
+        begin += len(where)
+
+
+def unpack(meta, jobs, tokens=()):
+    arrays = [array for pieces, _ in jobs for array, _ in pieces]
+    wheres = [[places for _, places in pieces] for pieces, _ in jobs]
     count = arrays[0].shape[2] // 2
     width = arrays[0].shape[3]
     return pl.pallas_call(
-        functools.partial(unpack_kernel, count, where),
-        out_shape=jax.ShapeDtypeStruct((blocks, PAD, width), jnp.bfloat16),
+        functools.partial(unpack_kernel, count, wheres, len(tokens)),
+        out_shape=[
+            jax.ShapeDtypeStruct((blocks, PAD, width), jnp.bfloat16) for _, blocks in jobs
+        ],
         grid_spec=pltpu.PrefetchScalarGridSpec(
             num_scalar_prefetch=1,
             grid=(1,),
-            in_specs=[whole()] * len(arrays),
-            out_specs=whole(),
+            in_specs=[whole()] * len(arrays) + [anywhere()] * len(tokens),
+            out_specs=[whole()] * len(jobs),
         ),
         compiler_params=params(),
-        name="unpack_panel",
-    )(meta, *arrays)
+        name="unpack_panels",
+    )(meta, *arrays, *tokens)
+
+
+def fetch_kernel(stored, token, out, sem):
+    half = out.shape[0]
+    start = (1 - lax.axis_index("rep")) * half
+    copy = pltpu.make_async_copy(stored.at[pl.ds(start, half)], out, sem)
+    copy.start()
+    copy.wait()
+
+
+def fetch_far(stored, token):
+    half = stored.shape[0] // 2
+    return pl.pallas_call(
+        fetch_kernel,
+        out_shape=jax.ShapeDtypeStruct((half,) + stored.shape[1:], stored.dtype),
+        in_specs=[in_hbm(), anywhere()],
+        out_specs=whole(),
+        scratch_shapes=[pltpu.SemaphoreType.DMA(())],
+        compiler_params=pltpu.CompilerParams(vmem_limit_bytes=VMEM_LIMIT),
+        name="fetch_far",
+    )(stored, token)
 
 
 def row_product(refs_and_rows, panel, contract):
@@ -95,66 +133,78 @@
 
 
 def first_kernel(
-    count, chunk, blocks, meta, cols, signs, stored,
-    panel, sent, mine, keep_row, near, far, keep, send, total,
+    count, chunk, blocks, meta, cols, signs_hbm, stored,
+    panel, sent, mine, keep_row, near, keep, send,
+    signs, far, total, sign_sem, sems,
 ):
-    step = pl.program_id(0)
     half = near.shape[0]
     rows = 2 * half
-
-    @pl.when(step == 0)
-    def _():
-        total[...] = jnp.zeros_like(total)
-        pad = jnp.zeros((PAD - count, signs.shape[1]), jnp.float32)
-
-        def body(b, carry):
-            value = signs[pl.ds(b, count, stride=blocks), :].astype(jnp.float32)
-            panel[b] = jnp.concatenate([value, pad], axis=0).astype(jnp.bfloat16)
+    chunks = half // chunk
+    rep = lax.axis_index("rep")
+
+    def copy(side, c):
+        place = (rep if side == 0 else 1 - rep) * half + c * chunk
+        return pltpu.make_async_copy(
+            stored.at[pl.ds(place, chunk)],
+            (near, far)[side].at[pl.ds(c * chunk, chunk)],
+            sems.at[side * chunks + c],
+        )
+
+    sign_copy = pltpu.make_async_copy(signs_hbm, signs, sign_sem)
+    sign_copy.start()
+    for side in (0, 1):
+        for c in range(chunks):
+            copy(side, c).start()
+    total[...] = jnp.zeros_like(total)
+    sign_copy.wait()
+    pad = jnp.zeros((PAD - count, signs.shape[1]), jnp.float32)
+
+    def convert(b, carry):
+        value = signs[pl.ds(b, count, stride=blocks), :].astype(jnp.float32)
+        panel[b] = jnp.concatenate([value, pad], axis=0).astype(jnp.bfloat16)
+        return carry
+
+    lax.fori_loop(0, blocks, convert, 0, unroll=8)
+    first_block = meta[0] * rows
+    for side, ref in ((0, near), (1, far)):
+        offset = meta[1] * half if side == 0 else (1 - meta[1]) * half
+
+        def body(c, carry, side=side, ref=ref, offset=offset):
+            copy(side, c).wait()
+            row = c * chunk
+            for i in range(0, chunk, 2):
+                results = [
+                    row_product([(ref, row + r, cols, offset + row + r)], panel, LAST)
+                    for r in (i, i + 1)
+                ]
+                pair = join_pair(results[0], results[1], count)
+                if side == 0:
+                    keep_row[(row + i) // 2] = pair
+                else:
+                    send[send.shape[0] - 1, (row + i) // 2] = pair.astype(jnp.bfloat16)
+                for r in (i, i + 1):
+                    scatter_row(
+                        panel[first_block + offset + row + r],
+                        [(ref, row + r, cols, offset + row + r)],
+                        total,
+                    )
             return carry
 
-        lax.fori_loop(0, blocks, body, 0, unroll=8)
-
-    row = step * chunk
-    side = row // half
-    base = row - side * half
-    first_block = meta[0] * rows
-    pairs = []
-    for i in range(0, chunk, 2):
-        results = [
-            row_product([(stored, r, cols, row + r)], panel, LAST) for r in (i, i + 1)
-        ]
-        pairs.append(join_pair(results[0], results[1], count))
-    for r in range(chunk):
-        scatter_row(panel[first_block + row + r], [(stored, r, cols, row + r)], total)
-
-    @pl.when(side == meta[1])
-    def _():
-        for i, pair in enumerate(pairs):
-            keep_row[base // 2 + i] = pair
-        near[pl.ds(base, chunk)] = stored[...]
-
-    @pl.when(side != meta[1])
-    def _():
-        for i, pair in enumerate(pairs):
-            send[send.shape[0] - 1, base // 2 + i] = pair.astype(jnp.bfloat16)
-        far[pl.ds(base, chunk)] = stored[...]
-
-    @pl.when(step == pl.num_programs(0) - 1)
-    def _():
-        parts, pair_rows = sent.shape[0], sent.shape[1]
-        for start, out, index in [
-            (meta[1] * (blocks // 2) + p * 2 * pair_rows, sent, p) for p in range(parts)
-        ] + [(first_block + meta[1] * half, mine, 0)]:
-
-            def pack(i, carry, start=start, out=out, index=index):
-                b = start + 2 * i
-                out[index, i] = join_pair(
-                    panel[b].astype(jnp.float32), panel[b + 1].astype(jnp.float32), count
-                ).astype(jnp.bfloat16)
-                return carry
-
-            lax.fori_loop(0, pair_rows, pack, 0, unroll=8 if pair_rows % 8 == 0 else 4)
-        give_totals(count, rows, meta, keep, send, total)
+        lax.fori_loop(0, chunks, body, 0)
+    parts, pair_rows = sent.shape[0], sent.shape[1]
+    for start, out, index in [
+        (meta[1] * (blocks // 2) + p * 2 * pair_rows, sent, p) for p in range(parts)
+    ] + [(first_block + meta[1] * half, mine, 0)]:
+
+        def pack(i, carry, start=start, out=out, index=index):
+            b = start + 2 * i
+            out[index, i] = join_pair(
+                panel[b].astype(jnp.float32), panel[b + 1].astype(jnp.float32), count
+            ).astype(jnp.bfloat16)
+            return carry
+
+        lax.fori_loop(0, pair_rows, pack, 0, unroll=8 if pair_rows % 8 == 0 else 4)
+    give_totals(count, rows, meta, keep, send, total)
 
 
 def first_step(meta, cols, signs, stored, blocks):
@@ -173,19 +223,21 @@
             shape((1,) + piece, jnp.bfloat16),
             shape(piece, jnp.float32),
             shape((half, slots, width, width), jnp.bfloat16),
-            shape((half, slots, width, width), jnp.bfloat16),
             shape((parts,) + piece, jnp.bfloat16),
             shape((parts + 1,) + piece, jnp.bfloat16),
         ),
         grid_spec=pltpu.PrefetchScalarGridSpec(
             num_scalar_prefetch=2,
-            grid=(rows // chunk,),
-            in_specs=[
-                whole(),
-                pl.BlockSpec((chunk, slots, width, width), lambda g, *_: (g, 0, 0, 0)),
+            grid=(1,),
+            in_specs=[in_hbm(), in_hbm()],
+            out_specs=(whole(),) * 7,
+            scratch_shapes=[
+                pltpu.VMEM(signs.shape, jnp.int32),
+                pltpu.VMEM((half, slots, width, width), jnp.bfloat16),
+                pltpu.VMEM((blocks, PAD, width), jnp.float32),
+                pltpu.SemaphoreType.DMA(()),
+                pltpu.SemaphoreType.DMA((2 * half // chunk,)),
             ],
-            out_specs=(whole(),) * 8,
-            scratch_shapes=[pltpu.VMEM((blocks, PAD, width), jnp.float32)],
         ),
         compiler_params=params(),
         cost_estimate=cost(2 * rows * slots, width),
@@ -202,9 +254,10 @@
 
 
 def forward_kernel(
-    count, chunk, rows, inverse, meta, cols_own, cols_other, own, other, panel, *rest
+    count, chunk, rows, inverse, where, meta, cols_own, cols_other, own, other, *rest
 ):
-    out = rest[-1]
+    panel, out = rest[-2:]
+    unpack_into(panel, rest[: len(where)], where, count, meta)
     half = rows // 2
     block = meta[0] * rows + meta[1] * half
 
@@ -216,7 +269,7 @@
                 product = row_product(
                     [
                         (own, row + r, cols_own, meta[1] * half + row + r),
-                        (other, row + r, cols_other, row + r),
+                        (other, row + r, cols_other, meta[1] * half + row + r),
                     ],
                     panel,
                     LAST,
@@ -230,22 +283,29 @@
     lax.fori_loop(0, half // chunk, body, 0)
 
 
-def forward(meta, cols_own, cols_other, own, other, panel, count, inverse, tokens):
+def forward(meta, cols_own, cols_other, own, other, pieces, blocks, inverse, tokens):
     half, slots, width = own.shape[0], own.shape[1], own.shape[3]
+    arrays = [array for array, _ in pieces]
+    count = arrays[0].shape[2] // 2
     chunk = min(16, half)
     return pl.pallas_call(
-        functools.partial(forward_kernel, count, chunk, 2 * half, inverse),
-        out_shape=jax.ShapeDtypeStruct((1, half // 2, 2 * count, width), jnp.bfloat16),
+        functools.partial(
+            forward_kernel, count, chunk, 2 * half, inverse, [places for _, places in pieces]
+        ),
+        out_shape=(
+            jax.ShapeDtypeStruct((blocks, PAD, width), jnp.bfloat16),
+            jax.ShapeDtypeStruct((1, half // 2, 2 * count, width), jnp.bfloat16),
+        ),
         grid_spec=pltpu.PrefetchScalarGridSpec(
             num_scalar_prefetch=3,
             grid=(1,),
-            in_specs=[whole()] * 3 + [pl.BlockSpec(memory_space=pl.ANY)] * len(tokens),
-            out_specs=whole(),
+            in_specs=[whole()] * (2 + len(arrays)) + [anywhere()] * len(tokens),
+            out_specs=(whole(), whole()),
         ),
         compiler_params=params(),
         cost_estimate=cost(2 * half * slots, width),
         name="forward_step",
-    )(meta, cols_own, cols_other, own, other, panel, *tokens)
+    )(meta, cols_own, cols_other, own, other, *arrays, *tokens)
 
 
 def scatter_row(value, refs_and_rows, total):
@@ -283,6 +343,7 @@
     count, chunk, meta, cols_own, cols_other, own, other, left, keep, send, total
 ):
     half = own.shape[0]
+    stored = ((own, cols_own), (other, cols_other))
     total[...] = jnp.zeros_like(total)
 
     def body(step, carry):
@@ -292,7 +353,7 @@
                 row = step * chunk + r
                 scatter_row(
                     value.astype(jnp.bfloat16),
-                    [(own, row, cols_own, meta[1] * half + row), (other, row, cols_other, row)],
+                    [(ref, row, cols, meta[1] * half + row) for ref, cols in stored],
                     total,
                 )
         return carry
@@ -379,6 +440,7 @@
     meta = jnp.stack([lax.axis_index("var"), rep_index]).astype(jnp.int32)
     signs = jnp.transpose(probe_signs, (1, 0, 2)).reshape(count * blocks, width)
     cols = columns.T
+    block_values = pltpu.with_memory_space_constraint(block_values, pltpu.HBM)
 
     def swap_rep(x):
         return lax.ppermute(x, "rep", [(0, 1), (1, 0)])
@@ -417,7 +479,7 @@
             others = [
                 (own_other, [0]), (swapped, [1, 2] + [None] * size), (swap_rep(last[:1]), [3]),
             ]
-            return pieces, others, summed, swapped[2:]
+            return pieces, others, summed, swapped[2:], near
         bits = [1 << i for i in range(n_var.bit_length() - 1)]
         held = {0: own}
         for bit in reversed(bits):
@@ -431,7 +493,7 @@
         pieces = [(jnp.concatenate([held[d] for d in range(n_var)], axis=0), list(range(n_var)))]
         swapped = swap_rep(jnp.concatenate([pieces[0][0], extra], axis=0))
         others = [(swapped, list(range(n_var)) + [None] * size)]
-        return pieces, others, sums[0], swapped[n_var:]
+        return pieces, others, sums[0], swapped[n_var:], own
 
     def home(d, h):
         if d is None:
@@ -455,14 +517,11 @@
     def sign_place(p, h):
         return lambda v, r: (r ^ h) * (blocks // 2) + p * half
 
-    other_columns = swap_rep(
-        lax.dynamic_slice_in_dim(cols, (1 - rep_index) * half, half, 1)
-    )
-    panel, sent, left_own, kept, near, far, keep, send = first_step(
+    other_columns = swap_rep(cols)
+    panel, sent, left_own, kept, near, keep, send = first_step(
         meta, cols, signs, block_values, blocks
     )
     received = swap_rep(send)
-    other = swap_rep(far)
     updated = narrow(wide(left_own) + inverse * (kept + wide(received[n_var]))[None])
     groups = n_probe - 1
     right = [[panel]] + [[] for _ in range(groups)]
@@ -473,55 +532,77 @@
         last = step == 2
         parts = [wide(keep[d : d + 1]) + wide(received[d : d + 1]) for d in range(n_var)]
         extra = travelling if step == 0 else jnp.concatenate([travelling, left_own], axis=0)
-        pieces, others, summed, extra_other = exchange(updated, parts, extra)
+        pieces, others, summed, extra_other, mark = exchange(updated, parts, extra)
+        if step == 0:
+            other = swap_rep(fetch_far(block_values, mark))
         size = n_var if step == 0 else n_var + 1
-        fresh = []
+        total = travelling.shape[0]
+        jobs = []
         for index in range(groups):
-            spots = {}
-            for h in (0, 1):
+
+            def spots(h, kind, index=index):
                 where = [None] * extra.shape[0]
                 for p in range(n_var):
-                    where[index * size + p] = sign_place(p, h) if step == 0 else home(p, h)
-                spots[h] = where
-            value = unpack(meta, [(travelling, spots[0][: travelling.shape[0]]), (extra_other, spots[1])], blocks)
-            right[1 + index].append(value)
-            fresh.append(value)
-            if step == 0:
-                left[1 + index].append(value)
-            else:
-                spots = {}
-                for h in (0, 1):
-                    where = [None] * extra.shape[0]
+                    if kind == "blocks":
+                        where[index * size + p] = sign_place(p, h) if step == 0 else home(p, h)
+                if kind == "rows":
                     where[index * size + n_var] = row_place(h)
-                    spots[h] = where
-                value = unpack(meta, [(travelling, spots[0][: travelling.shape[0]]), (extra_other, spots[1])], rows)
-                left[1 + index].append(value)
-                fresh.append(value)
+                return where
+
+            for kind in ("blocks",) if step == 0 else ("blocks", "rows"):
+                jobs.append(
+                    (
+                        [
+                            (travelling, spots(0, kind)[:total]),
+                            (extra_other, spots(1, kind)),
+                        ],
+                        blocks if kind == "blocks" else rows,
+                    )
+                )
         if step > 0:
             tail = [None] * (extra.shape[0] - 1)
-            value = unpack(
-                meta, [(left_own, [row_place(0)]), (extra_other, tail + [row_place(1)])], rows
+            jobs.append(
+                ([(left_own, [row_place(0)]), (extra_other, tail + [row_place(1)])], rows)
             )
-            left[0].append(value)
-            fresh.append(value)
-        panel = unpack(meta, place(pieces, 0) + place(others, 1), blocks)
-        right[0].append(panel)
+        fresh = unpack(meta, jobs)
+        found = list(fresh)
+        for index in range(groups):
+            value = found.pop(0)
+            right[1 + index].append(value)
+            left[1 + index].append(value if step == 0 else found.pop(0))
+        if step > 0:
+            left[0].append(found.pop(0))
+        sources = place(pieces, 0) + place(others, 1)
         left_own = narrow(wide(left_own) + inverse * summed)
         if not last:
-            travelling = from_probes(jnp.concatenate([joined(pieces), left_own], axis=0))
             keep, send = backward(meta, cols, other_columns, near, other, left_own, blocks)
             received = swap_rep(send)
-            updated = forward(
-                meta, cols, other_columns, near, other, panel, count, inverse, [send] + fresh
+            message = jnp.concatenate([joined(pieces), left_own], axis=0)
+            panel, updated = forward(
+                meta, cols, other_columns, near, other, sources, blocks, inverse,
+                [send] + list(fresh),
             )
+            right[0].append(panel)
+            travelling = from_probes(message)
+        else:
+            (panel,) = unpack(meta, [(sources, blocks)], fresh)
+            right[0].append(panel)
 
     if n_var == 4:
-        first = from_probes(jnp.concatenate([pieces[0][0], pieces[1][0][:1], pieces[2][0]], axis=0))
-        late = from_probes(jnp.concatenate([pieces[3][0][:1], left_own], axis=0))
-        arrays = [(first, [0, 1, 2]), (late, [3, "row"])]
+        arrays = [
+            (from_probes(pieces[0][0]), [0]),
+            (from_probes(jnp.concatenate([pieces[1][0][:1], pieces[2][0]], axis=0)), [1, 2]),
+            (from_probes(jnp.concatenate([pieces[3][0][:1], left_own], axis=0)), [3, "row"]),
+        ]
     else:
-        arrays = [(from_probes(jnp.concatenate([joined(pieces), left_own], axis=0)), list(range(n_var)) + ["row"])]
+        arrays = [
+            (
+                from_probes(jnp.concatenate([joined(pieces), left_own], axis=0)),
+                list(range(n_var)) + ["row"],
+            )
+        ]
     crossed = [swap_rep(array) for array, _ in arrays]
+    jobs = []
     for index in range(groups):
         blocks_in = []
         rows_in = []
@@ -534,11 +615,13 @@
                 if "row" in ds:
                     here = [row_place(h) if d == "row" else None for d in ds]
                     rows_in.append((array, lead + here + rest))
-        right[1 + index].append(unpack(meta, blocks_in, blocks))
-        left[1 + index].append(unpack(meta, rows_in, rows))
-    left[0].append(
-        unpack(meta, [(left_own, [row_place(0)]), (swap_rep(left_own), [row_place(1)])], rows)
-    )
+        jobs += [(blocks_in, blocks), (rows_in, rows)]
+    jobs.append(([(left_own, [row_place(0)]), (swap_rep(left_own), [row_place(1)])], rows))
+    found = unpack(meta, jobs, [panel])
+    for index in range(groups):
+        right[1 + index].append(found[2 * index])
+        left[1 + index].append(found[2 * index + 1])
+    left[0].append(found[-1])
 
     lefts = [group[t] for t in range(4) for group in left]
     rights = [group[3 - t] for t in range(4) for group in right]

time: 129 us -> 113 us (0.88)
  Pallas kernels: 39.4 us -> 27.5 us
  waiting for transfers between devices: 43.9 us -> 52.4 us
  local copies, waits for them, and re-layouts: 8.24 us -> 2.46 us
  other arithmetic: 5.15 us -> 1.11 us
  starting transfers between devices: 31.1 us -> 29.2 us
    ppermute x12, waiting for transfers between devices: 23.9 us -> 39.2 us  [shift_var(): return lax.ppermute(x, 'var', [(i, i ^ bit) for i in range(n_var)])]
    ppermute x17 -> x18, waiting for transfers between devices: 8.62 us -> 3.2 us  [swap_rep(): return lax.ppermute(x, 'rep', [(0, 1), (1, 0)])]
    ppermute x5 -> x6, starting transfers between devices: 9.62 us -> 4.56 us  [from_probes(): lax.ppermute(x, 'probe', [(i, (i + d) % n_probe) for i in range(n_probe)])]
    unnamed x25 -> x11, local copies, waits for them, and re-layouts: 7.27 us -> 2.21 us
    pallas_call x2, Pallas kernels: 8.15 us -> 4.34 us  [backward(): pl.pallas_call(functools.partial(backward_kernel, count, chunk), out_shap...]
    pallas_call x2, Pallas kernels: 8.7 us -> 5.51 us  [forward(): pl.pallas_call(functools.partial(forward_kernel, count, chunk, 2 * half,...]
    pallas_call x13 -> x6, Pallas kernels: 9.51 us -> 6.49 us  [the longest x5 4.59 us: unpack(): pl.pallas_call(functools.partial(unpack_kernel, count, wheres, len(tokens...]
    ppermute x12, starting transfers between devices: 18.6 us -> 20.7 us  [shift_var(): return lax.ppermute(x, 'var', [(i, i ^ bit) for i in range(n_var)])]
  transfers between devices with their start and end apart: 34 -> 36, of which waited for: 17 -> 15; matrix products, arithmetic and copies ran while one was open for 6% -> 1% of each run, Pallas kernels for 16% -> 9%
where the time goes in v4:
time: 113 us
  waiting for transfers between devices  52.4 us (46%)
  starting transfers between devices  29.2 us (26%)
  Pallas kernels  27.5 us (24%)
  local copies, waits for them, and re-layouts  2.46 us (2%)
    ppermute x12, waiting for transfers between devices, shift_var(): return lax.ppermute(x, 'var', [(i, i ^ bit) for i in range(n_var)])  39.2 us
    ppermute x12, starting transfers between devices, shift_var(): return lax.ppermute(x, 'var', [(i, i ^ bit) for i in range(n_var)])  20.7 us
    ppermute x6, waiting for transfers between devices, from_probes(): lax.ppermute(x, 'probe', [(i, (i + d) % n_probe) for i in range(n_probe)])  10.1 us
    pallas_call x1, Pallas kernels, first_step(): pl.pallas_call(functools.partial(first_kernel, count, chunk, blocks), out...  6.39 us
    pallas_call x2, Pallas kernels, forward(): pl.pallas_call(functools.partial(forward_kernel, count, chunk, 2 * half,...  5.51 us
    pallas_call x1, Pallas kernels, gradient(): pl.pallas_call(functools.partial(gradient_kernel, scale, chunk, rows, len...  4.77 us
    pallas_call x5, Pallas kernels, unpack(): pl.pallas_call(functools.partial(unpack_kernel, count, wheres, len(tokens...  4.59 us
    ppermute x6, starting transfers between devices, from_probes(): lax.ppermute(x, 'probe', [(i, (i + d) % n_probe) for i in range(n_probe)])  4.56 us
  transfers between devices with their start and end apart: 36, of which 15 were waited for; matrix products, arithmetic and copies ran while one was open for 1% of the time, Pallas kernels for 9%

profile of v4, /device:TPU:0, one launch (start us, length us, event | category | flops | bytes accessed | tf_op | source)
XLA Modules:
  0.0 113.1 jit_solution(4413374655950342984)
XLA Ops:
  0.0 0.1 pad_add_fusion.meta
  0.1 1.4 %copy-done = s32[256,12,128]{2,0,1:T(8,128)S(1)} copy-done((s32[256,12,128]{2,0,1:T(8,128)S(1)}, s32[256,12,128]{2,0,1:T(8,128)}, u32[]{:S(2)}) %copy-start) | copy-done | bytes 1572888
  1.5 0.7 copy-done.1
  2.2 6.4 %first_step.1 = (bf16[256,16,128]{2,1,0:T(8,128)(2,1)S(1)}, bf16[4,16,24,128]{3,2,1,0:T(8,128)(2,1)S(1)}, bf16[1,16,24,128]{3,2,1,0:T(8,128)(2,1)S(1)}, f32[16,2...) custom-call(s32[2]{0:T(128)S(1)} %pad_add_fusion.meta, ...), custom_call_target="tpu_custom_call" | custom-call | flops 1610612736 | bytes 50331648 | tf_op jit(solution)/shard_map/first_step/pallas_call | solution.py:218
  8.6 0.5 collective-permute-start.1
  9.1 1.5 %collective-permute-done.1 = bf16[5,16,24,128]{3,2,1,0:T(8,128)(2,1)S(1)} collective-permute-done((bf16[5,16,24,128]{3,2,1,0:T(8,128)(2,1)S(1)}, bf16[5,16,24,128]{3,2,1,0:T(8,128)(2,1)S(1)}, u32[]{:S(2)}, u32[]{:S(2)}) %collective-permute-start.1) | collective-permute-done | bytes 491552 | tf_op jit(solution)/shard_map/ppermute | solution.py:446
  10.7 3.0 %collective-permute-start.2 = (bf16[2,16,24,128]{3,2,1,0:T(8,128)(2,1)S(1)}, bf16[2,16,24,128]{3,2,1,0:T(8,128)(2,1)S(1)}, u32[]{:S(2)}, u32[]{:S(2)}) collective-permute-start(bf16[2,16,24,128]{3,2,1,0:T(8,128)(2,1)S(1)} %pad_maximum_fusion.3), channel_id=1, source_target_pairs={{0,4},{4,0},{8,12},{12,8},{1,5},{5,1},{9,13},{13,9},{2,6},{6,2},{1... | collective-permute-start | bytes 589832 | tf_op jit(solution)/shard_map/ppermute | solution.py:449
  13.7 5.2 %collective-permute-done.2.token.rest_1_ = bf16[2,16,24,128]{3,2,1,0:T(8,128)(2,1)S(1)} collective-permute-done((bf16[2,16,24,128]{3,2,1,0:T(8,128)(2,1)S(1)}, bf16[2,16,24,128]{3,2,1,0:T(8,128)(2,1)S(1)}, u32[]{:S(2)}, u32[]{:S(2)}) %collective-permute-start.2) | collective-permute-done | bytes 196640 | tf_op jit(solution)/shard_map/ppermute | solution.py:449
  18.9 1.9 %fetch_far.1 = bf16[32,3,128,128]{3,2,1,0:T(8,128)(2,1)S(1)} custom-call(bf16[64,3,128,128]{3,2,1,0:T(8,128)(2,1)} %stored.3, bf16[2,16,24,128]{3,2,1,0:T(8,128)(2,1)S(1)} %collective-permute-done.2.token.rest_1_), custom_call_target="tpu_custom_call" | custom-call | tf_op jit(solution)/shard_map/fetch_far/pallas_call | solution.py:105
  20.9 0.5 collective-permute-start.8
  21.4 1.7 %collective-permute-start = (bf16[4,16,24,128]{3,2,1,0:T(8,128)(2,1)S(1)}, bf16[4,16,24,128]{3,2,1,0:T(8,128)(2,1)S(1)}, u32[]{:S(2)}, u32[]{:S(2)}) collective-permute-start(bf16[4,16,24,128]{3,2,1,0:T(8,128)(2,1)S(1)} %get-tuple-element.30), channel_id=1, source_target_pairs={{0,2},{2,0},{1,3},{3,1},{4,6},{6,4},{5,7},{7,5},{8,10},{10,8},{9,1... | collective-permute-start | bytes 1179656 | tf_op jit(solution)/shard_map/ppermute | solution.py:454
  23.0 2.6 %collective-permute-start.3 = (bf16[1,16,24,128]{3,2,1,0:T(8,128)(2,1)S(1)}, bf16[1,16,24,128]{3,2,1,0:T(8,128)(2,1)S(1)}, u32[]{:S(2)}, u32[]{:S(2)}) collective-permute-start(bf16[1,16,24,128]{3,2,1,0:T(8,128)(2,1)S(1)} %get-tuple-element.58.rest_0_), channel_id=1, source_target_pairs={{0,8},{4,12},{8,0},{12,4},{1,9},{5,13},{9,1},{13,5},{2,10},{6,14},... | collective-permute-start | bytes 294920 | tf_op jit(solution)/shard_map/ppermute | solution.py:449
  25.7 0.4 collective-permute-start.6
  26.1 7.5 %collective-permute-done.3.rest_2_ = bf16[1,16,24,128]{3,2,1,0:T(8,128)(2,1)S(1)} collective-permute-done((bf16[1,16,24,128]{3,2,1,0:T(8,128)(2,1)S(1)}, bf16[1,16,24,128]{3,2,1,0:T(8,128)(2,1)S(1)}, u32[]{:S(2)}, u32[]{:S(2)}) %collective-permute-start.3) | collective-permute-done | bytes 98336 | tf_op jit(solution)/shard_map/ppermute | solution.py:449
  33.6 0.1 collective-permute-start.5
  33.8 0.1 collective-permute-start.4
  33.9 5.4 %collective-permute-done.5.rest_3_ = bf16[2,16,24,128]{3,2,1,0:T(8,128)(2,1)S(1)} collective-permute-done((bf16[2,16,24,128]{3,2,1,0:T(8,128)(2,1)S(1)}, bf16[2,16,24,128]{3,2,1,0:T(8,128)(2,1)S(1)}, u32[]{:S(2)}, u32[]{:S(2)}) %collective-permute-start.5) | collective-permute-done | bytes 196640 | tf_op jit(solution)/shard_map/ppermute | solution.py:449
  39.4 0.1 constant_dynamic-update-slice_fusion
  39.5 2.2 %backward_step.2 = (bf16[4,16,24,128]{3,2,1,0:T(8,128)(2,1)S(1)}, bf16[4,16,24,128]{3,2,1,0:T(8,128)(2,1)S(1)}) custom-call(s32[2]{0:T(128)S(1)} %pad_add_fusion.meta, s32[3,64]{1,0:T(4,128)S(1)} %bitcast.20, s32[3,64]{1,0:T(4,128)S(1)} %collective-permute-done.8.cols_other, bf16[32,3,128,128]{3,2,1,0:T(8,128)(2,1)S(1)} %get-tuple-element.35.own, ...), custom_call_target="tpu_custom_call" | custom-call | flops 805306368 | bytes 25165824 | tf_op jit(solution)/shard_map/backward_step/pallas_call | solution.py:372
  41.7 0.1 collective-permute-start.12
  41.8 0.5 collective-permute-start.10
  42.3 0.1 collective-permute-start.11
  42.4 0.8 unpack_panels.5.rest_8_.refs_1_.refs_15_
  43.3 0.4 collective-permute-done.10.rest_4_
  43.7 0.1 collective-permute-done.11.rest_6_
  43.8 2.7 %forward_step.2 = (bf16[256,16,128]{2,1,0:T(8,128)(2,1)S(1)}, bf16[1,16,24,128]{3,2,1,0:T(8,128)(2,1)S(1)}) custom-call(s32[2]{0:T(128)S(1)} %pad_add_fusion.meta, s32[3,64]{1,0:T(4,128)S(1)} %bitcast.21, s32[3,64]{1,0:T(4,128)S(1)} %collective-permute-done.8.cols_other, bf16[32,3,128,128]{3,2,1,0:T(8,128)(2,1)S(1)} %get-tuple-element.35.own, ...), custom_call_target="tpu_custom_call" | custom-call | flops 805306368 | bytes 25165824 | tf_op jit(solution)/shard_map/forward_step/pallas_call | solution.py:291
  46.6 0.9 collective-permute-start.13
  47.6 0.5 collective-permute-start.7
  48.1 3.4 %collective-permute-start.14 = (bf16[1,16,24,128]{3,2,1,0:T(8,128)(2,1)S(1)}, bf16[1,16,24,128]{3,2,1,0:T(8,128)(2,1)S(1)}, u32[]{:S(2)}, u32[]{:S(2)}) collective-permute-start(bf16[1,16,24,128]{3,2,1,0:T(8,128)(2,1)S(1)} %get-tuple-element.37.rest_0_), channel_id=1, source_target_pairs={{0,8},{4,12},{8,0},{12,4},{1,9},{5,13},{9,1},{13,5},{2,10},{6,14},... | collective-permute-start | bytes 294920 | tf_op jit(solution)/shard_map/ppermute | solution.py:449
  51.5 4.3 %collective-permute-done.13.rest_1_ = bf16[2,16,24,128]{3,2,1,0:T(8,128)(2,1)S(1)} collective-permute-done((bf16[2,16,24,128]{3,2,1,0:T(8,128)(2,1)S(1)}, bf16[2,16,24,128]{3,2,1,0:T(8,128)(2,1)S(1)}, u32[]{:S(2)}, u32[]{:S(2)}) %collective-permute-start.13) | collective-permute-done | bytes 196640 | tf_op jit(solution)/shard_map/ppermute | solution.py:449
  55.8 1.9 %collective-permute-start.17 = (bf16[1,16,24,128]{3,2,1,0:T(8,128)(2,1)S(1)}, bf16[1,16,24,128]{3,2,1,0:T(8,128)(2,1)S(1)}, u32[]{:S(2)}, u32[]{:S(2)}) collective-permute-start(bf16[1,16,24,128]{3,2,1,0:T(8,128)(2,1)S(1)} %get-tuple-element.63), channel_id=1, source_target_pairs={{0,8},{4,12},{8,0},{12,4},{1,9},{5,13},{9,1},{13,5},{2,10},{6,14},... | collective-permute-start | bytes 294920 | tf_op jit(solution)/shard_map/ppermute | solution.py:449
  57.7 2.5 %collective-permute-start.16 = (bf16[2,16,24,128]{3,2,1,0:T(8,128)(2,1)S(1)}, bf16[2,16,24,128]{3,2,1,0:T(8,128)(2,1)S(1)}, u32[]{:S(2)}, u32[]{:S(2)}) collective-permute-start(bf16[2,16,24,128]{3,2,1,0:T(8,128)(2,1)S(1)} %pad_maximum_fusion.6), channel_id=1, source_target_pairs={{0,4},{4,0},{8,12},{12,8},{1,5},{5,1},{9,13},{13,9},{2,6},{6,2},{1... | collective-permute-start | bytes 589832 | tf_op jit(solution)/shard_map/ppermute | solution.py:449
  60.3 0.3 collective-permute-done.7.refs_0_.refs_2_
  60.5 0.1 pad_maximum_fusion
  60.7 4.5 %collective-permute-done.16.rest_3_ = bf16[2,16,24,128]{3,2,1,0:T(8,128)(2,1)S(1)} collective-permute-done((bf16[2,16,24,128]{3,2,1,0:T(8,128)(2,1)S(1)}, bf16[2,16,24,128]{3,2,1,0:T(8,128)(2,1)S(1)}, u32[]{:S(2)}, u32[]{:S(2)}) %collective-permute-start.16) | collective-permute-done | bytes 196640 | tf_op jit(solution)/shard_map/ppermute | solution.py:449
  65.3 0.1 constant_dynamic-update-slice_fusion.5
  65.4 2.2 %backward_step.3 = (bf16[4,16,24,128]{3,2,1,0:T(8,128)(2,1)S(1)}, bf16[4,16,24,128]{3,2,1,0:T(8,128)(2,1)S(1)}) custom-call(s32[2]{0:T(128)S(1)} %pad_add_fusion.meta, s32[3,64]{1,0:T(4,128)S(1)} %bitcast.22, s32[3,64]{1,0:T(4,128)S(1)} %collective-permute-done.8.cols_other, bf16[32,3,128,128]{3,2,1,0:T(8,128)(2,1)S(1)} %get-tuple-element.35.own, ...), custom_call_target="tpu_custom_call" | custom-call | flops 805306368 | bytes 25165824 | tf_op jit(solution)/shard_map/backward_step/pallas_call | solution.py:372
  67.7 0.5 collective-permute-start.19
  68.2 0.1 collective-permute-start.20
  68.3 1.1 %collective-permute-done.21 = bf16[4,16,24,128]{3,2,1,0:T(8,128)(2,1)S(1)} collective-permute-done((bf16[4,16,24,128]{3,2,1,0:T(8,128)(2,1)S(1)}, bf16[4,16,24,128]{3,2,1,0:T(8,128)(2,1)S(1)}, u32[]{:S(2)}, u32[]{:S(2)}) %collective-permute-start.21) | collective-permute-done | bytes 393248 | tf_op jit(solution)/shard_map/ppermute | solution.py:446
  69.5 1.0 unpack_panels.6
  70.5 2.8 %forward_step.3 = (bf16[256,16,128]{2,1,0:T(8,128)(2,1)S(1)}, bf16[1,16,24,128]{3,2,1,0:T(8,128)(2,1)S(1)}) custom-call(s32[2]{0:T(128)S(1)} %pad_add_fusion.meta, s32[3,64]{1,0:T(4,128)S(1)} %bitcast.23, s32[3,64]{1,0:T(4,128)S(1)} %collective-permute-done.8.cols_other, bf16[32,3,128,128]{3,2,1,0:T(8,128)(2,1)S(1)} %get-tuple-element.35.own, ...), custom_call_target="tpu_custom_call" | custom-call | flops 805306368 | bytes 25165824 | tf_op jit(solution)/shard_map/forward_step/pallas_call | solution.py:291
  73.3 1.3 %collective-permute-start.22 = (bf16[2,16,24,128]{3,2,1,0:T(8,128)(2,1)S(1)}, bf16[2,16,24,128]{3,2,1,0:T(8,128)(2,1)S(1)}, u32[]{:S(2)}, u32[]{:S(2)}) collective-permute-start(bf16[2,16,24,128]{3,2,1,0:T(8,128)(2,1)S(1)} %pad_maximum_fusion.7), channel_id=1, source_target_pairs={{0,4},{4,0},{8,12},{12,8},{1,5},{5,1},{9,13},{13,9},{2,6},{6,2},{1... | collective-permute-start | bytes 589832 | tf_op jit(solution)/shard_map/ppermute | solution.py:449
  74.6 1.8 %collective-permute-start.23 = (bf16[1,16,24,128]{3,2,1,0:T(8,128)(2,1)S(1)}, bf16[1,16,24,128]{3,2,1,0:T(8,128)(2,1)S(1)}, u32[]{:S(2)}, u32[]{:S(2)}) collective-permute-start(bf16[1,16,24,128]{3,2,1,0:T(8,128)(2,1)S(1)} %get-tuple-element.43.refs_0_), channel_id=1, source_target_pairs={{0,8},{4,12},{8,0},{12,4},{1,9},{5,13},{9,1},{13,5},{2,10},{6,14},... | collective-permute-start | bytes 294920 | tf_op jit(solution)/shard_map/ppermute | solution.py:449
  76.4 6.0 %collective-permute-done.22.refs_1_ = bf16[2,16,24,128]{3,2,1,0:T(8,128)(2,1)S(1)} collective-permute-done((bf16[2,16,24,128]{3,2,1,0:T(8,128)(2,1)S(1)}, bf16[2,16,24,128]{3,2,1,0:T(8,128)(2,1)S(1)}, u32[]{:S(2)}, u32[]{:S(2)}) %collective-permute-start.22) | collective-permute-done | bytes 196640 | tf_op jit(solution)/shard_map/ppermute | solution.py:449
  82.4 0.1 add_convert_fusion.2
  82.6 1.2 %collective-permute-start.27 = (bf16[2,16,24,128]{3,2,1,0:T(8,128)(2,1)S(1)}, bf16[2,16,24,128]{3,2,1,0:T(8,128)(2,1)S(1)}, u32[]{:S(2)}, u32[]{:S(2)}) collective-permute-start(bf16[2,16,24,128]{3,2,1,0:T(8,128)(2,1)S(1)} %get-tuple-element.73), channel_id=1, source_target_pairs={{0,4},{4,0},{8,12},{12,8},{1,5},{5,1},{9,13},{13,9},{2,6},{6,2},{1... | collective-permute-start | bytes 589832 | tf_op jit(solution)/shard_map/ppermute | solution.py:449
  83.7 3.9 %collective-permute-done.18.refs_0_.refs_2_ = bf16[5,16,24,128]{3,2,1,0:T(8,128)(2,1)S(1)} collective-permute-done((bf16[5,16,24,128]{3,2,1,0:T(8,128)(2,1)S(1)}, bf16[5,16,24,128]{3,2,1,0:T(8,128)(2,1)S(1)}, u32[]{:S(2)}, u32[]{:S(2)}) %collective-permute-start.18) | collective-permute-done | bytes 491552 | tf_op jit(solution)/shard_map/ppermute | solution.py:454
  87.6 0.1 pad_maximum_fusion.1
  87.8 1.8 %collective-permute-start.28 = (bf16[1,16,24,128]{3,2,1,0:T(8,128)(2,1)S(1)}, bf16[1,16,24,128]{3,2,1,0:T(8,128)(2,1)S(1)}, u32[]{:S(2)}, u32[]{:S(2)}) collective-permute-start(bf16[1,16,24,128]{3,2,1,0:T(8,128)(2,1)S(1)} %get-tuple-element.62), channel_id=1, source_target_pairs={{0,8},{4,12},{8,0},{12,4},{1,9},{5,13},{9,1},{13,5},{2,10},{6,14},... | collective-permute-start | bytes 294920 | tf_op jit(solution)/shard_map/ppermute | solution.py:449
  89.6 0.3 collective-permute-start.26
  89.9 6.1 %collective-permute-done.28 = bf16[1,16,24,128]{3,2,1,0:T(8,128)(2,1)S(1)} collective-permute-done((bf16[1,16,24,128]{3,2,1,0:T(8,128)(2,1)S(1)}, bf16[1,16,24,128]{3,2,1,0:T(8,128)(2,1)S(1)}, u32[]{:S(2)}, u32[]{:S(2)}) %collective-permute-start.28) | collective-permute-done | bytes 98336 | tf_op jit(solution)/shard_map/ppermute | solution.py:449
  96.0 0.1 add_convert_fusion.refs_8_
  96.1 0.3 collective-permute-start.29
  96.4 1.7 %collective-permute-start.25 = (bf16[1,16,24,128]{3,2,1,0:T(8,128)(2,1)S(1)}, bf16[1,16,24,128]{3,2,1,0:T(8,128)(2,1)S(1)}, u32[]{:S(2)}, u32[]{:S(2)}) collective-permute-start(bf16[1,16,24,128]{3,2,1,0:T(8,128)(2,1)S(1)} %get-tuple-element.43.refs_0_), channel_id=1, source_target_pairs={{0,2},{2,0},{1,3},{3,1},{4,6},{6,4},{5,7},{7,5},{8,10},{10,8},{9,1... | collective-permute-start | bytes 294920 | tf_op jit(solution)/shard_map/ppermute | solution.py:454
  98.2 0.2 collective-permute-start.31
  98.4 5.4 %collective-permute-done.29.refs_2_.refs_6_ = bf16[2,16,24,128]{3,2,1,0:T(8,128)(2,1)S(1)} collective-permute-done((bf16[2,16,24,128]{3,2,1,0:T(8,128)(2,1)S(1)}, bf16[2,16,24,128]{3,2,1,0:T(8,128)(2,1)S(1)}, u32[]{:S(2)}, u32[]{:S(2)}) %collective-permute-start.29) | collective-permute-done | bytes 196640 | tf_op jit(solution)/shard_map/ppermute | solution.py:454
  103.8 0.5 collective-permute-start.35
  104.3 0.5 collective-permute-done.25.refs_0_
  104.9 0.5 collective-permute-start.33
  105.4 1.0 unpack_panels.7
  106.4 0.8 unpack_panels.8.refs_10_.refs_8_
  107.3 1.0 unpack_panels.9
  108.3 4.8 %gradient.1 = bf16[64,3,128,128]{3,2,1,0:T(8,128)(2,1)} custom-call(s32[2]{0:T(128)S(1)} %pad_add_fusion.meta, s32[3,64]{1,0:T(4,128)S(1)} %bitcast.24, bf16[256,16,128]{2,1,0:T(8,128)(2,1)S(1)} %get-tuple-element.29.refs_0_.refs_14_, bf16[256,16,128]{2,1,0:T(8,128)(2,1)S(1)} %unpack_panels.5.rest_8_.refs_1_.refs_15_, ...), custom_call_target="tpu_custom_call" | custom-call | tf_op jit(solution)/shard_map/gradient/pallas_call | solution.py:418
  (59 shorter events, 1.2 us)
Async XLA Ops:
  0.1 1.4 %copy-start = (s32[256,12,128]{2,0,1:T(8,128)S(1)}, s32[256,12,128]{2,0,1:T(8,128)}, u32[]{:S(2)}) copy-start(s32[256,12,128]{2,0,1:T(8,128)} %param.5) | copy-start | bytes 4718596
  1.5 0.7 copy-start.1
  8.6 2.0 %collective-permute-start.1 = (bf16[5,16,24,128]{3,2,1,0:T(8,128)(2,1)S(1)}, bf16[5,16,24,128]{3,2,1,0:T(8,128)(2,1)S(1)}, u32[]{:S(2)}, u32[]{:S(2)}) collective-permute-start(bf16[5,16,24,128]{3,2,1,0:T(8,128)(2,1)S(1)} %get-tuple-element.33), channel_id=1, source_target_pairs={{0,1},{1,0},{2,3},{3,2},{4,5},{5,4},{6,7},{7,6},{8,9},{9,8},{10,11... | collective-permute-start | bytes 1474568 | tf_op jit(solution)/shard_map/ppermute | solution.py:446
  10.7 8.2 %collective-permute-start.2 = (bf16[2,16,24,128]{3,2,1,0:T(8,128)(2,1)S(1)}, bf16[2,16,24,128]{3,2,1,0:T(8,128)(2,1)S(1)}, u32[]{:S(2)}, u32[]{:S(2)}) collective-permute-start(bf16[2,16,24,128]{3,2,1,0:T(8,128)(2,1)S(1)} %pad_maximum_fusion.3), channel_id=1, source_target_pairs={{0,4},{4,0},{8,12},{12,8},{1,5},{5,1},{9,13},{13,9},{2,6},{6,2},{1... | collective-permute-start | bytes 589832 | tf_op jit(solution)/shard_map/ppermute | solution.py:449
  20.8 18.7 %collective-permute-start.9 = (bf16[32,3,128,128]{3,2,1,0:T(8,128)(2,1)S(1)}, bf16[32,3,128,128]{3,2,1,0:T(8,128)(2,1)S(1)}, u32[]{:S(2)}, u32[]{:S(2)}) collective-permute-start(bf16[32,3,128,128]{3,2,1,0:T(8,128)(2,1)S(1)} %fetch_far.1), channel_id=1, source_target_pairs={{0,1},{1,0},{2,3},{3,2},{4,5},{5,4},{6,7},{7,6},{8,9},{9,8},{10,11... | collective-permute-start | bytes 9437192 | tf_op jit(solution)/shard_map/ppermute | solution.py:446
  20.9 18.6 %collective-permute-start.8 = (s32[3,64]{1,0:T(4,128)S(1)}, s32[3,64]{1,0:T(4,128)S(1)}, u32[]{:S(2)}, u32[]{:S(2)}) collective-permute-start(s32[3,64]{1,0:T(4,128)S(1)} %bitcast.19), channel_id=1, source_target_pairs={{0,1},{1,0},{2,3},{3,2},{4,5},{5,4},{6,7},{7,6},{8,9},{9,8},{10,11... | collective-permute-start | bytes 2312 | tf_op jit(solution)/shard_map/ppermute | solution.py:446
  21.4 12.4 %collective-permute-start = (bf16[4,16,24,128]{3,2,1,0:T(8,128)(2,1)S(1)}, bf16[4,16,24,128]{3,2,1,0:T(8,128)(2,1)S(1)}, u32[]{:S(2)}, u32[]{:S(2)}) collective-permute-start(bf16[4,16,24,128]{3,2,1,0:T(8,128)(2,1)S(1)} %get-tuple-element.30), channel_id=1, source_target_pairs={{0,2},{2,0},{1,3},{3,1},{4,6},{6,4},{5,7},{7,5},{8,10},{10,8},{9,1... | collective-permute-start | bytes 1179656 | tf_op jit(solution)/shard_map/ppermute | solution.py:454
  23.0 10.6 %collective-permute-start.3 = (bf16[1,16,24,128]{3,2,1,0:T(8,128)(2,1)S(1)}, bf16[1,16,24,128]{3,2,1,0:T(8,128)(2,1)S(1)}, u32[]{:S(2)}, u32[]{:S(2)}) collective-permute-start(bf16[1,16,24,128]{3,2,1,0:T(8,128)(2,1)S(1)} %get-tuple-element.58.rest_0_), channel_id=1, source_target_pairs={{0,8},{4,12},{8,0},{12,4},{1,9},{5,13},{9,1},{13,5},{2,10},{6,14},... | collective-permute-start | bytes 294920 | tf_op jit(solution)/shard_map/ppermute | solution.py:449
  25.7 13.7 %collective-permute-start.6 = (bf16[1,16,24,128]{3,2,1,0:T(8,128)(2,1)S(1)}, bf16[1,16,24,128]{3,2,1,0:T(8,128)(2,1)S(1)}, u32[]{:S(2)}, u32[]{:S(2)}) collective-permute-start(bf16[1,16,24,128]{3,2,1,0:T(8,128)(2,1)S(1)} %get-tuple-element.59), channel_id=1, source_target_pairs={{0,8},{4,12},{8,0},{12,4},{1,9},{5,13},{9,1},{13,5},{2,10},{6,14},... | collective-permute-start | bytes 294920 | tf_op jit(solution)/shard_map/ppermute | solution.py:449
  33.6 5.7 %collective-permute-start.5 = (bf16[2,16,24,128]{3,2,1,0:T(8,128)(2,1)S(1)}, bf16[2,16,24,128]{3,2,1,0:T(8,128)(2,1)S(1)}, u32[]{:S(2)}, u32[]{:S(2)}) collective-permute-start(bf16[2,16,24,128]{3,2,1,0:T(8,128)(2,1)S(1)} %pad_maximum_fusion.4), channel_id=1, source_target_pairs={{0,4},{4,0},{8,12},{12,8},{1,5},{5,1},{9,13},{13,9},{2,6},{6,2},{1... | collective-permute-start | bytes 589832 | tf_op jit(solution)/shard_map/ppermute | solution.py:449
  33.8 8.5 %collective-permute-start.4 = (bf16[6,16,24,128]{3,2,1,0:T(8,128)(2,1)S(1)}, bf16[6,16,24,128]{3,2,1,0:T(8,128)(2,1)S(1)}, u32[]{:S(2)}, u32[]{:S(2)}) collective-permute-start(bf16[6,16,24,128]{3,2,1,0:T(8,128)(2,1)S(1)} %pad_maximum_fusion.2), channel_id=1, source_target_pairs={{0,1},{1,0},{2,3},{3,2},{4,5},{5,4},{6,7},{7,6},{8,9},{9,8},{10,11... | collective-permute-start | bytes 1769480 | tf_op jit(solution)/shard_map/ppermute | solution.py:446
  41.7 4.8 %collective-permute-start.12 = (bf16[4,16,24,128]{3,2,1,0:T(8,128)(2,1)S(1)}, bf16[4,16,24,128]{3,2,1,0:T(8,128)(2,1)S(1)}, u32[]{:S(2)}, u32[]{:S(2)}) collective-permute-start(bf16[4,16,24,128]{3,2,1,0:T(8,128)(2,1)S(1)} %get-tuple-element.36.rest_7_), channel_id=1, source_target_pairs={{0,1},{1,0},{2,3},{3,2},{4,5},{5,4},{6,7},{7,6},{8,9},{9,8},{10,11... | collective-permute-start | bytes 1179656 | tf_op jit(solution)/shard_map/ppermute | solution.py:446
  41.8 1.9 %collective-permute-start.10 = (bf16[1,16,24,128]{3,2,1,0:T(8,128)(2,1)S(1)}, bf16[1,16,24,128]{3,2,1,0:T(8,128)(2,1)S(1)}, u32[]{:S(2)}, u32[]{:S(2)}) collective-permute-start(bf16[1,16,24,128]{3,2,1,0:T(8,128)(2,1)S(1)} %get-tuple-element.58.rest_0_), channel_id=1, source_target_pairs={{0,1},{1,0},{2,3},{3,2},{4,5},{5,4},{6,7},{7,6},{8,9},{9,8},{10,11... | collective-permute-start | bytes 294920 | tf_op jit(solution)/shard_map/ppermute | solution.py:446
  42.3 1.5 %collective-permute-start.11 = (bf16[1,16,24,128]{3,2,1,0:T(8,128)(2,1)S(1)}, bf16[1,16,24,128]{3,2,1,0:T(8,128)(2,1)S(1)}, u32[]{:S(2)}, u32[]{:S(2)}) collective-permute-start(bf16[1,16,24,128]{3,2,1,0:T(8,128)(2,1)S(1)} %get-tuple-element.69), channel_id=1, source_target_pairs={{0,1},{1,0},{2,3},{3,2},{4,5},{5,4},{6,7},{7,6},{8,9},{9,8},{10,11... | collective-permute-start | bytes 294920 | tf_op jit(solution)/shard_map/ppermute | solution.py:446
  46.6 9.1 %collective-permute-start.13 = (bf16[2,16,24,128]{3,2,1,0:T(8,128)(2,1)S(1)}, bf16[2,16,24,128]{3,2,1,0:T(8,128)(2,1)S(1)}, u32[]{:S(2)}, u32[]{:S(2)}) collective-permute-start(bf16[2,16,24,128]{3,2,1,0:T(8,128)(2,1)S(1)} %pad_maximum_fusion.5), channel_id=1, source_target_pairs={{0,4},{4,0},{8,12},{12,8},{1,5},{5,1},{9,13},{13,9},{2,6},{6,2},{1... | collective-permute-start | bytes 589832 | tf_op jit(solution)/shard_map/ppermute | solution.py:449
  47.6 13.0 %collective-permute-start.7 = (bf16[5,16,24,128]{3,2,1,0:T(8,128)(2,1)S(1)}, bf16[5,16,24,128]{3,2,1,0:T(8,128)(2,1)S(1)}, u32[]{:S(2)}, u32[]{:S(2)}) collective-permute-start(bf16[5,16,24,128]{3,2,1,0:T(8,128)(2,1)S(1)} %get-tuple-element.55), channel_id=1, source_target_pairs={{0,2},{2,0},{1,3},{3,1},{4,6},{6,4},{5,7},{7,5},{8,10},{10,8},{9,1... | collective-permute-start | bytes 1474568 | tf_op jit(solution)/shard_map/ppermute | solution.py:454
  48.1 9.6 %collective-permute-start.14 = (bf16[1,16,24,128]{3,2,1,0:T(8,128)(2,1)S(1)}, bf16[1,16,24,128]{3,2,1,0:T(8,128)(2,1)S(1)}, u32[]{:S(2)}, u32[]{:S(2)}) collective-permute-start(bf16[1,16,24,128]{3,2,1,0:T(8,128)(2,1)S(1)} %get-tuple-element.37.rest_0_), channel_id=1, source_target_pairs={{0,8},{4,12},{8,0},{12,4},{1,9},{5,13},{9,1},{13,5},{2,10},{6,14},... | collective-permute-start | bytes 294920 | tf_op jit(solution)/shard_map/ppermute | solution.py:449
  55.8 9.5 %collective-permute-start.17 = (bf16[1,16,24,128]{3,2,1,0:T(8,128)(2,1)S(1)}, bf16[1,16,24,128]{3,2,1,0:T(8,128)(2,1)S(1)}, u32[]{:S(2)}, u32[]{:S(2)}) collective-permute-start(bf16[1,16,24,128]{3,2,1,0:T(8,128)(2,1)S(1)} %get-tuple-element.63), channel_id=1, source_target_pairs={{0,8},{4,12},{8,0},{12,4},{1,9},{5,13},{9,1},{13,5},{2,10},{6,14},... | collective-permute-start | bytes 294920 | tf_op jit(solution)/shard_map/ppermute | solution.py:449
  57.7 7.6 %collective-permute-start.16 = (bf16[2,16,24,128]{3,2,1,0:T(8,128)(2,1)S(1)}, bf16[2,16,24,128]{3,2,1,0:T(8,128)(2,1)S(1)}, u32[]{:S(2)}, u32[]{:S(2)}) collective-permute-start(bf16[2,16,24,128]{3,2,1,0:T(8,128)(2,1)S(1)} %pad_maximum_fusion.6), channel_id=1, source_target_pairs={{0,4},{4,0},{8,12},{12,8},{1,5},{5,1},{9,13},{13,9},{2,6},{6,2},{1... | collective-permute-start | bytes 589832 | tf_op jit(solution)/shard_map/ppermute | solution.py:449
  60.6 8.8 %collective-permute-start.15 = (bf16[8,16,24,128]{3,2,1,0:T(8,128)(2,1)S(1)}, bf16[8,16,24,128]{3,2,1,0:T(8,128)(2,1)S(1)}, u32[]{:S(2)}, u32[]{:S(2)}) collective-permute-start(bf16[8,16,24,128]{3,2,1,0:T(8,128)(2,1)S(1)} %pad_maximum_fusion), channel_id=1, source_target_pairs={{0,1},{1,0},{2,3},{3,2},{4,5},{5,4},{6,7},{7,6},{8,9},{9,8},{10,11... | collective-permute-start | bytes 2359304 | tf_op jit(solution)/shard_map/ppermute | solution.py:446
  67.6 1.8 %collective-permute-start.21 = (bf16[4,16,24,128]{3,2,1,0:T(8,128)(2,1)S(1)}, bf16[4,16,24,128]{3,2,1,0:T(8,128)(2,1)S(1)}, u32[]{:S(2)}, u32[]{:S(2)}) collective-permute-start(bf16[4,16,24,128]{3,2,1,0:T(8,128)(2,1)S(1)} %get-tuple-element.41.rest_7_), channel_id=1, source_target_pairs={{0,1},{1,0},{2,3},{3,2},{4,5},{5,4},{6,7},{7,6},{8,9},{9,8},{10,11... | collective-permute-start | bytes 1179656 | tf_op jit(solution)/shard_map/ppermute | solution.py:446
  67.7 2.8 %collective-permute-start.19 = (bf16[1,16,24,128]{3,2,1,0:T(8,128)(2,1)S(1)}, bf16[1,16,24,128]{3,2,1,0:T(8,128)(2,1)S(1)}, u32[]{:S(2)}, u32[]{:S(2)}) collective-permute-start(bf16[1,16,24,128]{3,2,1,0:T(8,128)(2,1)S(1)} %get-tuple-element.37.rest_0_), channel_id=1, source_target_pairs={{0,1},{1,0},{2,3},{3,2},{4,5},{5,4},{6,7},{7,6},{8,9},{9,8},{10,11... | collective-permute-start | bytes 294920 | tf_op jit(solution)/shard_map/ppermute | solution.py:446
  68.2 2.3 %collective-permute-start.20 = (bf16[1,16,24,128]{3,2,1,0:T(8,128)(2,1)S(1)}, bf16[1,16,24,128]{3,2,1,0:T(8,128)(2,1)S(1)}, u32[]{:S(2)}, u32[]{:S(2)}) collective-permute-start(bf16[1,16,24,128]{3,2,1,0:T(8,128)(2,1)S(1)} %get-tuple-element.65), channel_id=1, source_target_pairs={{0,1},{1,0},{2,3},{3,2},{4,5},{5,4},{6,7},{7,6},{8,9},{9,8},{10,11... | collective-permute-start | bytes 294920 | tf_op jit(solution)/shard_map/ppermute | solution.py:446
  73.3 9.1 %collective-permute-start.22 = (bf16[2,16,24,128]{3,2,1,0:T(8,128)(2,1)S(1)}, bf16[2,16,24,128]{3,2,1,0:T(8,128)(2,1)S(1)}, u32[]{:S(2)}, u32[]{:S(2)}) collective-permute-start(bf16[2,16,24,128]{3,2,1,0:T(8,128)(2,1)S(1)} %pad_maximum_fusion.7), channel_id=1, source_target_pairs={{0,4},{4,0},{8,12},{12,8},{1,5},{5,1},{9,13},{13,9},{2,6},{6,2},{1... | collective-permute-start | bytes 589832 | tf_op jit(solution)/shard_map/ppermute | solution.py:449
  74.6 13.0 %collective-permute-start.18 = (bf16[5,16,24,128]{3,2,1,0:T(8,128)(2,1)S(1)}, bf16[5,16,24,128]{3,2,1,0:T(8,128)(2,1)S(1)}, u32[]{:S(2)}, u32[]{:S(2)}) collective-permute-start(bf16[5,16,24,128]{3,2,1,0:T(8,128)(2,1)S(1)} %get-tuple-element.53), channel_id=1, source_target_pairs={{0,2},{2,0},{1,3},{3,1},{4,6},{6,4},{5,7},{7,5},{8,10},{10,8},{9,1... | collective-permute-start | bytes 1474568 | tf_op jit(solution)/shard_map/ppermute | solution.py:454
  74.6 7.9 %collective-permute-start.23 = (bf16[1,16,24,128]{3,2,1,0:T(8,128)(2,1)S(1)}, bf16[1,16,24,128]{3,2,1,0:T(8,128)(2,1)S(1)}, u32[]{:S(2)}, u32[]{:S(2)}) collective-permute-start(bf16[1,16,24,128]{3,2,1,0:T(8,128)(2,1)S(1)} %get-tuple-element.43.refs_0_), channel_id=1, source_target_pairs={{0,8},{4,12},{8,0},{12,4},{1,9},{5,13},{9,1},{13,5},{2,10},{6,14},... | collective-permute-start | bytes 294920 | tf_op jit(solution)/shard_map/ppermute | solution.py:449
  82.6 7.3 %collective-permute-start.27 = (bf16[2,16,24,128]{3,2,1,0:T(8,128)(2,1)S(1)}, bf16[2,16,24,128]{3,2,1,0:T(8,128)(2,1)S(1)}, u32[]{:S(2)}, u32[]{:S(2)}) collective-permute-start(bf16[2,16,24,128]{3,2,1,0:T(8,128)(2,1)S(1)} %get-tuple-element.73), channel_id=1, source_target_pairs={{0,4},{4,0},{8,12},{12,8},{1,5},{5,1},{9,13},{13,9},{2,6},{6,2},{1... | collective-permute-start | bytes 589832 | tf_op jit(solution)/shard_map/ppermute | solution.py:449
  87.7 17.2 %collective-permute-start.24 = (bf16[8,16,24,128]{3,2,1,0:T(8,128)(2,1)S(1)}, bf16[8,16,24,128]{3,2,1,0:T(8,128)(2,1)S(1)}, u32[]{:S(2)}, u32[]{:S(2)}) collective-permute-start(bf16[8,16,24,128]{3,2,1,0:T(8,128)(2,1)S(1)} %pad_maximum_fusion.1), channel_id=1, source_target_pairs={{0,1},{1,0},{2,3},{3,2},{4,5},{5,4},{6,7},{7,6},{8,9},{9,8},{10,11... | collective-permute-start | bytes 2359304 | tf_op jit(solution)/shard_map/ppermute | solution.py:446
  87.8 8.2 %collective-permute-start.28 = (bf16[1,16,24,128]{3,2,1,0:T(8,128)(2,1)S(1)}, bf16[1,16,24,128]{3,2,1,0:T(8,128)(2,1)S(1)}, u32[]{:S(2)}, u32[]{:S(2)}) collective-permute-start(bf16[1,16,24,128]{3,2,1,0:T(8,128)(2,1)S(1)} %get-tuple-element.62), channel_id=1, source_target_pairs={{0,8},{4,12},{8,0},{12,4},{1,9},{5,13},{9,1},{13,5},{2,10},{6,14},... | collective-permute-start | bytes 294920 | tf_op jit(solution)/shard_map/ppermute | solution.py:449
  89.6 8.6 %collective-permute-start.26 = (bf16[2,16,24,128]{3,2,1,0:T(8,128)(2,1)S(1)}, bf16[2,16,24,128]{3,2,1,0:T(8,128)(2,1)S(1)}, u32[]{:S(2)}, u32[]{:S(2)}) collective-permute-start(bf16[2,16,24,128]{3,2,1,0:T(8,128)(2,1)S(1)} %get-tuple-element.74), channel_id=1, source_target_pairs={{0,2},{2,0},{1,3},{3,1},{4,6},{6,4},{5,7},{7,5},{8,10},{10,8},{9,1... | collective-permute-start | bytes 589832 | tf_op jit(solution)/shard_map/ppermute | solution.py:454
  96.1 7.7 %collective-permute-start.29 = (bf16[2,16,24,128]{3,2,1,0:T(8,128)(2,1)S(1)}, bf16[2,16,24,128]{3,2,1,0:T(8,128)(2,1)S(1)}, u32[]{:S(2)}, u32[]{:S(2)}) collective-permute-start(bf16[2,16,24,128]{3,2,1,0:T(8,128)(2,1)S(1)} %pad_maximum_fusion.10), channel_id=1, source_target_pairs={{0,2},{2,0},{1,3},{3,1},{4,6},{6,4},{5,7},{7,5},{8,10},{10,8},{9,1... | collective-permute-start | bytes 589832 | tf_op jit(solution)/shard_map/ppermute | solution.py:454
  96.4 7.4 %collective-permute-start.34 = (bf16[1,16,24,128]{3,2,1,0:T(8,128)(2,1)S(1)}, bf16[1,16,24,128]{3,2,1,0:T(8,128)(2,1)S(1)}, u32[]{:S(2)}, u32[]{:S(2)}) collective-permute-start(bf16[1,16,24,128]{3,2,1,0:T(8,128)(2,1)S(1)} %get-tuple-element.43.refs_0_), channel_id=1, source_target_pairs={{0,1},{1,0},{2,3},{3,2},{4,5},{5,4},{6,7},{7,6},{8,9},{9,8},{10,11... | collective-permute-start | bytes 294920 | tf_op jit(solution)/shard_map/ppermute | solution.py:446
  96.4 8.4 %collective-permute-start.25 = (bf16[1,16,24,128]{3,2,1,0:T(8,128)(2,1)S(1)}, bf16[1,16,24,128]{3,2,1,0:T(8,128)(2,1)S(1)}, u32[]{:S(2)}, u32[]{:S(2)}) collective-permute-start(bf16[1,16,24,128]{3,2,1,0:T(8,128)(2,1)S(1)} %get-tuple-element.43.refs_0_), channel_id=1, source_target_pairs={{0,2},{2,0},{1,3},{3,1},{4,6},{6,4},{5,7},{7,5},{8,10},{10,8},{9,1... | collective-permute-start | bytes 294920 | tf_op jit(solution)/shard_map/ppermute | solution.py:454
  98.2 9.1 %collective-permute-start.31 = (bf16[2,16,24,128]{3,2,1,0:T(8,128)(2,1)S(1)}, bf16[2,16,24,128]{3,2,1,0:T(8,128)(2,1)S(1)}, u32[]{:S(2)}, u32[]{:S(2)}) collective-permute-start(bf16[2,16,24,128]{3,2,1,0:T(8,128)(2,1)S(1)} %collective-permute-done.26.refs_1_), channel_id=1, source_target_pairs={{0,1},{1,0},{2,3},{3,2},{4,5},{5,4},{6,7},{7,6},{8,9},{9,8},{10,11... | collective-permute-start | bytes 589832 | tf_op jit(solution)/shard_map/ppermute | solution.py:446
  103.8 3.5 %collective-permute-start.32 = (bf16[2,16,24,128]{3,2,1,0:T(8,128)(2,1)S(1)}, bf16[2,16,24,128]{3,2,1,0:T(8,128)(2,1)S(1)}, u32[]{:S(2)}, u32[]{:S(2)}) collective-permute-start(bf16[2,16,24,128]{3,2,1,0:T(8,128)(2,1)S(1)} %collective-permute-done.29.refs_2_.refs_6_), channel_id=1, source_target_pairs={{0,1},{1,0},{2,3},{3,2},{4,5},{5,4},{6,7},{7,6},{8,9},{9,8},{10,11... | collective-permute-start | bytes 589832 | tf_op jit(solution)/shard_map/ppermute | solution.py:446
  103.8 2.6 %collective-permute-start.35 = (bf16[1,16,24,128]{3,2,1,0:T(8,128)(2,1)S(1)}, bf16[1,16,24,128]{3,2,1,0:T(8,128)(2,1)S(1)}, u32[]{:S(2)}, u32[]{:S(2)}) collective-permute-start(bf16[1,16,24,128]{3,2,1,0:T(8,128)(2,1)S(1)} %slice.189), channel_id=1, source_target_pairs={{0,1},{1,0},{2,3},{3,2},{4,5},{5,4},{6,7},{7,6},{8,9},{9,8},{10,11... | collective-permute-start | bytes 294920 | tf_op jit(solution)/shard_map/ppermute | solution.py:446
  104.9 2.4 %collective-permute-start.30 = (bf16[1,16,24,128]{3,2,1,0:T(8,128)(2,1)S(1)}, bf16[1,16,24,128]{3,2,1,0:T(8,128)(2,1)S(1)}, u32[]{:S(2)}, u32[]{:S(2)}) collective-permute-start(bf16[1,16,24,128]{3,2,1,0:T(8,128)(2,1)S(1)} %collective-permute-done.25.refs_0_), channel_id=1, source_target_pairs={{0,1},{1,0},{2,3},{3,2},{4,5},{5,4},{6,7},{7,6},{8,9},{9,8},{10,11... | collective-permute-start | bytes 294920 | tf_op jit(solution)/shard_map/ppermute | solution.py:446
  104.9 2.4 %collective-permute-start.33 = (bf16[1,16,24,128]{3,2,1,0:T(8,128)(2,1)S(1)}, bf16[1,16,24,128]{3,2,1,0:T(8,128)(2,1)S(1)}, u32[]{:S(2)}, u32[]{:S(2)}) collective-permute-start(bf16[1,16,24,128]{3,2,1,0:T(8,128)(2,1)S(1)} %add_convert_fusion.refs_8_), channel_id=1, source_target_pairs={{0,1},{1,0},{2,3},{3,2},{4,5},{5,4},{6,7},{7,6},{8,9},{9,8},{10,11... | collective-permute-start | bytes 294920 | tf_op jit(solution)/shard_map/ppermute | solution.py:446
  106.4 1.9 %copy-start.2 = (s32[64,3]{0,1:T(4,128)S(1)}, s32[64,3]{0,1:T(4,128)}, u32[]{:S(2)}) copy-start(s32[64,3]{0,1:T(4,128)} %param.4) | copy-start | bytes 2308

commit v5 on v4

--- a/solution.py
+++ b/solution.py
@@ -92,27 +92,6 @@
     )(meta, *arrays, *tokens)
 
 
-def fetch_kernel(stored, token, out, sem):
-    half = out.shape[0]
-    start = (1 - lax.axis_index("rep")) * half
-    copy = pltpu.make_async_copy(stored.at[pl.ds(start, half)], out, sem)
-    copy.start()
-    copy.wait()
-
-
-def fetch_far(stored, token):
-    half = stored.shape[0] // 2
-    return pl.pallas_call(
-        fetch_kernel,
-        out_shape=jax.ShapeDtypeStruct((half,) + stored.shape[1:], stored.dtype),
-        in_specs=[in_hbm(), anywhere()],
-        out_specs=whole(),
-        scratch_shapes=[pltpu.SemaphoreType.DMA(())],
-        compiler_params=pltpu.CompilerParams(vmem_limit_bytes=VMEM_LIMIT),
-        name="fetch_far",
-    )(stored, token)
-
-
 def row_product(refs_and_rows, panel, contract):
     picked = []
     stored = []
@@ -134,8 +113,8 @@
 
 def first_kernel(
     count, chunk, blocks, meta, cols, signs_hbm, stored,
-    panel, sent, mine, keep_row, near, keep, send,
-    signs, far, total, sign_sem, sems,
+    panel, sent, mine, keep_row, near, far, keep, send,
+    signs, total, sign_sem, sems,
 ):
     half = near.shape[0]
     rows = 2 * half
@@ -223,6 +202,7 @@
             shape((1,) + piece, jnp.bfloat16),
             shape(piece, jnp.float32),
             shape((half, slots, width, width), jnp.bfloat16),
+            shape((half, slots, width, width), jnp.bfloat16),
             shape((parts,) + piece, jnp.bfloat16),
             shape((parts + 1,) + piece, jnp.bfloat16),
         ),
@@ -230,10 +210,9 @@
             num_scalar_prefetch=2,
             grid=(1,),
             in_specs=[in_hbm(), in_hbm()],
-            out_specs=(whole(),) * 7,
+            out_specs=(whole(),) * 8,
             scratch_shapes=[
                 pltpu.VMEM(signs.shape, jnp.int32),
-                pltpu.VMEM((half, slots, width, width), jnp.bfloat16),
                 pltpu.VMEM((blocks, PAD, width), jnp.float32),
                 pltpu.SemaphoreType.DMA(()),
                 pltpu.SemaphoreType.DMA((2 * half // chunk,)),
@@ -340,8 +319,9 @@
 
 
 def backward_kernel(
-    count, chunk, meta, cols_own, cols_other, own, other, left, keep, send, total
+    count, chunk, meta, cols_own, cols_other, own, other, left, *rest
 ):
+    keep, send, total = rest[-3:]
     half = own.shape[0]
     stored = ((own, cols_own), (other, cols_other))
     total[...] = jnp.zeros_like(total)
@@ -362,7 +342,7 @@
     give_totals(count, 2 * half, meta, keep, send, total)
 
 
-def backward(meta, cols_own, cols_other, own, other, left, blocks):
+def backward(meta, cols_own, cols_other, own, other, left, blocks, tokens):
     half, slots, width = own.shape[0], own.shape[1], own.shape[3]
     count = left.shape[2] // 2
     chunk = min(16, half)
@@ -375,14 +355,14 @@
         grid_spec=pltpu.PrefetchScalarGridSpec(
             num_scalar_prefetch=3,
             grid=(1,),
-            in_specs=[whole()] * 3,
+            in_specs=[whole()] * 3 + [anywhere()] * len(tokens),
             out_specs=(whole(), whole()),
             scratch_shapes=[pltpu.VMEM((blocks, PAD, width), jnp.float32)],
         ),
         compiler_params=params(),
         cost_estimate=cost(2 * half * slots, width),
         name="backward_step",
-    )(meta, cols_own, cols_other, own, other, left)
+    )(meta, cols_own, cols_other, own, other, left, *tokens)
 
 
 def gradient_kernel(scale, chunk, rows, terms, meta, cols, *refs):
@@ -429,18 +409,23 @@
     )(meta, cols, *operands)
 
 
+def tie(x, *tokens):
+    return lax.optimization_barrier((x,) + tokens)[0]
+
+
 def local(block_values, columns, probe_signs):
     rows, slots, width = block_values.shape[0], block_values.shape[1], block_values.shape[3]
     blocks, count = probe_signs.shape[0], probe_signs.shape[1]
     half = rows // 2
     n_var = lax.axis_size("var")
     n_probe = lax.axis_size("probe")
+    groups = n_probe - 1
     inverse = 1.0 / math.sqrt(KS * width)
-    rep_index = lax.axis_index("rep")
-    meta = jnp.stack([lax.axis_index("var"), rep_index]).astype(jnp.int32)
+    meta = jnp.stack([lax.axis_index("var"), lax.axis_index("rep")]).astype(jnp.int32)
     signs = jnp.transpose(probe_signs, (1, 0, 2)).reshape(count * blocks, width)
+    signs = pltpu.with_memory_space_constraint(signs, pltpu.HBM)
+    block_values = pltpu.with_memory_space_constraint(block_values, pltpu.HBM)
     cols = columns.T
-    block_values = pltpu.with_memory_space_constraint(block_values, pltpu.HBM)
 
     def swap_rep(x):
         return lax.ppermute(x, "rep", [(0, 1), (1, 0)])
@@ -449,13 +434,15 @@
         return lax.ppermute(x, "var", [(i, i ^ bit) for i in range(n_var)])
 
     def from_probes(x):
-        return jnp.concatenate(
+        return stack(
             [
                 lax.ppermute(x, "probe", [(i, (i + d) % n_probe) for i in range(n_probe)])
                 for d in range(1, n_probe)
-            ],
-            axis=0,
+            ]
         )
+
+    def stack(arrays):
+        return arrays[0] if len(arrays) == 1 else jnp.concatenate(arrays, axis=0)
 
     def wide(x):
         return x.astype(jnp.float32)
@@ -463,53 +450,8 @@
     def narrow(x):
         return x.astype(jnp.bfloat16)
 
-    def exchange(own, parts, extra):
-        size = extra.shape[0]
-        if n_var == 4:
-            far = shift_var(own, 2)
-            near = shift_var(jnp.concatenate([own, narrow(parts[3])], axis=0), 1)
-            own_other = swap_rep(own)
-            crossed = shift_var(narrow(parts[2] + wide(near[1:])), 2)
-            last = shift_var(jnp.concatenate([far, narrow(parts[1])], axis=0), 1)
-            swapped = swap_rep(jnp.concatenate([near[:1], far, extra], axis=0))
-            summed = parts[0] + wide(last[1:]) + wide(crossed)
-            pieces = [
-                (own, [0]), (near, [1, None]), (far, [2]), (last, [3, None]),
-            ]
-            others = [
-                (own_other, [0]), (swapped, [1, 2] + [None] * size), (swap_rep(last[:1]), [3]),
-            ]
-            return pieces, others, summed, swapped[2:], near
-        bits = [1 << i for i in range(n_var.bit_length() - 1)]
-        held = {0: own}
-        for bit in reversed(bits):
-            for d in list(held):
-                held[d | bit] = shift_var(held[d], bit)
-        sums = dict(enumerate(parts))
-        for bit in bits:
-            for d in sorted(sums, reverse=True):
-                if d & bit:
-                    sums[d ^ bit] = sums[d ^ bit] + wide(shift_var(narrow(sums.pop(d)), bit))
-        pieces = [(jnp.concatenate([held[d] for d in range(n_var)], axis=0), list(range(n_var)))]
-        swapped = swap_rep(jnp.concatenate([pieces[0][0], extra], axis=0))
-        others = [(swapped, list(range(n_var)) + [None] * size)]
-        return pieces, others, sums[0], swapped[n_var:], own
-
     def home(d, h):
-        if d is None:
-            return None
         return lambda v, r: (v ^ d) * rows + (r ^ h) * half
-
-    def place(pieces, h):
-        return [(array, [home(d, h) for d in ds]) for array, ds in pieces]
-
-    def joined(pieces):
-        found = {}
-        for array, ds in pieces:
-            for i, d in enumerate(ds):
-                if d is not None:
-                    found[d] = array if len(ds) == 1 else array[i : i + 1]
-        return jnp.concatenate([found[d] for d in range(n_var)], axis=0)
 
     def row_place(h):
         return lambda v, r: (r ^ h) * half
@@ -517,111 +459,142 @@
     def sign_place(p, h):
         return lambda v, r: (r ^ h) * (blocks // 2) + p * half
 
-    other_columns = swap_rep(cols)
-    panel, sent, left_own, kept, near, keep, send = first_step(
+    def spot(label, h):
+        if label == "row":
+            return row_place(h)
+        return home(label, h) if label < n_var else sign_place(label - n_var, h)
+
+    def place(pieces, h):
+        return [
+            (array, [None if d is None else home(d, h) for d in ds]) for array, ds in pieces
+        ]
+
+    def jobs_of(entries):
+        jobs = []
+        for index in range(groups):
+            for kind in ("blocks", "rows"):
+                pieces = []
+                for h in (0, 1):
+                    for here, swapped, offset, labels in entries:
+                        array, skip = (here, 0) if h == 0 else (swapped, offset)
+                        where = [None] * array.shape[0]
+                        for i, label in enumerate(labels):
+                            if (label == "row") == (kind == "rows"):
+                                where[skip + index * len(labels) + i] = spot(label, h)
+                        if any(base is not None for base in where):
+                            pieces.append((array, where))
+                if pieces:
+                    jobs.append((pieces, blocks if kind == "blocks" else rows))
+        return jobs
+
+    def swap_all(arrays, labels, extra, tokens):
+        joined = list(arrays) + list(extra)
+        if tokens:
+            joined = [tie(array, *tokens) for array in joined]
+        swapped = swap_rep(stack(joined))
+        entries = []
+        offset = 0
+        for array, names in zip(arrays, labels):
+            entries.append((array, swapped, offset, names))
+            offset += array.shape[0]
+        return swapped, entries, offset
+
+    panel, sent, left_own, kept, near_blocks, far_blocks, keep, send = first_step(
         meta, cols, signs, block_values, blocks
     )
     received = swap_rep(send)
     updated = narrow(wide(left_own) + inverse * (kept + wide(received[n_var]))[None])
-    groups = n_probe - 1
+    other_blocks = swap_rep(tie(far_blocks, updated))
+    other_columns = swap_rep(cols)
     right = [[panel]] + [[] for _ in range(groups)]
     left = [[panel]] + [[] for _ in range(groups)]
-    travelling = from_probes(sent)
+    sent = from_probes(tie(sent, updated))
+    sign_labels = [n_var + p for p in range(n_var)]
+    incoming, incoming_labels = [], []
+    unpacked = []
 
     for step in range(3):
-        last = step == 2
         parts = [wide(keep[d : d + 1]) + wide(received[d : d + 1]) for d in range(n_var)]
-        extra = travelling if step == 0 else jnp.concatenate([travelling, left_own], axis=0)
-        pieces, others, summed, extra_other, mark = exchange(updated, parts, extra)
+        if n_var == 4:
+            far = shift_var(updated, 2)
+            both = shift_var(stack([updated, narrow(parts[3])]), 1)
+            near = both[:1]
+            own_other = swap_rep(updated)
+            crossed = shift_var(narrow(parts[2] + wide(both[1:])), 2)
+            final = shift_var(stack([tie(far, own_other), narrow(parts[1])]), 1)
+            last = final[:1]
+            middle_other = swap_rep(stack([near, far]))
+            summed = parts[0] + wide(final[1:]) + wide(crossed)
+            held = [updated, near, far, last]
+            others = [(own_other, [0]), (middle_other, [1, 2]), (swap_rep(last), [3])]
+            window, settled = [both], [middle_other]
+        else:
+            bits = [1 << i for i in range(n_var.bit_length() - 1)]
+            found = {0: updated}
+            for bit in reversed(bits):
+                for d in list(found):
+                    found[d | bit] = shift_var(found[d], bit)
+            held = [found[d] for d in range(n_var)]
+            sums = dict(enumerate(parts))
+            for bit in bits:
+                for d in sorted(sums, reverse=True):
+                    if d & bit:
+                        sums[d ^ bit] = sums[d ^ bit] + wide(
+                            shift_var(narrow(sums.pop(d)), bit)
+                        )
+            summed = sums[0]
+            others = [(swap_rep(stack(held)), list(range(n_var)))]
+            window, settled = [], []
+
         if step == 0:
-            other = swap_rep(fetch_far(block_values, mark))
-        size = n_var if step == 0 else n_var + 1
-        total = travelling.shape[0]
-        jobs = []
+            swapped, entries, _ = swap_all([sent], [sign_labels], [], window)
+            jobs = jobs_of(entries)
+        else:
+            swapped, entries, offset = swap_all(incoming, incoming_labels, [left_own], window)
+            tail = [None] * offset + [row_place(1)]
+            jobs = jobs_of(entries)
+            jobs.append(([(left_own, [row_place(0)]), (swapped, tail)], rows))
+        found = list(unpack(meta, jobs))
+        unpacked += found
+        if step > 0:
+            left[0].append(found.pop())
         for index in range(groups):
-
-            def spots(h, kind, index=index):
-                where = [None] * extra.shape[0]
-                for p in range(n_var):
-                    if kind == "blocks":
-                        where[index * size + p] = sign_place(p, h) if step == 0 else home(p, h)
-                if kind == "rows":
-                    where[index * size + n_var] = row_place(h)
-                return where
-
-            for kind in ("blocks",) if step == 0 else ("blocks", "rows"):
-                jobs.append(
-                    (
-                        [
-                            (travelling, spots(0, kind)[:total]),
-                            (extra_other, spots(1, kind)),
-                        ],
-                        blocks if kind == "blocks" else rows,
-                    )
-                )
-        if step > 0:
-            tail = [None] * (extra.shape[0] - 1)
-            jobs.append(
-                ([(left_own, [row_place(0)]), (extra_other, tail + [row_place(1)])], rows)
+            right[1 + index].append(found.pop(0))
+            left[1 + index].append(right[1 + index][0] if step == 0 else found.pop(0))
+
+        left_own = narrow(wide(tie(left_own, swapped, *settled)) + inverse * summed)
+        if step == 2 and n_var == 4:
+            incoming = [from_probes(stack(held[:3])), from_probes(stack([last, left_own]))]
+            incoming_labels = [[0, 1, 2], [3, "row"]]
+        else:
+            incoming = [from_probes(stack(held + [left_own]))]
+            incoming_labels = [list(range(n_var)) + ["row"]]
+        sources = place([(array, [d]) for d, array in enumerate(held)], 0) + place(others, 1)
+        if step < 2:
+            keep, send = backward(
+                meta, cols, other_columns, near_blocks, other_blocks, left_own, blocks, []
             )
-        fresh = unpack(meta, jobs)
-        found = list(fresh)
-        for index in range(groups):
-            value = found.pop(0)
-            right[1 + index].append(value)
-            left[1 + index].append(value if step == 0 else found.pop(0))
-        if step > 0:
-            left[0].append(found.pop(0))
-        sources = place(pieces, 0) + place(others, 1)
-        left_own = narrow(wide(left_own) + inverse * summed)
-        if not last:
-            keep, send = backward(meta, cols, other_columns, near, other, left_own, blocks)
             received = swap_rep(send)
-            message = jnp.concatenate([joined(pieces), left_own], axis=0)
             panel, updated = forward(
-                meta, cols, other_columns, near, other, sources, blocks, inverse,
-                [send] + list(fresh),
+                meta, cols, other_columns, near_blocks, other_blocks, sources, blocks, inverse,
+                [send],
             )
             right[0].append(panel)
-            travelling = from_probes(message)
-        else:
-            (panel,) = unpack(meta, [(sources, blocks)], fresh)
-            right[0].append(panel)
-
-    if n_var == 4:
-        arrays = [
-            (from_probes(pieces[0][0]), [0]),
-            (from_probes(jnp.concatenate([pieces[1][0][:1], pieces[2][0]], axis=0)), [1, 2]),
-            (from_probes(jnp.concatenate([pieces[3][0][:1], left_own], axis=0)), [3, "row"]),
-        ]
-    else:
-        arrays = [
-            (
-                from_probes(jnp.concatenate([joined(pieces), left_own], axis=0)),
-                list(range(n_var)) + ["row"],
-            )
-        ]
-    crossed = [swap_rep(array) for array, _ in arrays]
-    jobs = []
+
+    jobs = [(sources, blocks)]
+    jobs.append(([(left_own, [row_place(0)]), (swap_rep(left_own), [row_place(1)])], rows))
+    ready = list(unpack(meta, jobs))
+    right[0].append(ready[0])
+    left[0].append(ready[1])
+    entries = []
+    for array, labels in zip(incoming, incoming_labels):
+        tokens = ready + unpacked if array is incoming[-1] else []
+        _, entry, _ = swap_all([array], [labels], [], tokens)
+        entries += entry
+    found = list(unpack(meta, jobs_of(entries)))
     for index in range(groups):
-        blocks_in = []
-        rows_in = []
-        for h, versions in ((0, [array for array, _ in arrays]), (1, crossed)):
-            for array, (_, ds) in zip(versions, arrays):
-                lead = [None] * (index * len(ds))
-                rest = [None] * (array.shape[0] - (index + 1) * len(ds))
-                here = [None if d == "row" else home(d, h) for d in ds]
-                blocks_in.append((array, lead + here + rest))
-                if "row" in ds:
-                    here = [row_place(h) if d == "row" else None for d in ds]
-                    rows_in.append((array, lead + here + rest))
-        jobs += [(blocks_in, blocks), (rows_in, rows)]
-    jobs.append(([(left_own, [row_place(0)]), (swap_rep(left_own), [row_place(1)])], rows))
-    found = unpack(meta, jobs, [panel])
-    for index in range(groups):
-        right[1 + index].append(found[2 * index])
-        left[1 + index].append(found[2 * index + 1])
-    left[0].append(found[-1])
+        right[1 + index].append(found.pop(0))
+        left[1 + index].append(found.pop(0))
 
     lefts = [group[t] for t in range(4) for group in left]
     rights = [group[3 - t] for t in range(4) for group in right]

time: 113 us -> 99.8 us (0.88)
  waiting for transfers between devices: 52.4 us -> 30.9 us
  starting transfers between devices: 29.2 us -> 39.8 us
  local copies, waits for them, and re-layouts: 2.46 us -> 0.89 us
    ppermute x12, waiting for transfers between devices: 39.2 us -> 22.4 us  [shift_var(): return lax.ppermute(x, 'var', [(i, i ^ bit) for i in range(n_var)])]
    ppermute x6 -> x5, waiting for transfers between devices: 10.1 us -> 4.42 us  [from_probes(): lax.ppermute(x, 'probe', [(i, (i + d) % n_probe) for i in range(n_probe)])]
    ppermute x12, starting transfers between devices: 20.7 us -> 26.1 us  [shift_var(): return lax.ppermute(x, 'var', [(i, i ^ bit) for i in range(n_var)])]
    ppermute x6 -> x5, starting transfers between devices: 4.56 us -> 9.29 us  [from_probes(): lax.ppermute(x, 'probe', [(i, (i + d) % n_probe) for i in range(n_probe)])]
    pallas_call x1 -> x0, Pallas kernels: 1.9 us -> none  [fetch_far(): pl.pallas_call(fetch_kernel, out_shape=jax.ShapeDtypeStruct((half,) + sto...]
    unnamed x11 -> x7, local copies, waits for them, and re-layouts: 2.21 us -> 0.73 us
    ppermute x18 -> x20, waiting for transfers between devices: 3.2 us -> 4.03 us  [swap_rep(): return lax.ppermute(x, 'rep', [(0, 1), (1, 0)])]
    ppermute x18 -> x20, starting transfers between devices: 3.85 us -> 4.41 us  [swap_rep(): return lax.ppermute(x, 'rep', [(0, 1), (1, 0)])]
  transfers between devices with their start and end apart: 36 -> 37, of which waited for: 15 -> 14; matrix products, arithmetic and copies ran while one was open for 1% -> 1% of each run, Pallas kernels for 9% -> 9%
where the time goes in v5:
time: 99.8 us; the launch traced here: 99.6 us
  starting transfers between devices  39.8 us (40%)
  waiting for transfers between devices  30.9 us (31%)
  Pallas kernels  26.6 us (27%)
  other arithmetic  1.04 us (1%)
    ppermute x12, starting transfers between devices, shift_var(): return lax.ppermute(x, 'var', [(i, i ^ bit) for i in range(n_var)])  26.1 us
    ppermute x12, waiting for transfers between devices, shift_var(): return lax.ppermute(x, 'var', [(i, i ^ bit) for i in range(n_var)])  22.4 us
    ppermute x5, starting transfers between devices, from_probes(): lax.ppermute(x, 'probe', [(i, (i + d) % n_probe) for i in range(n_probe)])  9.29 us
    pallas_call x1, Pallas kernels, first_step(): pl.pallas_call(functools.partial(first_kernel, count, chunk, blocks), out...  7.38 us
    pallas_call x2, Pallas kernels, forward(): pl.pallas_call(functools.partial(forward_kernel, count, chunk, 2 * half,...  5.5 us
    pallas_call x1, Pallas kernels, gradient(): pl.pallas_call(functools.partial(gradient_kernel, scale, chunk, rows, len...  4.78 us
    pallas_call x5, Pallas kernels, unpack(): pl.pallas_call(functools.partial(unpack_kernel, count, wheres, len(tokens...  4.59 us
    ppermute x5, waiting for transfers between devices, from_probes(): lax.ppermute(x, 'probe', [(i, (i + d) % n_probe) for i in range(n_probe)])  4.42 us
  transfers between devices with their start and end apart: 37, of which 14 were waited for; matrix products, arithmetic and copies ran while one was open for 1% of the time, Pallas kernels for 9%

profile of v5, /device:TPU:0, one launch (start us, length us, event | category | flops | bytes accessed | tf_op | source)
XLA Modules:
  0.0 99.6 jit_solution(217403924150071651)
XLA Ops:
  0.0 0.1 pad_add_fusion.meta
  0.1 0.7 copy-done
  0.8 7.4 %first_step.1 = (bf16[256,16,128]{2,1,0:T(8,128)(2,1)S(1)}, bf16[4,16,24,128]{3,2,1,0:T(8,128)(2,1)S(1)}, bf16[1,16,24,128]{3,2,1,0:T(8,128)(2,1)S(1)}, f32[16,2...) custom-call(s32[2]{0:T(128)S(1)} %pad_add_fusion.meta, ...), custom_call_target="tpu_custom_call" | custom-call | flops 1610612736 | bytes 50331648 | tf_op jit(solution)/shard_map/first_step/pallas_call | solution.py:197
  8.1 0.5 collective-permute-start
  8.7 1.5 %collective-permute-done = bf16[5,16,24,128]{3,2,1,0:T(8,128)(2,1)S(1)} collective-permute-done((bf16[5,16,24,128]{3,2,1,0:T(8,128)(2,1)S(1)}, bf16[5,16,24,128]{3,2,1,0:T(8,128)(2,1)S(1)}, u32[]{:S(2)}, u32[]{:S(2)}) %collective-permute-start) | collective-permute-done | bytes 491552 | tf_op jit(solution)/shard_map/ppermute | solution.py:431
  10.2 0.4 collective-permute-start.11
  10.7 2.8 %collective-permute-start.2 = (bf16[2,16,24,128]{3,2,1,0:T(8,128)(2,1)S(1)}, bf16[2,16,24,128]{3,2,1,0:T(8,128)(2,1)S(1)}, u32[]{:S(2)}, u32[]{:S(2)}) collective-permute-start(bf16[2,16,24,128]{3,2,1,0:T(8,128)(2,1)S(1)} %pad_maximum_fusion.3), channel_id=1, source_target_pairs={{0,4},{4,0},{8,12},{12,8},{1,5},{5,1},{9,13},{13,9},{2,6},{6,2},{1... | collective-permute-start | bytes 589832 | tf_op jit(solution)/shard_map/ppermute | solution.py:434
  13.5 0.1 collective-permute-start.5
  13.6 2.6 %collective-permute-start.4 = (bf16[1,16,24,128]{3,2,1,0:T(8,128)(2,1)S(1)}, bf16[1,16,24,128]{3,2,1,0:T(8,128)(2,1)S(1)}, u32[]{:S(2)}, u32[]{:S(2)}) collective-permute-start(bf16[1,16,24,128]{3,2,1,0:T(8,128)(2,1)S(1)} %get-tuple-element.90.rest_0_), channel_id=1, source_target_pairs={{0,8},{4,12},{8,0},{12,4},{1,9},{5,13},{9,1},{13,5},{2,10},{6,14},... | collective-permute-start | bytes 294920 | tf_op jit(solution)/shard_map/ppermute | solution.py:434
  16.2 0.2 collective-permute-start.10
  16.3 2.6 %collective-permute-start.1 = (bf16[4,16,24,128]{3,2,1,0:T(8,128)(2,1)S(1)}, bf16[4,16,24,128]{3,2,1,0:T(8,128)(2,1)S(1)}, u32[]{:S(2)}, u32[]{:S(2)}) collective-permute-start(bf16[4,16,24,128]{3,2,1,0:T(8,128)(2,1)S(1)} %get-tuple-element.50), channel_id=1, source_target_pairs={{0,2},{2,0},{1,3},{3,1},{4,6},{6,4},{5,7},{7,5},{8,10},{10,8},{9,1... | collective-permute-start | bytes 1179656 | tf_op jit(solution)/shard_map/ppermute | solution.py:439
  18.9 1.4 %collective-permute-done.4.rest_2_ = bf16[1,16,24,128]{3,2,1,0:T(8,128)(2,1)S(1)} collective-permute-done((bf16[1,16,24,128]{3,2,1,0:T(8,128)(2,1)S(1)}, bf16[1,16,24,128]{3,2,1,0:T(8,128)(2,1)S(1)}, u32[]{:S(2)}, u32[]{:S(2)}) %collective-permute-start.4) | collective-permute-done | bytes 98336 | tf_op jit(solution)/shard_map/ppermute | solution.py:434
  20.3 0.7 collective-permute-done.2
  21.0 0.1 add_convert_fusion.9
  21.1 2.7 %collective-permute-start.8 = (bf16[1,16,24,128]{3,2,1,0:T(8,128)(2,1)S(1)}, bf16[1,16,24,128]{3,2,1,0:T(8,128)(2,1)S(1)}, u32[]{:S(2)}, u32[]{:S(2)}) collective-permute-start(bf16[1,16,24,128]{3,2,1,0:T(8,128)(2,1)S(1)} %get-tuple-element.91), channel_id=1, source_target_pairs={{0,8},{4,12},{8,0},{12,4},{1,9},{5,13},{9,1},{13,5},{2,10},{6,14},... | collective-permute-start | bytes 294920 | tf_op jit(solution)/shard_map/ppermute | solution.py:434
  23.8 1.8 %collective-permute-start.6 = (bf16[2,16,24,128]{3,2,1,0:T(8,128)(2,1)S(1)}, bf16[2,16,24,128]{3,2,1,0:T(8,128)(2,1)S(1)}, u32[]{:S(2)}, u32[]{:S(2)}) collective-permute-start(bf16[2,16,24,128]{3,2,1,0:T(8,128)(2,1)S(1)} %pad_maximum_fusion.4), channel_id=1, source_target_pairs={{0,4},{4,0},{8,12},{12,8},{1,5},{5,1},{9,13},{13,9},{2,6},{6,2},{1... | collective-permute-start | bytes 589832 | tf_op jit(solution)/shard_map/ppermute | solution.py:434
  25.6 2.7 %collective-permute-done.1.refs_0_ = bf16[4,16,24,128]{3,2,1,0:T(8,128)(2,1)S(1)} collective-permute-done((bf16[4,16,24,128]{3,2,1,0:T(8,128)(2,1)S(1)}, bf16[4,16,24,128]{3,2,1,0:T(8,128)(2,1)S(1)}, u32[]{:S(2)}, u32[]{:S(2)}) %collective-permute-start.1) | collective-permute-done | bytes 393248 | tf_op jit(solution)/shard_map/ppermute | solution.py:439
  28.4 2.5 %collective-permute-done.6 = bf16[2,16,24,128]{3,2,1,0:T(8,128)(2,1)S(1)} collective-permute-done((bf16[2,16,24,128]{3,2,1,0:T(8,128)(2,1)S(1)}, bf16[2,16,24,128]{3,2,1,0:T(8,128)(2,1)S(1)}, u32[]{:S(2)}, u32[]{:S(2)}) %collective-permute-start.6) | collective-permute-done | bytes 196640 | tf_op jit(solution)/shard_map/ppermute | solution.py:434
  30.9 1.4 %collective-permute-done.7.rest_5_ = bf16[2,16,24,128]{3,2,1,0:T(8,128)(2,1)S(1)} collective-permute-done((bf16[2,16,24,128]{3,2,1,0:T(8,128)(2,1)S(1)}, bf16[2,16,24,128]{3,2,1,0:T(8,128)(2,1)S(1)}, u32[]{:S(2)}, u32[]{:S(2)}) %collective-permute-start.7) | collective-permute-done | bytes 196640 | tf_op jit(solution)/shard_map/ppermute | solution.py:431
  32.3 0.1 constant_dynamic-update-slice_fusion
  32.5 2.2 %backward_step.2 = (bf16[4,16,24,128]{3,2,1,0:T(8,128)(2,1)S(1)}, bf16[4,16,24,128]{3,2,1,0:T(8,128)(2,1)S(1)}) custom-call(s32[2]{0:T(128)S(1)} %pad_add_fusion.meta, s32[3,64]{1,0:T(4,128)S(1)} %bitcast.21, s32[3,64]{1,0:T(4,128)S(1)} %collective-permute-done.10.cols_other, bf16[32,3,128,128]{3,2,1,0:T(8,128)(2,1)S(1)} %get-tuple-element.55.own, ...), custom_call_target="tpu_custom_call" | custom-call | flops 805306368 | bytes 25165824 | tf_op jit(solution)/shard_map/backward_step/pallas_call | solution.py:352
  34.7 0.2 collective-permute-start.13
  34.9 0.4 collective-permute-start.12
  35.2 1.6 %collective-permute-start.9 = (bf16[5,16,24,128]{3,2,1,0:T(8,128)(2,1)S(1)}, bf16[5,16,24,128]{3,2,1,0:T(8,128)(2,1)S(1)}, u32[]{:S(2)}, u32[]{:S(2)}) collective-permute-start(bf16[5,16,24,128]{3,2,1,0:T(8,128)(2,1)S(1)} %get-tuple-element.87), channel_id=1, source_target_pairs={{0,2},{2,0},{1,3},{3,1},{4,6},{6,4},{5,7},{7,5},{8,10},{10,8},{9,1... | collective-permute-start | bytes 1474568 | tf_op jit(solution)/shard_map/ppermute | solution.py:439
  36.9 2.8 %forward_step.2 = (bf16[256,16,128]{2,1,0:T(8,128)(2,1)S(1)}, bf16[1,16,24,128]{3,2,1,0:T(8,128)(2,1)S(1)}) custom-call(s32[2]{0:T(128)S(1)} %pad_add_fusion.meta, s32[3,64]{1,0:T(4,128)S(1)} %bitcast.22, s32[3,64]{1,0:T(4,128)S(1)} %collective-permute-done.10.cols_other, bf16[32,3,128,128]{3,2,1,0:T(8,128)(2,1)S(1)} %get-tuple-element.55.own, ...), custom_call_target="tpu_custom_call" | custom-call | flops 805306368 | bytes 25165824 | tf_op jit(solution)/shard_map/forward_step/pallas_call | solution.py:270
  39.7 1.7 %collective-permute-start.14 = (bf16[2,16,24,128]{3,2,1,0:T(8,128)(2,1)S(1)}, bf16[2,16,24,128]{3,2,1,0:T(8,128)(2,1)S(1)}, u32[]{:S(2)}, u32[]{:S(2)}) collective-permute-start(bf16[2,16,24,128]{3,2,1,0:T(8,128)(2,1)S(1)} %pad_maximum_fusion.6), channel_id=1, source_target_pairs={{0,4},{4,0},{8,12},{12,8},{1,5},{5,1},{9,13},{13,9},{2,6},{6,2},{1... | collective-permute-start | bytes 589832 | tf_op jit(solution)/shard_map/ppermute | solution.py:434
  41.4 2.5 %collective-permute-start.16 = (bf16[1,16,24,128]{3,2,1,0:T(8,128)(2,1)S(1)}, bf16[1,16,24,128]{3,2,1,0:T(8,128)(2,1)S(1)}, u32[]{:S(2)}, u32[]{:S(2)}) collective-permute-start(bf16[1,16,24,128]{3,2,1,0:T(8,128)(2,1)S(1)} %get-tuple-element.59.rest_0_), channel_id=1, source_target_pairs={{0,8},{4,12},{8,0},{12,4},{1,9},{5,13},{9,1},{13,5},{2,10},{6,14},... | collective-permute-start | bytes 294920 | tf_op jit(solution)/shard_map/ppermute | solution.py:434
  43.9 3.9 %collective-permute-done.16.rest_2_ = bf16[1,16,24,128]{3,2,1,0:T(8,128)(2,1)S(1)} collective-permute-done((bf16[1,16,24,128]{3,2,1,0:T(8,128)(2,1)S(1)}, bf16[1,16,24,128]{3,2,1,0:T(8,128)(2,1)S(1)}, u32[]{:S(2)}, u32[]{:S(2)}) %collective-permute-start.16) | collective-permute-done | bytes 98336 | tf_op jit(solution)/shard_map/ppermute | solution.py:434
  47.8 0.7 collective-permute-done.14
  48.6 0.1 add_convert_fusion.5
  48.6 2.7 %collective-permute-start.20 = (bf16[1,16,24,128]{3,2,1,0:T(8,128)(2,1)S(1)}, bf16[1,16,24,128]{3,2,1,0:T(8,128)(2,1)S(1)}, u32[]{:S(2)}, u32[]{:S(2)}) collective-permute-start(bf16[1,16,24,128]{3,2,1,0:T(8,128)(2,1)S(1)} %get-tuple-element.95), channel_id=1, source_target_pairs={{0,8},{4,12},{8,0},{12,4},{1,9},{5,13},{9,1},{13,5},{2,10},{6,14},... | collective-permute-start | bytes 294920 | tf_op jit(solution)/shard_map/ppermute | solution.py:434
  51.4 1.6 %collective-permute-start.18 = (bf16[2,16,24,128]{3,2,1,0:T(8,128)(2,1)S(1)}, bf16[2,16,24,128]{3,2,1,0:T(8,128)(2,1)S(1)}, u32[]{:S(2)}, u32[]{:S(2)}) collective-permute-start(bf16[2,16,24,128]{3,2,1,0:T(8,128)(2,1)S(1)} %pad_maximum_fusion.7), channel_id=1, source_target_pairs={{0,4},{4,0},{8,12},{12,8},{1,5},{5,1},{9,13},{13,9},{2,6},{6,2},{1... | collective-permute-start | bytes 589832 | tf_op jit(solution)/shard_map/ppermute | solution.py:434
  53.0 0.1 collective-permute-start.15
  53.2 0.6 collective-permute-start.19
  53.8 4.4 %collective-permute-done.18 = bf16[2,16,24,128]{3,2,1,0:T(8,128)(2,1)S(1)} collective-permute-done((bf16[2,16,24,128]{3,2,1,0:T(8,128)(2,1)S(1)}, bf16[2,16,24,128]{3,2,1,0:T(8,128)(2,1)S(1)}, u32[]{:S(2)}, u32[]{:S(2)}) %collective-permute-start.18) | collective-permute-done | bytes 196640 | tf_op jit(solution)/shard_map/ppermute | solution.py:434
  58.2 0.1 constant_dynamic-update-slice_fusion.5
  58.3 2.2 %backward_step.3 = (bf16[4,16,24,128]{3,2,1,0:T(8,128)(2,1)S(1)}, bf16[4,16,24,128]{3,2,1,0:T(8,128)(2,1)S(1)}) custom-call(s32[2]{0:T(128)S(1)} %pad_add_fusion.meta, s32[3,64]{1,0:T(4,128)S(1)} %bitcast.23, s32[3,64]{1,0:T(4,128)S(1)} %collective-permute-done.10.cols_other, bf16[32,3,128,128]{3,2,1,0:T(8,128)(2,1)S(1)} %get-tuple-element.55.own, ...), custom_call_target="tpu_custom_call" | custom-call | flops 805306368 | bytes 25165824 | tf_op jit(solution)/shard_map/backward_step/pallas_call | solution.py:352
  60.5 0.1 collective-permute-start.23
  60.6 0.5 collective-permute-start.22
  61.1 1.7 %collective-permute-start.21 = (bf16[5,16,24,128]{3,2,1,0:T(8,128)(2,1)S(1)}, bf16[5,16,24,128]{3,2,1,0:T(8,128)(2,1)S(1)}, u32[]{:S(2)}, u32[]{:S(2)}) collective-permute-start(bf16[5,16,24,128]{3,2,1,0:T(8,128)(2,1)S(1)} %get-tuple-element.85), channel_id=1, source_target_pairs={{0,2},{2,0},{1,3},{3,1},{4,6},{6,4},{5,7},{7,5},{8,10},{10,8},{9,1... | collective-permute-start | bytes 1474568 | tf_op jit(solution)/shard_map/ppermute | solution.py:439
  62.7 2.8 %forward_step.3 = (bf16[256,16,128]{2,1,0:T(8,128)(2,1)S(1)}, bf16[1,16,24,128]{3,2,1,0:T(8,128)(2,1)S(1)}) custom-call(s32[2]{0:T(128)S(1)} %pad_add_fusion.meta, s32[3,64]{1,0:T(4,128)S(1)} %bitcast.24, s32[3,64]{1,0:T(4,128)S(1)} %collective-permute-done.10.cols_other, bf16[32,3,128,128]{3,2,1,0:T(8,128)(2,1)S(1)} %get-tuple-element.55.own, ...), custom_call_target="tpu_custom_call" | custom-call | flops 805306368 | bytes 25165824 | tf_op jit(solution)/shard_map/forward_step/pallas_call | solution.py:270
  65.6 1.6 %collective-permute-start.24 = (bf16[2,16,24,128]{3,2,1,0:T(8,128)(2,1)S(1)}, bf16[2,16,24,128]{3,2,1,0:T(8,128)(2,1)S(1)}, u32[]{:S(2)}, u32[]{:S(2)}) collective-permute-start(bf16[2,16,24,128]{3,2,1,0:T(8,128)(2,1)S(1)} %pad_maximum_fusion.9), channel_id=1, source_target_pairs={{0,4},{4,0},{8,12},{12,8},{1,5},{5,1},{9,13},{13,9},{2,6},{6,2},{1... | collective-permute-start | bytes 589832 | tf_op jit(solution)/shard_map/ppermute | solution.py:434
  67.2 2.3 %collective-permute-start.26 = (bf16[1,16,24,128]{3,2,1,0:T(8,128)(2,1)S(1)}, bf16[1,16,24,128]{3,2,1,0:T(8,128)(2,1)S(1)}, u32[]{:S(2)}, u32[]{:S(2)}) collective-permute-start(bf16[1,16,24,128]{3,2,1,0:T(8,128)(2,1)S(1)} %get-tuple-element.68.refs_0_), channel_id=1, source_target_pairs={{0,8},{4,12},{8,0},{12,4},{1,9},{5,13},{9,1},{13,5},{2,10},{6,14},... | collective-permute-start | bytes 294920 | tf_op jit(solution)/shard_map/ppermute | solution.py:434
  69.5 4.5 %collective-permute-done.26.refs_2_ = bf16[1,16,24,128]{3,2,1,0:T(8,128)(2,1)S(1)} collective-permute-done((bf16[1,16,24,128]{3,2,1,0:T(8,128)(2,1)S(1)}, bf16[1,16,24,128]{3,2,1,0:T(8,128)(2,1)S(1)}, u32[]{:S(2)}, u32[]{:S(2)}) %collective-permute-start.26) | collective-permute-done | bytes 98336 | tf_op jit(solution)/shard_map/ppermute | solution.py:434
  74.0 0.4 collective-permute-done.24
  74.4 0.1 collective-permute-start.25
  74.5 0.1 add_convert_fusion.1
  74.6 2.2 %collective-permute-start.28 = (bf16[2,16,24,128]{3,2,1,0:T(8,128)(2,1)S(1)}, bf16[2,16,24,128]{3,2,1,0:T(8,128)(2,1)S(1)}, u32[]{:S(2)}, u32[]{:S(2)}) collective-permute-start(bf16[2,16,24,128]{3,2,1,0:T(8,128)(2,1)S(1)} %pad_maximum_fusion.10), channel_id=1, source_target_pairs={{0,4},{4,0},{8,12},{12,8},{1,5},{5,1},{9,13},{13,9},{2,6},{6,2},{1... | collective-permute-start | bytes 589832 | tf_op jit(solution)/shard_map/ppermute | solution.py:434
  76.8 0.3 collective-permute-start.29
  77.1 1.7 %collective-permute-start.31 = (bf16[1,16,24,128]{3,2,1,0:T(8,128)(2,1)S(1)}, bf16[1,16,24,128]{3,2,1,0:T(8,128)(2,1)S(1)}, u32[]{:S(2)}, u32[]{:S(2)}) collective-permute-start(bf16[1,16,24,128]{3,2,1,0:T(8,128)(2,1)S(1)} %get-tuple-element.93), channel_id=1, source_target_pairs={{0,8},{4,12},{8,0},{12,4},{1,9},{5,13},{9,1},{13,5},{2,10},{6,14},... | collective-permute-start | bytes 294920 | tf_op jit(solution)/shard_map/ppermute | solution.py:434
  78.9 1.7 %collective-permute-start.33 = (bf16[3,16,24,128]{3,2,1,0:T(8,128)(2,1)S(1)}, bf16[3,16,24,128]{3,2,1,0:T(8,128)(2,1)S(1)}, u32[]{:S(2)}, u32[]{:S(2)}) collective-permute-start(bf16[3,16,24,128]{3,2,1,0:T(8,128)(2,1)S(1)} %pad_maximum_fusion.2), channel_id=1, source_target_pairs={{0,2},{2,0},{1,3},{3,1},{4,6},{6,4},{5,7},{7,5},{8,10},{10,8},{9,1... | collective-permute-start | bytes 884744 | tf_op jit(solution)/shard_map/ppermute | solution.py:439
  80.6 3.9 %collective-permute-done.28 = bf16[2,16,24,128]{3,2,1,0:T(8,128)(2,1)S(1)} collective-permute-done((bf16[2,16,24,128]{3,2,1,0:T(8,128)(2,1)S(1)}, bf16[2,16,24,128]{3,2,1,0:T(8,128)(2,1)S(1)}, u32[]{:S(2)}, u32[]{:S(2)}) %collective-permute-start.28) | collective-permute-done | bytes 196640 | tf_op jit(solution)/shard_map/ppermute | solution.py:434
  84.5 0.1 add_convert_fusion.refs_7_
  84.6 1.7 %collective-permute-start.34 = (bf16[2,16,24,128]{3,2,1,0:T(8,128)(2,1)S(1)}, bf16[2,16,24,128]{3,2,1,0:T(8,128)(2,1)S(1)}, u32[]{:S(2)}, u32[]{:S(2)}) collective-permute-start(bf16[2,16,24,128]{3,2,1,0:T(8,128)(2,1)S(1)} %pad_maximum_fusion.12), channel_id=1, source_target_pairs={{0,2},{2,0},{1,3},{3,1},{4,6},{6,4},{5,7},{7,5},{8,10},{10,8},{9,1... | collective-permute-start | bytes 589832 | tf_op jit(solution)/shard_map/ppermute | solution.py:439
  86.3 0.5 collective-permute-start.32
  86.8 1.7 %collective-permute-done.33.refs_0_ = bf16[3,16,24,128]{3,2,1,0:T(8,128)(2,1)S(1)} collective-permute-done((bf16[3,16,24,128]{3,2,1,0:T(8,128)(2,1)S(1)}, bf16[3,16,24,128]{3,2,1,0:T(8,128)(2,1)S(1)}, u32[]{:S(2)}, u32[]{:S(2)}) %collective-permute-start.33) | collective-permute-done | bytes 294944 | tf_op jit(solution)/shard_map/ppermute | solution.py:439
  88.5 0.8 unpack_panels.5.refs_1_.refs_15_
  89.4 1.0 unpack_panels.6
  90.3 1.0 unpack_panels.7
  91.3 0.9 unpack_panels.8
  92.3 0.6 collective-permute-start.36
  92.8 1.1 %collective-permute-done.36.refs_3_.refs_5_ = bf16[2,16,24,128]{3,2,1,0:T(8,128)(2,1)S(1)} collective-permute-done((bf16[2,16,24,128]{3,2,1,0:T(8,128)(2,1)S(1)}, bf16[2,16,24,128]{3,2,1,0:T(8,128)(2,1)S(1)}, u32[]{:S(2)}, u32[]{:S(2)}) %collective-permute-start.36) | collective-permute-done | bytes 196640 | tf_op jit(solution)/shard_map/ppermute | solution.py:431
  93.9 0.9 unpack_panels.9
  94.8 4.8 %gradient.1 = bf16[64,3,128,128]{3,2,1,0:T(8,128)(2,1)} custom-call(s32[2]{0:T(128)S(1)} %pad_add_fusion.meta, s32[3,64]{1,0:T(4,128)S(1)} %bitcast.25, bf16[256,16,128]{2,1,0:T(8,128)(2,1)S(1)} %get-tuple-element.45.refs_0_.refs_14_, bf16[256,16,128]{2,1,0:T(8,128)(2,1)S(1)} %unpack_panels.5.refs_1_.refs_15_, ...), custom_call_target="tpu_custom_call" | custom-call | tf_op jit(solution)/shard_map/gradient/pallas_call | solution.py:398
  (58 shorter events, 0.8 us)
Async XLA Ops:
  0.1 0.7 copy-start
  8.1 2.0 %collective-permute-start = (bf16[5,16,24,128]{3,2,1,0:T(8,128)(2,1)S(1)}, bf16[5,16,24,128]{3,2,1,0:T(8,128)(2,1)S(1)}, u32[]{:S(2)}, u32[]{:S(2)}) collective-permute-start(bf16[5,16,24,128]{3,2,1,0:T(8,128)(2,1)S(1)} %get-tuple-element.49), channel_id=1, source_target_pairs={{0,1},{1,0},{2,3},{3,2},{4,5},{5,4},{6,7},{7,6},{8,9},{9,8},{10,11... | collective-permute-start | bytes 1474568 | tf_op jit(solution)/shard_map/ppermute | solution.py:431
  10.2 22.2 %collective-permute-start.11 = (bf16[32,3,128,128]{3,2,1,0:T(8,128)(2,1)S(1)}, bf16[32,3,128,128]{3,2,1,0:T(8,128)(2,1)S(1)}, u32[]{:S(2)}, u32[]{:S(2)}) collective-permute-start(bf16[32,3,128,128]{3,2,1,0:T(8,128)(2,1)S(1)} %get-tuple-element.57), channel_id=1, source_target_pairs={{0,1},{1,0},{2,3},{3,2},{4,5},{5,4},{6,7},{7,6},{8,9},{9,8},{10,11... | collective-permute-start | bytes 9437192 | tf_op jit(solution)/shard_map/ppermute | solution.py:431
  10.7 10.3 %collective-permute-start.2 = (bf16[2,16,24,128]{3,2,1,0:T(8,128)(2,1)S(1)}, bf16[2,16,24,128]{3,2,1,0:T(8,128)(2,1)S(1)}, u32[]{:S(2)}, u32[]{:S(2)}) collective-permute-start(bf16[2,16,24,128]{3,2,1,0:T(8,128)(2,1)S(1)} %pad_maximum_fusion.3), channel_id=1, source_target_pairs={{0,4},{4,0},{8,12},{12,8},{1,5},{5,1},{9,13},{13,9},{2,6},{6,2},{1... | collective-permute-start | bytes 589832 | tf_op jit(solution)/shard_map/ppermute | solution.py:434
  13.5 2.8 %collective-permute-start.5 = (bf16[1,16,24,128]{3,2,1,0:T(8,128)(2,1)S(1)}, bf16[1,16,24,128]{3,2,1,0:T(8,128)(2,1)S(1)}, u32[]{:S(2)}, u32[]{:S(2)}) collective-permute-start(bf16[1,16,24,128]{3,2,1,0:T(8,128)(2,1)S(1)} %get-tuple-element.90.rest_0_), channel_id=1, source_target_pairs={{0,1},{1,0},{2,3},{3,2},{4,5},{5,4},{6,7},{7,6},{8,9},{9,8},{10,11... | collective-permute-start | bytes 294920 | tf_op jit(solution)/shard_map/ppermute | solution.py:431
  13.6 6.7 %collective-permute-start.4 = (bf16[1,16,24,128]{3,2,1,0:T(8,128)(2,1)S(1)}, bf16[1,16,24,128]{3,2,1,0:T(8,128)(2,1)S(1)}, u32[]{:S(2)}, u32[]{:S(2)}) collective-permute-start(bf16[1,16,24,128]{3,2,1,0:T(8,128)(2,1)S(1)} %get-tuple-element.90.rest_0_), channel_id=1, source_target_pairs={{0,8},{4,12},{8,0},{12,4},{1,9},{5,13},{9,1},{13,5},{2,10},{6,14},... | collective-permute-start | bytes 294920 | tf_op jit(solution)/shard_map/ppermute | solution.py:434
  16.2 16.3 %collective-permute-start.10 = (s32[3,64]{1,0:T(4,128)S(1)}, s32[3,64]{1,0:T(4,128)S(1)}, u32[]{:S(2)}, u32[]{:S(2)}) collective-permute-start(s32[3,64]{1,0:T(4,128)S(1)} %bitcast.20), channel_id=1, source_target_pairs={{0,1},{1,0},{2,3},{3,2},{4,5},{5,4},{6,7},{7,6},{8,9},{9,8},{10,11... | collective-permute-start | bytes 2312 | tf_op jit(solution)/shard_map/ppermute | solution.py:431
  16.3 12.0 %collective-permute-start.1 = (bf16[4,16,24,128]{3,2,1,0:T(8,128)(2,1)S(1)}, bf16[4,16,24,128]{3,2,1,0:T(8,128)(2,1)S(1)}, u32[]{:S(2)}, u32[]{:S(2)}) collective-permute-start(bf16[4,16,24,128]{3,2,1,0:T(8,128)(2,1)S(1)} %get-tuple-element.50), channel_id=1, source_target_pairs={{0,2},{2,0},{1,3},{3,1},{4,6},{6,4},{5,7},{7,5},{8,10},{10,8},{9,1... | collective-permute-start | bytes 1179656 | tf_op jit(solution)/shard_map/ppermute | solution.py:439
  21.1 11.2 %collective-permute-start.8 = (bf16[1,16,24,128]{3,2,1,0:T(8,128)(2,1)S(1)}, bf16[1,16,24,128]{3,2,1,0:T(8,128)(2,1)S(1)}, u32[]{:S(2)}, u32[]{:S(2)}) collective-permute-start(bf16[1,16,24,128]{3,2,1,0:T(8,128)(2,1)S(1)} %get-tuple-element.91), channel_id=1, source_target_pairs={{0,8},{4,12},{8,0},{12,4},{1,9},{5,13},{9,1},{13,5},{2,10},{6,14},... | collective-permute-start | bytes 294920 | tf_op jit(solution)/shard_map/ppermute | solution.py:434
  23.8 7.1 %collective-permute-start.6 = (bf16[2,16,24,128]{3,2,1,0:T(8,128)(2,1)S(1)}, bf16[2,16,24,128]{3,2,1,0:T(8,128)(2,1)S(1)}, u32[]{:S(2)}, u32[]{:S(2)}) collective-permute-start(bf16[2,16,24,128]{3,2,1,0:T(8,128)(2,1)S(1)} %pad_maximum_fusion.4), channel_id=1, source_target_pairs={{0,4},{4,0},{8,12},{12,8},{1,5},{5,1},{9,13},{13,9},{2,6},{6,2},{1... | collective-permute-start | bytes 589832 | tf_op jit(solution)/shard_map/ppermute | solution.py:434
  28.3 4.0 %collective-permute-start.3 = (bf16[4,16,24,128]{3,2,1,0:T(8,128)(2,1)S(1)}, bf16[4,16,24,128]{3,2,1,0:T(8,128)(2,1)S(1)}, u32[]{:S(2)}, u32[]{:S(2)}) collective-permute-start(bf16[4,16,24,128]{3,2,1,0:T(8,128)(2,1)S(1)} %collective-permute-done.1.refs_0_), channel_id=1, source_target_pairs={{0,1},{1,0},{2,3},{3,2},{4,5},{5,4},{6,7},{7,6},{8,9},{9,8},{10,11... | collective-permute-start | bytes 1179656 | tf_op jit(solution)/shard_map/ppermute | solution.py:431
  30.9 1.4 %collective-permute-start.7 = (bf16[2,16,24,128]{3,2,1,0:T(8,128)(2,1)S(1)}, bf16[2,16,24,128]{3,2,1,0:T(8,128)(2,1)S(1)}, u32[]{:S(2)}, u32[]{:S(2)}) collective-permute-start(bf16[2,16,24,128]{3,2,1,0:T(8,128)(2,1)S(1)} %pad_maximum_fusion.5), channel_id=1, source_target_pairs={{0,1},{1,0},{2,3},{3,2},{4,5},{5,4},{6,7},{7,6},{8,9},{9,8},{10,11... | collective-permute-start | bytes 589832 | tf_op jit(solution)/shard_map/ppermute | solution.py:431
  32.5 4.4 %copy-start.1 = (s32[64,3]{0,1:T(4,128)S(1)}, s32[64,3]{0,1:T(4,128)}, u32[]{:S(2)}) copy-start(s32[64,3]{0,1:T(4,128)} %param.4) | copy-start | bytes 2308
  34.7 5.0 %collective-permute-start.13 = (bf16[4,16,24,128]{3,2,1,0:T(8,128)(2,1)S(1)}, bf16[4,16,24,128]{3,2,1,0:T(8,128)(2,1)S(1)}, u32[]{:S(2)}, u32[]{:S(2)}) collective-permute-start(bf16[4,16,24,128]{3,2,1,0:T(8,128)(2,1)S(1)} %get-tuple-element.58.rest_7_), channel_id=1, source_target_pairs={{0,1},{1,0},{2,3},{3,2},{4,5},{5,4},{6,7},{7,6},{8,9},{9,8},{10,11... | collective-permute-start | bytes 1179656 | tf_op jit(solution)/shard_map/ppermute | solution.py:431
  34.9 2.0 %collective-permute-start.12 = (bf16[1,16,24,128]{3,2,1,0:T(8,128)(2,1)S(1)}, bf16[1,16,24,128]{3,2,1,0:T(8,128)(2,1)S(1)}, u32[]{:S(2)}, u32[]{:S(2)}) collective-permute-start(bf16[1,16,24,128]{3,2,1,0:T(8,128)(2,1)S(1)} %get-tuple-element.101.rest_3_), channel_id=1, source_target_pairs={{0,1},{1,0},{2,3},{3,2},{4,5},{5,4},{6,7},{7,6},{8,9},{9,8},{10,11... | collective-permute-start | bytes 294920 | tf_op jit(solution)/shard_map/ppermute | solution.py:431
  35.2 13.3 %collective-permute-start.9 = (bf16[5,16,24,128]{3,2,1,0:T(8,128)(2,1)S(1)}, bf16[5,16,24,128]{3,2,1,0:T(8,128)(2,1)S(1)}, u32[]{:S(2)}, u32[]{:S(2)}) collective-permute-start(bf16[5,16,24,128]{3,2,1,0:T(8,128)(2,1)S(1)} %get-tuple-element.87), channel_id=1, source_target_pairs={{0,2},{2,0},{1,3},{3,1},{4,6},{6,4},{5,7},{7,5},{8,10},{10,8},{9,1... | collective-permute-start | bytes 1474568 | tf_op jit(solution)/shard_map/ppermute | solution.py:439
  39.7 8.8 %collective-permute-start.14 = (bf16[2,16,24,128]{3,2,1,0:T(8,128)(2,1)S(1)}, bf16[2,16,24,128]{3,2,1,0:T(8,128)(2,1)S(1)}, u32[]{:S(2)}, u32[]{:S(2)}) collective-permute-start(bf16[2,16,24,128]{3,2,1,0:T(8,128)(2,1)S(1)} %pad_maximum_fusion.6), channel_id=1, source_target_pairs={{0,4},{4,0},{8,12},{12,8},{1,5},{5,1},{9,13},{13,9},{2,6},{6,2},{1... | collective-permute-start | bytes 589832 | tf_op jit(solution)/shard_map/ppermute | solution.py:434
  41.4 2.5 %collective-permute-start.17 = (bf16[1,16,24,128]{3,2,1,0:T(8,128)(2,1)S(1)}, bf16[1,16,24,128]{3,2,1,0:T(8,128)(2,1)S(1)}, u32[]{:S(2)}, u32[]{:S(2)}) collective-permute-start(bf16[1,16,24,128]{3,2,1,0:T(8,128)(2,1)S(1)} %get-tuple-element.59.rest_0_), channel_id=1, source_target_pairs={{0,1},{1,0},{2,3},{3,2},{4,5},{5,4},{6,7},{7,6},{8,9},{9,8},{10,11... | collective-permute-start | bytes 294920 | tf_op jit(solution)/shard_map/ppermute | solution.py:431
  41.4 6.4 %collective-permute-start.16 = (bf16[1,16,24,128]{3,2,1,0:T(8,128)(2,1)S(1)}, bf16[1,16,24,128]{3,2,1,0:T(8,128)(2,1)S(1)}, u32[]{:S(2)}, u32[]{:S(2)}) collective-permute-start(bf16[1,16,24,128]{3,2,1,0:T(8,128)(2,1)S(1)} %get-tuple-element.59.rest_0_), channel_id=1, source_target_pairs={{0,8},{4,12},{8,0},{12,4},{1,9},{5,13},{9,1},{13,5},{2,10},{6,14},... | collective-permute-start | bytes 294920 | tf_op jit(solution)/shard_map/ppermute | solution.py:434
  48.6 9.6 %collective-permute-start.20 = (bf16[1,16,24,128]{3,2,1,0:T(8,128)(2,1)S(1)}, bf16[1,16,24,128]{3,2,1,0:T(8,128)(2,1)S(1)}, u32[]{:S(2)}, u32[]{:S(2)}) collective-permute-start(bf16[1,16,24,128]{3,2,1,0:T(8,128)(2,1)S(1)} %get-tuple-element.95), channel_id=1, source_target_pairs={{0,8},{4,12},{8,0},{12,4},{1,9},{5,13},{9,1},{13,5},{2,10},{6,14},... | collective-permute-start | bytes 294920 | tf_op jit(solution)/shard_map/ppermute | solution.py:434
  51.4 6.8 %collective-permute-start.18 = (bf16[2,16,24,128]{3,2,1,0:T(8,128)(2,1)S(1)}, bf16[2,16,24,128]{3,2,1,0:T(8,128)(2,1)S(1)}, u32[]{:S(2)}, u32[]{:S(2)}) collective-permute-start(bf16[2,16,24,128]{3,2,1,0:T(8,128)(2,1)S(1)} %pad_maximum_fusion.7), channel_id=1, source_target_pairs={{0,4},{4,0},{8,12},{12,8},{1,5},{5,1},{9,13},{13,9},{2,6},{6,2},{1... | collective-permute-start | bytes 589832 | tf_op jit(solution)/shard_map/ppermute | solution.py:434
  53.0 5.2 %collective-permute-start.15 = (bf16[6,16,24,128]{3,2,1,0:T(8,128)(2,1)S(1)}, bf16[6,16,24,128]{3,2,1,0:T(8,128)(2,1)S(1)}, u32[]{:S(2)}, u32[]{:S(2)}) collective-permute-start(bf16[6,16,24,128]{3,2,1,0:T(8,128)(2,1)S(1)} %pad_maximum_fusion), channel_id=1, source_target_pairs={{0,1},{1,0},{2,3},{3,2},{4,5},{5,4},{6,7},{7,6},{8,9},{9,8},{10,11... | collective-permute-start | bytes 1769480 | tf_op jit(solution)/shard_map/ppermute | solution.py:431
  53.2 5.0 %collective-permute-start.19 = (bf16[2,16,24,128]{3,2,1,0:T(8,128)(2,1)S(1)}, bf16[2,16,24,128]{3,2,1,0:T(8,128)(2,1)S(1)}, u32[]{:S(2)}, u32[]{:S(2)}) collective-permute-start(bf16[2,16,24,128]{3,2,1,0:T(8,128)(2,1)S(1)} %pad_maximum_fusion.8), channel_id=1, source_target_pairs={{0,1},{1,0},{2,3},{3,2},{4,5},{5,4},{6,7},{7,6},{8,9},{9,8},{10,11... | collective-permute-start | bytes 589832 | tf_op jit(solution)/shard_map/ppermute | solution.py:431
  60.5 5.0 %collective-permute-start.23 = (bf16[4,16,24,128]{3,2,1,0:T(8,128)(2,1)S(1)}, bf16[4,16,24,128]{3,2,1,0:T(8,128)(2,1)S(1)}, u32[]{:S(2)}, u32[]{:S(2)}) collective-permute-start(bf16[4,16,24,128]{3,2,1,0:T(8,128)(2,1)S(1)} %get-tuple-element.67.rest_7_), channel_id=1, source_target_pairs={{0,1},{1,0},{2,3},{3,2},{4,5},{5,4},{6,7},{7,6},{8,9},{9,8},{10,11... | collective-permute-start | bytes 1179656 | tf_op jit(solution)/shard_map/ppermute | solution.py:431
  60.6 2.2 %collective-permute-start.22 = (bf16[1,16,24,128]{3,2,1,0:T(8,128)(2,1)S(1)}, bf16[1,16,24,128]{3,2,1,0:T(8,128)(2,1)S(1)}, u32[]{:S(2)}, u32[]{:S(2)}) collective-permute-start(bf16[1,16,24,128]{3,2,1,0:T(8,128)(2,1)S(1)} %get-tuple-element.97.rest_3_), channel_id=1, source_target_pairs={{0,1},{1,0},{2,3},{3,2},{4,5},{5,4},{6,7},{7,6},{8,9},{9,8},{10,11... | collective-permute-start | bytes 294920 | tf_op jit(solution)/shard_map/ppermute | solution.py:431
  61.1 13.3 %collective-permute-start.21 = (bf16[5,16,24,128]{3,2,1,0:T(8,128)(2,1)S(1)}, bf16[5,16,24,128]{3,2,1,0:T(8,128)(2,1)S(1)}, u32[]{:S(2)}, u32[]{:S(2)}) collective-permute-start(bf16[5,16,24,128]{3,2,1,0:T(8,128)(2,1)S(1)} %get-tuple-element.85), channel_id=1, source_target_pairs={{0,2},{2,0},{1,3},{3,1},{4,6},{6,4},{5,7},{7,5},{8,10},{10,8},{9,1... | collective-permute-start | bytes 1474568 | tf_op jit(solution)/shard_map/ppermute | solution.py:439
  65.6 8.8 %collective-permute-start.24 = (bf16[2,16,24,128]{3,2,1,0:T(8,128)(2,1)S(1)}, bf16[2,16,24,128]{3,2,1,0:T(8,128)(2,1)S(1)}, u32[]{:S(2)}, u32[]{:S(2)}) collective-permute-start(bf16[2,16,24,128]{3,2,1,0:T(8,128)(2,1)S(1)} %pad_maximum_fusion.9), channel_id=1, source_target_pairs={{0,4},{4,0},{8,12},{12,8},{1,5},{5,1},{9,13},{13,9},{2,6},{6,2},{1... | collective-permute-start | bytes 589832 | tf_op jit(solution)/shard_map/ppermute | solution.py:434
  67.2 2.3 %collective-permute-start.27 = (bf16[1,16,24,128]{3,2,1,0:T(8,128)(2,1)S(1)}, bf16[1,16,24,128]{3,2,1,0:T(8,128)(2,1)S(1)}, u32[]{:S(2)}, u32[]{:S(2)}) collective-permute-start(bf16[1,16,24,128]{3,2,1,0:T(8,128)(2,1)S(1)} %get-tuple-element.68.refs_0_), channel_id=1, source_target_pairs={{0,1},{1,0},{2,3},{3,2},{4,5},{5,4},{6,7},{7,6},{8,9},{9,8},{10,11... | collective-permute-start | bytes 294920 | tf_op jit(solution)/shard_map/ppermute | solution.py:431
  67.2 6.8 %collective-permute-start.26 = (bf16[1,16,24,128]{3,2,1,0:T(8,128)(2,1)S(1)}, bf16[1,16,24,128]{3,2,1,0:T(8,128)(2,1)S(1)}, u32[]{:S(2)}, u32[]{:S(2)}) collective-permute-start(bf16[1,16,24,128]{3,2,1,0:T(8,128)(2,1)S(1)} %get-tuple-element.68.refs_0_), channel_id=1, source_target_pairs={{0,8},{4,12},{8,0},{12,4},{1,9},{5,13},{9,1},{13,5},{2,10},{6,14},... | collective-permute-start | bytes 294920 | tf_op jit(solution)/shard_map/ppermute | solution.py:434
  74.4 10.0 %collective-permute-start.25 = (bf16[6,16,24,128]{3,2,1,0:T(8,128)(2,1)S(1)}, bf16[6,16,24,128]{3,2,1,0:T(8,128)(2,1)S(1)}, u32[]{:S(2)}, u32[]{:S(2)}) collective-permute-start(bf16[6,16,24,128]{3,2,1,0:T(8,128)(2,1)S(1)} %pad_maximum_fusion.1), channel_id=1, source_target_pairs={{0,1},{1,0},{2,3},{3,2},{4,5},{5,4},{6,7},{7,6},{8,9},{9,8},{10,11... | collective-permute-start | bytes 1769480 | tf_op jit(solution)/shard_map/ppermute | solution.py:431
  74.6 9.8 %collective-permute-start.28 = (bf16[2,16,24,128]{3,2,1,0:T(8,128)(2,1)S(1)}, bf16[2,16,24,128]{3,2,1,0:T(8,128)(2,1)S(1)}, u32[]{:S(2)}, u32[]{:S(2)}) collective-permute-start(bf16[2,16,24,128]{3,2,1,0:T(8,128)(2,1)S(1)} %pad_maximum_fusion.10), channel_id=1, source_target_pairs={{0,4},{4,0},{8,12},{12,8},{1,5},{5,1},{9,13},{13,9},{2,6},{6,2},{1... | collective-permute-start | bytes 589832 | tf_op jit(solution)/shard_map/ppermute | solution.py:434
  76.8 7.6 %collective-permute-start.29 = (bf16[2,16,24,128]{3,2,1,0:T(8,128)(2,1)S(1)}, bf16[2,16,24,128]{3,2,1,0:T(8,128)(2,1)S(1)}, u32[]{:S(2)}, u32[]{:S(2)}) collective-permute-start(bf16[2,16,24,128]{3,2,1,0:T(8,128)(2,1)S(1)} %pad_maximum_fusion.11), channel_id=1, source_target_pairs={{0,1},{1,0},{2,3},{3,2},{4,5},{5,4},{6,7},{7,6},{8,9},{9,8},{10,11... | collective-permute-start | bytes 589832 | tf_op jit(solution)/shard_map/ppermute | solution.py:431
  77.1 7.4 %collective-permute-start.31 = (bf16[1,16,24,128]{3,2,1,0:T(8,128)(2,1)S(1)}, bf16[1,16,24,128]{3,2,1,0:T(8,128)(2,1)S(1)}, u32[]{:S(2)}, u32[]{:S(2)}) collective-permute-start(bf16[1,16,24,128]{3,2,1,0:T(8,128)(2,1)S(1)} %get-tuple-element.93), channel_id=1, source_target_pairs={{0,8},{4,12},{8,0},{12,4},{1,9},{5,13},{9,1},{13,5},{2,10},{6,14},... | collective-permute-start | bytes 294920 | tf_op jit(solution)/shard_map/ppermute | solution.py:434
  78.9 9.6 %collective-permute-start.33 = (bf16[3,16,24,128]{3,2,1,0:T(8,128)(2,1)S(1)}, bf16[3,16,24,128]{3,2,1,0:T(8,128)(2,1)S(1)}, u32[]{:S(2)}, u32[]{:S(2)}) collective-permute-start(bf16[3,16,24,128]{3,2,1,0:T(8,128)(2,1)S(1)} %pad_maximum_fusion.2), channel_id=1, source_target_pairs={{0,2},{2,0},{1,3},{3,1},{4,6},{6,4},{5,7},{7,5},{8,10},{10,8},{9,1... | collective-permute-start | bytes 884744 | tf_op jit(solution)/shard_map/ppermute | solution.py:439
  84.6 7.6 %collective-permute-start.34 = (bf16[2,16,24,128]{3,2,1,0:T(8,128)(2,1)S(1)}, bf16[2,16,24,128]{3,2,1,0:T(8,128)(2,1)S(1)}, u32[]{:S(2)}, u32[]{:S(2)}) collective-permute-start(bf16[2,16,24,128]{3,2,1,0:T(8,128)(2,1)S(1)} %pad_maximum_fusion.12), channel_id=1, source_target_pairs={{0,2},{2,0},{1,3},{3,1},{4,6},{6,4},{5,7},{7,5},{8,10},{10,8},{9,1... | collective-permute-start | bytes 589832 | tf_op jit(solution)/shard_map/ppermute | solution.py:439
  86.3 5.0 %collective-permute-start.30 = (bf16[1,16,24,128]{3,2,1,0:T(8,128)(2,1)S(1)}, bf16[1,16,24,128]{3,2,1,0:T(8,128)(2,1)S(1)}, u32[]{:S(2)}, u32[]{:S(2)}) collective-permute-start(bf16[1,16,24,128]{3,2,1,0:T(8,128)(2,1)S(1)} %slice.168.refs_3_), channel_id=1, source_target_pairs={{0,1},{1,0},{2,3},{3,2},{4,5},{5,4},{6,7},{7,6},{8,9},{9,8},{10,11... | collective-permute-start | bytes 294920 | tf_op jit(solution)/shard_map/ppermute | solution.py:431
  86.3 5.0 %collective-permute-start.32 = (bf16[1,16,24,128]{3,2,1,0:T(8,128)(2,1)S(1)}, bf16[1,16,24,128]{3,2,1,0:T(8,128)(2,1)S(1)}, u32[]{:S(2)}, u32[]{:S(2)}) collective-permute-start(bf16[1,16,24,128]{3,2,1,0:T(8,128)(2,1)S(1)} %add_convert_fusion.refs_7_), channel_id=1, source_target_pairs={{0,1},{1,0},{2,3},{3,2},{4,5},{5,4},{6,7},{7,6},{8,9},{9,8},{10,11... | collective-permute-start | bytes 294920 | tf_op jit(solution)/shard_map/ppermute | solution.py:431
  88.5 4.3 %collective-permute-start.35 = (bf16[3,16,24,128]{3,2,1,0:T(8,128)(2,1)S(1)}, bf16[3,16,24,128]{3,2,1,0:T(8,128)(2,1)S(1)}, u32[]{:S(2)}, u32[]{:S(2)}) collective-permute-start(bf16[3,16,24,128]{3,2,1,0:T(8,128)(2,1)S(1)} %collective-permute-done.33.refs_0_), channel_id=1, source_target_pairs={{0,1},{1,0},{2,3},{3,2},{4,5},{5,4},{6,7},{7,6},{8,9},{9,8},{10,11... | collective-permute-start | bytes 884744 | tf_op jit(solution)/shard_map/ppermute | solution.py:431
  92.3 1.6 %collective-permute-start.36 = (bf16[2,16,24,128]{3,2,1,0:T(8,128)(2,1)S(1)}, bf16[2,16,24,128]{3,2,1,0:T(8,128)(2,1)S(1)}, u32[]{:S(2)}, u32[]{:S(2)}) collective-permute-start(bf16[2,16,24,128]{3,2,1,0:T(8,128)(2,1)S(1)} %collective-permute-done.34.refs_1_.refs_4_), channel_id=1, source_target_pairs={{0,1},{1,0},{2,3},{3,2},{4,5},{5,4},{6,7},{7,6},{8,9},{9,8},{10,11... | collective-permute-start | bytes 589832 | tf_op jit(solution)/shard_map/ppermute | solution.py:431

commit v6 on v5

--- a/solution.py
+++ b/solution.py
@@ -426,6 +426,7 @@
     signs = pltpu.with_memory_space_constraint(signs, pltpu.HBM)
     block_values = pltpu.with_memory_space_constraint(block_values, pltpu.HBM)
     cols = columns.T
+    cols_hbm = pltpu.with_memory_space_constraint(cols, pltpu.HBM)
 
     def swap_rep(x):
         return lax.ppermute(x, "rep", [(0, 1), (1, 0)])
@@ -500,7 +501,7 @@
         return swapped, entries, offset
 
     panel, sent, left_own, kept, near_blocks, far_blocks, keep, send = first_step(
-        meta, cols, signs, block_values, blocks
+        meta, cols_hbm, signs, block_values, blocks
     )
     received = swap_rep(send)
     updated = narrow(wide(left_own) + inverse * (kept + wide(received[n_var]))[None])
@@ -527,7 +528,7 @@
             summed = parts[0] + wide(final[1:]) + wide(crossed)
             held = [updated, near, far, last]
             others = [(own_other, [0]), (middle_other, [1, 2]), (swap_rep(last), [3])]
-            window, settled = [both], [middle_other]
+            window, settled = [both], [middle_other] if step > 0 else []
         else:
             bits = [1 << i for i in range(n_var.bit_length() - 1)]
             found = {0: updated}

time: 99.8 us -> 98.7 us (0.989)
  starting transfers between devices: 39.8 us -> 37.4 us
  waiting for transfers between devices: 30.9 us -> 32.5 us
    ppermute x12, waiting for transfers between devices: 22.4 us -> 26 us  [shift_var(): return lax.ppermute(x, 'var', [(i, i ^ bit) for i in range(n_var)])]
    ppermute x5, starting transfers between devices: 9.29 us -> 7.53 us  [from_probes(): lax.ppermute(x, 'probe', [(i, (i + d) % n_probe) for i in range(n_probe)])]
    ppermute x20, waiting for transfers between devices: 4.03 us -> 2.63 us  [swap_rep(): return lax.ppermute(x, 'rep', [(0, 1), (1, 0)])]
  transfers between devices with their start and end apart: 37 -> 37, of which waited for: 14 -> 13; matrix products, arithmetic and copies ran while one was open for 1% -> 1% of each run, Pallas kernels for 9% -> 9%
where the time goes in v6:
time: 98.7 us; the launch traced here: 98.6 us
  starting transfers between devices  37.4 us (38%)
  waiting for transfers between devices  32.5 us (33%)
  Pallas kernels  27 us (27%)
  other arithmetic  1.05 us (1%)
    ppermute x12, waiting for transfers between devices, shift_var(): return lax.ppermute(x, 'var', [(i, i ^ bit) for i in range(n_var)])  26 us
    ppermute x12, starting transfers between devices, shift_var(): return lax.ppermute(x, 'var', [(i, i ^ bit) for i in range(n_var)])  25.5 us
    pallas_call x1, Pallas kernels, first_step(): pl.pallas_call(functools.partial(first_kernel, count, chunk, blocks), out...  7.66 us
    ppermute x5, starting transfers between devices, from_probes(): lax.ppermute(x, 'probe', [(i, (i + d) % n_probe) for i in range(n_probe)])  7.53 us
    pallas_call x2, Pallas kernels, forward(): pl.pallas_call(functools.partial(forward_kernel, count, chunk, 2 * half,...  5.53 us
    pallas_call x1, Pallas kernels, gradient(): pl.pallas_call(functools.partial(gradient_kernel, scale, chunk, rows, len...  4.77 us
    pallas_call x5, Pallas kernels, unpack(): pl.pallas_call(functools.partial(unpack_kernel, count, wheres, len(tokens...  4.59 us
    pallas_call x2, Pallas kernels, backward(): pl.pallas_call(functools.partial(backward_kernel, count, chunk), out_shap...  4.44 us
  transfers between devices with their start and end apart: 37, of which 13 were waited for; matrix products, arithmetic and copies ran while one was open for 1% of the time, Pallas kernels for 9%

profile of v6, /device:TPU:0, one launch (start us, length us, event | category | flops | bytes accessed | tf_op | source)
XLA Modules:
  0.0 98.6 jit_solution(14455747380186607428)
XLA Ops:
  0.0 0.1 pad_add_fusion.meta
  0.1 7.7 %first_step.1 = (bf16[256,16,128]{2,1,0:T(8,128)(2,1)S(1)}, bf16[4,16,24,128]{3,2,1,0:T(8,128)(2,1)S(1)}, bf16[1,16,24,128]{3,2,1,0:T(8,128)(2,1)S(1)}, f32[16,2...) custom-call(s32[2]{0:T(128)S(1)} %pad_add_fusion.meta, ...), custom_call_target="tpu_custom_call" | custom-call | flops 1610612736 | bytes 50331648 | tf_op jit(solution)/shard_map/first_step/pallas_call | solution.py:197
  7.7 0.5 collective-permute-start
  8.3 1.5 %collective-permute-done = bf16[5,16,24,128]{3,2,1,0:T(8,128)(2,1)S(1)} collective-permute-done((bf16[5,16,24,128]{3,2,1,0:T(8,128)(2,1)S(1)}, bf16[5,16,24,128]{3,2,1,0:T(8,128)(2,1)S(1)}, u32[]{:S(2)}, u32[]{:S(2)}) %collective-permute-start) | collective-permute-done | bytes 491552 | tf_op jit(solution)/shard_map/ppermute | solution.py:432
  9.8 0.4 collective-permute-start.10
  10.3 2.8 %collective-permute-start.2 = (bf16[2,16,24,128]{3,2,1,0:T(8,128)(2,1)S(1)}, bf16[2,16,24,128]{3,2,1,0:T(8,128)(2,1)S(1)}, u32[]{:S(2)}, u32[]{:S(2)}) collective-permute-start(bf16[2,16,24,128]{3,2,1,0:T(8,128)(2,1)S(1)} %pad_maximum_fusion.3), channel_id=1, source_target_pairs={{0,4},{4,0},{8,12},{12,8},{1,5},{5,1},{9,13},{13,9},{2,6},{6,2},{1... | collective-permute-start | bytes 589832 | tf_op jit(solution)/shard_map/ppermute | solution.py:435
  13.1 0.1 collective-permute-start.5
  13.2 2.6 %collective-permute-start.4 = (bf16[1,16,24,128]{3,2,1,0:T(8,128)(2,1)S(1)}, bf16[1,16,24,128]{3,2,1,0:T(8,128)(2,1)S(1)}, u32[]{:S(2)}, u32[]{:S(2)}) collective-permute-start(bf16[1,16,24,128]{3,2,1,0:T(8,128)(2,1)S(1)} %get-tuple-element.90.rest_0_), channel_id=1, source_target_pairs={{0,8},{4,12},{8,0},{12,4},{1,9},{5,13},{9,1},{13,5},{2,10},{6,14},... | collective-permute-start | bytes 294920 | tf_op jit(solution)/shard_map/ppermute | solution.py:435
  15.8 1.5 %collective-permute-start.1 = (bf16[4,16,24,128]{3,2,1,0:T(8,128)(2,1)S(1)}, bf16[4,16,24,128]{3,2,1,0:T(8,128)(2,1)S(1)}, u32[]{:S(2)}, u32[]{:S(2)}) collective-permute-start(bf16[4,16,24,128]{3,2,1,0:T(8,128)(2,1)S(1)} %get-tuple-element.50), channel_id=1, source_target_pairs={{0,2},{2,0},{1,3},{3,1},{4,6},{6,4},{5,7},{7,5},{8,10},{10,8},{9,1... | collective-permute-start | bytes 1179656 | tf_op jit(solution)/shard_map/ppermute | solution.py:440
  17.3 2.6 %collective-permute-done.4.rest_2_ = bf16[1,16,24,128]{3,2,1,0:T(8,128)(2,1)S(1)} collective-permute-done((bf16[1,16,24,128]{3,2,1,0:T(8,128)(2,1)S(1)}, bf16[1,16,24,128]{3,2,1,0:T(8,128)(2,1)S(1)}, u32[]{:S(2)}, u32[]{:S(2)}) %collective-permute-start.4) | collective-permute-done | bytes 98336 | tf_op jit(solution)/shard_map/ppermute | solution.py:435
  19.9 0.7 collective-permute-done.2
  20.6 0.1 add_convert_fusion.9
  20.7 2.7 %collective-permute-start.7 = (bf16[1,16,24,128]{3,2,1,0:T(8,128)(2,1)S(1)}, bf16[1,16,24,128]{3,2,1,0:T(8,128)(2,1)S(1)}, u32[]{:S(2)}, u32[]{:S(2)}) collective-permute-start(bf16[1,16,24,128]{3,2,1,0:T(8,128)(2,1)S(1)} %get-tuple-element.91), channel_id=1, source_target_pairs={{0,8},{4,12},{8,0},{12,4},{1,9},{5,13},{9,1},{13,5},{2,10},{6,14},... | collective-permute-start | bytes 294920 | tf_op jit(solution)/shard_map/ppermute | solution.py:435
  23.4 1.7 %collective-permute-start.6 = (bf16[2,16,24,128]{3,2,1,0:T(8,128)(2,1)S(1)}, bf16[2,16,24,128]{3,2,1,0:T(8,128)(2,1)S(1)}, u32[]{:S(2)}, u32[]{:S(2)}) collective-permute-start(bf16[2,16,24,128]{3,2,1,0:T(8,128)(2,1)S(1)} %pad_maximum_fusion.4), channel_id=1, source_target_pairs={{0,4},{4,0},{8,12},{12,8},{1,5},{5,1},{9,13},{13,9},{2,6},{6,2},{1... | collective-permute-start | bytes 589832 | tf_op jit(solution)/shard_map/ppermute | solution.py:435
  25.2 1.8 %collective-permute-done.1.refs_0_ = bf16[4,16,24,128]{3,2,1,0:T(8,128)(2,1)S(1)} collective-permute-done((bf16[4,16,24,128]{3,2,1,0:T(8,128)(2,1)S(1)}, bf16[4,16,24,128]{3,2,1,0:T(8,128)(2,1)S(1)}, u32[]{:S(2)}, u32[]{:S(2)}) %collective-permute-start.1) | collective-permute-done | bytes 393248 | tf_op jit(solution)/shard_map/ppermute | solution.py:440
  27.0 3.5 %collective-permute-done.6 = bf16[2,16,24,128]{3,2,1,0:T(8,128)(2,1)S(1)} collective-permute-done((bf16[2,16,24,128]{3,2,1,0:T(8,128)(2,1)S(1)}, bf16[2,16,24,128]{3,2,1,0:T(8,128)(2,1)S(1)}, u32[]{:S(2)}, u32[]{:S(2)}) %collective-permute-start.6) | collective-permute-done | bytes 196640 | tf_op jit(solution)/shard_map/ppermute | solution.py:435
  30.5 0.1 constant_dynamic-update-slice_fusion
  30.7 2.2 %backward_step.2 = (bf16[4,16,24,128]{3,2,1,0:T(8,128)(2,1)S(1)}, bf16[4,16,24,128]{3,2,1,0:T(8,128)(2,1)S(1)}) custom-call(s32[2]{0:T(128)S(1)} %pad_add_fusion.meta, s32[3,64]{1,0:T(4,128)S(1)} %bitcast.21, s32[3,64]{1,0:T(4,128)S(1)} %collective-permute-done.9.cols_other, bf16[32,3,128,128]{3,2,1,0:T(8,128)(2,1)S(1)} %get-tuple-element.55.own, ...), custom_call_target="tpu_custom_call" | custom-call | flops 805306368 | bytes 25165824 | tf_op jit(solution)/shard_map/backward_step/pallas_call | solution.py:352
  32.9 0.1 collective-permute-start.13
  33.0 0.6 collective-permute-start.11
  33.6 0.1 collective-permute-start.12
  33.6 1.6 %collective-permute-start.8 = (bf16[5,16,24,128]{3,2,1,0:T(8,128)(2,1)S(1)}, bf16[5,16,24,128]{3,2,1,0:T(8,128)(2,1)S(1)}, u32[]{:S(2)}, u32[]{:S(2)}) collective-permute-start(bf16[5,16,24,128]{3,2,1,0:T(8,128)(2,1)S(1)} %get-tuple-element.87), channel_id=1, source_target_pairs={{0,2},{2,0},{1,3},{3,1},{4,6},{6,4},{5,7},{7,5},{8,10},{10,8},{9,1... | collective-permute-start | bytes 1474568 | tf_op jit(solution)/shard_map/ppermute | solution.py:440
  35.3 2.8 %forward_step.2 = (bf16[256,16,128]{2,1,0:T(8,128)(2,1)S(1)}, bf16[1,16,24,128]{3,2,1,0:T(8,128)(2,1)S(1)}) custom-call(s32[2]{0:T(128)S(1)} %pad_add_fusion.meta, s32[3,64]{1,0:T(4,128)S(1)} %bitcast.22, s32[3,64]{1,0:T(4,128)S(1)} %collective-permute-done.9.cols_other, bf16[32,3,128,128]{3,2,1,0:T(8,128)(2,1)S(1)} %get-tuple-element.55.own, ...), custom_call_target="tpu_custom_call" | custom-call | flops 805306368 | bytes 25165824 | tf_op jit(solution)/shard_map/forward_step/pallas_call | solution.py:270
  38.1 1.7 %collective-permute-start.14 = (bf16[2,16,24,128]{3,2,1,0:T(8,128)(2,1)S(1)}, bf16[2,16,24,128]{3,2,1,0:T(8,128)(2,1)S(1)}, u32[]{:S(2)}, u32[]{:S(2)}) collective-permute-start(bf16[2,16,24,128]{3,2,1,0:T(8,128)(2,1)S(1)} %pad_maximum_fusion.6), channel_id=1, source_target_pairs={{0,4},{4,0},{8,12},{12,8},{1,5},{5,1},{9,13},{13,9},{2,6},{6,2},{1... | collective-permute-start | bytes 589832 | tf_op jit(solution)/shard_map/ppermute | solution.py:435
  39.8 2.5 %collective-permute-start.16 = (bf16[1,16,24,128]{3,2,1,0:T(8,128)(2,1)S(1)}, bf16[1,16,24,128]{3,2,1,0:T(8,128)(2,1)S(1)}, u32[]{:S(2)}, u32[]{:S(2)}) collective-permute-start(bf16[1,16,24,128]{3,2,1,0:T(8,128)(2,1)S(1)} %get-tuple-element.59.rest_0_), channel_id=1, source_target_pairs={{0,8},{4,12},{8,0},{12,4},{1,9},{5,13},{9,1},{13,5},{2,10},{6,14},... | collective-permute-start | bytes 294920 | tf_op jit(solution)/shard_map/ppermute | solution.py:435
  42.3 4.1 %collective-permute-done.16.rest_2_ = bf16[1,16,24,128]{3,2,1,0:T(8,128)(2,1)S(1)} collective-permute-done((bf16[1,16,24,128]{3,2,1,0:T(8,128)(2,1)S(1)}, bf16[1,16,24,128]{3,2,1,0:T(8,128)(2,1)S(1)}, u32[]{:S(2)}, u32[]{:S(2)}) %collective-permute-start.16) | collective-permute-done | bytes 98336 | tf_op jit(solution)/shard_map/ppermute | solution.py:435
  46.4 0.9 collective-permute-done.14
  47.3 0.1 add_convert_fusion.5
  47.3 2.6 %collective-permute-start.20 = (bf16[1,16,24,128]{3,2,1,0:T(8,128)(2,1)S(1)}, bf16[1,16,24,128]{3,2,1,0:T(8,128)(2,1)S(1)}, u32[]{:S(2)}, u32[]{:S(2)}) collective-permute-start(bf16[1,16,24,128]{3,2,1,0:T(8,128)(2,1)S(1)} %get-tuple-element.95), channel_id=1, source_target_pairs={{0,8},{4,12},{8,0},{12,4},{1,9},{5,13},{9,1},{13,5},{2,10},{6,14},... | collective-permute-start | bytes 294920 | tf_op jit(solution)/shard_map/ppermute | solution.py:435
  49.9 1.7 %collective-permute-start.18 = (bf16[2,16,24,128]{3,2,1,0:T(8,128)(2,1)S(1)}, bf16[2,16,24,128]{3,2,1,0:T(8,128)(2,1)S(1)}, u32[]{:S(2)}, u32[]{:S(2)}) collective-permute-start(bf16[2,16,24,128]{3,2,1,0:T(8,128)(2,1)S(1)} %pad_maximum_fusion.7), channel_id=1, source_target_pairs={{0,4},{4,0},{8,12},{12,8},{1,5},{5,1},{9,13},{13,9},{2,6},{6,2},{1... | collective-permute-start | bytes 589832 | tf_op jit(solution)/shard_map/ppermute | solution.py:435
  51.6 0.1 pad_maximum_fusion
  51.7 0.1 collective-permute-start.15
  51.8 0.6 collective-permute-start.19
  52.4 4.7 %collective-permute-done.18 = bf16[2,16,24,128]{3,2,1,0:T(8,128)(2,1)S(1)} collective-permute-done((bf16[2,16,24,128]{3,2,1,0:T(8,128)(2,1)S(1)}, bf16[2,16,24,128]{3,2,1,0:T(8,128)(2,1)S(1)}, u32[]{:S(2)}, u32[]{:S(2)}) %collective-permute-start.18) | collective-permute-done | bytes 196640 | tf_op jit(solution)/shard_map/ppermute | solution.py:435
  57.2 0.1 constant_dynamic-update-slice_fusion.5
  57.3 2.2 %backward_step.3 = (bf16[4,16,24,128]{3,2,1,0:T(8,128)(2,1)S(1)}, bf16[4,16,24,128]{3,2,1,0:T(8,128)(2,1)S(1)}) custom-call(s32[2]{0:T(128)S(1)} %pad_add_fusion.meta, s32[3,64]{1,0:T(4,128)S(1)} %bitcast.23, s32[3,64]{1,0:T(4,128)S(1)} %collective-permute-done.9.cols_other, bf16[32,3,128,128]{3,2,1,0:T(8,128)(2,1)S(1)} %get-tuple-element.55.own, ...), custom_call_target="tpu_custom_call" | custom-call | flops 805306368 | bytes 25165824 | tf_op jit(solution)/shard_map/backward_step/pallas_call | solution.py:352
  59.5 0.1 collective-permute-start.23
  59.6 0.5 collective-permute-start.22
  60.1 1.5 %collective-permute-start.21 = (bf16[5,16,24,128]{3,2,1,0:T(8,128)(2,1)S(1)}, bf16[5,16,24,128]{3,2,1,0:T(8,128)(2,1)S(1)}, u32[]{:S(2)}, u32[]{:S(2)}) collective-permute-start(bf16[5,16,24,128]{3,2,1,0:T(8,128)(2,1)S(1)} %get-tuple-element.85), channel_id=1, source_target_pairs={{0,2},{2,0},{1,3},{3,1},{4,6},{6,4},{5,7},{7,5},{8,10},{10,8},{9,1... | collective-permute-start | bytes 1474568 | tf_op jit(solution)/shard_map/ppermute | solution.py:440
  61.6 2.8 %forward_step.3 = (bf16[256,16,128]{2,1,0:T(8,128)(2,1)S(1)}, bf16[1,16,24,128]{3,2,1,0:T(8,128)(2,1)S(1)}) custom-call(s32[2]{0:T(128)S(1)} %pad_add_fusion.meta, s32[3,64]{1,0:T(4,128)S(1)} %bitcast.24, s32[3,64]{1,0:T(4,128)S(1)} %collective-permute-done.9.cols_other, bf16[32,3,128,128]{3,2,1,0:T(8,128)(2,1)S(1)} %get-tuple-element.55.own, ...), custom_call_target="tpu_custom_call" | custom-call | flops 805306368 | bytes 25165824 | tf_op jit(solution)/shard_map/forward_step/pallas_call | solution.py:270
  64.5 1.6 %collective-permute-start.24 = (bf16[2,16,24,128]{3,2,1,0:T(8,128)(2,1)S(1)}, bf16[2,16,24,128]{3,2,1,0:T(8,128)(2,1)S(1)}, u32[]{:S(2)}, u32[]{:S(2)}) collective-permute-start(bf16[2,16,24,128]{3,2,1,0:T(8,128)(2,1)S(1)} %pad_maximum_fusion.9), channel_id=1, source_target_pairs={{0,4},{4,0},{8,12},{12,8},{1,5},{5,1},{9,13},{13,9},{2,6},{6,2},{1... | collective-permute-start | bytes 589832 | tf_op jit(solution)/shard_map/ppermute | solution.py:435
  66.1 2.0 %collective-permute-start.26 = (bf16[1,16,24,128]{3,2,1,0:T(8,128)(2,1)S(1)}, bf16[1,16,24,128]{3,2,1,0:T(8,128)(2,1)S(1)}, u32[]{:S(2)}, u32[]{:S(2)}) collective-permute-start(bf16[1,16,24,128]{3,2,1,0:T(8,128)(2,1)S(1)} %get-tuple-element.68.refs_0_), channel_id=1, source_target_pairs={{0,8},{4,12},{8,0},{12,4},{1,9},{5,13},{9,1},{13,5},{2,10},{6,14},... | collective-permute-start | bytes 294920 | tf_op jit(solution)/shard_map/ppermute | solution.py:435
  68.1 4.6 %collective-permute-done.26.refs_2_ = bf16[1,16,24,128]{3,2,1,0:T(8,128)(2,1)S(1)} collective-permute-done((bf16[1,16,24,128]{3,2,1,0:T(8,128)(2,1)S(1)}, bf16[1,16,24,128]{3,2,1,0:T(8,128)(2,1)S(1)}, u32[]{:S(2)}, u32[]{:S(2)}) %collective-permute-start.26) | collective-permute-done | bytes 98336 | tf_op jit(solution)/shard_map/ppermute | solution.py:435
  72.6 0.8 collective-permute-done.24
  73.4 0.1 pad_maximum_fusion.1
  73.5 0.1 collective-permute-start.25
  73.6 0.1 add_convert_fusion.1
  73.7 1.9 %collective-permute-start.28 = (bf16[2,16,24,128]{3,2,1,0:T(8,128)(2,1)S(1)}, bf16[2,16,24,128]{3,2,1,0:T(8,128)(2,1)S(1)}, u32[]{:S(2)}, u32[]{:S(2)}) collective-permute-start(bf16[2,16,24,128]{3,2,1,0:T(8,128)(2,1)S(1)} %pad_maximum_fusion.10), channel_id=1, source_target_pairs={{0,4},{4,0},{8,12},{12,8},{1,5},{5,1},{9,13},{13,9},{2,6},{6,2},{1... | collective-permute-start | bytes 589832 | tf_op jit(solution)/shard_map/ppermute | solution.py:435
  75.7 0.3 collective-permute-start.29
  76.0 1.7 %collective-permute-start.31 = (bf16[1,16,24,128]{3,2,1,0:T(8,128)(2,1)S(1)}, bf16[1,16,24,128]{3,2,1,0:T(8,128)(2,1)S(1)}, u32[]{:S(2)}, u32[]{:S(2)}) collective-permute-start(bf16[1,16,24,128]{3,2,1,0:T(8,128)(2,1)S(1)} %get-tuple-element.93), channel_id=1, source_target_pairs={{0,8},{4,12},{8,0},{12,4},{1,9},{5,13},{9,1},{13,5},{2,10},{6,14},... | collective-permute-start | bytes 294920 | tf_op jit(solution)/shard_map/ppermute | solution.py:435
  77.7 1.5 %collective-permute-start.33 = (bf16[3,16,24,128]{3,2,1,0:T(8,128)(2,1)S(1)}, bf16[3,16,24,128]{3,2,1,0:T(8,128)(2,1)S(1)}, u32[]{:S(2)}, u32[]{:S(2)}) collective-permute-start(bf16[3,16,24,128]{3,2,1,0:T(8,128)(2,1)S(1)} %pad_maximum_fusion.2), channel_id=1, source_target_pairs={{0,2},{2,0},{1,3},{3,1},{4,6},{6,4},{5,7},{7,5},{8,10},{10,8},{9,1... | collective-permute-start | bytes 884744 | tf_op jit(solution)/shard_map/ppermute | solution.py:440
  79.2 4.1 %collective-permute-done.28 = bf16[2,16,24,128]{3,2,1,0:T(8,128)(2,1)S(1)} collective-permute-done((bf16[2,16,24,128]{3,2,1,0:T(8,128)(2,1)S(1)}, bf16[2,16,24,128]{3,2,1,0:T(8,128)(2,1)S(1)}, u32[]{:S(2)}, u32[]{:S(2)}) %collective-permute-start.28) | collective-permute-done | bytes 196640 | tf_op jit(solution)/shard_map/ppermute | solution.py:435
  83.3 0.1 add_convert_fusion.refs_7_
  83.5 1.5 %collective-permute-start.34 = (bf16[2,16,24,128]{3,2,1,0:T(8,128)(2,1)S(1)}, bf16[2,16,24,128]{3,2,1,0:T(8,128)(2,1)S(1)}, u32[]{:S(2)}, u32[]{:S(2)}) collective-permute-start(bf16[2,16,24,128]{3,2,1,0:T(8,128)(2,1)S(1)} %pad_maximum_fusion.12), channel_id=1, source_target_pairs={{0,2},{2,0},{1,3},{3,1},{4,6},{6,4},{5,7},{7,5},{8,10},{10,8},{9,1... | collective-permute-start | bytes 589832 | tf_op jit(solution)/shard_map/ppermute | solution.py:440
  84.9 0.5 collective-permute-start.32
  85.4 2.1 %collective-permute-done.33.refs_0_ = bf16[3,16,24,128]{3,2,1,0:T(8,128)(2,1)S(1)} collective-permute-done((bf16[3,16,24,128]{3,2,1,0:T(8,128)(2,1)S(1)}, bf16[3,16,24,128]{3,2,1,0:T(8,128)(2,1)S(1)}, u32[]{:S(2)}, u32[]{:S(2)}) %collective-permute-start.33) | collective-permute-done | bytes 294944 | tf_op jit(solution)/shard_map/ppermute | solution.py:440
  87.5 0.8 unpack_panels.5.refs_1_.refs_15_
  88.3 1.0 unpack_panels.6
  89.3 1.0 unpack_panels.7
  90.3 0.9 unpack_panels.8
  91.2 0.6 collective-permute-start.36
  91.8 1.1 %collective-permute-done.36.refs_3_.refs_5_ = bf16[2,16,24,128]{3,2,1,0:T(8,128)(2,1)S(1)} collective-permute-done((bf16[2,16,24,128]{3,2,1,0:T(8,128)(2,1)S(1)}, bf16[2,16,24,128]{3,2,1,0:T(8,128)(2,1)S(1)}, u32[]{:S(2)}, u32[]{:S(2)}) %collective-permute-start.36) | collective-permute-done | bytes 196640 | tf_op jit(solution)/shard_map/ppermute | solution.py:432
  92.9 0.9 unpack_panels.9
  93.8 4.8 %gradient.1 = bf16[64,3,128,128]{3,2,1,0:T(8,128)(2,1)} custom-call(s32[2]{0:T(128)S(1)} %pad_add_fusion.meta, s32[3,64]{1,0:T(4,128)S(1)} %bitcast.25, bf16[256,16,128]{2,1,0:T(8,128)(2,1)S(1)} %get-tuple-element.45.refs_0_.refs_14_, bf16[256,16,128]{2,1,0:T(8,128)(2,1)S(1)} %unpack_panels.5.refs_1_.refs_15_, ...), custom_call_target="tpu_custom_call" | custom-call | tf_op jit(solution)/shard_map/gradient/pallas_call | solution.py:398
  (56 shorter events, 0.7 us)
Async XLA Ops:
  0.1 17.2 %copy-start = (s32[64,3]{0,1:T(4,128)S(1)}, s32[64,3]{0,1:T(4,128)}, u32[]{:S(2)}) copy-start(s32[64,3]{0,1:T(4,128)} %param.4) | copy-start | bytes 2308
  7.7 2.0 %collective-permute-start = (bf16[5,16,24,128]{3,2,1,0:T(8,128)(2,1)S(1)}, bf16[5,16,24,128]{3,2,1,0:T(8,128)(2,1)S(1)}, u32[]{:S(2)}, u32[]{:S(2)}) collective-permute-start(bf16[5,16,24,128]{3,2,1,0:T(8,128)(2,1)S(1)} %get-tuple-element.49), channel_id=1, source_target_pairs={{0,1},{1,0},{2,3},{3,2},{4,5},{5,4},{6,7},{7,6},{8,9},{9,8},{10,11... | collective-permute-start | bytes 1474568 | tf_op jit(solution)/shard_map/ppermute | solution.py:432
  9.8 20.9 %collective-permute-start.10 = (bf16[32,3,128,128]{3,2,1,0:T(8,128)(2,1)S(1)}, bf16[32,3,128,128]{3,2,1,0:T(8,128)(2,1)S(1)}, u32[]{:S(2)}, u32[]{:S(2)}) collective-permute-start(bf16[32,3,128,128]{3,2,1,0:T(8,128)(2,1)S(1)} %get-tuple-element.57), channel_id=1, source_target_pairs={{0,1},{1,0},{2,3},{3,2},{4,5},{5,4},{6,7},{7,6},{8,9},{9,8},{10,11... | collective-permute-start | bytes 9437192 | tf_op jit(solution)/shard_map/ppermute | solution.py:432
  10.3 10.3 %collective-permute-start.2 = (bf16[2,16,24,128]{3,2,1,0:T(8,128)(2,1)S(1)}, bf16[2,16,24,128]{3,2,1,0:T(8,128)(2,1)S(1)}, u32[]{:S(2)}, u32[]{:S(2)}) collective-permute-start(bf16[2,16,24,128]{3,2,1,0:T(8,128)(2,1)S(1)} %pad_maximum_fusion.3), channel_id=1, source_target_pairs={{0,4},{4,0},{8,12},{12,8},{1,5},{5,1},{9,13},{13,9},{2,6},{6,2},{1... | collective-permute-start | bytes 589832 | tf_op jit(solution)/shard_map/ppermute | solution.py:435
  13.1 4.2 %collective-permute-start.5 = (bf16[1,16,24,128]{3,2,1,0:T(8,128)(2,1)S(1)}, bf16[1,16,24,128]{3,2,1,0:T(8,128)(2,1)S(1)}, u32[]{:S(2)}, u32[]{:S(2)}) collective-permute-start(bf16[1,16,24,128]{3,2,1,0:T(8,128)(2,1)S(1)} %get-tuple-element.90.rest_0_), channel_id=1, source_target_pairs={{0,1},{1,0},{2,3},{3,2},{4,5},{5,4},{6,7},{7,6},{8,9},{9,8},{10,11... | collective-permute-start | bytes 294920 | tf_op jit(solution)/shard_map/ppermute | solution.py:432
  13.2 6.7 %collective-permute-start.4 = (bf16[1,16,24,128]{3,2,1,0:T(8,128)(2,1)S(1)}, bf16[1,16,24,128]{3,2,1,0:T(8,128)(2,1)S(1)}, u32[]{:S(2)}, u32[]{:S(2)}) collective-permute-start(bf16[1,16,24,128]{3,2,1,0:T(8,128)(2,1)S(1)} %get-tuple-element.90.rest_0_), channel_id=1, source_target_pairs={{0,8},{4,12},{8,0},{12,4},{1,9},{5,13},{9,1},{13,5},{2,10},{6,14},... | collective-permute-start | bytes 294920 | tf_op jit(solution)/shard_map/ppermute | solution.py:435
  15.8 11.2 %collective-permute-start.1 = (bf16[4,16,24,128]{3,2,1,0:T(8,128)(2,1)S(1)}, bf16[4,16,24,128]{3,2,1,0:T(8,128)(2,1)S(1)}, u32[]{:S(2)}, u32[]{:S(2)}) collective-permute-start(bf16[4,16,24,128]{3,2,1,0:T(8,128)(2,1)S(1)} %get-tuple-element.50), channel_id=1, source_target_pairs={{0,2},{2,0},{1,3},{3,1},{4,6},{6,4},{5,7},{7,5},{8,10},{10,8},{9,1... | collective-permute-start | bytes 1179656 | tf_op jit(solution)/shard_map/ppermute | solution.py:440
  17.2 13.4 %collective-permute-start.9 = (s32[3,64]{1,0:T(4,128)S(1)}, s32[3,64]{1,0:T(4,128)S(1)}, u32[]{:S(2)}, u32[]{:S(2)}) collective-permute-start(s32[3,64]{1,0:T(4,128)S(1)} %bitcast.20), channel_id=1, source_target_pairs={{0,1},{1,0},{2,3},{3,2},{4,5},{5,4},{6,7},{7,6},{8,9},{9,8},{10,11... | collective-permute-start | bytes 2312 | tf_op jit(solution)/shard_map/ppermute | solution.py:432
  20.7 9.8 %collective-permute-start.7 = (bf16[1,16,24,128]{3,2,1,0:T(8,128)(2,1)S(1)}, bf16[1,16,24,128]{3,2,1,0:T(8,128)(2,1)S(1)}, u32[]{:S(2)}, u32[]{:S(2)}) collective-permute-start(bf16[1,16,24,128]{3,2,1,0:T(8,128)(2,1)S(1)} %get-tuple-element.91), channel_id=1, source_target_pairs={{0,8},{4,12},{8,0},{12,4},{1,9},{5,13},{9,1},{13,5},{2,10},{6,14},... | collective-permute-start | bytes 294920 | tf_op jit(solution)/shard_map/ppermute | solution.py:435
  23.4 7.1 %collective-permute-start.6 = (bf16[2,16,24,128]{3,2,1,0:T(8,128)(2,1)S(1)}, bf16[2,16,24,128]{3,2,1,0:T(8,128)(2,1)S(1)}, u32[]{:S(2)}, u32[]{:S(2)}) collective-permute-start(bf16[2,16,24,128]{3,2,1,0:T(8,128)(2,1)S(1)} %pad_maximum_fusion.4), channel_id=1, source_target_pairs={{0,4},{4,0},{8,12},{12,8},{1,5},{5,1},{9,13},{13,9},{2,6},{6,2},{1... | collective-permute-start | bytes 589832 | tf_op jit(solution)/shard_map/ppermute | solution.py:435
  26.9 3.6 %collective-permute-start.3 = (bf16[4,16,24,128]{3,2,1,0:T(8,128)(2,1)S(1)}, bf16[4,16,24,128]{3,2,1,0:T(8,128)(2,1)S(1)}, u32[]{:S(2)}, u32[]{:S(2)}) collective-permute-start(bf16[4,16,24,128]{3,2,1,0:T(8,128)(2,1)S(1)} %collective-permute-done.1.refs_0_), channel_id=1, source_target_pairs={{0,1},{1,0},{2,3},{3,2},{4,5},{5,4},{6,7},{7,6},{8,9},{9,8},{10,11... | collective-permute-start | bytes 1179656 | tf_op jit(solution)/shard_map/ppermute | solution.py:432
  32.9 5.2 %collective-permute-start.13 = (bf16[4,16,24,128]{3,2,1,0:T(8,128)(2,1)S(1)}, bf16[4,16,24,128]{3,2,1,0:T(8,128)(2,1)S(1)}, u32[]{:S(2)}, u32[]{:S(2)}) collective-permute-start(bf16[4,16,24,128]{3,2,1,0:T(8,128)(2,1)S(1)} %get-tuple-element.58.rest_7_), channel_id=1, source_target_pairs={{0,1},{1,0},{2,3},{3,2},{4,5},{5,4},{6,7},{7,6},{8,9},{9,8},{10,11... | collective-permute-start | bytes 1179656 | tf_op jit(solution)/shard_map/ppermute | solution.py:432
  33.0 2.3 %collective-permute-start.11 = (bf16[2,16,24,128]{3,2,1,0:T(8,128)(2,1)S(1)}, bf16[2,16,24,128]{3,2,1,0:T(8,128)(2,1)S(1)}, u32[]{:S(2)}, u32[]{:S(2)}) collective-permute-start(bf16[2,16,24,128]{3,2,1,0:T(8,128)(2,1)S(1)} %pad_maximum_fusion.5), channel_id=1, source_target_pairs={{0,1},{1,0},{2,3},{3,2},{4,5},{5,4},{6,7},{7,6},{8,9},{9,8},{10,11... | collective-permute-start | bytes 589832 | tf_op jit(solution)/shard_map/ppermute | solution.py:432
  33.6 1.7 %collective-permute-start.12 = (bf16[1,16,24,128]{3,2,1,0:T(8,128)(2,1)S(1)}, bf16[1,16,24,128]{3,2,1,0:T(8,128)(2,1)S(1)}, u32[]{:S(2)}, u32[]{:S(2)}) collective-permute-start(bf16[1,16,24,128]{3,2,1,0:T(8,128)(2,1)S(1)} %get-tuple-element.101.rest_3_), channel_id=1, source_target_pairs={{0,1},{1,0},{2,3},{3,2},{4,5},{5,4},{6,7},{7,6},{8,9},{9,8},{10,11... | collective-permute-start | bytes 294920 | tf_op jit(solution)/shard_map/ppermute | solution.py:432
  33.6 13.6 %collective-permute-start.8 = (bf16[5,16,24,128]{3,2,1,0:T(8,128)(2,1)S(1)}, bf16[5,16,24,128]{3,2,1,0:T(8,128)(2,1)S(1)}, u32[]{:S(2)}, u32[]{:S(2)}) collective-permute-start(bf16[5,16,24,128]{3,2,1,0:T(8,128)(2,1)S(1)} %get-tuple-element.87), channel_id=1, source_target_pairs={{0,2},{2,0},{1,3},{3,1},{4,6},{6,4},{5,7},{7,5},{8,10},{10,8},{9,1... | collective-permute-start | bytes 1474568 | tf_op jit(solution)/shard_map/ppermute | solution.py:440
  38.1 9.1 %collective-permute-start.14 = (bf16[2,16,24,128]{3,2,1,0:T(8,128)(2,1)S(1)}, bf16[2,16,24,128]{3,2,1,0:T(8,128)(2,1)S(1)}, u32[]{:S(2)}, u32[]{:S(2)}) collective-permute-start(bf16[2,16,24,128]{3,2,1,0:T(8,128)(2,1)S(1)} %pad_maximum_fusion.6), channel_id=1, source_target_pairs={{0,4},{4,0},{8,12},{12,8},{1,5},{5,1},{9,13},{13,9},{2,6},{6,2},{1... | collective-permute-start | bytes 589832 | tf_op jit(solution)/shard_map/ppermute | solution.py:435
  39.8 2.5 %collective-permute-start.17 = (bf16[1,16,24,128]{3,2,1,0:T(8,128)(2,1)S(1)}, bf16[1,16,24,128]{3,2,1,0:T(8,128)(2,1)S(1)}, u32[]{:S(2)}, u32[]{:S(2)}) collective-permute-start(bf16[1,16,24,128]{3,2,1,0:T(8,128)(2,1)S(1)} %get-tuple-element.59.rest_0_), channel_id=1, source_target_pairs={{0,1},{1,0},{2,3},{3,2},{4,5},{5,4},{6,7},{7,6},{8,9},{9,8},{10,11... | collective-permute-start | bytes 294920 | tf_op jit(solution)/shard_map/ppermute | solution.py:432
  39.8 6.6 %collective-permute-start.16 = (bf16[1,16,24,128]{3,2,1,0:T(8,128)(2,1)S(1)}, bf16[1,16,24,128]{3,2,1,0:T(8,128)(2,1)S(1)}, u32[]{:S(2)}, u32[]{:S(2)}) collective-permute-start(bf16[1,16,24,128]{3,2,1,0:T(8,128)(2,1)S(1)} %get-tuple-element.59.rest_0_), channel_id=1, source_target_pairs={{0,8},{4,12},{8,0},{12,4},{1,9},{5,13},{9,1},{13,5},{2,10},{6,14},... | collective-permute-start | bytes 294920 | tf_op jit(solution)/shard_map/ppermute | solution.py:435
  47.3 9.9 %collective-permute-start.20 = (bf16[1,16,24,128]{3,2,1,0:T(8,128)(2,1)S(1)}, bf16[1,16,24,128]{3,2,1,0:T(8,128)(2,1)S(1)}, u32[]{:S(2)}, u32[]{:S(2)}) collective-permute-start(bf16[1,16,24,128]{3,2,1,0:T(8,128)(2,1)S(1)} %get-tuple-element.95), channel_id=1, source_target_pairs={{0,8},{4,12},{8,0},{12,4},{1,9},{5,13},{9,1},{13,5},{2,10},{6,14},... | collective-permute-start | bytes 294920 | tf_op jit(solution)/shard_map/ppermute | solution.py:435
  49.9 7.2 %collective-permute-start.18 = (bf16[2,16,24,128]{3,2,1,0:T(8,128)(2,1)S(1)}, bf16[2,16,24,128]{3,2,1,0:T(8,128)(2,1)S(1)}, u32[]{:S(2)}, u32[]{:S(2)}) collective-permute-start(bf16[2,16,24,128]{3,2,1,0:T(8,128)(2,1)S(1)} %pad_maximum_fusion.7), channel_id=1, source_target_pairs={{0,4},{4,0},{8,12},{12,8},{1,5},{5,1},{9,13},{13,9},{2,6},{6,2},{1... | collective-permute-start | bytes 589832 | tf_op jit(solution)/shard_map/ppermute | solution.py:435
  51.7 5.5 %collective-permute-start.15 = (bf16[6,16,24,128]{3,2,1,0:T(8,128)(2,1)S(1)}, bf16[6,16,24,128]{3,2,1,0:T(8,128)(2,1)S(1)}, u32[]{:S(2)}, u32[]{:S(2)}) collective-permute-start(bf16[6,16,24,128]{3,2,1,0:T(8,128)(2,1)S(1)} %pad_maximum_fusion), channel_id=1, source_target_pairs={{0,1},{1,0},{2,3},{3,2},{4,5},{5,4},{6,7},{7,6},{8,9},{9,8},{10,11... | collective-permute-start | bytes 1769480 | tf_op jit(solution)/shard_map/ppermute | solution.py:432
  51.8 5.3 %collective-permute-start.19 = (bf16[2,16,24,128]{3,2,1,0:T(8,128)(2,1)S(1)}, bf16[2,16,24,128]{3,2,1,0:T(8,128)(2,1)S(1)}, u32[]{:S(2)}, u32[]{:S(2)}) collective-permute-start(bf16[2,16,24,128]{3,2,1,0:T(8,128)(2,1)S(1)} %pad_maximum_fusion.8), channel_id=1, source_target_pairs={{0,1},{1,0},{2,3},{3,2},{4,5},{5,4},{6,7},{7,6},{8,9},{9,8},{10,11... | collective-permute-start | bytes 589832 | tf_op jit(solution)/shard_map/ppermute | solution.py:432
  59.5 4.9 %collective-permute-start.23 = (bf16[4,16,24,128]{3,2,1,0:T(8,128)(2,1)S(1)}, bf16[4,16,24,128]{3,2,1,0:T(8,128)(2,1)S(1)}, u32[]{:S(2)}, u32[]{:S(2)}) collective-permute-start(bf16[4,16,24,128]{3,2,1,0:T(8,128)(2,1)S(1)} %get-tuple-element.67.rest_7_), channel_id=1, source_target_pairs={{0,1},{1,0},{2,3},{3,2},{4,5},{5,4},{6,7},{7,6},{8,9},{9,8},{10,11... | collective-permute-start | bytes 1179656 | tf_op jit(solution)/shard_map/ppermute | solution.py:432
  59.6 2.0 %collective-permute-start.22 = (bf16[1,16,24,128]{3,2,1,0:T(8,128)(2,1)S(1)}, bf16[1,16,24,128]{3,2,1,0:T(8,128)(2,1)S(1)}, u32[]{:S(2)}, u32[]{:S(2)}) collective-permute-start(bf16[1,16,24,128]{3,2,1,0:T(8,128)(2,1)S(1)} %get-tuple-element.97.rest_3_), channel_id=1, source_target_pairs={{0,1},{1,0},{2,3},{3,2},{4,5},{5,4},{6,7},{7,6},{8,9},{9,8},{10,11... | collective-permute-start | bytes 294920 | tf_op jit(solution)/shard_map/ppermute | solution.py:432
  60.1 13.3 %collective-permute-start.21 = (bf16[5,16,24,128]{3,2,1,0:T(8,128)(2,1)S(1)}, bf16[5,16,24,128]{3,2,1,0:T(8,128)(2,1)S(1)}, u32[]{:S(2)}, u32[]{:S(2)}) collective-permute-start(bf16[5,16,24,128]{3,2,1,0:T(8,128)(2,1)S(1)} %get-tuple-element.85), channel_id=1, source_target_pairs={{0,2},{2,0},{1,3},{3,1},{4,6},{6,4},{5,7},{7,5},{8,10},{10,8},{9,1... | collective-permute-start | bytes 1474568 | tf_op jit(solution)/shard_map/ppermute | solution.py:440
  64.5 9.0 %collective-permute-start.24 = (bf16[2,16,24,128]{3,2,1,0:T(8,128)(2,1)S(1)}, bf16[2,16,24,128]{3,2,1,0:T(8,128)(2,1)S(1)}, u32[]{:S(2)}, u32[]{:S(2)}) collective-permute-start(bf16[2,16,24,128]{3,2,1,0:T(8,128)(2,1)S(1)} %pad_maximum_fusion.9), channel_id=1, source_target_pairs={{0,4},{4,0},{8,12},{12,8},{1,5},{5,1},{9,13},{13,9},{2,6},{6,2},{1... | collective-permute-start | bytes 589832 | tf_op jit(solution)/shard_map/ppermute | solution.py:435
  66.1 2.0 %collective-permute-start.27 = (bf16[1,16,24,128]{3,2,1,0:T(8,128)(2,1)S(1)}, bf16[1,16,24,128]{3,2,1,0:T(8,128)(2,1)S(1)}, u32[]{:S(2)}, u32[]{:S(2)}) collective-permute-start(bf16[1,16,24,128]{3,2,1,0:T(8,128)(2,1)S(1)} %get-tuple-element.68.refs_0_), channel_id=1, source_target_pairs={{0,1},{1,0},{2,3},{3,2},{4,5},{5,4},{6,7},{7,6},{8,9},{9,8},{10,11... | collective-permute-start | bytes 294920 | tf_op jit(solution)/shard_map/ppermute | solution.py:432
  66.1 6.5 %collective-permute-start.26 = (bf16[1,16,24,128]{3,2,1,0:T(8,128)(2,1)S(1)}, bf16[1,16,24,128]{3,2,1,0:T(8,128)(2,1)S(1)}, u32[]{:S(2)}, u32[]{:S(2)}) collective-permute-start(bf16[1,16,24,128]{3,2,1,0:T(8,128)(2,1)S(1)} %get-tuple-element.68.refs_0_), channel_id=1, source_target_pairs={{0,8},{4,12},{8,0},{12,4},{1,9},{5,13},{9,1},{13,5},{2,10},{6,14},... | collective-permute-start | bytes 294920 | tf_op jit(solution)/shard_map/ppermute | solution.py:435
  73.5 9.8 %collective-permute-start.25 = (bf16[6,16,24,128]{3,2,1,0:T(8,128)(2,1)S(1)}, bf16[6,16,24,128]{3,2,1,0:T(8,128)(2,1)S(1)}, u32[]{:S(2)}, u32[]{:S(2)}) collective-permute-start(bf16[6,16,24,128]{3,2,1,0:T(8,128)(2,1)S(1)} %pad_maximum_fusion.1), channel_id=1, source_target_pairs={{0,1},{1,0},{2,3},{3,2},{4,5},{5,4},{6,7},{7,6},{8,9},{9,8},{10,11... | collective-permute-start | bytes 1769480 | tf_op jit(solution)/shard_map/ppermute | solution.py:432
  73.7 9.6 %collective-permute-start.28 = (bf16[2,16,24,128]{3,2,1,0:T(8,128)(2,1)S(1)}, bf16[2,16,24,128]{3,2,1,0:T(8,128)(2,1)S(1)}, u32[]{:S(2)}, u32[]{:S(2)}) collective-permute-start(bf16[2,16,24,128]{3,2,1,0:T(8,128)(2,1)S(1)} %pad_maximum_fusion.10), channel_id=1, source_target_pairs={{0,4},{4,0},{8,12},{12,8},{1,5},{5,1},{9,13},{13,9},{2,6},{6,2},{1... | collective-permute-start | bytes 589832 | tf_op jit(solution)/shard_map/ppermute | solution.py:435
  75.7 7.6 %collective-permute-start.29 = (bf16[2,16,24,128]{3,2,1,0:T(8,128)(2,1)S(1)}, bf16[2,16,24,128]{3,2,1,0:T(8,128)(2,1)S(1)}, u32[]{:S(2)}, u32[]{:S(2)}) collective-permute-start(bf16[2,16,24,128]{3,2,1,0:T(8,128)(2,1)S(1)} %pad_maximum_fusion.11), channel_id=1, source_target_pairs={{0,1},{1,0},{2,3},{3,2},{4,5},{5,4},{6,7},{7,6},{8,9},{9,8},{10,11... | collective-permute-start | bytes 589832 | tf_op jit(solution)/shard_map/ppermute | solution.py:432
  76.0 7.4 %collective-permute-start.31 = (bf16[1,16,24,128]{3,2,1,0:T(8,128)(2,1)S(1)}, bf16[1,16,24,128]{3,2,1,0:T(8,128)(2,1)S(1)}, u32[]{:S(2)}, u32[]{:S(2)}) collective-permute-start(bf16[1,16,24,128]{3,2,1,0:T(8,128)(2,1)S(1)} %get-tuple-element.93), channel_id=1, source_target_pairs={{0,8},{4,12},{8,0},{12,4},{1,9},{5,13},{9,1},{13,5},{2,10},{6,14},... | collective-permute-start | bytes 294920 | tf_op jit(solution)/shard_map/ppermute | solution.py:435
  77.7 9.8 %collective-permute-start.33 = (bf16[3,16,24,128]{3,2,1,0:T(8,128)(2,1)S(1)}, bf16[3,16,24,128]{3,2,1,0:T(8,128)(2,1)S(1)}, u32[]{:S(2)}, u32[]{:S(2)}) collective-permute-start(bf16[3,16,24,128]{3,2,1,0:T(8,128)(2,1)S(1)} %pad_maximum_fusion.2), channel_id=1, source_target_pairs={{0,2},{2,0},{1,3},{3,1},{4,6},{6,4},{5,7},{7,5},{8,10},{10,8},{9,1... | collective-permute-start | bytes 884744 | tf_op jit(solution)/shard_map/ppermute | solution.py:440
  83.5 7.8 %collective-permute-start.34 = (bf16[2,16,24,128]{3,2,1,0:T(8,128)(2,1)S(1)}, bf16[2,16,24,128]{3,2,1,0:T(8,128)(2,1)S(1)}, u32[]{:S(2)}, u32[]{:S(2)}) collective-permute-start(bf16[2,16,24,128]{3,2,1,0:T(8,128)(2,1)S(1)} %pad_maximum_fusion.12), channel_id=1, source_target_pairs={{0,2},{2,0},{1,3},{3,1},{4,6},{6,4},{5,7},{7,5},{8,10},{10,8},{9,1... | collective-permute-start | bytes 589832 | tf_op jit(solution)/shard_map/ppermute | solution.py:440
  84.9 5.4 %collective-permute-start.30 = (bf16[1,16,24,128]{3,2,1,0:T(8,128)(2,1)S(1)}, bf16[1,16,24,128]{3,2,1,0:T(8,128)(2,1)S(1)}, u32[]{:S(2)}, u32[]{:S(2)}) collective-permute-start(bf16[1,16,24,128]{3,2,1,0:T(8,128)(2,1)S(1)} %slice.168.refs_3_), channel_id=1, source_target_pairs={{0,1},{1,0},{2,3},{3,2},{4,5},{5,4},{6,7},{7,6},{8,9},{9,8},{10,11... | collective-permute-start | bytes 294920 | tf_op jit(solution)/shard_map/ppermute | solution.py:432
  84.9 5.4 %collective-permute-start.32 = (bf16[1,16,24,128]{3,2,1,0:T(8,128)(2,1)S(1)}, bf16[1,16,24,128]{3,2,1,0:T(8,128)(2,1)S(1)}, u32[]{:S(2)}, u32[]{:S(2)}) collective-permute-start(bf16[1,16,24,128]{3,2,1,0:T(8,128)(2,1)S(1)} %add_convert_fusion.refs_7_), channel_id=1, source_target_pairs={{0,1},{1,0},{2,3},{3,2},{4,5},{5,4},{6,7},{7,6},{8,9},{9,8},{10,11... | collective-permute-start | bytes 294920 | tf_op jit(solution)/shard_map/ppermute | solution.py:432
  87.5 4.3 %collective-permute-start.35 = (bf16[3,16,24,128]{3,2,1,0:T(8,128)(2,1)S(1)}, bf16[3,16,24,128]{3,2,1,0:T(8,128)(2,1)S(1)}, u32[]{:S(2)}, u32[]{:S(2)}) collective-permute-start(bf16[3,16,24,128]{3,2,1,0:T(8,128)(2,1)S(1)} %collective-permute-done.33.refs_0_), channel_id=1, source_target_pairs={{0,1},{1,0},{2,3},{3,2},{4,5},{5,4},{6,7},{7,6},{8,9},{9,8},{10,11... | collective-permute-start | bytes 884744 | tf_op jit(solution)/shard_map/ppermute | solution.py:432
  91.2 1.6 %collective-permute-start.36 = (bf16[2,16,24,128]{3,2,1,0:T(8,128)(2,1)S(1)}, bf16[2,16,24,128]{3,2,1,0:T(8,128)(2,1)S(1)}, u32[]{:S(2)}, u32[]{:S(2)}) collective-permute-start(bf16[2,16,24,128]{3,2,1,0:T(8,128)(2,1)S(1)} %collective-permute-done.34.refs_1_.refs_4_), channel_id=1, source_target_pairs={{0,1},{1,0},{2,3},{3,2},{4,5},{5,4},{6,7},{7,6},{8,9},{9,8},{10,11... | collective-permute-start | bytes 589832 | tf_op jit(solution)/shard_map/ppermute | solution.py:432

commit v7 on v6

--- a/solution.py
+++ b/solution.py
@@ -10,6 +10,7 @@
 
 KS = 6
 PAD = 16
+GRADIENT_ROWS = 8
 VMEM_LIMIT = 16 * 1024 * 1024
 
 
@@ -190,7 +191,7 @@
     rows, slots, width = stored.shape[0], stored.shape[1], stored.shape[3]
     count = signs.shape[0] // blocks
     half = rows // 2
-    chunk = min(16, half)
+    chunk = min(32, half)
     parts = blocks // rows
     shape = jax.ShapeDtypeStruct
     piece = (half // 2, 2 * count, width)
@@ -266,7 +267,7 @@
     half, slots, width = own.shape[0], own.shape[1], own.shape[3]
     arrays = [array for array, _ in pieces]
     count = arrays[0].shape[2] // 2
-    chunk = min(16, half)
+    chunk = min(32, half)
     return pl.pallas_call(
         functools.partial(
             forward_kernel, count, chunk, 2 * half, inverse, [places for _, places in pieces]
@@ -345,7 +346,7 @@
 def backward(meta, cols_own, cols_other, own, other, left, blocks, tokens):
     half, slots, width = own.shape[0], own.shape[1], own.shape[3]
     count = left.shape[2] // 2
-    chunk = min(16, half)
+    chunk = min(32, half)
     result = jax.ShapeDtypeStruct(
         (blocks // (2 * half), half // 2, 2 * count, width), jnp.bfloat16
     )
@@ -366,43 +367,61 @@
 
 
 def gradient_kernel(scale, chunk, rows, terms, meta, cols, *refs):
-    out = refs[-1]
+    out, made, sems = refs[-3:]
     lefts = refs[: 4 * terms]
     rights = refs[4 * terms : 8 * terms]
-    step = pl.program_id(0)
-    slots = out.shape[1]
+    slots, width = out.shape[1], out.shape[3]
     contract = (((0,), (0,)), ((), ()))
-    for r in range(chunk):
-        row = step * chunk + r
-        left = []
-        for position, ref in enumerate(lefts):
-            start = meta[0] * rows if position < terms else 0
-            left.append(ref[start + row])
-        left = jnp.concatenate(left, axis=0)
-        right = []
-        for k in range(slots):
-            target = cols[k, row]
-            right.append(jnp.concatenate([ref[target] for ref in rights], axis=0))
-        product = lax.dot_general(
-            left, jnp.concatenate(right, axis=1), contract, preferred_element_type=jnp.float32
-        )
-        width = out.shape[3]
-        for k in range(slots):
-            out[r, k] = (product[:, k * width : (k + 1) * width] * scale).astype(jnp.bfloat16)
+
+    def copy(step):
+        part = pl.ds(step * chunk, chunk)
+        return pltpu.make_async_copy(made.at[part], out.at[part], sems.at[step])
+
+    def body(step, carry):
+        for r in range(chunk):
+            row = step * chunk + r
+            left = []
+            for position, ref in enumerate(lefts):
+                start = meta[0] * rows if position < terms else 0
+                left.append(ref[start + row])
+            left = jnp.concatenate(left, axis=0)
+            right = []
+            for k in range(slots):
+                target = cols[k, row]
+                right.append(jnp.concatenate([ref[target] for ref in rights], axis=0))
+            product = lax.dot_general(
+                left, jnp.concatenate(right, axis=1), contract, preferred_element_type=jnp.float32
+            )
+            for k in range(slots):
+                made[row, k] = (product[:, k * width : (k + 1) * width] * scale).astype(
+                    jnp.bfloat16
+                )
+        copy(step).start()
+        return carry
+
+    for step in range(rows // chunk):
+        body(step, 0)
+    for step in range(rows // chunk):
+        copy(step).wait()
 
 
 def gradient(meta, cols, lefts, rights, rows, slots, scale):
     width = lefts[0].shape[2]
-    chunk = min(16, rows)
+    chunk = min(GRADIENT_ROWS, rows)
     operands = list(lefts) + list(rights)
+    shape = (rows, slots, width, width)
     return pl.pallas_call(
         functools.partial(gradient_kernel, scale, chunk, rows, len(lefts) // 4),
-        out_shape=jax.ShapeDtypeStruct((rows, slots, width, width), jnp.bfloat16),
+        out_shape=jax.ShapeDtypeStruct(shape, jnp.bfloat16),
         grid_spec=pltpu.PrefetchScalarGridSpec(
             num_scalar_prefetch=2,
-            grid=(rows // chunk,),
+            grid=(1,),
             in_specs=[whole()] * len(operands),
-            out_specs=pl.BlockSpec((chunk, slots, width, width), lambda g, *_: (g, 0, 0, 0)),
+            out_specs=anywhere(),
+            scratch_shapes=[
+                pltpu.VMEM(shape, jnp.bfloat16),
+                pltpu.SemaphoreType.DMA((rows // chunk,)),
+            ],
         ),
         compiler_params=params(),
         name="gradient",

time: 98.7 us -> 97.2 us (0.985)
  Pallas kernels: 27 us -> 25.3 us
    pallas_call x1, Pallas kernels: 4.77 us -> 3.72 us  [gradient(): pl.pallas_call(functools.partial(gradient_kernel, scale, chunk, rows, len...]
  transfers between devices with their start and end apart: 37 -> 37, of which waited for: 13 -> 14; matrix products, arithmetic and copies ran while one was open for 1% -> 1% of each run, Pallas kernels for 9% -> 9%
where the time goes in v7:
time: 97.2 us; the launch traced here: 97 us
  starting transfers between devices  37.4 us (38%)
  waiting for transfers between devices  32.5 us (33%)
  Pallas kernels  25.3 us (26%)
  other arithmetic  1.05 us (1%)
    ppermute x12, waiting for transfers between devices, shift_var(): return lax.ppermute(x, 'var', [(i, i ^ bit) for i in range(n_var)])  26 us
    ppermute x12, starting transfers between devices, shift_var(): return lax.ppermute(x, 'var', [(i, i ^ bit) for i in range(n_var)])  25.4 us
    ppermute x5, starting transfers between devices, from_probes(): lax.ppermute(x, 'probe', [(i, (i + d) % n_probe) for i in range(n_probe)])  7.69 us
    pallas_call x1, Pallas kernels, first_step(): pl.pallas_call(functools.partial(first_kernel, count, chunk, blocks), out...  7.42 us
    pallas_call x2, Pallas kernels, forward(): pl.pallas_call(functools.partial(forward_kernel, count, chunk, 2 * half,...  5.43 us
    pallas_call x5, Pallas kernels, unpack(): pl.pallas_call(functools.partial(unpack_kernel, count, wheres, len(tokens...  4.59 us
    ppermute x20, starting transfers between devices, swap_rep(): return lax.ppermute(x, 'rep', [(0, 1), (1, 0)])  4.38 us
    pallas_call x2, Pallas kernels, backward(): pl.pallas_call(functools.partial(backward_kernel, count, chunk), out_shap...  4.13 us
  transfers between devices with their start and end apart: 37, of which 14 were waited for; matrix products, arithmetic and copies ran while one was open for 1% of the time, Pallas kernels for 9%

profile of v7, /device:TPU:0, one launch (start us, length us, event | category | flops | bytes accessed | tf_op | source)
XLA Modules:
  0.0 97.0 jit_solution(3195121003000755828)
XLA Ops:
  0.0 0.1 pad_add_fusion.meta
  0.1 7.4 %first_step.1 = (bf16[256,16,128]{2,1,0:T(8,128)(2,1)S(1)}, bf16[4,16,24,128]{3,2,1,0:T(8,128)(2,1)S(1)}, bf16[1,16,24,128]{3,2,1,0:T(8,128)(2,1)S(1)}, f32[16,2...) custom-call(s32[2]{0:T(128)S(1)} %pad_add_fusion.meta, ...), custom_call_target="tpu_custom_call" | custom-call | flops 1610612736 | bytes 50331648 | tf_op jit(solution)/shard_map/first_step/pallas_call | solution.py:198
  7.5 0.5 collective-permute-start
  8.0 1.5 %collective-permute-done = bf16[5,16,24,128]{3,2,1,0:T(8,128)(2,1)S(1)} collective-permute-done((bf16[5,16,24,128]{3,2,1,0:T(8,128)(2,1)S(1)}, bf16[5,16,24,128]{3,2,1,0:T(8,128)(2,1)S(1)}, u32[]{:S(2)}, u32[]{:S(2)}) %collective-permute-start) | collective-permute-done | bytes 491552 | tf_op jit(solution)/shard_map/ppermute | solution.py:451
  9.6 0.4 collective-permute-start.10
  10.1 2.8 %collective-permute-start.2 = (bf16[2,16,24,128]{3,2,1,0:T(8,128)(2,1)S(1)}, bf16[2,16,24,128]{3,2,1,0:T(8,128)(2,1)S(1)}, u32[]{:S(2)}, u32[]{:S(2)}) collective-permute-start(bf16[2,16,24,128]{3,2,1,0:T(8,128)(2,1)S(1)} %pad_maximum_fusion.3), channel_id=1, source_target_pairs={{0,4},{4,0},{8,12},{12,8},{1,5},{5,1},{9,13},{13,9},{2,6},{6,2},{1... | collective-permute-start | bytes 589832 | tf_op jit(solution)/shard_map/ppermute | solution.py:454
  12.9 0.1 collective-permute-start.5
  12.9 2.6 %collective-permute-start.4 = (bf16[1,16,24,128]{3,2,1,0:T(8,128)(2,1)S(1)}, bf16[1,16,24,128]{3,2,1,0:T(8,128)(2,1)S(1)}, u32[]{:S(2)}, u32[]{:S(2)}) collective-permute-start(bf16[1,16,24,128]{3,2,1,0:T(8,128)(2,1)S(1)} %get-tuple-element.90.rest_0_), channel_id=1, source_target_pairs={{0,8},{4,12},{8,0},{12,4},{1,9},{5,13},{9,1},{13,5},{2,10},{6,14},... | collective-permute-start | bytes 294920 | tf_op jit(solution)/shard_map/ppermute | solution.py:454
  15.5 1.5 %collective-permute-start.1 = (bf16[4,16,24,128]{3,2,1,0:T(8,128)(2,1)S(1)}, bf16[4,16,24,128]{3,2,1,0:T(8,128)(2,1)S(1)}, u32[]{:S(2)}, u32[]{:S(2)}) collective-permute-start(bf16[4,16,24,128]{3,2,1,0:T(8,128)(2,1)S(1)} %get-tuple-element.50), channel_id=1, source_target_pairs={{0,2},{2,0},{1,3},{3,1},{4,6},{6,4},{5,7},{7,5},{8,10},{10,8},{9,1... | collective-permute-start | bytes 1179656 | tf_op jit(solution)/shard_map/ppermute | solution.py:459
  17.0 2.6 %collective-permute-done.4.rest_2_ = bf16[1,16,24,128]{3,2,1,0:T(8,128)(2,1)S(1)} collective-permute-done((bf16[1,16,24,128]{3,2,1,0:T(8,128)(2,1)S(1)}, bf16[1,16,24,128]{3,2,1,0:T(8,128)(2,1)S(1)}, u32[]{:S(2)}, u32[]{:S(2)}) %collective-permute-start.4) | collective-permute-done | bytes 98336 | tf_op jit(solution)/shard_map/ppermute | solution.py:454
  19.6 0.7 collective-permute-done.2
  20.4 0.1 add_convert_fusion.9
  20.5 2.7 %collective-permute-start.7 = (bf16[1,16,24,128]{3,2,1,0:T(8,128)(2,1)S(1)}, bf16[1,16,24,128]{3,2,1,0:T(8,128)(2,1)S(1)}, u32[]{:S(2)}, u32[]{:S(2)}) collective-permute-start(bf16[1,16,24,128]{3,2,1,0:T(8,128)(2,1)S(1)} %get-tuple-element.91), channel_id=1, source_target_pairs={{0,8},{4,12},{8,0},{12,4},{1,9},{5,13},{9,1},{13,5},{2,10},{6,14},... | collective-permute-start | bytes 294920 | tf_op jit(solution)/shard_map/ppermute | solution.py:454
  23.2 1.8 %collective-permute-start.6 = (bf16[2,16,24,128]{3,2,1,0:T(8,128)(2,1)S(1)}, bf16[2,16,24,128]{3,2,1,0:T(8,128)(2,1)S(1)}, u32[]{:S(2)}, u32[]{:S(2)}) collective-permute-start(bf16[2,16,24,128]{3,2,1,0:T(8,128)(2,1)S(1)} %pad_maximum_fusion.4), channel_id=1, source_target_pairs={{0,4},{4,0},{8,12},{12,8},{1,5},{5,1},{9,13},{13,9},{2,6},{6,2},{1... | collective-permute-start | bytes 589832 | tf_op jit(solution)/shard_map/ppermute | solution.py:454
  24.9 1.8 %collective-permute-done.1.refs_0_ = bf16[4,16,24,128]{3,2,1,0:T(8,128)(2,1)S(1)} collective-permute-done((bf16[4,16,24,128]{3,2,1,0:T(8,128)(2,1)S(1)}, bf16[4,16,24,128]{3,2,1,0:T(8,128)(2,1)S(1)}, u32[]{:S(2)}, u32[]{:S(2)}) %collective-permute-start.1) | collective-permute-done | bytes 393248 | tf_op jit(solution)/shard_map/ppermute | solution.py:459
  26.8 3.5 %collective-permute-done.6 = bf16[2,16,24,128]{3,2,1,0:T(8,128)(2,1)S(1)} collective-permute-done((bf16[2,16,24,128]{3,2,1,0:T(8,128)(2,1)S(1)}, bf16[2,16,24,128]{3,2,1,0:T(8,128)(2,1)S(1)}, u32[]{:S(2)}, u32[]{:S(2)}) %collective-permute-start.6) | collective-permute-done | bytes 196640 | tf_op jit(solution)/shard_map/ppermute | solution.py:454
  30.3 0.1 constant_dynamic-update-slice_fusion
  30.4 2.1 %backward_step.2 = (bf16[4,16,24,128]{3,2,1,0:T(8,128)(2,1)S(1)}, bf16[4,16,24,128]{3,2,1,0:T(8,128)(2,1)S(1)}) custom-call(s32[2]{0:T(128)S(1)} %pad_add_fusion.meta, s32[3,64]{1,0:T(4,128)S(1)} %bitcast.21, s32[3,64]{1,0:T(4,128)S(1)} %collective-permute-done.9.cols_other, bf16[32,3,128,128]{3,2,1,0:T(8,128)(2,1)S(1)} %get-tuple-element.55.own, ...), custom_call_target="tpu_custom_call" | custom-call | flops 805306368 | bytes 25165824 | tf_op jit(solution)/shard_map/backward_step/pallas_call | solution.py:353
  32.5 0.1 collective-permute-start.13
  32.6 0.6 collective-permute-start.11
  33.2 0.1 collective-permute-start.12
  33.2 1.6 %collective-permute-start.8 = (bf16[5,16,24,128]{3,2,1,0:T(8,128)(2,1)S(1)}, bf16[5,16,24,128]{3,2,1,0:T(8,128)(2,1)S(1)}, u32[]{:S(2)}, u32[]{:S(2)}) collective-permute-start(bf16[5,16,24,128]{3,2,1,0:T(8,128)(2,1)S(1)} %get-tuple-element.87), channel_id=1, source_target_pairs={{0,2},{2,0},{1,3},{3,1},{4,6},{6,4},{5,7},{7,5},{8,10},{10,8},{9,1... | collective-permute-start | bytes 1474568 | tf_op jit(solution)/shard_map/ppermute | solution.py:459
  34.9 2.6 %forward_step.2 = (bf16[256,16,128]{2,1,0:T(8,128)(2,1)S(1)}, bf16[1,16,24,128]{3,2,1,0:T(8,128)(2,1)S(1)}) custom-call(s32[2]{0:T(128)S(1)} %pad_add_fusion.meta, s32[3,64]{1,0:T(4,128)S(1)} %bitcast.22, s32[3,64]{1,0:T(4,128)S(1)} %collective-permute-done.9.cols_other, bf16[32,3,128,128]{3,2,1,0:T(8,128)(2,1)S(1)} %get-tuple-element.55.own, ...), custom_call_target="tpu_custom_call" | custom-call | flops 805306368 | bytes 25165824 | tf_op jit(solution)/shard_map/forward_step/pallas_call | solution.py:271
  37.6 1.7 %collective-permute-start.14 = (bf16[2,16,24,128]{3,2,1,0:T(8,128)(2,1)S(1)}, bf16[2,16,24,128]{3,2,1,0:T(8,128)(2,1)S(1)}, u32[]{:S(2)}, u32[]{:S(2)}) collective-permute-start(bf16[2,16,24,128]{3,2,1,0:T(8,128)(2,1)S(1)} %pad_maximum_fusion.6), channel_id=1, source_target_pairs={{0,4},{4,0},{8,12},{12,8},{1,5},{5,1},{9,13},{13,9},{2,6},{6,2},{1... | collective-permute-start | bytes 589832 | tf_op jit(solution)/shard_map/ppermute | solution.py:454
  39.3 2.5 %collective-permute-start.16 = (bf16[1,16,24,128]{3,2,1,0:T(8,128)(2,1)S(1)}, bf16[1,16,24,128]{3,2,1,0:T(8,128)(2,1)S(1)}, u32[]{:S(2)}, u32[]{:S(2)}) collective-permute-start(bf16[1,16,24,128]{3,2,1,0:T(8,128)(2,1)S(1)} %get-tuple-element.59.rest_0_), channel_id=1, source_target_pairs={{0,8},{4,12},{8,0},{12,4},{1,9},{5,13},{9,1},{13,5},{2,10},{6,14},... | collective-permute-start | bytes 294920 | tf_op jit(solution)/shard_map/ppermute | solution.py:454
  41.8 4.1 %collective-permute-done.16.rest_2_ = bf16[1,16,24,128]{3,2,1,0:T(8,128)(2,1)S(1)} collective-permute-done((bf16[1,16,24,128]{3,2,1,0:T(8,128)(2,1)S(1)}, bf16[1,16,24,128]{3,2,1,0:T(8,128)(2,1)S(1)}, u32[]{:S(2)}, u32[]{:S(2)}) %collective-permute-start.16) | collective-permute-done | bytes 98336 | tf_op jit(solution)/shard_map/ppermute | solution.py:454
  45.9 0.9 collective-permute-done.14
  46.7 0.1 collective-permute-done.8.refs_0_.refs_2_
  46.8 0.1 add_convert_fusion.5
  46.9 2.5 %collective-permute-start.20 = (bf16[1,16,24,128]{3,2,1,0:T(8,128)(2,1)S(1)}, bf16[1,16,24,128]{3,2,1,0:T(8,128)(2,1)S(1)}, u32[]{:S(2)}, u32[]{:S(2)}) collective-permute-start(bf16[1,16,24,128]{3,2,1,0:T(8,128)(2,1)S(1)} %get-tuple-element.95), channel_id=1, source_target_pairs={{0,8},{4,12},{8,0},{12,4},{1,9},{5,13},{9,1},{13,5},{2,10},{6,14},... | collective-permute-start | bytes 294920 | tf_op jit(solution)/shard_map/ppermute | solution.py:454
  49.4 1.8 %collective-permute-start.18 = (bf16[2,16,24,128]{3,2,1,0:T(8,128)(2,1)S(1)}, bf16[2,16,24,128]{3,2,1,0:T(8,128)(2,1)S(1)}, u32[]{:S(2)}, u32[]{:S(2)}) collective-permute-start(bf16[2,16,24,128]{3,2,1,0:T(8,128)(2,1)S(1)} %pad_maximum_fusion.7), channel_id=1, source_target_pairs={{0,4},{4,0},{8,12},{12,8},{1,5},{5,1},{9,13},{13,9},{2,6},{6,2},{1... | collective-permute-start | bytes 589832 | tf_op jit(solution)/shard_map/ppermute | solution.py:454
  51.3 0.1 pad_maximum_fusion
  51.3 0.1 collective-permute-start.15
  51.5 0.6 collective-permute-start.19
  52.0 4.6 %collective-permute-done.18 = bf16[2,16,24,128]{3,2,1,0:T(8,128)(2,1)S(1)} collective-permute-done((bf16[2,16,24,128]{3,2,1,0:T(8,128)(2,1)S(1)}, bf16[2,16,24,128]{3,2,1,0:T(8,128)(2,1)S(1)}, u32[]{:S(2)}, u32[]{:S(2)}) %collective-permute-start.18) | collective-permute-done | bytes 196640 | tf_op jit(solution)/shard_map/ppermute | solution.py:454
  56.8 0.1 constant_dynamic-update-slice_fusion.5
  56.9 2.1 %backward_step.3 = (bf16[4,16,24,128]{3,2,1,0:T(8,128)(2,1)S(1)}, bf16[4,16,24,128]{3,2,1,0:T(8,128)(2,1)S(1)}) custom-call(s32[2]{0:T(128)S(1)} %pad_add_fusion.meta, s32[3,64]{1,0:T(4,128)S(1)} %bitcast.23, s32[3,64]{1,0:T(4,128)S(1)} %collective-permute-done.9.cols_other, bf16[32,3,128,128]{3,2,1,0:T(8,128)(2,1)S(1)} %get-tuple-element.55.own, ...), custom_call_target="tpu_custom_call" | custom-call | flops 805306368 | bytes 25165824 | tf_op jit(solution)/shard_map/backward_step/pallas_call | solution.py:353
  58.9 0.1 collective-permute-start.23
  59.0 0.5 collective-permute-start.22
  59.5 1.6 %collective-permute-start.21 = (bf16[5,16,24,128]{3,2,1,0:T(8,128)(2,1)S(1)}, bf16[5,16,24,128]{3,2,1,0:T(8,128)(2,1)S(1)}, u32[]{:S(2)}, u32[]{:S(2)}) collective-permute-start(bf16[5,16,24,128]{3,2,1,0:T(8,128)(2,1)S(1)} %get-tuple-element.85), channel_id=1, source_target_pairs={{0,2},{2,0},{1,3},{3,1},{4,6},{6,4},{5,7},{7,5},{8,10},{10,8},{9,1... | collective-permute-start | bytes 1474568 | tf_op jit(solution)/shard_map/ppermute | solution.py:459
  61.1 2.8 %forward_step.3 = (bf16[256,16,128]{2,1,0:T(8,128)(2,1)S(1)}, bf16[1,16,24,128]{3,2,1,0:T(8,128)(2,1)S(1)}) custom-call(s32[2]{0:T(128)S(1)} %pad_add_fusion.meta, s32[3,64]{1,0:T(4,128)S(1)} %bitcast.24, s32[3,64]{1,0:T(4,128)S(1)} %collective-permute-done.9.cols_other, bf16[32,3,128,128]{3,2,1,0:T(8,128)(2,1)S(1)} %get-tuple-element.55.own, ...), custom_call_target="tpu_custom_call" | custom-call | flops 805306368 | bytes 25165824 | tf_op jit(solution)/shard_map/forward_step/pallas_call | solution.py:271
  64.0 1.5 %collective-permute-start.24 = (bf16[2,16,24,128]{3,2,1,0:T(8,128)(2,1)S(1)}, bf16[2,16,24,128]{3,2,1,0:T(8,128)(2,1)S(1)}, u32[]{:S(2)}, u32[]{:S(2)}) collective-permute-start(bf16[2,16,24,128]{3,2,1,0:T(8,128)(2,1)S(1)} %pad_maximum_fusion.9), channel_id=1, source_target_pairs={{0,4},{4,0},{8,12},{12,8},{1,5},{5,1},{9,13},{13,9},{2,6},{6,2},{1... | collective-permute-start | bytes 589832 | tf_op jit(solution)/shard_map/ppermute | solution.py:454
  65.5 1.9 %collective-permute-start.26 = (bf16[1,16,24,128]{3,2,1,0:T(8,128)(2,1)S(1)}, bf16[1,16,24,128]{3,2,1,0:T(8,128)(2,1)S(1)}, u32[]{:S(2)}, u32[]{:S(2)}) collective-permute-start(bf16[1,16,24,128]{3,2,1,0:T(8,128)(2,1)S(1)} %get-tuple-element.68.refs_0_), channel_id=1, source_target_pairs={{0,8},{4,12},{8,0},{12,4},{1,9},{5,13},{9,1},{13,5},{2,10},{6,14},... | collective-permute-start | bytes 294920 | tf_op jit(solution)/shard_map/ppermute | solution.py:454
  67.4 4.7 %collective-permute-done.26.refs_2_ = bf16[1,16,24,128]{3,2,1,0:T(8,128)(2,1)S(1)} collective-permute-done((bf16[1,16,24,128]{3,2,1,0:T(8,128)(2,1)S(1)}, bf16[1,16,24,128]{3,2,1,0:T(8,128)(2,1)S(1)}, u32[]{:S(2)}, u32[]{:S(2)}) %collective-permute-start.26) | collective-permute-done | bytes 98336 | tf_op jit(solution)/shard_map/ppermute | solution.py:454
  72.1 0.8 collective-permute-done.24
  72.9 0.1 collective-permute-start.25
  73.0 0.1 add_convert_fusion.1
  73.1 1.9 %collective-permute-start.28 = (bf16[2,16,24,128]{3,2,1,0:T(8,128)(2,1)S(1)}, bf16[2,16,24,128]{3,2,1,0:T(8,128)(2,1)S(1)}, u32[]{:S(2)}, u32[]{:S(2)}) collective-permute-start(bf16[2,16,24,128]{3,2,1,0:T(8,128)(2,1)S(1)} %pad_maximum_fusion.10), channel_id=1, source_target_pairs={{0,4},{4,0},{8,12},{12,8},{1,5},{5,1},{9,13},{13,9},{2,6},{6,2},{1... | collective-permute-start | bytes 589832 | tf_op jit(solution)/shard_map/ppermute | solution.py:454
  75.0 0.3 collective-permute-start.29
  75.3 1.7 %collective-permute-start.31 = (bf16[1,16,24,128]{3,2,1,0:T(8,128)(2,1)S(1)}, bf16[1,16,24,128]{3,2,1,0:T(8,128)(2,1)S(1)}, u32[]{:S(2)}, u32[]{:S(2)}) collective-permute-start(bf16[1,16,24,128]{3,2,1,0:T(8,128)(2,1)S(1)} %get-tuple-element.93), channel_id=1, source_target_pairs={{0,8},{4,12},{8,0},{12,4},{1,9},{5,13},{9,1},{13,5},{2,10},{6,14},... | collective-permute-start | bytes 294920 | tf_op jit(solution)/shard_map/ppermute | solution.py:454
  77.1 1.5 %collective-permute-start.33 = (bf16[3,16,24,128]{3,2,1,0:T(8,128)(2,1)S(1)}, bf16[3,16,24,128]{3,2,1,0:T(8,128)(2,1)S(1)}, u32[]{:S(2)}, u32[]{:S(2)}) collective-permute-start(bf16[3,16,24,128]{3,2,1,0:T(8,128)(2,1)S(1)} %pad_maximum_fusion.2), channel_id=1, source_target_pairs={{0,2},{2,0},{1,3},{3,1},{4,6},{6,4},{5,7},{7,5},{8,10},{10,8},{9,1... | collective-permute-start | bytes 884744 | tf_op jit(solution)/shard_map/ppermute | solution.py:459
  78.5 4.1 %collective-permute-done.28 = bf16[2,16,24,128]{3,2,1,0:T(8,128)(2,1)S(1)} collective-permute-done((bf16[2,16,24,128]{3,2,1,0:T(8,128)(2,1)S(1)}, bf16[2,16,24,128]{3,2,1,0:T(8,128)(2,1)S(1)}, u32[]{:S(2)}, u32[]{:S(2)}) %collective-permute-start.28) | collective-permute-done | bytes 196640 | tf_op jit(solution)/shard_map/ppermute | solution.py:454
  82.7 0.1 add_convert_fusion.refs_7_
  82.8 1.6 %collective-permute-start.34 = (bf16[2,16,24,128]{3,2,1,0:T(8,128)(2,1)S(1)}, bf16[2,16,24,128]{3,2,1,0:T(8,128)(2,1)S(1)}, u32[]{:S(2)}, u32[]{:S(2)}) collective-permute-start(bf16[2,16,24,128]{3,2,1,0:T(8,128)(2,1)S(1)} %pad_maximum_fusion.12), channel_id=1, source_target_pairs={{0,2},{2,0},{1,3},{3,1},{4,6},{6,4},{5,7},{7,5},{8,10},{10,8},{9,1... | collective-permute-start | bytes 589832 | tf_op jit(solution)/shard_map/ppermute | solution.py:459
  84.4 0.5 collective-permute-start.32
  84.9 2.0 %collective-permute-done.33.refs_0_ = bf16[3,16,24,128]{3,2,1,0:T(8,128)(2,1)S(1)} collective-permute-done((bf16[3,16,24,128]{3,2,1,0:T(8,128)(2,1)S(1)}, bf16[3,16,24,128]{3,2,1,0:T(8,128)(2,1)S(1)}, u32[]{:S(2)}, u32[]{:S(2)}) %collective-permute-start.33) | collective-permute-done | bytes 294944 | tf_op jit(solution)/shard_map/ppermute | solution.py:459
  86.8 0.8 unpack_panels.5.refs_1_.refs_15_
  87.7 1.0 %unpack_panels.6 = (bf16[256,16,128]{2,1,0:T(8,128)(2,1)S(1)}, bf16[64,16,128]{2,1,0:T(8,128)(2,1)S(1)}, bf16[64,16,128]{2,1,0:T(8,128)(2,1)S(1)}) custom-call(s32[2]{0:T(128)S(1)} %pad_add_fusion.meta, bf16[5,16,24,128]{3,2,1,0:T(8,128)(2,1)S(1)} %collective-permute-done.8.refs_0_.refs_2_, ...), custom_call_target="tpu_custom_call" | custom-call | tf_op jit(solution)/shard_map/unpack_panels/pallas_call | solution.py:80
  88.7 1.0 %unpack_panels.7 = (bf16[256,16,128]{2,1,0:T(8,128)(2,1)S(1)}, bf16[64,16,128]{2,1,0:T(8,128)(2,1)S(1)}, bf16[64,16,128]{2,1,0:T(8,128)(2,1)S(1)}) custom-call(s32[2]{0:T(128)S(1)} %pad_add_fusion.meta, bf16[5,16,24,128]{3,2,1,0:T(8,128)(2,1)S(1)} %collective-permute-done.21.refs_0_.refs_2_, ...), custom_call_target="tpu_custom_call" | custom-call | tf_op jit(solution)/shard_map/unpack_panels/pallas_call | solution.py:80
  89.7 0.9 unpack_panels.8
  90.6 0.6 collective-permute-start.36
  91.2 1.1 %collective-permute-done.36.refs_3_.refs_5_ = bf16[2,16,24,128]{3,2,1,0:T(8,128)(2,1)S(1)} collective-permute-done((bf16[2,16,24,128]{3,2,1,0:T(8,128)(2,1)S(1)}, bf16[2,16,24,128]{3,2,1,0:T(8,128)(2,1)S(1)}, u32[]{:S(2)}, u32[]{:S(2)}) %collective-permute-start.36) | collective-permute-done | bytes 196640 | tf_op jit(solution)/shard_map/ppermute | solution.py:451
  92.2 0.9 unpack_panels.9
  93.1 3.7 %gradient.1 = bf16[64,3,128,128]{3,2,1,0:T(8,128)(2,1)} custom-call(s32[2]{0:T(128)S(1)} %pad_add_fusion.meta, s32[3,64]{1,0:T(4,128)S(1)} %bitcast.25, bf16[256,16,128]{2,1,0:T(8,128)(2,1)S(1)} %get-tuple-element.45.refs_0_.refs_14_, bf16[256,16,128]{2,1,0:T(8,128)(2,1)S(1)} %unpack_panels.5.refs_1_.refs_15_, ...), custom_call_target="tpu_custom_call" | custom-call | tf_op jit(solution)/shard_map/gradient/pallas_call | solution.py:413
  (56 shorter events, 0.7 us)
Async XLA Ops:
  0.1 16.9 %copy-start = (s32[64,3]{0,1:T(4,128)S(1)}, s32[64,3]{0,1:T(4,128)}, u32[]{:S(2)}) copy-start(s32[64,3]{0,1:T(4,128)} %param.4) | copy-start | bytes 2308
  7.5 2.0 %collective-permute-start = (bf16[5,16,24,128]{3,2,1,0:T(8,128)(2,1)S(1)}, bf16[5,16,24,128]{3,2,1,0:T(8,128)(2,1)S(1)}, u32[]{:S(2)}, u32[]{:S(2)}) collective-permute-start(bf16[5,16,24,128]{3,2,1,0:T(8,128)(2,1)S(1)} %get-tuple-element.49), channel_id=1, source_target_pairs={{0,1},{1,0},{2,3},{3,2},{4,5},{5,4},{6,7},{7,6},{8,9},{9,8},{10,11... | collective-permute-start | bytes 1474568 | tf_op jit(solution)/shard_map/ppermute | solution.py:451
  9.6 20.9 %collective-permute-start.10 = (bf16[32,3,128,128]{3,2,1,0:T(8,128)(2,1)S(1)}, bf16[32,3,128,128]{3,2,1,0:T(8,128)(2,1)S(1)}, u32[]{:S(2)}, u32[]{:S(2)}) collective-permute-start(bf16[32,3,128,128]{3,2,1,0:T(8,128)(2,1)S(1)} %get-tuple-element.57), channel_id=1, source_target_pairs={{0,1},{1,0},{2,3},{3,2},{4,5},{5,4},{6,7},{7,6},{8,9},{9,8},{10,11... | collective-permute-start | bytes 9437192 | tf_op jit(solution)/shard_map/ppermute | solution.py:451
  10.1 10.3 %collective-permute-start.2 = (bf16[2,16,24,128]{3,2,1,0:T(8,128)(2,1)S(1)}, bf16[2,16,24,128]{3,2,1,0:T(8,128)(2,1)S(1)}, u32[]{:S(2)}, u32[]{:S(2)}) collective-permute-start(bf16[2,16,24,128]{3,2,1,0:T(8,128)(2,1)S(1)} %pad_maximum_fusion.3), channel_id=1, source_target_pairs={{0,4},{4,0},{8,12},{12,8},{1,5},{5,1},{9,13},{13,9},{2,6},{6,2},{1... | collective-permute-start | bytes 589832 | tf_op jit(solution)/shard_map/ppermute | solution.py:454
  12.9 4.2 %collective-permute-start.5 = (bf16[1,16,24,128]{3,2,1,0:T(8,128)(2,1)S(1)}, bf16[1,16,24,128]{3,2,1,0:T(8,128)(2,1)S(1)}, u32[]{:S(2)}, u32[]{:S(2)}) collective-permute-start(bf16[1,16,24,128]{3,2,1,0:T(8,128)(2,1)S(1)} %get-tuple-element.90.rest_0_), channel_id=1, source_target_pairs={{0,1},{1,0},{2,3},{3,2},{4,5},{5,4},{6,7},{7,6},{8,9},{9,8},{10,11... | collective-permute-start | bytes 294920 | tf_op jit(solution)/shard_map/ppermute | solution.py:451
  12.9 6.7 %collective-permute-start.4 = (bf16[1,16,24,128]{3,2,1,0:T(8,128)(2,1)S(1)}, bf16[1,16,24,128]{3,2,1,0:T(8,128)(2,1)S(1)}, u32[]{:S(2)}, u32[]{:S(2)}) collective-permute-start(bf16[1,16,24,128]{3,2,1,0:T(8,128)(2,1)S(1)} %get-tuple-element.90.rest_0_), channel_id=1, source_target_pairs={{0,8},{4,12},{8,0},{12,4},{1,9},{5,13},{9,1},{13,5},{2,10},{6,14},... | collective-permute-start | bytes 294920 | tf_op jit(solution)/shard_map/ppermute | solution.py:454
  15.5 11.2 %collective-permute-start.1 = (bf16[4,16,24,128]{3,2,1,0:T(8,128)(2,1)S(1)}, bf16[4,16,24,128]{3,2,1,0:T(8,128)(2,1)S(1)}, u32[]{:S(2)}, u32[]{:S(2)}) collective-permute-start(bf16[4,16,24,128]{3,2,1,0:T(8,128)(2,1)S(1)} %get-tuple-element.50), channel_id=1, source_target_pairs={{0,2},{2,0},{1,3},{3,1},{4,6},{6,4},{5,7},{7,5},{8,10},{10,8},{9,1... | collective-permute-start | bytes 1179656 | tf_op jit(solution)/shard_map/ppermute | solution.py:459
  17.0 13.4 %collective-permute-start.9 = (s32[3,64]{1,0:T(4,128)S(1)}, s32[3,64]{1,0:T(4,128)S(1)}, u32[]{:S(2)}, u32[]{:S(2)}) collective-permute-start(s32[3,64]{1,0:T(4,128)S(1)} %bitcast.20), channel_id=1, source_target_pairs={{0,1},{1,0},{2,3},{3,2},{4,5},{5,4},{6,7},{7,6},{8,9},{9,8},{10,11... | collective-permute-start | bytes 2312 | tf_op jit(solution)/shard_map/ppermute | solution.py:451
  20.5 9.8 %collective-permute-start.7 = (bf16[1,16,24,128]{3,2,1,0:T(8,128)(2,1)S(1)}, bf16[1,16,24,128]{3,2,1,0:T(8,128)(2,1)S(1)}, u32[]{:S(2)}, u32[]{:S(2)}) collective-permute-start(bf16[1,16,24,128]{3,2,1,0:T(8,128)(2,1)S(1)} %get-tuple-element.91), channel_id=1, source_target_pairs={{0,8},{4,12},{8,0},{12,4},{1,9},{5,13},{9,1},{13,5},{2,10},{6,14},... | collective-permute-start | bytes 294920 | tf_op jit(solution)/shard_map/ppermute | solution.py:454
  23.2 7.1 %collective-permute-start.6 = (bf16[2,16,24,128]{3,2,1,0:T(8,128)(2,1)S(1)}, bf16[2,16,24,128]{3,2,1,0:T(8,128)(2,1)S(1)}, u32[]{:S(2)}, u32[]{:S(2)}) collective-permute-start(bf16[2,16,24,128]{3,2,1,0:T(8,128)(2,1)S(1)} %pad_maximum_fusion.4), channel_id=1, source_target_pairs={{0,4},{4,0},{8,12},{12,8},{1,5},{5,1},{9,13},{13,9},{2,6},{6,2},{1... | collective-permute-start | bytes 589832 | tf_op jit(solution)/shard_map/ppermute | solution.py:454
  26.7 3.6 %collective-permute-start.3 = (bf16[4,16,24,128]{3,2,1,0:T(8,128)(2,1)S(1)}, bf16[4,16,24,128]{3,2,1,0:T(8,128)(2,1)S(1)}, u32[]{:S(2)}, u32[]{:S(2)}) collective-permute-start(bf16[4,16,24,128]{3,2,1,0:T(8,128)(2,1)S(1)} %collective-permute-done.1.refs_0_), channel_id=1, source_target_pairs={{0,1},{1,0},{2,3},{3,2},{4,5},{5,4},{6,7},{7,6},{8,9},{9,8},{10,11... | collective-permute-start | bytes 1179656 | tf_op jit(solution)/shard_map/ppermute | solution.py:451
  32.5 5.0 %collective-permute-start.13 = (bf16[4,16,24,128]{3,2,1,0:T(8,128)(2,1)S(1)}, bf16[4,16,24,128]{3,2,1,0:T(8,128)(2,1)S(1)}, u32[]{:S(2)}, u32[]{:S(2)}) collective-permute-start(bf16[4,16,24,128]{3,2,1,0:T(8,128)(2,1)S(1)} %get-tuple-element.58.rest_7_), channel_id=1, source_target_pairs={{0,1},{1,0},{2,3},{3,2},{4,5},{5,4},{6,7},{7,6},{8,9},{9,8},{10,11... | collective-permute-start | bytes 1179656 | tf_op jit(solution)/shard_map/ppermute | solution.py:451
  32.6 2.3 %collective-permute-start.11 = (bf16[2,16,24,128]{3,2,1,0:T(8,128)(2,1)S(1)}, bf16[2,16,24,128]{3,2,1,0:T(8,128)(2,1)S(1)}, u32[]{:S(2)}, u32[]{:S(2)}) collective-permute-start(bf16[2,16,24,128]{3,2,1,0:T(8,128)(2,1)S(1)} %pad_maximum_fusion.5), channel_id=1, source_target_pairs={{0,1},{1,0},{2,3},{3,2},{4,5},{5,4},{6,7},{7,6},{8,9},{9,8},{10,11... | collective-permute-start | bytes 589832 | tf_op jit(solution)/shard_map/ppermute | solution.py:451
  33.2 1.7 %collective-permute-start.12 = (bf16[1,16,24,128]{3,2,1,0:T(8,128)(2,1)S(1)}, bf16[1,16,24,128]{3,2,1,0:T(8,128)(2,1)S(1)}, u32[]{:S(2)}, u32[]{:S(2)}) collective-permute-start(bf16[1,16,24,128]{3,2,1,0:T(8,128)(2,1)S(1)} %get-tuple-element.101.rest_3_), channel_id=1, source_target_pairs={{0,1},{1,0},{2,3},{3,2},{4,5},{5,4},{6,7},{7,6},{8,9},{9,8},{10,11... | collective-permute-start | bytes 294920 | tf_op jit(solution)/shard_map/ppermute | solution.py:451
  33.2 13.6 %collective-permute-start.8 = (bf16[5,16,24,128]{3,2,1,0:T(8,128)(2,1)S(1)}, bf16[5,16,24,128]{3,2,1,0:T(8,128)(2,1)S(1)}, u32[]{:S(2)}, u32[]{:S(2)}) collective-permute-start(bf16[5,16,24,128]{3,2,1,0:T(8,128)(2,1)S(1)} %get-tuple-element.87), channel_id=1, source_target_pairs={{0,2},{2,0},{1,3},{3,1},{4,6},{6,4},{5,7},{7,5},{8,10},{10,8},{9,1... | collective-permute-start | bytes 1474568 | tf_op jit(solution)/shard_map/ppermute | solution.py:459
  37.6 9.1 %collective-permute-start.14 = (bf16[2,16,24,128]{3,2,1,0:T(8,128)(2,1)S(1)}, bf16[2,16,24,128]{3,2,1,0:T(8,128)(2,1)S(1)}, u32[]{:S(2)}, u32[]{:S(2)}) collective-permute-start(bf16[2,16,24,128]{3,2,1,0:T(8,128)(2,1)S(1)} %pad_maximum_fusion.6), channel_id=1, source_target_pairs={{0,4},{4,0},{8,12},{12,8},{1,5},{5,1},{9,13},{13,9},{2,6},{6,2},{1... | collective-permute-start | bytes 589832 | tf_op jit(solution)/shard_map/ppermute | solution.py:454
  39.3 2.5 %collective-permute-start.17 = (bf16[1,16,24,128]{3,2,1,0:T(8,128)(2,1)S(1)}, bf16[1,16,24,128]{3,2,1,0:T(8,128)(2,1)S(1)}, u32[]{:S(2)}, u32[]{:S(2)}) collective-permute-start(bf16[1,16,24,128]{3,2,1,0:T(8,128)(2,1)S(1)} %get-tuple-element.59.rest_0_), channel_id=1, source_target_pairs={{0,1},{1,0},{2,3},{3,2},{4,5},{5,4},{6,7},{7,6},{8,9},{9,8},{10,11... | collective-permute-start | bytes 294920 | tf_op jit(solution)/shard_map/ppermute | solution.py:451
  39.3 6.6 %collective-permute-start.16 = (bf16[1,16,24,128]{3,2,1,0:T(8,128)(2,1)S(1)}, bf16[1,16,24,128]{3,2,1,0:T(8,128)(2,1)S(1)}, u32[]{:S(2)}, u32[]{:S(2)}) collective-permute-start(bf16[1,16,24,128]{3,2,1,0:T(8,128)(2,1)S(1)} %get-tuple-element.59.rest_0_), channel_id=1, source_target_pairs={{0,8},{4,12},{8,0},{12,4},{1,9},{5,13},{9,1},{13,5},{2,10},{6,14},... | collective-permute-start | bytes 294920 | tf_op jit(solution)/shard_map/ppermute | solution.py:454
  46.9 9.9 %collective-permute-start.20 = (bf16[1,16,24,128]{3,2,1,0:T(8,128)(2,1)S(1)}, bf16[1,16,24,128]{3,2,1,0:T(8,128)(2,1)S(1)}, u32[]{:S(2)}, u32[]{:S(2)}) collective-permute-start(bf16[1,16,24,128]{3,2,1,0:T(8,128)(2,1)S(1)} %get-tuple-element.95), channel_id=1, source_target_pairs={{0,8},{4,12},{8,0},{12,4},{1,9},{5,13},{9,1},{13,5},{2,10},{6,14},... | collective-permute-start | bytes 294920 | tf_op jit(solution)/shard_map/ppermute | solution.py:454
  49.4 7.3 %collective-permute-start.18 = (bf16[2,16,24,128]{3,2,1,0:T(8,128)(2,1)S(1)}, bf16[2,16,24,128]{3,2,1,0:T(8,128)(2,1)S(1)}, u32[]{:S(2)}, u32[]{:S(2)}) collective-permute-start(bf16[2,16,24,128]{3,2,1,0:T(8,128)(2,1)S(1)} %pad_maximum_fusion.7), channel_id=1, source_target_pairs={{0,4},{4,0},{8,12},{12,8},{1,5},{5,1},{9,13},{13,9},{2,6},{6,2},{1... | collective-permute-start | bytes 589832 | tf_op jit(solution)/shard_map/ppermute | solution.py:454
  51.3 5.4 %collective-permute-start.15 = (bf16[6,16,24,128]{3,2,1,0:T(8,128)(2,1)S(1)}, bf16[6,16,24,128]{3,2,1,0:T(8,128)(2,1)S(1)}, u32[]{:S(2)}, u32[]{:S(2)}) collective-permute-start(bf16[6,16,24,128]{3,2,1,0:T(8,128)(2,1)S(1)} %pad_maximum_fusion), channel_id=1, source_target_pairs={{0,1},{1,0},{2,3},{3,2},{4,5},{5,4},{6,7},{7,6},{8,9},{9,8},{10,11... | collective-permute-start | bytes 1769480 | tf_op jit(solution)/shard_map/ppermute | solution.py:451
  51.5 5.3 %collective-permute-start.19 = (bf16[2,16,24,128]{3,2,1,0:T(8,128)(2,1)S(1)}, bf16[2,16,24,128]{3,2,1,0:T(8,128)(2,1)S(1)}, u32[]{:S(2)}, u32[]{:S(2)}) collective-permute-start(bf16[2,16,24,128]{3,2,1,0:T(8,128)(2,1)S(1)} %pad_maximum_fusion.8), channel_id=1, source_target_pairs={{0,1},{1,0},{2,3},{3,2},{4,5},{5,4},{6,7},{7,6},{8,9},{9,8},{10,11... | collective-permute-start | bytes 589832 | tf_op jit(solution)/shard_map/ppermute | solution.py:451
  58.9 5.0 %collective-permute-start.23 = (bf16[4,16,24,128]{3,2,1,0:T(8,128)(2,1)S(1)}, bf16[4,16,24,128]{3,2,1,0:T(8,128)(2,1)S(1)}, u32[]{:S(2)}, u32[]{:S(2)}) collective-permute-start(bf16[4,16,24,128]{3,2,1,0:T(8,128)(2,1)S(1)} %get-tuple-element.67.rest_7_), channel_id=1, source_target_pairs={{0,1},{1,0},{2,3},{3,2},{4,5},{5,4},{6,7},{7,6},{8,9},{9,8},{10,11... | collective-permute-start | bytes 1179656 | tf_op jit(solution)/shard_map/ppermute | solution.py:451
  59.0 2.1 %collective-permute-start.22 = (bf16[1,16,24,128]{3,2,1,0:T(8,128)(2,1)S(1)}, bf16[1,16,24,128]{3,2,1,0:T(8,128)(2,1)S(1)}, u32[]{:S(2)}, u32[]{:S(2)}) collective-permute-start(bf16[1,16,24,128]{3,2,1,0:T(8,128)(2,1)S(1)} %get-tuple-element.97.rest_3_), channel_id=1, source_target_pairs={{0,1},{1,0},{2,3},{3,2},{4,5},{5,4},{6,7},{7,6},{8,9},{9,8},{10,11... | collective-permute-start | bytes 294920 | tf_op jit(solution)/shard_map/ppermute | solution.py:451
  59.5 13.4 %collective-permute-start.21 = (bf16[5,16,24,128]{3,2,1,0:T(8,128)(2,1)S(1)}, bf16[5,16,24,128]{3,2,1,0:T(8,128)(2,1)S(1)}, u32[]{:S(2)}, u32[]{:S(2)}) collective-permute-start(bf16[5,16,24,128]{3,2,1,0:T(8,128)(2,1)S(1)} %get-tuple-element.85), channel_id=1, source_target_pairs={{0,2},{2,0},{1,3},{3,1},{4,6},{6,4},{5,7},{7,5},{8,10},{10,8},{9,1... | collective-permute-start | bytes 1474568 | tf_op jit(solution)/shard_map/ppermute | solution.py:459
  64.0 8.9 %collective-permute-start.24 = (bf16[2,16,24,128]{3,2,1,0:T(8,128)(2,1)S(1)}, bf16[2,16,24,128]{3,2,1,0:T(8,128)(2,1)S(1)}, u32[]{:S(2)}, u32[]{:S(2)}) collective-permute-start(bf16[2,16,24,128]{3,2,1,0:T(8,128)(2,1)S(1)} %pad_maximum_fusion.9), channel_id=1, source_target_pairs={{0,4},{4,0},{8,12},{12,8},{1,5},{5,1},{9,13},{13,9},{2,6},{6,2},{1... | collective-permute-start | bytes 589832 | tf_op jit(solution)/shard_map/ppermute | solution.py:454
  65.5 1.9 %collective-permute-start.27 = (bf16[1,16,24,128]{3,2,1,0:T(8,128)(2,1)S(1)}, bf16[1,16,24,128]{3,2,1,0:T(8,128)(2,1)S(1)}, u32[]{:S(2)}, u32[]{:S(2)}) collective-permute-start(bf16[1,16,24,128]{3,2,1,0:T(8,128)(2,1)S(1)} %get-tuple-element.68.refs_0_), channel_id=1, source_target_pairs={{0,1},{1,0},{2,3},{3,2},{4,5},{5,4},{6,7},{7,6},{8,9},{9,8},{10,11... | collective-permute-start | bytes 294920 | tf_op jit(solution)/shard_map/ppermute | solution.py:451
  65.5 6.6 %collective-permute-start.26 = (bf16[1,16,24,128]{3,2,1,0:T(8,128)(2,1)S(1)}, bf16[1,16,24,128]{3,2,1,0:T(8,128)(2,1)S(1)}, u32[]{:S(2)}, u32[]{:S(2)}) collective-permute-start(bf16[1,16,24,128]{3,2,1,0:T(8,128)(2,1)S(1)} %get-tuple-element.68.refs_0_), channel_id=1, source_target_pairs={{0,8},{4,12},{8,0},{12,4},{1,9},{5,13},{9,1},{13,5},{2,10},{6,14},... | collective-permute-start | bytes 294920 | tf_op jit(solution)/shard_map/ppermute | solution.py:454
  72.9 9.8 %collective-permute-start.25 = (bf16[6,16,24,128]{3,2,1,0:T(8,128)(2,1)S(1)}, bf16[6,16,24,128]{3,2,1,0:T(8,128)(2,1)S(1)}, u32[]{:S(2)}, u32[]{:S(2)}) collective-permute-start(bf16[6,16,24,128]{3,2,1,0:T(8,128)(2,1)S(1)} %pad_maximum_fusion.1), channel_id=1, source_target_pairs={{0,1},{1,0},{2,3},{3,2},{4,5},{5,4},{6,7},{7,6},{8,9},{9,8},{10,11... | collective-permute-start | bytes 1769480 | tf_op jit(solution)/shard_map/ppermute | solution.py:451
  73.1 9.5 %collective-permute-start.28 = (bf16[2,16,24,128]{3,2,1,0:T(8,128)(2,1)S(1)}, bf16[2,16,24,128]{3,2,1,0:T(8,128)(2,1)S(1)}, u32[]{:S(2)}, u32[]{:S(2)}) collective-permute-start(bf16[2,16,24,128]{3,2,1,0:T(8,128)(2,1)S(1)} %pad_maximum_fusion.10), channel_id=1, source_target_pairs={{0,4},{4,0},{8,12},{12,8},{1,5},{5,1},{9,13},{13,9},{2,6},{6,2},{1... | collective-permute-start | bytes 589832 | tf_op jit(solution)/shard_map/ppermute | solution.py:454
  75.0 7.6 %collective-permute-start.29 = (bf16[2,16,24,128]{3,2,1,0:T(8,128)(2,1)S(1)}, bf16[2,16,24,128]{3,2,1,0:T(8,128)(2,1)S(1)}, u32[]{:S(2)}, u32[]{:S(2)}) collective-permute-start(bf16[2,16,24,128]{3,2,1,0:T(8,128)(2,1)S(1)} %pad_maximum_fusion.11), channel_id=1, source_target_pairs={{0,1},{1,0},{2,3},{3,2},{4,5},{5,4},{6,7},{7,6},{8,9},{9,8},{10,11... | collective-permute-start | bytes 589832 | tf_op jit(solution)/shard_map/ppermute | solution.py:451
  75.3 7.4 %collective-permute-start.31 = (bf16[1,16,24,128]{3,2,1,0:T(8,128)(2,1)S(1)}, bf16[1,16,24,128]{3,2,1,0:T(8,128)(2,1)S(1)}, u32[]{:S(2)}, u32[]{:S(2)}) collective-permute-start(bf16[1,16,24,128]{3,2,1,0:T(8,128)(2,1)S(1)} %get-tuple-element.93), channel_id=1, source_target_pairs={{0,8},{4,12},{8,0},{12,4},{1,9},{5,13},{9,1},{13,5},{2,10},{6,14},... | collective-permute-start | bytes 294920 | tf_op jit(solution)/shard_map/ppermute | solution.py:454
  77.1 9.8 %collective-permute-start.33 = (bf16[3,16,24,128]{3,2,1,0:T(8,128)(2,1)S(1)}, bf16[3,16,24,128]{3,2,1,0:T(8,128)(2,1)S(1)}, u32[]{:S(2)}, u32[]{:S(2)}) collective-permute-start(bf16[3,16,24,128]{3,2,1,0:T(8,128)(2,1)S(1)} %pad_maximum_fusion.2), channel_id=1, source_target_pairs={{0,2},{2,0},{1,3},{3,1},{4,6},{6,4},{5,7},{7,5},{8,10},{10,8},{9,1... | collective-permute-start | bytes 884744 | tf_op jit(solution)/shard_map/ppermute | solution.py:459
  82.8 7.8 %collective-permute-start.34 = (bf16[2,16,24,128]{3,2,1,0:T(8,128)(2,1)S(1)}, bf16[2,16,24,128]{3,2,1,0:T(8,128)(2,1)S(1)}, u32[]{:S(2)}, u32[]{:S(2)}) collective-permute-start(bf16[2,16,24,128]{3,2,1,0:T(8,128)(2,1)S(1)} %pad_maximum_fusion.12), channel_id=1, source_target_pairs={{0,2},{2,0},{1,3},{3,1},{4,6},{6,4},{5,7},{7,5},{8,10},{10,8},{9,1... | collective-permute-start | bytes 589832 | tf_op jit(solution)/shard_map/ppermute | solution.py:459
  84.4 5.3 %collective-permute-start.30 = (bf16[1,16,24,128]{3,2,1,0:T(8,128)(2,1)S(1)}, bf16[1,16,24,128]{3,2,1,0:T(8,128)(2,1)S(1)}, u32[]{:S(2)}, u32[]{:S(2)}) collective-permute-start(bf16[1,16,24,128]{3,2,1,0:T(8,128)(2,1)S(1)} %slice.168.refs_3_), channel_id=1, source_target_pairs={{0,1},{1,0},{2,3},{3,2},{4,5},{5,4},{6,7},{7,6},{8,9},{9,8},{10,11... | collective-permute-start | bytes 294920 | tf_op jit(solution)/shard_map/ppermute | solution.py:451
  84.4 5.3 %collective-permute-start.32 = (bf16[1,16,24,128]{3,2,1,0:T(8,128)(2,1)S(1)}, bf16[1,16,24,128]{3,2,1,0:T(8,128)(2,1)S(1)}, u32[]{:S(2)}, u32[]{:S(2)}) collective-permute-start(bf16[1,16,24,128]{3,2,1,0:T(8,128)(2,1)S(1)} %add_convert_fusion.refs_7_), channel_id=1, source_target_pairs={{0,1},{1,0},{2,3},{3,2},{4,5},{5,4},{6,7},{7,6},{8,9},{9,8},{10,11... | collective-permute-start | bytes 294920 | tf_op jit(solution)/shard_map/ppermute | solution.py:451
  86.8 4.3 %collective-permute-start.35 = (bf16[3,16,24,128]{3,2,1,0:T(8,128)(2,1)S(1)}, bf16[3,16,24,128]{3,2,1,0:T(8,128)(2,1)S(1)}, u32[]{:S(2)}, u32[]{:S(2)}) collective-permute-start(bf16[3,16,24,128]{3,2,1,0:T(8,128)(2,1)S(1)} %collective-permute-done.33.refs_0_), channel_id=1, source_target_pairs={{0,1},{1,0},{2,3},{3,2},{4,5},{5,4},{6,7},{7,6},{8,9},{9,8},{10,11... | collective-permute-start | bytes 884744 | tf_op jit(solution)/shard_map/ppermute | solution.py:451
  90.6 1.6 %collective-permute-start.36 = (bf16[2,16,24,128]{3,2,1,0:T(8,128)(2,1)S(1)}, bf16[2,16,24,128]{3,2,1,0:T(8,128)(2,1)S(1)}, u32[]{:S(2)}, u32[]{:S(2)}) collective-permute-start(bf16[2,16,24,128]{3,2,1,0:T(8,128)(2,1)S(1)} %collective-permute-done.34.refs_1_.refs_4_), channel_id=1, source_target_pairs={{0,1},{1,0},{2,3},{3,2},{4,5},{5,4},{6,7},{7,6},{8,9},{9,8},{10,11... | collective-permute-start | bytes 589832 | tf_op jit(solution)/shard_map/ppermute | solution.py:451

commit v8 on v7

--- a/solution.py
+++ b/solution.py
@@ -539,14 +539,13 @@
             far = shift_var(updated, 2)
             both = shift_var(stack([updated, narrow(parts[3])]), 1)
             near = both[:1]
-            own_other = swap_rep(updated)
             crossed = shift_var(narrow(parts[2] + wide(both[1:])), 2)
-            final = shift_var(stack([tie(far, own_other), narrow(parts[1])]), 1)
+            final = shift_var(stack([far, narrow(parts[1])]), 1)
             last = final[:1]
-            middle_other = swap_rep(stack([near, far]))
+            middle_other = swap_rep(stack([updated, near, far]))
             summed = parts[0] + wide(final[1:]) + wide(crossed)
             held = [updated, near, far, last]
-            others = [(own_other, [0]), (middle_other, [1, 2]), (swap_rep(last), [3])]
+            others = [(middle_other, [0, 1, 2]), (swap_rep(last), [3])]
             window, settled = [both], [middle_other] if step > 0 else []
         else:
             bits = [1 << i for i in range(n_var.bit_length() - 1)]

time: 97.2 us -> 95 us (0.977)
  starting transfers between devices: 37.4 us -> 36 us
    ppermute x5, waiting for transfers between devices: 3.81 us -> 0.15 us  [from_probes(): lax.ppermute(x, 'probe', [(i, (i + d) % n_probe) for i in range(n_probe)])]
    ppermute x12, waiting for transfers between devices: 26 us -> 28.9 us  [shift_var(): return lax.ppermute(x, 'var', [(i, i ^ bit) for i in range(n_var)])]
    ppermute x12, starting transfers between devices: 25.4 us -> 22.8 us  [shift_var(): return lax.ppermute(x, 'var', [(i, i ^ bit) for i in range(n_var)])]
    ppermute x5, starting transfers between devices: 7.69 us -> 8.7 us  [from_probes(): lax.ppermute(x, 'probe', [(i, (i + d) % n_probe) for i in range(n_probe)])]
    ppermute x20 -> x17, starting transfers between devices: 4.38 us -> 4.51 us  [swap_rep(): return lax.ppermute(x, 'rep', [(0, 1), (1, 0)])]
    ppermute x20 -> x17, waiting for transfers between devices: 2.62 us -> 2.61 us  [swap_rep(): return lax.ppermute(x, 'rep', [(0, 1), (1, 0)])]
  transfers between devices with their start and end apart: 37 -> 34, of which waited for: 14 -> 9; matrix products, arithmetic and copies ran while one was open for 1% -> 1% of each run, Pallas kernels for 9% -> 10%
where the time goes in v8:
time: 95 us; the launch traced here: 94.9 us
  starting transfers between devices  36 us (38%)
  waiting for transfers between devices  31.7 us (33%)
  Pallas kernels  25.3 us (27%)
  other arithmetic  1.06 us (1%)
    ppermute x12, waiting for transfers between devices, shift_var(): return lax.ppermute(x, 'var', [(i, i ^ bit) for i in range(n_var)])  28.9 us
    ppermute x12, starting transfers between devices, shift_var(): return lax.ppermute(x, 'var', [(i, i ^ bit) for i in range(n_var)])  22.8 us
    ppermute x5, starting transfers between devices, from_probes(): lax.ppermute(x, 'probe', [(i, (i + d) % n_probe) for i in range(n_probe)])  8.7 us
    pallas_call x1, Pallas kernels, first_step(): pl.pallas_call(functools.partial(first_kernel, count, chunk, blocks), out...  7.42 us
    pallas_call x2, Pallas kernels, forward(): pl.pallas_call(functools.partial(forward_kernel, count, chunk, 2 * half,...  5.25 us
    pallas_call x5, Pallas kernels, unpack(): pl.pallas_call(functools.partial(unpack_kernel, count, wheres, len(tokens...  4.77 us
    ppermute x17, starting transfers between devices, swap_rep(): return lax.ppermute(x, 'rep', [(0, 1), (1, 0)])  4.51 us
    pallas_call x2, Pallas kernels, backward(): pl.pallas_call(functools.partial(backward_kernel, count, chunk), out_shap...  4.13 us
  transfers between devices with their start and end apart: 34, of which 9 were waited for; matrix products, arithmetic and copies ran while one was open for 1% of the time, Pallas kernels for 10%

profile of v8, /device:TPU:0, one launch (start us, length us, event | category | flops | bytes accessed | tf_op | source)
XLA Modules:
  0.0 94.9 jit_solution(15212395811226980888)
XLA Ops:
  0.0 0.1 pad_add_fusion.meta
  0.1 7.4 %first_step.1 = (bf16[256,16,128]{2,1,0:T(8,128)(2,1)S(1)}, bf16[4,16,24,128]{3,2,1,0:T(8,128)(2,1)S(1)}, bf16[1,16,24,128]{3,2,1,0:T(8,128)(2,1)S(1)}, f32[16,2...) custom-call(s32[2]{0:T(128)S(1)} %pad_add_fusion.meta, ...), custom_call_target="tpu_custom_call" | custom-call | flops 1610612736 | bytes 50331648 | tf_op jit(solution)/shard_map/first_step/pallas_call | solution.py:198
  7.5 0.5 collective-permute-start
  8.0 1.5 %collective-permute-done = bf16[5,16,24,128]{3,2,1,0:T(8,128)(2,1)S(1)} collective-permute-done((bf16[5,16,24,128]{3,2,1,0:T(8,128)(2,1)S(1)}, bf16[5,16,24,128]{3,2,1,0:T(8,128)(2,1)S(1)}, u32[]{:S(2)}, u32[]{:S(2)}) %collective-permute-start) | collective-permute-done | bytes 491552 | tf_op jit(solution)/shard_map/ppermute | solution.py:451
  9.6 0.4 collective-permute-start.9
  10.1 2.8 %collective-permute-start.2 = (bf16[2,16,24,128]{3,2,1,0:T(8,128)(2,1)S(1)}, bf16[2,16,24,128]{3,2,1,0:T(8,128)(2,1)S(1)}, u32[]{:S(2)}, u32[]{:S(2)}) collective-permute-start(bf16[2,16,24,128]{3,2,1,0:T(8,128)(2,1)S(1)} %pad_maximum_fusion.5), channel_id=1, source_target_pairs={{0,4},{4,0},{8,12},{12,8},{1,5},{5,1},{9,13},{13,9},{2,6},{6,2},{1... | collective-permute-start | bytes 589832 | tf_op jit(solution)/shard_map/ppermute | solution.py:454
  12.9 1.5 %collective-permute-start.1 = (bf16[4,16,24,128]{3,2,1,0:T(8,128)(2,1)S(1)}, bf16[4,16,24,128]{3,2,1,0:T(8,128)(2,1)S(1)}, u32[]{:S(2)}, u32[]{:S(2)}) collective-permute-start(bf16[4,16,24,128]{3,2,1,0:T(8,128)(2,1)S(1)} %get-tuple-element.47), channel_id=1, source_target_pairs={{0,2},{2,0},{1,3},{3,1},{4,6},{6,4},{5,7},{7,5},{8,10},{10,8},{9,1... | collective-permute-start | bytes 1179656 | tf_op jit(solution)/shard_map/ppermute | solution.py:459
  14.4 2.6 %collective-permute-start.4 = (bf16[1,16,24,128]{3,2,1,0:T(8,128)(2,1)S(1)}, bf16[1,16,24,128]{3,2,1,0:T(8,128)(2,1)S(1)}, u32[]{:S(2)}, u32[]{:S(2)}) collective-permute-start(bf16[1,16,24,128]{3,2,1,0:T(8,128)(2,1)S(1)} %get-tuple-element.84.rest_0_), channel_id=1, source_target_pairs={{0,8},{4,12},{8,0},{12,4},{1,9},{5,13},{9,1},{13,5},{2,10},{6,14},... | collective-permute-start | bytes 294920 | tf_op jit(solution)/shard_map/ppermute | solution.py:454
  16.9 1.3 %collective-permute-done.2 = bf16[2,16,24,128]{3,2,1,0:T(8,128)(2,1)S(1)} collective-permute-done((bf16[2,16,24,128]{3,2,1,0:T(8,128)(2,1)S(1)}, bf16[2,16,24,128]{3,2,1,0:T(8,128)(2,1)S(1)}, u32[]{:S(2)}, u32[]{:S(2)}) %collective-permute-start.2) | collective-permute-done | bytes 196640 | tf_op jit(solution)/shard_map/ppermute | solution.py:454
  18.3 0.1 add_convert_fusion.9
  18.4 3.4 %collective-permute-start.6 = (bf16[1,16,24,128]{3,2,1,0:T(8,128)(2,1)S(1)}, bf16[1,16,24,128]{3,2,1,0:T(8,128)(2,1)S(1)}, u32[]{:S(2)}, u32[]{:S(2)}) collective-permute-start(bf16[1,16,24,128]{3,2,1,0:T(8,128)(2,1)S(1)} %get-tuple-element.85), channel_id=1, source_target_pairs={{0,8},{4,12},{8,0},{12,4},{1,9},{5,13},{9,1},{13,5},{2,10},{6,14},... | collective-permute-start | bytes 294920 | tf_op jit(solution)/shard_map/ppermute | solution.py:454
  21.8 2.2 %collective-permute-start.5 = (bf16[2,16,24,128]{3,2,1,0:T(8,128)(2,1)S(1)}, bf16[2,16,24,128]{3,2,1,0:T(8,128)(2,1)S(1)}, u32[]{:S(2)}, u32[]{:S(2)}) collective-permute-start(bf16[2,16,24,128]{3,2,1,0:T(8,128)(2,1)S(1)} %pad_maximum_fusion.6), channel_id=1, source_target_pairs={{0,4},{4,0},{8,12},{12,8},{1,5},{5,1},{9,13},{13,9},{2,6},{6,2},{1... | collective-permute-start | bytes 589832 | tf_op jit(solution)/shard_map/ppermute | solution.py:454
  23.9 0.0 collective-permute-done.1.refs_0_
  24.0 5.2 %collective-permute-done.5 = bf16[2,16,24,128]{3,2,1,0:T(8,128)(2,1)S(1)} collective-permute-done((bf16[2,16,24,128]{3,2,1,0:T(8,128)(2,1)S(1)}, bf16[2,16,24,128]{3,2,1,0:T(8,128)(2,1)S(1)}, u32[]{:S(2)}, u32[]{:S(2)}) %collective-permute-start.5) | collective-permute-done | bytes 196640 | tf_op jit(solution)/shard_map/ppermute | solution.py:454
  29.2 0.1 constant_dynamic-update-slice_fusion
  29.4 2.1 %backward_step.2 = (bf16[4,16,24,128]{3,2,1,0:T(8,128)(2,1)S(1)}, bf16[4,16,24,128]{3,2,1,0:T(8,128)(2,1)S(1)}) custom-call(s32[2]{0:T(128)S(1)} %pad_add_fusion.meta, s32[3,64]{1,0:T(4,128)S(1)} %bitcast.21, s32[3,64]{1,0:T(4,128)S(1)} %collective-permute-done.8.cols_other, bf16[32,3,128,128]{3,2,1,0:T(8,128)(2,1)S(1)} %get-tuple-element.51.own, ...), custom_call_target="tpu_custom_call" | custom-call | flops 805306368 | bytes 25165824 | tf_op jit(solution)/shard_map/backward_step/pallas_call | solution.py:353
  31.4 0.1 collective-permute-start.12
  31.5 0.6 collective-permute-start.10
  32.1 0.1 collective-permute-start.11
  32.2 2.6 %collective-permute-start.7 = (bf16[5,16,24,128]{3,2,1,0:T(8,128)(2,1)S(1)}, bf16[5,16,24,128]{3,2,1,0:T(8,128)(2,1)S(1)}, u32[]{:S(2)}, u32[]{:S(2)}) collective-permute-start(bf16[5,16,24,128]{3,2,1,0:T(8,128)(2,1)S(1)} %get-tuple-element.81), channel_id=1, source_target_pairs={{0,2},{2,0},{1,3},{3,1},{4,6},{6,4},{5,7},{7,5},{8,10},{10,8},{9,1... | collective-permute-start | bytes 1474568 | tf_op jit(solution)/shard_map/ppermute | solution.py:459
  34.8 2.6 %forward_step.2 = (bf16[256,16,128]{2,1,0:T(8,128)(2,1)S(1)}, bf16[1,16,24,128]{3,2,1,0:T(8,128)(2,1)S(1)}) custom-call(s32[2]{0:T(128)S(1)} %pad_add_fusion.meta, s32[3,64]{1,0:T(4,128)S(1)} %bitcast.22, s32[3,64]{1,0:T(4,128)S(1)} %collective-permute-done.8.cols_other, bf16[32,3,128,128]{3,2,1,0:T(8,128)(2,1)S(1)} %get-tuple-element.51.own, ...), custom_call_target="tpu_custom_call" | custom-call | flops 805306368 | bytes 25165824 | tf_op jit(solution)/shard_map/forward_step/pallas_call | solution.py:271
  37.5 0.0 collective-permute-done.12
  37.6 0.8 collective-permute-start.13
  38.4 2.5 %collective-permute-start.15 = (bf16[1,16,24,128]{3,2,1,0:T(8,128)(2,1)S(1)}, bf16[1,16,24,128]{3,2,1,0:T(8,128)(2,1)S(1)}, u32[]{:S(2)}, u32[]{:S(2)}) collective-permute-start(bf16[1,16,24,128]{3,2,1,0:T(8,128)(2,1)S(1)} %get-tuple-element.55.rest_0_), channel_id=1, source_target_pairs={{0,8},{4,12},{8,0},{12,4},{1,9},{5,13},{9,1},{13,5},{2,10},{6,14},... | collective-permute-start | bytes 294920 | tf_op jit(solution)/shard_map/ppermute | solution.py:454
  40.9 5.8 %collective-permute-done.13 = bf16[2,16,24,128]{3,2,1,0:T(8,128)(2,1)S(1)} collective-permute-done((bf16[2,16,24,128]{3,2,1,0:T(8,128)(2,1)S(1)}, bf16[2,16,24,128]{3,2,1,0:T(8,128)(2,1)S(1)}, u32[]{:S(2)}, u32[]{:S(2)}) %collective-permute-start.13) | collective-permute-done | bytes 196640 | tf_op jit(solution)/shard_map/ppermute | solution.py:454
  46.7 0.1 add_convert_fusion.5
  46.8 1.1 %collective-permute-start.18 = (bf16[1,16,24,128]{3,2,1,0:T(8,128)(2,1)S(1)}, bf16[1,16,24,128]{3,2,1,0:T(8,128)(2,1)S(1)}, u32[]{:S(2)}, u32[]{:S(2)}) collective-permute-start(bf16[1,16,24,128]{3,2,1,0:T(8,128)(2,1)S(1)} %get-tuple-element.89), channel_id=1, source_target_pairs={{0,8},{4,12},{8,0},{12,4},{1,9},{5,13},{9,1},{13,5},{2,10},{6,14},... | collective-permute-start | bytes 294920 | tf_op jit(solution)/shard_map/ppermute | solution.py:454
  47.9 2.3 %collective-permute-start.16 = (bf16[2,16,24,128]{3,2,1,0:T(8,128)(2,1)S(1)}, bf16[2,16,24,128]{3,2,1,0:T(8,128)(2,1)S(1)}, u32[]{:S(2)}, u32[]{:S(2)}) collective-permute-start(bf16[2,16,24,128]{3,2,1,0:T(8,128)(2,1)S(1)} %pad_maximum_fusion.8), channel_id=1, source_target_pairs={{0,4},{4,0},{8,12},{12,8},{1,5},{5,1},{9,13},{13,9},{2,6},{6,2},{1... | collective-permute-start | bytes 589832 | tf_op jit(solution)/shard_map/ppermute | solution.py:454
  50.2 0.1 pad_maximum_fusion
  50.2 0.1 collective-permute-start.14
  50.4 0.6 collective-permute-start.17
  51.0 5.4 %collective-permute-done.16 = bf16[2,16,24,128]{3,2,1,0:T(8,128)(2,1)S(1)} collective-permute-done((bf16[2,16,24,128]{3,2,1,0:T(8,128)(2,1)S(1)}, bf16[2,16,24,128]{3,2,1,0:T(8,128)(2,1)S(1)}, u32[]{:S(2)}, u32[]{:S(2)}) %collective-permute-start.16) | collective-permute-done | bytes 196640 | tf_op jit(solution)/shard_map/ppermute | solution.py:454
  56.5 0.1 constant_dynamic-update-slice_fusion.5
  56.6 2.1 %backward_step.3 = (bf16[4,16,24,128]{3,2,1,0:T(8,128)(2,1)S(1)}, bf16[4,16,24,128]{3,2,1,0:T(8,128)(2,1)S(1)}) custom-call(s32[2]{0:T(128)S(1)} %pad_add_fusion.meta, s32[3,64]{1,0:T(4,128)S(1)} %bitcast.23, s32[3,64]{1,0:T(4,128)S(1)} %collective-permute-done.8.cols_other, bf16[32,3,128,128]{3,2,1,0:T(8,128)(2,1)S(1)} %get-tuple-element.51.own, ...), custom_call_target="tpu_custom_call" | custom-call | flops 805306368 | bytes 25165824 | tf_op jit(solution)/shard_map/backward_step/pallas_call | solution.py:353
  58.7 0.1 collective-permute-start.21
  58.7 0.5 collective-permute-start.20
  59.2 1.5 %collective-permute-start.19 = (bf16[5,16,24,128]{3,2,1,0:T(8,128)(2,1)S(1)}, bf16[5,16,24,128]{3,2,1,0:T(8,128)(2,1)S(1)}, u32[]{:S(2)}, u32[]{:S(2)}) collective-permute-start(bf16[5,16,24,128]{3,2,1,0:T(8,128)(2,1)S(1)} %get-tuple-element.79), channel_id=1, source_target_pairs={{0,2},{2,0},{1,3},{3,1},{4,6},{6,4},{5,7},{7,5},{8,10},{10,8},{9,1... | collective-permute-start | bytes 1474568 | tf_op jit(solution)/shard_map/ppermute | solution.py:459
  60.7 2.6 %forward_step.3 = (bf16[256,16,128]{2,1,0:T(8,128)(2,1)S(1)}, bf16[1,16,24,128]{3,2,1,0:T(8,128)(2,1)S(1)}) custom-call(s32[2]{0:T(128)S(1)} %pad_add_fusion.meta, s32[3,64]{1,0:T(4,128)S(1)} %bitcast.24, s32[3,64]{1,0:T(4,128)S(1)} %collective-permute-done.8.cols_other, bf16[32,3,128,128]{3,2,1,0:T(8,128)(2,1)S(1)} %get-tuple-element.51.own, ...), custom_call_target="tpu_custom_call" | custom-call | flops 805306368 | bytes 25165824 | tf_op jit(solution)/shard_map/forward_step/pallas_call | solution.py:271
  63.3 0.0 collective-permute-done.21
  63.4 0.6 collective-permute-start.22
  64.0 2.1 %collective-permute-start.24 = (bf16[1,16,24,128]{3,2,1,0:T(8,128)(2,1)S(1)}, bf16[1,16,24,128]{3,2,1,0:T(8,128)(2,1)S(1)}, u32[]{:S(2)}, u32[]{:S(2)}) collective-permute-start(bf16[1,16,24,128]{3,2,1,0:T(8,128)(2,1)S(1)} %get-tuple-element.63.refs_0_), channel_id=1, source_target_pairs={{0,8},{4,12},{8,0},{12,4},{1,9},{5,13},{9,1},{13,5},{2,10},{6,14},... | collective-permute-start | bytes 294920 | tf_op jit(solution)/shard_map/ppermute | solution.py:454
  66.1 6.3 %collective-permute-done.22 = bf16[2,16,24,128]{3,2,1,0:T(8,128)(2,1)S(1)} collective-permute-done((bf16[2,16,24,128]{3,2,1,0:T(8,128)(2,1)S(1)}, bf16[2,16,24,128]{3,2,1,0:T(8,128)(2,1)S(1)}, u32[]{:S(2)}, u32[]{:S(2)}) %collective-permute-start.22) | collective-permute-done | bytes 196640 | tf_op jit(solution)/shard_map/ppermute | solution.py:454
  72.4 0.0 collective-permute-done.19.refs_0_.refs_2_
  72.4 0.1 pad_maximum_fusion.1
  72.5 0.1 collective-permute-start.23
  72.6 0.6 collective-permute-start.26
  73.2 0.1 add_convert_fusion.1
  73.3 0.3 collective-permute-start.25
  73.6 2.2 %collective-permute-start.28 = (bf16[1,16,24,128]{3,2,1,0:T(8,128)(2,1)S(1)}, bf16[1,16,24,128]{3,2,1,0:T(8,128)(2,1)S(1)}, u32[]{:S(2)}, u32[]{:S(2)}) collective-permute-start(bf16[1,16,24,128]{3,2,1,0:T(8,128)(2,1)S(1)} %get-tuple-element.87), channel_id=1, source_target_pairs={{0,8},{4,12},{8,0},{12,4},{1,9},{5,13},{9,1},{13,5},{2,10},{6,14},... | collective-permute-start | bytes 294920 | tf_op jit(solution)/shard_map/ppermute | solution.py:454
  75.9 1.6 %collective-permute-start.30 = (bf16[3,16,24,128]{3,2,1,0:T(8,128)(2,1)S(1)}, bf16[3,16,24,128]{3,2,1,0:T(8,128)(2,1)S(1)}, u32[]{:S(2)}, u32[]{:S(2)}) collective-permute-start(bf16[3,16,24,128]{3,2,1,0:T(8,128)(2,1)S(1)} %pad_maximum_fusion.4), channel_id=1, source_target_pairs={{0,2},{2,0},{1,3},{3,1},{4,6},{6,4},{5,7},{7,5},{8,10},{10,8},{9,1... | collective-permute-start | bytes 884744 | tf_op jit(solution)/shard_map/ppermute | solution.py:459
  77.4 4.9 %collective-permute-done.25 = bf16[2,16,24,128]{3,2,1,0:T(8,128)(2,1)S(1)} collective-permute-done((bf16[2,16,24,128]{3,2,1,0:T(8,128)(2,1)S(1)}, bf16[2,16,24,128]{3,2,1,0:T(8,128)(2,1)S(1)}, u32[]{:S(2)}, u32[]{:S(2)}) %collective-permute-start.25) | collective-permute-done | bytes 196640 | tf_op jit(solution)/shard_map/ppermute | solution.py:454
  82.3 0.1 add_convert_fusion.refs_6_
  82.5 1.5 %collective-permute-start.31 = (bf16[2,16,24,128]{3,2,1,0:T(8,128)(2,1)S(1)}, bf16[2,16,24,128]{3,2,1,0:T(8,128)(2,1)S(1)}, u32[]{:S(2)}, u32[]{:S(2)}) collective-permute-start(bf16[2,16,24,128]{3,2,1,0:T(8,128)(2,1)S(1)} %pad_maximum_fusion.11), channel_id=1, source_target_pairs={{0,2},{2,0},{1,3},{3,1},{4,6},{6,4},{5,7},{7,5},{8,10},{10,8},{9,1... | collective-permute-start | bytes 589832 | tf_op jit(solution)/shard_map/ppermute | solution.py:459
  84.0 0.5 collective-permute-start.29
  84.5 0.0 collective-permute-start.32
  84.5 0.8 unpack_panels.5.refs_1_.refs_15_
  85.3 1.2 %unpack_panels.6 = (bf16[256,16,128]{2,1,0:T(8,128)(2,1)S(1)}, bf16[64,16,128]{2,1,0:T(8,128)(2,1)S(1)}, bf16[64,16,128]{2,1,0:T(8,128)(2,1)S(1)}) custom-call(s32[2]{0:T(128)S(1)} %pad_add_fusion.meta, bf16[5,16,24,128]{3,2,1,0:T(8,128)(2,1)S(1)} %collective-permute-done.7.refs_0_.refs_2_, ...), custom_call_target="tpu_custom_call" | custom-call | tf_op jit(solution)/shard_map/unpack_panels/pallas_call | solution.py:80
  86.5 1.0 %unpack_panels.7 = (bf16[256,16,128]{2,1,0:T(8,128)(2,1)S(1)}, bf16[64,16,128]{2,1,0:T(8,128)(2,1)S(1)}, bf16[64,16,128]{2,1,0:T(8,128)(2,1)S(1)}) custom-call(s32[2]{0:T(128)S(1)} %pad_add_fusion.meta, bf16[5,16,24,128]{3,2,1,0:T(8,128)(2,1)S(1)} %collective-permute-done.19.refs_0_.refs_2_, ...), custom_call_target="tpu_custom_call" | custom-call | tf_op jit(solution)/shard_map/unpack_panels/pallas_call | solution.py:80
  87.5 0.9 unpack_panels.8
  88.4 0.1 collective-permute-done.31.refs_1_.refs_4_
  88.5 0.5 collective-permute-start.33
  89.0 1.1 %collective-permute-done.33.refs_3_.refs_5_ = bf16[2,16,24,128]{3,2,1,0:T(8,128)(2,1)S(1)} collective-permute-done((bf16[2,16,24,128]{3,2,1,0:T(8,128)(2,1)S(1)}, bf16[2,16,24,128]{3,2,1,0:T(8,128)(2,1)S(1)}, u32[]{:S(2)}, u32[]{:S(2)}) %collective-permute-start.33) | collective-permute-done | bytes 196640 | tf_op jit(solution)/shard_map/ppermute | solution.py:451
  90.1 0.9 unpack_panels.9
  91.0 3.7 %gradient.1 = bf16[64,3,128,128]{3,2,1,0:T(8,128)(2,1)} custom-call(s32[2]{0:T(128)S(1)} %pad_add_fusion.meta, s32[3,64]{1,0:T(4,128)S(1)} %bitcast.25, bf16[256,16,128]{2,1,0:T(8,128)(2,1)S(1)} %get-tuple-element.42.refs_0_.refs_14_, bf16[256,16,128]{2,1,0:T(8,128)(2,1)S(1)} %unpack_panels.5.refs_1_.refs_15_, ...), custom_call_target="tpu_custom_call" | custom-call | tf_op jit(solution)/shard_map/gradient/pallas_call | solution.py:413
  (49 shorter events, 0.7 us)
Async XLA Ops:
  0.1 14.3 %copy-start = (s32[64,3]{0,1:T(4,128)S(1)}, s32[64,3]{0,1:T(4,128)}, u32[]{:S(2)}) copy-start(s32[64,3]{0,1:T(4,128)} %param.4) | copy-start | bytes 2308
  7.5 2.0 %collective-permute-start = (bf16[5,16,24,128]{3,2,1,0:T(8,128)(2,1)S(1)}, bf16[5,16,24,128]{3,2,1,0:T(8,128)(2,1)S(1)}, u32[]{:S(2)}, u32[]{:S(2)}) collective-permute-start(bf16[5,16,24,128]{3,2,1,0:T(8,128)(2,1)S(1)} %get-tuple-element.46), channel_id=1, source_target_pairs={{0,1},{1,0},{2,3},{3,2},{4,5},{5,4},{6,7},{7,6},{8,9},{9,8},{10,11... | collective-permute-start | bytes 1474568 | tf_op jit(solution)/shard_map/ppermute | solution.py:451
  9.6 19.8 %collective-permute-start.9 = (bf16[32,3,128,128]{3,2,1,0:T(8,128)(2,1)S(1)}, bf16[32,3,128,128]{3,2,1,0:T(8,128)(2,1)S(1)}, u32[]{:S(2)}, u32[]{:S(2)}) collective-permute-start(bf16[32,3,128,128]{3,2,1,0:T(8,128)(2,1)S(1)} %get-tuple-element.53), channel_id=1, source_target_pairs={{0,1},{1,0},{2,3},{3,2},{4,5},{5,4},{6,7},{7,6},{8,9},{9,8},{10,11... | collective-permute-start | bytes 9437192 | tf_op jit(solution)/shard_map/ppermute | solution.py:451
  10.1 8.2 %collective-permute-start.2 = (bf16[2,16,24,128]{3,2,1,0:T(8,128)(2,1)S(1)}, bf16[2,16,24,128]{3,2,1,0:T(8,128)(2,1)S(1)}, u32[]{:S(2)}, u32[]{:S(2)}) collective-permute-start(bf16[2,16,24,128]{3,2,1,0:T(8,128)(2,1)S(1)} %pad_maximum_fusion.5), channel_id=1, source_target_pairs={{0,4},{4,0},{8,12},{12,8},{1,5},{5,1},{9,13},{13,9},{2,6},{6,2},{1... | collective-permute-start | bytes 589832 | tf_op jit(solution)/shard_map/ppermute | solution.py:454
  12.9 11.1 %collective-permute-start.1 = (bf16[4,16,24,128]{3,2,1,0:T(8,128)(2,1)S(1)}, bf16[4,16,24,128]{3,2,1,0:T(8,128)(2,1)S(1)}, u32[]{:S(2)}, u32[]{:S(2)}) collective-permute-start(bf16[4,16,24,128]{3,2,1,0:T(8,128)(2,1)S(1)} %get-tuple-element.47), channel_id=1, source_target_pairs={{0,2},{2,0},{1,3},{3,1},{4,6},{6,4},{5,7},{7,5},{8,10},{10,8},{9,1... | collective-permute-start | bytes 1179656 | tf_op jit(solution)/shard_map/ppermute | solution.py:459
  14.3 15.0 %collective-permute-start.8 = (s32[3,64]{1,0:T(4,128)S(1)}, s32[3,64]{1,0:T(4,128)S(1)}, u32[]{:S(2)}, u32[]{:S(2)}) collective-permute-start(s32[3,64]{1,0:T(4,128)S(1)} %bitcast.20), channel_id=1, source_target_pairs={{0,1},{1,0},{2,3},{3,2},{4,5},{5,4},{6,7},{7,6},{8,9},{9,8},{10,11... | collective-permute-start | bytes 2312 | tf_op jit(solution)/shard_map/ppermute | solution.py:451
  14.4 7.4 %collective-permute-start.4 = (bf16[1,16,24,128]{3,2,1,0:T(8,128)(2,1)S(1)}, bf16[1,16,24,128]{3,2,1,0:T(8,128)(2,1)S(1)}, u32[]{:S(2)}, u32[]{:S(2)}) collective-permute-start(bf16[1,16,24,128]{3,2,1,0:T(8,128)(2,1)S(1)} %get-tuple-element.84.rest_0_), channel_id=1, source_target_pairs={{0,8},{4,12},{8,0},{12,4},{1,9},{5,13},{9,1},{13,5},{2,10},{6,14},... | collective-permute-start | bytes 294920 | tf_op jit(solution)/shard_map/ppermute | solution.py:454
  18.4 10.9 %collective-permute-start.6 = (bf16[1,16,24,128]{3,2,1,0:T(8,128)(2,1)S(1)}, bf16[1,16,24,128]{3,2,1,0:T(8,128)(2,1)S(1)}, u32[]{:S(2)}, u32[]{:S(2)}) collective-permute-start(bf16[1,16,24,128]{3,2,1,0:T(8,128)(2,1)S(1)} %get-tuple-element.85), channel_id=1, source_target_pairs={{0,8},{4,12},{8,0},{12,4},{1,9},{5,13},{9,1},{13,5},{2,10},{6,14},... | collective-permute-start | bytes 294920 | tf_op jit(solution)/shard_map/ppermute | solution.py:454
  21.8 7.4 %collective-permute-start.5 = (bf16[2,16,24,128]{3,2,1,0:T(8,128)(2,1)S(1)}, bf16[2,16,24,128]{3,2,1,0:T(8,128)(2,1)S(1)}, u32[]{:S(2)}, u32[]{:S(2)}) collective-permute-start(bf16[2,16,24,128]{3,2,1,0:T(8,128)(2,1)S(1)} %pad_maximum_fusion.6), channel_id=1, source_target_pairs={{0,4},{4,0},{8,12},{12,8},{1,5},{5,1},{9,13},{13,9},{2,6},{6,2},{1... | collective-permute-start | bytes 589832 | tf_op jit(solution)/shard_map/ppermute | solution.py:454
  24.0 5.3 %collective-permute-start.3 = (bf16[4,16,24,128]{3,2,1,0:T(8,128)(2,1)S(1)}, bf16[4,16,24,128]{3,2,1,0:T(8,128)(2,1)S(1)}, u32[]{:S(2)}, u32[]{:S(2)}) collective-permute-start(bf16[4,16,24,128]{3,2,1,0:T(8,128)(2,1)S(1)} %collective-permute-done.1.refs_0_), channel_id=1, source_target_pairs={{0,1},{1,0},{2,3},{3,2},{4,5},{5,4},{6,7},{7,6},{8,9},{9,8},{10,11... | collective-permute-start | bytes 1179656 | tf_op jit(solution)/shard_map/ppermute | solution.py:451
  31.4 6.1 %collective-permute-start.12 = (bf16[4,16,24,128]{3,2,1,0:T(8,128)(2,1)S(1)}, bf16[4,16,24,128]{3,2,1,0:T(8,128)(2,1)S(1)}, u32[]{:S(2)}, u32[]{:S(2)}) collective-permute-start(bf16[4,16,24,128]{3,2,1,0:T(8,128)(2,1)S(1)} %get-tuple-element.54.rest_6_), channel_id=1, source_target_pairs={{0,1},{1,0},{2,3},{3,2},{4,5},{5,4},{6,7},{7,6},{8,9},{9,8},{10,11... | collective-permute-start | bytes 1179656 | tf_op jit(solution)/shard_map/ppermute | solution.py:451
  31.5 3.3 %collective-permute-start.10 = (bf16[3,16,24,128]{3,2,1,0:T(8,128)(2,1)S(1)}, bf16[3,16,24,128]{3,2,1,0:T(8,128)(2,1)S(1)}, u32[]{:S(2)}, u32[]{:S(2)}) collective-permute-start(bf16[3,16,24,128]{3,2,1,0:T(8,128)(2,1)S(1)} %pad_maximum_fusion.2), channel_id=1, source_target_pairs={{0,1},{1,0},{2,3},{3,2},{4,5},{5,4},{6,7},{7,6},{8,9},{9,8},{10,11... | collective-permute-start | bytes 884744 | tf_op jit(solution)/shard_map/ppermute | solution.py:451
  32.1 2.7 %collective-permute-start.11 = (bf16[1,16,24,128]{3,2,1,0:T(8,128)(2,1)S(1)}, bf16[1,16,24,128]{3,2,1,0:T(8,128)(2,1)S(1)}, u32[]{:S(2)}, u32[]{:S(2)}) collective-permute-start(bf16[1,16,24,128]{3,2,1,0:T(8,128)(2,1)S(1)} %get-tuple-element.95.rest_3_), channel_id=1, source_target_pairs={{0,1},{1,0},{2,3},{3,2},{4,5},{5,4},{6,7},{7,6},{8,9},{9,8},{10,11... | collective-permute-start | bytes 294920 | tf_op jit(solution)/shard_map/ppermute | solution.py:451
  32.2 14.6 %collective-permute-start.7 = (bf16[5,16,24,128]{3,2,1,0:T(8,128)(2,1)S(1)}, bf16[5,16,24,128]{3,2,1,0:T(8,128)(2,1)S(1)}, u32[]{:S(2)}, u32[]{:S(2)}) collective-permute-start(bf16[5,16,24,128]{3,2,1,0:T(8,128)(2,1)S(1)} %get-tuple-element.81), channel_id=1, source_target_pairs={{0,2},{2,0},{1,3},{3,1},{4,6},{6,4},{5,7},{7,5},{8,10},{10,8},{9,1... | collective-permute-start | bytes 1474568 | tf_op jit(solution)/shard_map/ppermute | solution.py:459
  37.6 9.1 %collective-permute-start.13 = (bf16[2,16,24,128]{3,2,1,0:T(8,128)(2,1)S(1)}, bf16[2,16,24,128]{3,2,1,0:T(8,128)(2,1)S(1)}, u32[]{:S(2)}, u32[]{:S(2)}) collective-permute-start(bf16[2,16,24,128]{3,2,1,0:T(8,128)(2,1)S(1)} %pad_maximum_fusion.7), channel_id=1, source_target_pairs={{0,4},{4,0},{8,12},{12,8},{1,5},{5,1},{9,13},{13,9},{2,6},{6,2},{1... | collective-permute-start | bytes 589832 | tf_op jit(solution)/shard_map/ppermute | solution.py:454
  38.4 9.5 %collective-permute-start.15 = (bf16[1,16,24,128]{3,2,1,0:T(8,128)(2,1)S(1)}, bf16[1,16,24,128]{3,2,1,0:T(8,128)(2,1)S(1)}, u32[]{:S(2)}, u32[]{:S(2)}) collective-permute-start(bf16[1,16,24,128]{3,2,1,0:T(8,128)(2,1)S(1)} %get-tuple-element.55.rest_0_), channel_id=1, source_target_pairs={{0,8},{4,12},{8,0},{12,4},{1,9},{5,13},{9,1},{13,5},{2,10},{6,14},... | collective-permute-start | bytes 294920 | tf_op jit(solution)/shard_map/ppermute | solution.py:454
  46.8 9.7 %collective-permute-start.18 = (bf16[1,16,24,128]{3,2,1,0:T(8,128)(2,1)S(1)}, bf16[1,16,24,128]{3,2,1,0:T(8,128)(2,1)S(1)}, u32[]{:S(2)}, u32[]{:S(2)}) collective-permute-start(bf16[1,16,24,128]{3,2,1,0:T(8,128)(2,1)S(1)} %get-tuple-element.89), channel_id=1, source_target_pairs={{0,8},{4,12},{8,0},{12,4},{1,9},{5,13},{9,1},{13,5},{2,10},{6,14},... | collective-permute-start | bytes 294920 | tf_op jit(solution)/shard_map/ppermute | solution.py:454
  47.9 8.5 %collective-permute-start.16 = (bf16[2,16,24,128]{3,2,1,0:T(8,128)(2,1)S(1)}, bf16[2,16,24,128]{3,2,1,0:T(8,128)(2,1)S(1)}, u32[]{:S(2)}, u32[]{:S(2)}) collective-permute-start(bf16[2,16,24,128]{3,2,1,0:T(8,128)(2,1)S(1)} %pad_maximum_fusion.8), channel_id=1, source_target_pairs={{0,4},{4,0},{8,12},{12,8},{1,5},{5,1},{9,13},{13,9},{2,6},{6,2},{1... | collective-permute-start | bytes 589832 | tf_op jit(solution)/shard_map/ppermute | solution.py:454
  50.2 6.2 %collective-permute-start.14 = (bf16[6,16,24,128]{3,2,1,0:T(8,128)(2,1)S(1)}, bf16[6,16,24,128]{3,2,1,0:T(8,128)(2,1)S(1)}, u32[]{:S(2)}, u32[]{:S(2)}) collective-permute-start(bf16[6,16,24,128]{3,2,1,0:T(8,128)(2,1)S(1)} %pad_maximum_fusion), channel_id=1, source_target_pairs={{0,1},{1,0},{2,3},{3,2},{4,5},{5,4},{6,7},{7,6},{8,9},{9,8},{10,11... | collective-permute-start | bytes 1769480 | tf_op jit(solution)/shard_map/ppermute | solution.py:451
  50.4 6.1 %collective-permute-start.17 = (bf16[3,16,24,128]{3,2,1,0:T(8,128)(2,1)S(1)}, bf16[3,16,24,128]{3,2,1,0:T(8,128)(2,1)S(1)}, u32[]{:S(2)}, u32[]{:S(2)}) collective-permute-start(bf16[3,16,24,128]{3,2,1,0:T(8,128)(2,1)S(1)} %pad_maximum_fusion.3), channel_id=1, source_target_pairs={{0,1},{1,0},{2,3},{3,2},{4,5},{5,4},{6,7},{7,6},{8,9},{9,8},{10,11... | collective-permute-start | bytes 884744 | tf_op jit(solution)/shard_map/ppermute | solution.py:451
  58.7 4.7 %collective-permute-start.21 = (bf16[4,16,24,128]{3,2,1,0:T(8,128)(2,1)S(1)}, bf16[4,16,24,128]{3,2,1,0:T(8,128)(2,1)S(1)}, u32[]{:S(2)}, u32[]{:S(2)}) collective-permute-start(bf16[4,16,24,128]{3,2,1,0:T(8,128)(2,1)S(1)} %get-tuple-element.62.rest_6_), channel_id=1, source_target_pairs={{0,1},{1,0},{2,3},{3,2},{4,5},{5,4},{6,7},{7,6},{8,9},{9,8},{10,11... | collective-permute-start | bytes 1179656 | tf_op jit(solution)/shard_map/ppermute | solution.py:451
  58.7 2.0 %collective-permute-start.20 = (bf16[1,16,24,128]{3,2,1,0:T(8,128)(2,1)S(1)}, bf16[1,16,24,128]{3,2,1,0:T(8,128)(2,1)S(1)}, u32[]{:S(2)}, u32[]{:S(2)}) collective-permute-start(bf16[1,16,24,128]{3,2,1,0:T(8,128)(2,1)S(1)} %get-tuple-element.91.rest_3_), channel_id=1, source_target_pairs={{0,1},{1,0},{2,3},{3,2},{4,5},{5,4},{6,7},{7,6},{8,9},{9,8},{10,11... | collective-permute-start | bytes 294920 | tf_op jit(solution)/shard_map/ppermute | solution.py:451
  59.2 13.2 %collective-permute-start.19 = (bf16[5,16,24,128]{3,2,1,0:T(8,128)(2,1)S(1)}, bf16[5,16,24,128]{3,2,1,0:T(8,128)(2,1)S(1)}, u32[]{:S(2)}, u32[]{:S(2)}) collective-permute-start(bf16[5,16,24,128]{3,2,1,0:T(8,128)(2,1)S(1)} %get-tuple-element.79), channel_id=1, source_target_pairs={{0,2},{2,0},{1,3},{3,1},{4,6},{6,4},{5,7},{7,5},{8,10},{10,8},{9,1... | collective-permute-start | bytes 1474568 | tf_op jit(solution)/shard_map/ppermute | solution.py:459
  63.4 9.0 %collective-permute-start.22 = (bf16[2,16,24,128]{3,2,1,0:T(8,128)(2,1)S(1)}, bf16[2,16,24,128]{3,2,1,0:T(8,128)(2,1)S(1)}, u32[]{:S(2)}, u32[]{:S(2)}) collective-permute-start(bf16[2,16,24,128]{3,2,1,0:T(8,128)(2,1)S(1)} %pad_maximum_fusion.9), channel_id=1, source_target_pairs={{0,4},{4,0},{8,12},{12,8},{1,5},{5,1},{9,13},{13,9},{2,6},{6,2},{1... | collective-permute-start | bytes 589832 | tf_op jit(solution)/shard_map/ppermute | solution.py:454
  64.0 8.6 %collective-permute-start.24 = (bf16[1,16,24,128]{3,2,1,0:T(8,128)(2,1)S(1)}, bf16[1,16,24,128]{3,2,1,0:T(8,128)(2,1)S(1)}, u32[]{:S(2)}, u32[]{:S(2)}) collective-permute-start(bf16[1,16,24,128]{3,2,1,0:T(8,128)(2,1)S(1)} %get-tuple-element.63.refs_0_), channel_id=1, source_target_pairs={{0,8},{4,12},{8,0},{12,4},{1,9},{5,13},{9,1},{13,5},{2,10},{6,14},... | collective-permute-start | bytes 294920 | tf_op jit(solution)/shard_map/ppermute | solution.py:454
  72.5 9.8 %collective-permute-start.23 = (bf16[6,16,24,128]{3,2,1,0:T(8,128)(2,1)S(1)}, bf16[6,16,24,128]{3,2,1,0:T(8,128)(2,1)S(1)}, u32[]{:S(2)}, u32[]{:S(2)}) collective-permute-start(bf16[6,16,24,128]{3,2,1,0:T(8,128)(2,1)S(1)} %pad_maximum_fusion.1), channel_id=1, source_target_pairs={{0,1},{1,0},{2,3},{3,2},{4,5},{5,4},{6,7},{7,6},{8,9},{9,8},{10,11... | collective-permute-start | bytes 1769480 | tf_op jit(solution)/shard_map/ppermute | solution.py:451
  72.6 9.7 %collective-permute-start.26 = (bf16[3,16,24,128]{3,2,1,0:T(8,128)(2,1)S(1)}, bf16[3,16,24,128]{3,2,1,0:T(8,128)(2,1)S(1)}, u32[]{:S(2)}, u32[]{:S(2)}) collective-permute-start(bf16[3,16,24,128]{3,2,1,0:T(8,128)(2,1)S(1)} %pad_maximum_fusion.4), channel_id=1, source_target_pairs={{0,1},{1,0},{2,3},{3,2},{4,5},{5,4},{6,7},{7,6},{8,9},{9,8},{10,11... | collective-permute-start | bytes 884744 | tf_op jit(solution)/shard_map/ppermute | solution.py:451
  73.3 9.0 %collective-permute-start.25 = (bf16[2,16,24,128]{3,2,1,0:T(8,128)(2,1)S(1)}, bf16[2,16,24,128]{3,2,1,0:T(8,128)(2,1)S(1)}, u32[]{:S(2)}, u32[]{:S(2)}) collective-permute-start(bf16[2,16,24,128]{3,2,1,0:T(8,128)(2,1)S(1)} %pad_maximum_fusion.10), channel_id=1, source_target_pairs={{0,4},{4,0},{8,12},{12,8},{1,5},{5,1},{9,13},{13,9},{2,6},{6,2},{1... | collective-permute-start | bytes 589832 | tf_op jit(solution)/shard_map/ppermute | solution.py:454
  73.6 8.7 %collective-permute-start.28 = (bf16[1,16,24,128]{3,2,1,0:T(8,128)(2,1)S(1)}, bf16[1,16,24,128]{3,2,1,0:T(8,128)(2,1)S(1)}, u32[]{:S(2)}, u32[]{:S(2)}) collective-permute-start(bf16[1,16,24,128]{3,2,1,0:T(8,128)(2,1)S(1)} %get-tuple-element.87), channel_id=1, source_target_pairs={{0,8},{4,12},{8,0},{12,4},{1,9},{5,13},{9,1},{13,5},{2,10},{6,14},... | collective-permute-start | bytes 294920 | tf_op jit(solution)/shard_map/ppermute | solution.py:454
  75.9 8.6 %collective-permute-start.30 = (bf16[3,16,24,128]{3,2,1,0:T(8,128)(2,1)S(1)}, bf16[3,16,24,128]{3,2,1,0:T(8,128)(2,1)S(1)}, u32[]{:S(2)}, u32[]{:S(2)}) collective-permute-start(bf16[3,16,24,128]{3,2,1,0:T(8,128)(2,1)S(1)} %pad_maximum_fusion.4), channel_id=1, source_target_pairs={{0,2},{2,0},{1,3},{3,1},{4,6},{6,4},{5,7},{7,5},{8,10},{10,8},{9,1... | collective-permute-start | bytes 884744 | tf_op jit(solution)/shard_map/ppermute | solution.py:459
  82.5 6.0 %collective-permute-start.31 = (bf16[2,16,24,128]{3,2,1,0:T(8,128)(2,1)S(1)}, bf16[2,16,24,128]{3,2,1,0:T(8,128)(2,1)S(1)}, u32[]{:S(2)}, u32[]{:S(2)}) collective-permute-start(bf16[2,16,24,128]{3,2,1,0:T(8,128)(2,1)S(1)} %pad_maximum_fusion.11), channel_id=1, source_target_pairs={{0,2},{2,0},{1,3},{3,1},{4,6},{6,4},{5,7},{7,5},{8,10},{10,8},{9,1... | collective-permute-start | bytes 589832 | tf_op jit(solution)/shard_map/ppermute | solution.py:459
  84.0 3.5 %collective-permute-start.27 = (bf16[1,16,24,128]{3,2,1,0:T(8,128)(2,1)S(1)}, bf16[1,16,24,128]{3,2,1,0:T(8,128)(2,1)S(1)}, u32[]{:S(2)}, u32[]{:S(2)}) collective-permute-start(bf16[1,16,24,128]{3,2,1,0:T(8,128)(2,1)S(1)} %slice.168.refs_3_), channel_id=1, source_target_pairs={{0,1},{1,0},{2,3},{3,2},{4,5},{5,4},{6,7},{7,6},{8,9},{9,8},{10,11... | collective-permute-start | bytes 294920 | tf_op jit(solution)/shard_map/ppermute | solution.py:451
  84.0 3.5 %collective-permute-start.29 = (bf16[1,16,24,128]{3,2,1,0:T(8,128)(2,1)S(1)}, bf16[1,16,24,128]{3,2,1,0:T(8,128)(2,1)S(1)}, u32[]{:S(2)}, u32[]{:S(2)}) collective-permute-start(bf16[1,16,24,128]{3,2,1,0:T(8,128)(2,1)S(1)} %add_convert_fusion.refs_6_), channel_id=1, source_target_pairs={{0,1},{1,0},{2,3},{3,2},{4,5},{5,4},{6,7},{7,6},{8,9},{9,8},{10,11... | collective-permute-start | bytes 294920 | tf_op jit(solution)/shard_map/ppermute | solution.py:451
  84.5 4.5 %collective-permute-start.32 = (bf16[3,16,24,128]{3,2,1,0:T(8,128)(2,1)S(1)}, bf16[3,16,24,128]{3,2,1,0:T(8,128)(2,1)S(1)}, u32[]{:S(2)}, u32[]{:S(2)}) collective-permute-start(bf16[3,16,24,128]{3,2,1,0:T(8,128)(2,1)S(1)} %collective-permute-done.30.refs_0_), channel_id=1, source_target_pairs={{0,1},{1,0},{2,3},{3,2},{4,5},{5,4},{6,7},{7,6},{8,9},{9,8},{10,11... | collective-permute-start | bytes 884744 | tf_op jit(solution)/shard_map/ppermute | solution.py:451
  88.5 1.6 %collective-permute-start.33 = (bf16[2,16,24,128]{3,2,1,0:T(8,128)(2,1)S(1)}, bf16[2,16,24,128]{3,2,1,0:T(8,128)(2,1)S(1)}, u32[]{:S(2)}, u32[]{:S(2)}) collective-permute-start(bf16[2,16,24,128]{3,2,1,0:T(8,128)(2,1)S(1)} %collective-permute-done.31.refs_1_.refs_4_), channel_id=1, source_target_pairs={{0,1},{1,0},{2,3},{3,2},{4,5},{5,4},{6,7},{7,6},{8,9},{9,8},{10,11... | collective-permute-start | bytes 589832 | tf_op jit(solution)/shard_map/ppermute | solution.py:451

commit v9 on v8

--- a/solution.py
+++ b/solution.py
@@ -539,14 +539,16 @@
             far = shift_var(updated, 2)
             both = shift_var(stack([updated, narrow(parts[3])]), 1)
             near = both[:1]
-            crossed = shift_var(narrow(parts[2] + wide(both[1:])), 2)
-            final = shift_var(stack([far, narrow(parts[1])]), 1)
+            third = narrow(parts[2] + wide(both[1:]))
+            crossed = shift_var(third, 2)
+            pair = stack([far, narrow(parts[1])])
+            final = shift_var(pair, 1)
             last = final[:1]
             middle_other = swap_rep(stack([updated, near, far]))
             summed = parts[0] + wide(final[1:]) + wide(crossed)
             held = [updated, near, far, last]
             others = [(middle_other, [0, 1, 2]), (swap_rep(last), [3])]
-            window, settled = [both], [middle_other] if step > 0 else []
+            window, settled = [third, pair], [middle_other] if step > 0 else []
         else:
             bits = [1 << i for i in range(n_var.bit_length() - 1)]
             found = {0: updated}
@@ -583,7 +585,10 @@
 
         left_own = narrow(wide(tie(left_own, swapped, *settled)) + inverse * summed)
         if step == 2 and n_var == 4:
-            incoming = [from_probes(stack(held[:3])), from_probes(stack([last, left_own]))]
+            ending = stack([last, left_own])
+            ending_other = swap_rep(ending)
+            others = [(middle_other, [0, 1, 2]), (ending_other, [3, None])]
+            incoming = [from_probes(stack(held[:3])), from_probes(ending)]
             incoming_labels = [[0, 1, 2], [3, "row"]]
         else:
             incoming = [from_probes(stack(held + [left_own]))]
@@ -601,7 +606,11 @@
             right[0].append(panel)
 
     jobs = [(sources, blocks)]
-    jobs.append(([(left_own, [row_place(0)]), (swap_rep(left_own), [row_place(1)])], rows))
+    if n_var == 4:
+        rows_other = (ending_other, [None, row_place(1)])
+    else:
+        rows_other = (swap_rep(left_own), [row_place(1)])
+    jobs.append(([(left_own, [row_place(0)]), rows_other], rows))
     ready = list(unpack(meta, jobs))
     right[0].append(ready[0])
     left[0].append(ready[1])

time: 95 us -> 92.9 us (0.978)
  waiting for transfers between devices: 31.7 us -> 27.8 us
  starting transfers between devices: 36 us -> 37.9 us
    ppermute x12, waiting for transfers between devices: 28.9 us -> 20.1 us  [shift_var(): return lax.ppermute(x, 'var', [(i, i ^ bit) for i in range(n_var)])]
    ppermute x5, waiting for transfers between devices: 0.15 us -> 5.11 us  [from_probes(): lax.ppermute(x, 'probe', [(i, (i + d) % n_probe) for i in range(n_probe)])]
    ppermute x12, starting transfers between devices: 22.8 us -> 26.1 us  [shift_var(): return lax.ppermute(x, 'var', [(i, i ^ bit) for i in range(n_var)])]
    ppermute x5, starting transfers between devices: 8.7 us -> 7.63 us  [from_probes(): lax.ppermute(x, 'probe', [(i, (i + d) % n_probe) for i in range(n_probe)])]
    ppermute x17 -> x16, starting transfers between devices: 4.51 us -> 4.15 us  [swap_rep(): return lax.ppermute(x, 'rep', [(0, 1), (1, 0)])]
    ppermute x17 -> x16, waiting for transfers between devices: 2.61 us -> 2.66 us  [swap_rep(): return lax.ppermute(x, 'rep', [(0, 1), (1, 0)])]
  transfers between devices with their start and end apart: 34 -> 33, of which waited for: 9 -> 14; matrix products, arithmetic and copies ran while one was open for 1% -> 1% of each run, Pallas kernels for 10% -> 10%
where the time goes in v9:
time: 92.9 us; the launch traced here: 92.8 us
  starting transfers between devices  37.9 us (41%)
  waiting for transfers between devices  27.8 us (30%)
  Pallas kernels  25.3 us (27%)
  other arithmetic  1.06 us (1%)
    ppermute x12, starting transfers between devices, shift_var(): return lax.ppermute(x, 'var', [(i, i ^ bit) for i in range(n_var)])  26.1 us
    ppermute x12, waiting for transfers between devices, shift_var(): return lax.ppermute(x, 'var', [(i, i ^ bit) for i in range(n_var)])  20.1 us
    ppermute x5, starting transfers between devices, from_probes(): lax.ppermute(x, 'probe', [(i, (i + d) % n_probe) for i in range(n_probe)])  7.63 us
    pallas_call x1, Pallas kernels, first_step(): pl.pallas_call(functools.partial(first_kernel, count, chunk, blocks), out...  7.42 us
    pallas_call x2, Pallas kernels, forward(): pl.pallas_call(functools.partial(forward_kernel, count, chunk, 2 * half,...  5.25 us
    ppermute x5, waiting for transfers between devices, from_probes(): lax.ppermute(x, 'probe', [(i, (i + d) % n_probe) for i in range(n_probe)])  5.11 us
    pallas_call x5, Pallas kernels, unpack(): pl.pallas_call(functools.partial(unpack_kernel, count, wheres, len(tokens...  4.77 us
    ppermute x16, starting transfers between devices, swap_rep(): return lax.ppermute(x, 'rep', [(0, 1), (1, 0)])  4.15 us
  transfers between devices with their start and end apart: 33, of which 14 were waited for; matrix products, arithmetic and copies ran while one was open for 1% of the time, Pallas kernels for 10%

profile of v9, /device:TPU:0, one launch (start us, length us, event | category | flops | bytes accessed | tf_op | source)
XLA Modules:
  0.0 92.8 jit_solution(13244248591767968633)
XLA Ops:
  0.0 0.1 pad_add_fusion.meta
  0.1 7.4 %first_step.1 = (bf16[256,16,128]{2,1,0:T(8,128)(2,1)S(1)}, bf16[4,16,24,128]{3,2,1,0:T(8,128)(2,1)S(1)}, bf16[1,16,24,128]{3,2,1,0:T(8,128)(2,1)S(1)}, f32[16,2...) custom-call(s32[2]{0:T(128)S(1)} %pad_add_fusion.meta, ...), custom_call_target="tpu_custom_call" | custom-call | flops 1610612736 | bytes 50331648 | tf_op jit(solution)/shard_map/first_step/pallas_call | solution.py:198
  7.5 0.5 collective-permute-start
  8.0 1.5 %collective-permute-done = bf16[5,16,24,128]{3,2,1,0:T(8,128)(2,1)S(1)} collective-permute-done((bf16[5,16,24,128]{3,2,1,0:T(8,128)(2,1)S(1)}, bf16[5,16,24,128]{3,2,1,0:T(8,128)(2,1)S(1)}, u32[]{:S(2)}, u32[]{:S(2)}) %collective-permute-start) | collective-permute-done | bytes 491552 | tf_op jit(solution)/shard_map/ppermute | solution.py:451
  9.6 0.4 collective-permute-start.9
  10.0 3.7 %collective-permute-start.3 = (bf16[1,16,24,128]{3,2,1,0:T(8,128)(2,1)S(1)}, bf16[1,16,24,128]{3,2,1,0:T(8,128)(2,1)S(1)}, u32[]{:S(2)}, u32[]{:S(2)}) collective-permute-start(bf16[1,16,24,128]{3,2,1,0:T(8,128)(2,1)S(1)} %get-tuple-element.84.rest_0_), channel_id=1, source_target_pairs={{0,8},{4,12},{8,0},{12,4},{1,9},{5,13},{9,1},{13,5},{2,10},{6,14},... | collective-permute-start | bytes 294920 | tf_op jit(solution)/shard_map/ppermute | solution.py:454
  13.7 0.1 add_convert_fusion.9
  13.8 1.6 %collective-permute-start.2 = (bf16[2,16,24,128]{3,2,1,0:T(8,128)(2,1)S(1)}, bf16[2,16,24,128]{3,2,1,0:T(8,128)(2,1)S(1)}, u32[]{:S(2)}, u32[]{:S(2)}) collective-permute-start(bf16[2,16,24,128]{3,2,1,0:T(8,128)(2,1)S(1)} %pad_maximum_fusion.5), channel_id=1, source_target_pairs={{0,4},{4,0},{8,12},{12,8},{1,5},{5,1},{9,13},{13,9},{2,6},{6,2},{1... | collective-permute-start | bytes 589832 | tf_op jit(solution)/shard_map/ppermute | solution.py:454
  15.5 1.5 %collective-permute-start.1 = (bf16[4,16,24,128]{3,2,1,0:T(8,128)(2,1)S(1)}, bf16[4,16,24,128]{3,2,1,0:T(8,128)(2,1)S(1)}, u32[]{:S(2)}, u32[]{:S(2)}) collective-permute-start(bf16[4,16,24,128]{3,2,1,0:T(8,128)(2,1)S(1)} %get-tuple-element.47), channel_id=1, source_target_pairs={{0,2},{2,0},{1,3},{3,1},{4,6},{6,4},{5,7},{7,5},{8,10},{10,8},{9,1... | collective-permute-start | bytes 1179656 | tf_op jit(solution)/shard_map/ppermute | solution.py:459
  17.0 2.3 %collective-permute-done.3.rest_2_ = bf16[1,16,24,128]{3,2,1,0:T(8,128)(2,1)S(1)} collective-permute-done((bf16[1,16,24,128]{3,2,1,0:T(8,128)(2,1)S(1)}, bf16[1,16,24,128]{3,2,1,0:T(8,128)(2,1)S(1)}, u32[]{:S(2)}, u32[]{:S(2)}) %collective-permute-start.3) | collective-permute-done | bytes 98336 | tf_op jit(solution)/shard_map/ppermute | solution.py:454
  19.3 0.8 collective-permute-start.5
  20.0 1.7 %collective-permute-done.2 = bf16[2,16,24,128]{3,2,1,0:T(8,128)(2,1)S(1)} collective-permute-done((bf16[2,16,24,128]{3,2,1,0:T(8,128)(2,1)S(1)}, bf16[2,16,24,128]{3,2,1,0:T(8,128)(2,1)S(1)}, u32[]{:S(2)}, u32[]{:S(2)}) %collective-permute-start.2) | collective-permute-done | bytes 196640 | tf_op jit(solution)/shard_map/ppermute | solution.py:454
  21.8 1.8 %collective-permute-start.6 = (bf16[1,16,24,128]{3,2,1,0:T(8,128)(2,1)S(1)}, bf16[1,16,24,128]{3,2,1,0:T(8,128)(2,1)S(1)}, u32[]{:S(2)}, u32[]{:S(2)}) collective-permute-start(bf16[1,16,24,128]{3,2,1,0:T(8,128)(2,1)S(1)} %add_convert_fusion.10), channel_id=1, source_target_pairs={{0,8},{4,12},{8,0},{12,4},{1,9},{5,13},{9,1},{13,5},{2,10},{6,14},... | collective-permute-start | bytes 294920 | tf_op jit(solution)/shard_map/ppermute | solution.py:454
  23.6 2.7 %collective-permute-done.1.refs_0_ = bf16[4,16,24,128]{3,2,1,0:T(8,128)(2,1)S(1)} collective-permute-done((bf16[4,16,24,128]{3,2,1,0:T(8,128)(2,1)S(1)}, bf16[4,16,24,128]{3,2,1,0:T(8,128)(2,1)S(1)}, u32[]{:S(2)}, u32[]{:S(2)}) %collective-permute-start.1) | collective-permute-done | bytes 393248 | tf_op jit(solution)/shard_map/ppermute | solution.py:459
  26.4 1.7 %collective-permute-done.5 = bf16[2,16,24,128]{3,2,1,0:T(8,128)(2,1)S(1)} collective-permute-done((bf16[2,16,24,128]{3,2,1,0:T(8,128)(2,1)S(1)}, bf16[2,16,24,128]{3,2,1,0:T(8,128)(2,1)S(1)}, u32[]{:S(2)}, u32[]{:S(2)}) %collective-permute-start.5) | collective-permute-done | bytes 196640 | tf_op jit(solution)/shard_map/ppermute | solution.py:454
  28.1 0.1 constant_dynamic-update-slice_fusion
  28.2 2.1 %backward_step.2 = (bf16[4,16,24,128]{3,2,1,0:T(8,128)(2,1)S(1)}, bf16[4,16,24,128]{3,2,1,0:T(8,128)(2,1)S(1)}) custom-call(s32[2]{0:T(128)S(1)} %pad_add_fusion.meta, s32[3,64]{1,0:T(4,128)S(1)} %bitcast.21, s32[3,64]{1,0:T(4,128)S(1)} %collective-permute-done.8.cols_other, bf16[32,3,128,128]{3,2,1,0:T(8,128)(2,1)S(1)} %get-tuple-element.51.own, ...), custom_call_target="tpu_custom_call" | custom-call | flops 805306368 | bytes 25165824 | tf_op jit(solution)/shard_map/backward_step/pallas_call | solution.py:353
  30.3 0.1 collective-permute-start.10
  30.4 0.5 collective-permute-start.11
  31.0 0.1 collective-permute-start.12
  31.0 1.5 %collective-permute-start.7 = (bf16[5,16,24,128]{3,2,1,0:T(8,128)(2,1)S(1)}, bf16[5,16,24,128]{3,2,1,0:T(8,128)(2,1)S(1)}, u32[]{:S(2)}, u32[]{:S(2)}) collective-permute-start(bf16[5,16,24,128]{3,2,1,0:T(8,128)(2,1)S(1)} %get-tuple-element.81), channel_id=1, source_target_pairs={{0,2},{2,0},{1,3},{3,1},{4,6},{6,4},{5,7},{7,5},{8,10},{10,8},{9,1... | collective-permute-start | bytes 1474568 | tf_op jit(solution)/shard_map/ppermute | solution.py:459
  32.6 0.1 collective-permute-done.12.rest_5_
  32.6 2.6 %forward_step.2 = (bf16[256,16,128]{2,1,0:T(8,128)(2,1)S(1)}, bf16[1,16,24,128]{3,2,1,0:T(8,128)(2,1)S(1)}) custom-call(s32[2]{0:T(128)S(1)} %pad_add_fusion.meta, s32[3,64]{1,0:T(4,128)S(1)} %bitcast.22, s32[3,64]{1,0:T(4,128)S(1)} %collective-permute-done.8.cols_other, bf16[32,3,128,128]{3,2,1,0:T(8,128)(2,1)S(1)} %get-tuple-element.51.own, ...), custom_call_target="tpu_custom_call" | custom-call | flops 805306368 | bytes 25165824 | tf_op jit(solution)/shard_map/forward_step/pallas_call | solution.py:271
  35.3 2.3 %collective-permute-start.14 = (bf16[1,16,24,128]{3,2,1,0:T(8,128)(2,1)S(1)}, bf16[1,16,24,128]{3,2,1,0:T(8,128)(2,1)S(1)}, u32[]{:S(2)}, u32[]{:S(2)}) collective-permute-start(bf16[1,16,24,128]{3,2,1,0:T(8,128)(2,1)S(1)} %get-tuple-element.56.rest_0_), channel_id=1, source_target_pairs={{0,8},{4,12},{8,0},{12,4},{1,9},{5,13},{9,1},{13,5},{2,10},{6,14},... | collective-permute-start | bytes 294920 | tf_op jit(solution)/shard_map/ppermute | solution.py:454
  37.5 0.1 add_convert_fusion.5
  37.6 2.1 %collective-permute-start.13 = (bf16[2,16,24,128]{3,2,1,0:T(8,128)(2,1)S(1)}, bf16[2,16,24,128]{3,2,1,0:T(8,128)(2,1)S(1)}, u32[]{:S(2)}, u32[]{:S(2)}) collective-permute-start(bf16[2,16,24,128]{3,2,1,0:T(8,128)(2,1)S(1)} %pad_maximum_fusion.7), channel_id=1, source_target_pairs={{0,4},{4,0},{8,12},{12,8},{1,5},{5,1},{9,13},{13,9},{2,6},{6,2},{1... | collective-permute-start | bytes 589832 | tf_op jit(solution)/shard_map/ppermute | solution.py:454
  39.7 2.7 %collective-permute-done.14.rest_2_ = bf16[1,16,24,128]{3,2,1,0:T(8,128)(2,1)S(1)} collective-permute-done((bf16[1,16,24,128]{3,2,1,0:T(8,128)(2,1)S(1)}, bf16[1,16,24,128]{3,2,1,0:T(8,128)(2,1)S(1)}, u32[]{:S(2)}, u32[]{:S(2)}) %collective-permute-start.14) | collective-permute-done | bytes 98336 | tf_op jit(solution)/shard_map/ppermute | solution.py:454
  42.4 2.1 %collective-permute-start.16 = (bf16[2,16,24,128]{3,2,1,0:T(8,128)(2,1)S(1)}, bf16[2,16,24,128]{3,2,1,0:T(8,128)(2,1)S(1)}, u32[]{:S(2)}, u32[]{:S(2)}) collective-permute-start(bf16[2,16,24,128]{3,2,1,0:T(8,128)(2,1)S(1)} %pad_maximum_fusion.8), channel_id=1, source_target_pairs={{0,4},{4,0},{8,12},{12,8},{1,5},{5,1},{9,13},{13,9},{2,6},{6,2},{1... | collective-permute-start | bytes 589832 | tf_op jit(solution)/shard_map/ppermute | solution.py:454
  44.5 1.0 %collective-permute-done.13 = bf16[2,16,24,128]{3,2,1,0:T(8,128)(2,1)S(1)} collective-permute-done((bf16[2,16,24,128]{3,2,1,0:T(8,128)(2,1)S(1)}, bf16[2,16,24,128]{3,2,1,0:T(8,128)(2,1)S(1)}, u32[]{:S(2)}, u32[]{:S(2)}) %collective-permute-start.13) | collective-permute-done | bytes 196640 | tf_op jit(solution)/shard_map/ppermute | solution.py:454
  45.6 2.4 %collective-permute-start.18 = (bf16[1,16,24,128]{3,2,1,0:T(8,128)(2,1)S(1)}, bf16[1,16,24,128]{3,2,1,0:T(8,128)(2,1)S(1)}, u32[]{:S(2)}, u32[]{:S(2)}) collective-permute-start(bf16[1,16,24,128]{3,2,1,0:T(8,128)(2,1)S(1)} %add_convert_fusion.6), channel_id=1, source_target_pairs={{0,8},{4,12},{8,0},{12,4},{1,9},{5,13},{9,1},{13,5},{2,10},{6,14},... | collective-permute-start | bytes 294920 | tf_op jit(solution)/shard_map/ppermute | solution.py:454
  47.9 0.1 pad_maximum_fusion
  48.0 0.1 collective-permute-start.15
  48.2 0.6 collective-permute-start.17
  48.7 2.8 %collective-permute-done.16 = bf16[2,16,24,128]{3,2,1,0:T(8,128)(2,1)S(1)} collective-permute-done((bf16[2,16,24,128]{3,2,1,0:T(8,128)(2,1)S(1)}, bf16[2,16,24,128]{3,2,1,0:T(8,128)(2,1)S(1)}, u32[]{:S(2)}, u32[]{:S(2)}) %collective-permute-start.16) | collective-permute-done | bytes 196640 | tf_op jit(solution)/shard_map/ppermute | solution.py:454
  51.6 0.1 constant_dynamic-update-slice_fusion.5
  51.7 2.1 %backward_step.3 = (bf16[4,16,24,128]{3,2,1,0:T(8,128)(2,1)S(1)}, bf16[4,16,24,128]{3,2,1,0:T(8,128)(2,1)S(1)}) custom-call(s32[2]{0:T(128)S(1)} %pad_add_fusion.meta, s32[3,64]{1,0:T(4,128)S(1)} %bitcast.23, s32[3,64]{1,0:T(4,128)S(1)} %collective-permute-done.8.cols_other, bf16[32,3,128,128]{3,2,1,0:T(8,128)(2,1)S(1)} %get-tuple-element.51.own, ...), custom_call_target="tpu_custom_call" | custom-call | flops 805306368 | bytes 25165824 | tf_op jit(solution)/shard_map/backward_step/pallas_call | solution.py:353
  53.8 0.1 collective-permute-start.20
  53.9 0.5 collective-permute-start.21
  54.4 1.5 %collective-permute-start.19 = (bf16[5,16,24,128]{3,2,1,0:T(8,128)(2,1)S(1)}, bf16[5,16,24,128]{3,2,1,0:T(8,128)(2,1)S(1)}, u32[]{:S(2)}, u32[]{:S(2)}) collective-permute-start(bf16[5,16,24,128]{3,2,1,0:T(8,128)(2,1)S(1)} %get-tuple-element.79), channel_id=1, source_target_pairs={{0,2},{2,0},{1,3},{3,1},{4,6},{6,4},{5,7},{7,5},{8,10},{10,8},{9,1... | collective-permute-start | bytes 1474568 | tf_op jit(solution)/shard_map/ppermute | solution.py:459
  55.9 2.6 %forward_step.3 = (bf16[256,16,128]{2,1,0:T(8,128)(2,1)S(1)}, bf16[1,16,24,128]{3,2,1,0:T(8,128)(2,1)S(1)}) custom-call(s32[2]{0:T(128)S(1)} %pad_add_fusion.meta, s32[3,64]{1,0:T(4,128)S(1)} %bitcast.24, s32[3,64]{1,0:T(4,128)S(1)} %collective-permute-done.8.cols_other, bf16[32,3,128,128]{3,2,1,0:T(8,128)(2,1)S(1)} %get-tuple-element.51.own, ...), custom_call_target="tpu_custom_call" | custom-call | flops 805306368 | bytes 25165824 | tf_op jit(solution)/shard_map/forward_step/pallas_call | solution.py:271
  58.5 2.2 %collective-permute-start.23 = (bf16[1,16,24,128]{3,2,1,0:T(8,128)(2,1)S(1)}, bf16[1,16,24,128]{3,2,1,0:T(8,128)(2,1)S(1)}, u32[]{:S(2)}, u32[]{:S(2)}) collective-permute-start(bf16[1,16,24,128]{3,2,1,0:T(8,128)(2,1)S(1)} %get-tuple-element.64.refs_0_), channel_id=1, source_target_pairs={{0,8},{4,12},{8,0},{12,4},{1,9},{5,13},{9,1},{13,5},{2,10},{6,14},... | collective-permute-start | bytes 294920 | tf_op jit(solution)/shard_map/ppermute | solution.py:454
  60.8 0.1 add_convert_fusion.1
  60.9 2.7 %collective-permute-start.22 = (bf16[2,16,24,128]{3,2,1,0:T(8,128)(2,1)S(1)}, bf16[2,16,24,128]{3,2,1,0:T(8,128)(2,1)S(1)}, u32[]{:S(2)}, u32[]{:S(2)}) collective-permute-start(bf16[2,16,24,128]{3,2,1,0:T(8,128)(2,1)S(1)} %pad_maximum_fusion.9), channel_id=1, source_target_pairs={{0,4},{4,0},{8,12},{12,8},{1,5},{5,1},{9,13},{13,9},{2,6},{6,2},{1... | collective-permute-start | bytes 589832 | tf_op jit(solution)/shard_map/ppermute | solution.py:454
  63.6 1.8 %collective-permute-done.23.refs_2_ = bf16[1,16,24,128]{3,2,1,0:T(8,128)(2,1)S(1)} collective-permute-done((bf16[1,16,24,128]{3,2,1,0:T(8,128)(2,1)S(1)}, bf16[1,16,24,128]{3,2,1,0:T(8,128)(2,1)S(1)}, u32[]{:S(2)}, u32[]{:S(2)}) %collective-permute-start.23) | collective-permute-done | bytes 98336 | tf_op jit(solution)/shard_map/ppermute | solution.py:454
  65.4 3.0 %collective-permute-done.22 = bf16[2,16,24,128]{3,2,1,0:T(8,128)(2,1)S(1)} collective-permute-done((bf16[2,16,24,128]{3,2,1,0:T(8,128)(2,1)S(1)}, bf16[2,16,24,128]{3,2,1,0:T(8,128)(2,1)S(1)}, u32[]{:S(2)}, u32[]{:S(2)}) %collective-permute-start.22) | collective-permute-done | bytes 196640 | tf_op jit(solution)/shard_map/ppermute | solution.py:454
  68.4 0.1 pad_maximum_fusion.1
  68.5 0.1 collective-permute-start.24
  68.6 0.6 collective-permute-start.26
  69.2 1.7 %collective-permute-start.25 = (bf16[2,16,24,128]{3,2,1,0:T(8,128)(2,1)S(1)}, bf16[2,16,24,128]{3,2,1,0:T(8,128)(2,1)S(1)}, u32[]{:S(2)}, u32[]{:S(2)}) collective-permute-start(bf16[2,16,24,128]{3,2,1,0:T(8,128)(2,1)S(1)} %pad_maximum_fusion.10), channel_id=1, source_target_pairs={{0,4},{4,0},{8,12},{12,8},{1,5},{5,1},{9,13},{13,9},{2,6},{6,2},{1... | collective-permute-start | bytes 589832 | tf_op jit(solution)/shard_map/ppermute | solution.py:454
  70.9 2.7 %collective-permute-start.27 = (bf16[1,16,24,128]{3,2,1,0:T(8,128)(2,1)S(1)}, bf16[1,16,24,128]{3,2,1,0:T(8,128)(2,1)S(1)}, u32[]{:S(2)}, u32[]{:S(2)}) collective-permute-start(bf16[1,16,24,128]{3,2,1,0:T(8,128)(2,1)S(1)} %add_convert_fusion.2), channel_id=1, source_target_pairs={{0,8},{4,12},{8,0},{12,4},{1,9},{5,13},{9,1},{13,5},{2,10},{6,14},... | collective-permute-start | bytes 294920 | tf_op jit(solution)/shard_map/ppermute | solution.py:454
  73.6 1.5 %collective-permute-start.29 = (bf16[3,16,24,128]{3,2,1,0:T(8,128)(2,1)S(1)}, bf16[3,16,24,128]{3,2,1,0:T(8,128)(2,1)S(1)}, u32[]{:S(2)}, u32[]{:S(2)}) collective-permute-start(bf16[3,16,24,128]{3,2,1,0:T(8,128)(2,1)S(1)} %pad_maximum_fusion.4), channel_id=1, source_target_pairs={{0,2},{2,0},{1,3},{3,1},{4,6},{6,4},{5,7},{7,5},{8,10},{10,8},{9,1... | collective-permute-start | bytes 884744 | tf_op jit(solution)/shard_map/ppermute | solution.py:459
  75.1 3.1 %collective-permute-done.25 = bf16[2,16,24,128]{3,2,1,0:T(8,128)(2,1)S(1)} collective-permute-done((bf16[2,16,24,128]{3,2,1,0:T(8,128)(2,1)S(1)}, bf16[2,16,24,128]{3,2,1,0:T(8,128)(2,1)S(1)}, u32[]{:S(2)}, u32[]{:S(2)}) %collective-permute-start.25) | collective-permute-done | bytes 196640 | tf_op jit(solution)/shard_map/ppermute | solution.py:454
  78.2 0.1 add_convert_fusion.refs_6_
  78.3 0.1 collective-permute-start.28
  78.4 1.6 %collective-permute-start.30 = (bf16[2,16,24,128]{3,2,1,0:T(8,128)(2,1)S(1)}, bf16[2,16,24,128]{3,2,1,0:T(8,128)(2,1)S(1)}, u32[]{:S(2)}, u32[]{:S(2)}) collective-permute-start(bf16[2,16,24,128]{3,2,1,0:T(8,128)(2,1)S(1)} %pad_maximum_fusion.11), channel_id=1, source_target_pairs={{0,2},{2,0},{1,3},{3,1},{4,6},{6,4},{5,7},{7,5},{8,10},{10,8},{9,1... | collective-permute-start | bytes 589832 | tf_op jit(solution)/shard_map/ppermute | solution.py:459
  80.0 2.4 %collective-permute-done.29.refs_0_ = bf16[3,16,24,128]{3,2,1,0:T(8,128)(2,1)S(1)} collective-permute-done((bf16[3,16,24,128]{3,2,1,0:T(8,128)(2,1)S(1)}, bf16[3,16,24,128]{3,2,1,0:T(8,128)(2,1)S(1)}, u32[]{:S(2)}, u32[]{:S(2)}) %collective-permute-start.29) | collective-permute-done | bytes 294944 | tf_op jit(solution)/shard_map/ppermute | solution.py:459
  82.4 0.8 unpack_panels.5.refs_1_.refs_15_
  83.3 1.2 %unpack_panels.6 = (bf16[256,16,128]{2,1,0:T(8,128)(2,1)S(1)}, bf16[64,16,128]{2,1,0:T(8,128)(2,1)S(1)}, bf16[64,16,128]{2,1,0:T(8,128)(2,1)S(1)}) custom-call(s32[2]{0:T(128)S(1)} %pad_add_fusion.meta, bf16[5,16,24,128]{3,2,1,0:T(8,128)(2,1)S(1)} %collective-permute-done.7.refs_0_.refs_2_, ...), custom_call_target="tpu_custom_call" | custom-call | tf_op jit(solution)/shard_map/unpack_panels/pallas_call | solution.py:80
  84.4 1.0 %unpack_panels.7 = (bf16[256,16,128]{2,1,0:T(8,128)(2,1)S(1)}, bf16[64,16,128]{2,1,0:T(8,128)(2,1)S(1)}, bf16[64,16,128]{2,1,0:T(8,128)(2,1)S(1)}) custom-call(s32[2]{0:T(128)S(1)} %pad_add_fusion.meta, bf16[5,16,24,128]{3,2,1,0:T(8,128)(2,1)S(1)} %collective-permute-done.19.refs_0_.refs_2_, ...), custom_call_target="tpu_custom_call" | custom-call | tf_op jit(solution)/shard_map/unpack_panels/pallas_call | solution.py:80
  85.4 0.9 unpack_panels.8
  86.3 0.6 collective-permute-start.32
  86.9 1.1 %collective-permute-done.32.refs_3_.refs_5_ = bf16[2,16,24,128]{3,2,1,0:T(8,128)(2,1)S(1)} collective-permute-done((bf16[2,16,24,128]{3,2,1,0:T(8,128)(2,1)S(1)}, bf16[2,16,24,128]{3,2,1,0:T(8,128)(2,1)S(1)}, u32[]{:S(2)}, u32[]{:S(2)}) %collective-permute-start.32) | collective-permute-done | bytes 196640 | tf_op jit(solution)/shard_map/ppermute | solution.py:451
  88.0 0.9 unpack_panels.9
  88.9 3.7 %gradient.1 = bf16[64,3,128,128]{3,2,1,0:T(8,128)(2,1)} custom-call(s32[2]{0:T(128)S(1)} %pad_add_fusion.meta, s32[3,64]{1,0:T(4,128)S(1)} %bitcast.25, bf16[256,16,128]{2,1,0:T(8,128)(2,1)S(1)} %get-tuple-element.42.refs_0_.refs_14_, bf16[256,16,128]{2,1,0:T(8,128)(2,1)S(1)} %unpack_panels.5.refs_1_.refs_15_, ...), custom_call_target="tpu_custom_call" | custom-call | tf_op jit(solution)/shard_map/gradient/pallas_call | solution.py:413
  (47 shorter events, 0.7 us)
Async XLA Ops:
  0.1 16.9 %copy-start = (s32[64,3]{0,1:T(4,128)S(1)}, s32[64,3]{0,1:T(4,128)}, u32[]{:S(2)}) copy-start(s32[64,3]{0,1:T(4,128)} %param.4) | copy-start | bytes 2308
  7.5 2.0 %collective-permute-start = (bf16[5,16,24,128]{3,2,1,0:T(8,128)(2,1)S(1)}, bf16[5,16,24,128]{3,2,1,0:T(8,128)(2,1)S(1)}, u32[]{:S(2)}, u32[]{:S(2)}) collective-permute-start(bf16[5,16,24,128]{3,2,1,0:T(8,128)(2,1)S(1)} %get-tuple-element.46), channel_id=1, source_target_pairs={{0,1},{1,0},{2,3},{3,2},{4,5},{5,4},{6,7},{7,6},{8,9},{9,8},{10,11... | collective-permute-start | bytes 1474568 | tf_op jit(solution)/shard_map/ppermute | solution.py:451
  9.6 18.6 %collective-permute-start.9 = (bf16[32,3,128,128]{3,2,1,0:T(8,128)(2,1)S(1)}, bf16[32,3,128,128]{3,2,1,0:T(8,128)(2,1)S(1)}, u32[]{:S(2)}, u32[]{:S(2)}) collective-permute-start(bf16[32,3,128,128]{3,2,1,0:T(8,128)(2,1)S(1)} %get-tuple-element.53), channel_id=1, source_target_pairs={{0,1},{1,0},{2,3},{3,2},{4,5},{5,4},{6,7},{7,6},{8,9},{9,8},{10,11... | collective-permute-start | bytes 9437192 | tf_op jit(solution)/shard_map/ppermute | solution.py:451
  10.0 9.3 %collective-permute-start.3 = (bf16[1,16,24,128]{3,2,1,0:T(8,128)(2,1)S(1)}, bf16[1,16,24,128]{3,2,1,0:T(8,128)(2,1)S(1)}, u32[]{:S(2)}, u32[]{:S(2)}) collective-permute-start(bf16[1,16,24,128]{3,2,1,0:T(8,128)(2,1)S(1)} %get-tuple-element.84.rest_0_), channel_id=1, source_target_pairs={{0,8},{4,12},{8,0},{12,4},{1,9},{5,13},{9,1},{13,5},{2,10},{6,14},... | collective-permute-start | bytes 294920 | tf_op jit(solution)/shard_map/ppermute | solution.py:454
  13.8 7.9 %collective-permute-start.2 = (bf16[2,16,24,128]{3,2,1,0:T(8,128)(2,1)S(1)}, bf16[2,16,24,128]{3,2,1,0:T(8,128)(2,1)S(1)}, u32[]{:S(2)}, u32[]{:S(2)}) collective-permute-start(bf16[2,16,24,128]{3,2,1,0:T(8,128)(2,1)S(1)} %pad_maximum_fusion.5), channel_id=1, source_target_pairs={{0,4},{4,0},{8,12},{12,8},{1,5},{5,1},{9,13},{13,9},{2,6},{6,2},{1... | collective-permute-start | bytes 589832 | tf_op jit(solution)/shard_map/ppermute | solution.py:454
  15.5 10.8 %collective-permute-start.1 = (bf16[4,16,24,128]{3,2,1,0:T(8,128)(2,1)S(1)}, bf16[4,16,24,128]{3,2,1,0:T(8,128)(2,1)S(1)}, u32[]{:S(2)}, u32[]{:S(2)}) collective-permute-start(bf16[4,16,24,128]{3,2,1,0:T(8,128)(2,1)S(1)} %get-tuple-element.47), channel_id=1, source_target_pairs={{0,2},{2,0},{1,3},{3,1},{4,6},{6,4},{5,7},{7,5},{8,10},{10,8},{9,1... | collective-permute-start | bytes 1179656 | tf_op jit(solution)/shard_map/ppermute | solution.py:459
  17.0 11.2 %collective-permute-start.8 = (s32[3,64]{1,0:T(4,128)S(1)}, s32[3,64]{1,0:T(4,128)S(1)}, u32[]{:S(2)}, u32[]{:S(2)}) collective-permute-start(s32[3,64]{1,0:T(4,128)S(1)} %bitcast.20), channel_id=1, source_target_pairs={{0,1},{1,0},{2,3},{3,2},{4,5},{5,4},{6,7},{7,6},{8,9},{9,8},{10,11... | collective-permute-start | bytes 2312 | tf_op jit(solution)/shard_map/ppermute | solution.py:451
  19.3 8.7 %collective-permute-start.5 = (bf16[2,16,24,128]{3,2,1,0:T(8,128)(2,1)S(1)}, bf16[2,16,24,128]{3,2,1,0:T(8,128)(2,1)S(1)}, u32[]{:S(2)}, u32[]{:S(2)}) collective-permute-start(bf16[2,16,24,128]{3,2,1,0:T(8,128)(2,1)S(1)} %pad_maximum_fusion.6), channel_id=1, source_target_pairs={{0,4},{4,0},{8,12},{12,8},{1,5},{5,1},{9,13},{13,9},{2,6},{6,2},{1... | collective-permute-start | bytes 589832 | tf_op jit(solution)/shard_map/ppermute | solution.py:454
  21.8 6.3 %collective-permute-start.6 = (bf16[1,16,24,128]{3,2,1,0:T(8,128)(2,1)S(1)}, bf16[1,16,24,128]{3,2,1,0:T(8,128)(2,1)S(1)}, u32[]{:S(2)}, u32[]{:S(2)}) collective-permute-start(bf16[1,16,24,128]{3,2,1,0:T(8,128)(2,1)S(1)} %add_convert_fusion.10), channel_id=1, source_target_pairs={{0,8},{4,12},{8,0},{12,4},{1,9},{5,13},{9,1},{13,5},{2,10},{6,14},... | collective-permute-start | bytes 294920 | tf_op jit(solution)/shard_map/ppermute | solution.py:454
  26.3 1.8 %collective-permute-start.4 = (bf16[4,16,24,128]{3,2,1,0:T(8,128)(2,1)S(1)}, bf16[4,16,24,128]{3,2,1,0:T(8,128)(2,1)S(1)}, u32[]{:S(2)}, u32[]{:S(2)}) collective-permute-start(bf16[4,16,24,128]{3,2,1,0:T(8,128)(2,1)S(1)} %collective-permute-done.1.refs_0_), channel_id=1, source_target_pairs={{0,1},{1,0},{2,3},{3,2},{4,5},{5,4},{6,7},{7,6},{8,9},{9,8},{10,11... | collective-permute-start | bytes 1179656 | tf_op jit(solution)/shard_map/ppermute | solution.py:451
  30.3 7.2 %collective-permute-start.10 = (bf16[4,16,24,128]{3,2,1,0:T(8,128)(2,1)S(1)}, bf16[4,16,24,128]{3,2,1,0:T(8,128)(2,1)S(1)}, u32[]{:S(2)}, u32[]{:S(2)}) collective-permute-start(bf16[4,16,24,128]{3,2,1,0:T(8,128)(2,1)S(1)} %get-tuple-element.55.rest_6_), channel_id=1, source_target_pairs={{0,1},{1,0},{2,3},{3,2},{4,5},{5,4},{6,7},{7,6},{8,9},{9,8},{10,11... | collective-permute-start | bytes 1179656 | tf_op jit(solution)/shard_map/ppermute | solution.py:451
  30.4 2.2 %collective-permute-start.11 = (bf16[3,16,24,128]{3,2,1,0:T(8,128)(2,1)S(1)}, bf16[3,16,24,128]{3,2,1,0:T(8,128)(2,1)S(1)}, u32[]{:S(2)}, u32[]{:S(2)}) collective-permute-start(bf16[3,16,24,128]{3,2,1,0:T(8,128)(2,1)S(1)} %pad_maximum_fusion.2), channel_id=1, source_target_pairs={{0,1},{1,0},{2,3},{3,2},{4,5},{5,4},{6,7},{7,6},{8,9},{9,8},{10,11... | collective-permute-start | bytes 884744 | tf_op jit(solution)/shard_map/ppermute | solution.py:451
  31.0 1.7 %collective-permute-start.12 = (bf16[1,16,24,128]{3,2,1,0:T(8,128)(2,1)S(1)}, bf16[1,16,24,128]{3,2,1,0:T(8,128)(2,1)S(1)}, u32[]{:S(2)}, u32[]{:S(2)}) collective-permute-start(bf16[1,16,24,128]{3,2,1,0:T(8,128)(2,1)S(1)} %get-tuple-element.95.rest_3_), channel_id=1, source_target_pairs={{0,1},{1,0},{2,3},{3,2},{4,5},{5,4},{6,7},{7,6},{8,9},{9,8},{10,11... | collective-permute-start | bytes 294920 | tf_op jit(solution)/shard_map/ppermute | solution.py:451
  31.0 16.9 %collective-permute-start.7 = (bf16[5,16,24,128]{3,2,1,0:T(8,128)(2,1)S(1)}, bf16[5,16,24,128]{3,2,1,0:T(8,128)(2,1)S(1)}, u32[]{:S(2)}, u32[]{:S(2)}) collective-permute-start(bf16[5,16,24,128]{3,2,1,0:T(8,128)(2,1)S(1)} %get-tuple-element.81), channel_id=1, source_target_pairs={{0,2},{2,0},{1,3},{3,1},{4,6},{6,4},{5,7},{7,5},{8,10},{10,8},{9,1... | collective-permute-start | bytes 1474568 | tf_op jit(solution)/shard_map/ppermute | solution.py:459
  35.3 7.1 %collective-permute-start.14 = (bf16[1,16,24,128]{3,2,1,0:T(8,128)(2,1)S(1)}, bf16[1,16,24,128]{3,2,1,0:T(8,128)(2,1)S(1)}, u32[]{:S(2)}, u32[]{:S(2)}) collective-permute-start(bf16[1,16,24,128]{3,2,1,0:T(8,128)(2,1)S(1)} %get-tuple-element.56.rest_0_), channel_id=1, source_target_pairs={{0,8},{4,12},{8,0},{12,4},{1,9},{5,13},{9,1},{13,5},{2,10},{6,14},... | collective-permute-start | bytes 294920 | tf_op jit(solution)/shard_map/ppermute | solution.py:454
  37.6 7.9 %collective-permute-start.13 = (bf16[2,16,24,128]{3,2,1,0:T(8,128)(2,1)S(1)}, bf16[2,16,24,128]{3,2,1,0:T(8,128)(2,1)S(1)}, u32[]{:S(2)}, u32[]{:S(2)}) collective-permute-start(bf16[2,16,24,128]{3,2,1,0:T(8,128)(2,1)S(1)} %pad_maximum_fusion.7), channel_id=1, source_target_pairs={{0,4},{4,0},{8,12},{12,8},{1,5},{5,1},{9,13},{13,9},{2,6},{6,2},{1... | collective-permute-start | bytes 589832 | tf_op jit(solution)/shard_map/ppermute | solution.py:454
  42.4 9.1 %collective-permute-start.16 = (bf16[2,16,24,128]{3,2,1,0:T(8,128)(2,1)S(1)}, bf16[2,16,24,128]{3,2,1,0:T(8,128)(2,1)S(1)}, u32[]{:S(2)}, u32[]{:S(2)}) collective-permute-start(bf16[2,16,24,128]{3,2,1,0:T(8,128)(2,1)S(1)} %pad_maximum_fusion.8), channel_id=1, source_target_pairs={{0,4},{4,0},{8,12},{12,8},{1,5},{5,1},{9,13},{13,9},{2,6},{6,2},{1... | collective-permute-start | bytes 589832 | tf_op jit(solution)/shard_map/ppermute | solution.py:454
  45.6 6.1 %collective-permute-start.18 = (bf16[1,16,24,128]{3,2,1,0:T(8,128)(2,1)S(1)}, bf16[1,16,24,128]{3,2,1,0:T(8,128)(2,1)S(1)}, u32[]{:S(2)}, u32[]{:S(2)}) collective-permute-start(bf16[1,16,24,128]{3,2,1,0:T(8,128)(2,1)S(1)} %add_convert_fusion.6), channel_id=1, source_target_pairs={{0,8},{4,12},{8,0},{12,4},{1,9},{5,13},{9,1},{13,5},{2,10},{6,14},... | collective-permute-start | bytes 294920 | tf_op jit(solution)/shard_map/ppermute | solution.py:454
  48.0 3.6 %collective-permute-start.15 = (bf16[6,16,24,128]{3,2,1,0:T(8,128)(2,1)S(1)}, bf16[6,16,24,128]{3,2,1,0:T(8,128)(2,1)S(1)}, u32[]{:S(2)}, u32[]{:S(2)}) collective-permute-start(bf16[6,16,24,128]{3,2,1,0:T(8,128)(2,1)S(1)} %pad_maximum_fusion), channel_id=1, source_target_pairs={{0,1},{1,0},{2,3},{3,2},{4,5},{5,4},{6,7},{7,6},{8,9},{9,8},{10,11... | collective-permute-start | bytes 1769480 | tf_op jit(solution)/shard_map/ppermute | solution.py:451
  48.2 3.4 %collective-permute-start.17 = (bf16[3,16,24,128]{3,2,1,0:T(8,128)(2,1)S(1)}, bf16[3,16,24,128]{3,2,1,0:T(8,128)(2,1)S(1)}, u32[]{:S(2)}, u32[]{:S(2)}) collective-permute-start(bf16[3,16,24,128]{3,2,1,0:T(8,128)(2,1)S(1)} %pad_maximum_fusion.3), channel_id=1, source_target_pairs={{0,1},{1,0},{2,3},{3,2},{4,5},{5,4},{6,7},{7,6},{8,9},{9,8},{10,11... | collective-permute-start | bytes 884744 | tf_op jit(solution)/shard_map/ppermute | solution.py:451
  53.8 7.0 %collective-permute-start.20 = (bf16[4,16,24,128]{3,2,1,0:T(8,128)(2,1)S(1)}, bf16[4,16,24,128]{3,2,1,0:T(8,128)(2,1)S(1)}, u32[]{:S(2)}, u32[]{:S(2)}) collective-permute-start(bf16[4,16,24,128]{3,2,1,0:T(8,128)(2,1)S(1)} %get-tuple-element.63.rest_6_), channel_id=1, source_target_pairs={{0,1},{1,0},{2,3},{3,2},{4,5},{5,4},{6,7},{7,6},{8,9},{9,8},{10,11... | collective-permute-start | bytes 1179656 | tf_op jit(solution)/shard_map/ppermute | solution.py:451
  53.9 2.0 %collective-permute-start.21 = (bf16[1,16,24,128]{3,2,1,0:T(8,128)(2,1)S(1)}, bf16[1,16,24,128]{3,2,1,0:T(8,128)(2,1)S(1)}, u32[]{:S(2)}, u32[]{:S(2)}) collective-permute-start(bf16[1,16,24,128]{3,2,1,0:T(8,128)(2,1)S(1)} %get-tuple-element.91.rest_3_), channel_id=1, source_target_pairs={{0,1},{1,0},{2,3},{3,2},{4,5},{5,4},{6,7},{7,6},{8,9},{9,8},{10,11... | collective-permute-start | bytes 294920 | tf_op jit(solution)/shard_map/ppermute | solution.py:451
  54.4 14.1 %collective-permute-start.19 = (bf16[5,16,24,128]{3,2,1,0:T(8,128)(2,1)S(1)}, bf16[5,16,24,128]{3,2,1,0:T(8,128)(2,1)S(1)}, u32[]{:S(2)}, u32[]{:S(2)}) collective-permute-start(bf16[5,16,24,128]{3,2,1,0:T(8,128)(2,1)S(1)} %get-tuple-element.79), channel_id=1, source_target_pairs={{0,2},{2,0},{1,3},{3,1},{4,6},{6,4},{5,7},{7,5},{8,10},{10,8},{9,1... | collective-permute-start | bytes 1474568 | tf_op jit(solution)/shard_map/ppermute | solution.py:459
  58.5 6.8 %collective-permute-start.23 = (bf16[1,16,24,128]{3,2,1,0:T(8,128)(2,1)S(1)}, bf16[1,16,24,128]{3,2,1,0:T(8,128)(2,1)S(1)}, u32[]{:S(2)}, u32[]{:S(2)}) collective-permute-start(bf16[1,16,24,128]{3,2,1,0:T(8,128)(2,1)S(1)} %get-tuple-element.64.refs_0_), channel_id=1, source_target_pairs={{0,8},{4,12},{8,0},{12,4},{1,9},{5,13},{9,1},{13,5},{2,10},{6,14},... | collective-permute-start | bytes 294920 | tf_op jit(solution)/shard_map/ppermute | solution.py:454
  60.9 7.5 %collective-permute-start.22 = (bf16[2,16,24,128]{3,2,1,0:T(8,128)(2,1)S(1)}, bf16[2,16,24,128]{3,2,1,0:T(8,128)(2,1)S(1)}, u32[]{:S(2)}, u32[]{:S(2)}) collective-permute-start(bf16[2,16,24,128]{3,2,1,0:T(8,128)(2,1)S(1)} %pad_maximum_fusion.9), channel_id=1, source_target_pairs={{0,4},{4,0},{8,12},{12,8},{1,5},{5,1},{9,13},{13,9},{2,6},{6,2},{1... | collective-permute-start | bytes 589832 | tf_op jit(solution)/shard_map/ppermute | solution.py:454
  68.5 9.7 %collective-permute-start.24 = (bf16[6,16,24,128]{3,2,1,0:T(8,128)(2,1)S(1)}, bf16[6,16,24,128]{3,2,1,0:T(8,128)(2,1)S(1)}, u32[]{:S(2)}, u32[]{:S(2)}) collective-permute-start(bf16[6,16,24,128]{3,2,1,0:T(8,128)(2,1)S(1)} %pad_maximum_fusion.1), channel_id=1, source_target_pairs={{0,1},{1,0},{2,3},{3,2},{4,5},{5,4},{6,7},{7,6},{8,9},{9,8},{10,11... | collective-permute-start | bytes 1769480 | tf_op jit(solution)/shard_map/ppermute | solution.py:451
  68.6 9.6 %collective-permute-start.26 = (bf16[3,16,24,128]{3,2,1,0:T(8,128)(2,1)S(1)}, bf16[3,16,24,128]{3,2,1,0:T(8,128)(2,1)S(1)}, u32[]{:S(2)}, u32[]{:S(2)}) collective-permute-start(bf16[3,16,24,128]{3,2,1,0:T(8,128)(2,1)S(1)} %pad_maximum_fusion.4), channel_id=1, source_target_pairs={{0,1},{1,0},{2,3},{3,2},{4,5},{5,4},{6,7},{7,6},{8,9},{9,8},{10,11... | collective-permute-start | bytes 884744 | tf_op jit(solution)/shard_map/ppermute | solution.py:451
  69.2 9.0 %collective-permute-start.25 = (bf16[2,16,24,128]{3,2,1,0:T(8,128)(2,1)S(1)}, bf16[2,16,24,128]{3,2,1,0:T(8,128)(2,1)S(1)}, u32[]{:S(2)}, u32[]{:S(2)}) collective-permute-start(bf16[2,16,24,128]{3,2,1,0:T(8,128)(2,1)S(1)} %pad_maximum_fusion.10), channel_id=1, source_target_pairs={{0,4},{4,0},{8,12},{12,8},{1,5},{5,1},{9,13},{13,9},{2,6},{6,2},{1... | collective-permute-start | bytes 589832 | tf_op jit(solution)/shard_map/ppermute | solution.py:454
  70.9 7.3 %collective-permute-start.27 = (bf16[1,16,24,128]{3,2,1,0:T(8,128)(2,1)S(1)}, bf16[1,16,24,128]{3,2,1,0:T(8,128)(2,1)S(1)}, u32[]{:S(2)}, u32[]{:S(2)}) collective-permute-start(bf16[1,16,24,128]{3,2,1,0:T(8,128)(2,1)S(1)} %add_convert_fusion.2), channel_id=1, source_target_pairs={{0,8},{4,12},{8,0},{12,4},{1,9},{5,13},{9,1},{13,5},{2,10},{6,14},... | collective-permute-start | bytes 294920 | tf_op jit(solution)/shard_map/ppermute | solution.py:454
  73.6 8.8 %collective-permute-start.29 = (bf16[3,16,24,128]{3,2,1,0:T(8,128)(2,1)S(1)}, bf16[3,16,24,128]{3,2,1,0:T(8,128)(2,1)S(1)}, u32[]{:S(2)}, u32[]{:S(2)}) collective-permute-start(bf16[3,16,24,128]{3,2,1,0:T(8,128)(2,1)S(1)} %pad_maximum_fusion.4), channel_id=1, source_target_pairs={{0,2},{2,0},{1,3},{3,1},{4,6},{6,4},{5,7},{7,5},{8,10},{10,8},{9,1... | collective-permute-start | bytes 884744 | tf_op jit(solution)/shard_map/ppermute | solution.py:459
  78.3 7.1 %collective-permute-start.28 = (bf16[2,16,24,128]{3,2,1,0:T(8,128)(2,1)S(1)}, bf16[2,16,24,128]{3,2,1,0:T(8,128)(2,1)S(1)}, u32[]{:S(2)}, u32[]{:S(2)}) collective-permute-start(bf16[2,16,24,128]{3,2,1,0:T(8,128)(2,1)S(1)} %pad_maximum_fusion.11), channel_id=1, source_target_pairs={{0,1},{1,0},{2,3},{3,2},{4,5},{5,4},{6,7},{7,6},{8,9},{9,8},{10,11... | collective-permute-start | bytes 589832 | tf_op jit(solution)/shard_map/ppermute | solution.py:451
  78.4 7.9 %collective-permute-start.30 = (bf16[2,16,24,128]{3,2,1,0:T(8,128)(2,1)S(1)}, bf16[2,16,24,128]{3,2,1,0:T(8,128)(2,1)S(1)}, u32[]{:S(2)}, u32[]{:S(2)}) collective-permute-start(bf16[2,16,24,128]{3,2,1,0:T(8,128)(2,1)S(1)} %pad_maximum_fusion.11), channel_id=1, source_target_pairs={{0,2},{2,0},{1,3},{3,1},{4,6},{6,4},{5,7},{7,5},{8,10},{10,8},{9,1... | collective-permute-start | bytes 589832 | tf_op jit(solution)/shard_map/ppermute | solution.py:459
  82.4 4.5 %collective-permute-start.31 = (bf16[3,16,24,128]{3,2,1,0:T(8,128)(2,1)S(1)}, bf16[3,16,24,128]{3,2,1,0:T(8,128)(2,1)S(1)}, u32[]{:S(2)}, u32[]{:S(2)}) collective-permute-start(bf16[3,16,24,128]{3,2,1,0:T(8,128)(2,1)S(1)} %collective-permute-done.29.refs_0_), channel_id=1, source_target_pairs={{0,1},{1,0},{2,3},{3,2},{4,5},{5,4},{6,7},{7,6},{8,9},{9,8},{10,11... | collective-permute-start | bytes 884744 | tf_op jit(solution)/shard_map/ppermute | solution.py:451
  86.3 1.6 %collective-permute-start.32 = (bf16[2,16,24,128]{3,2,1,0:T(8,128)(2,1)S(1)}, bf16[2,16,24,128]{3,2,1,0:T(8,128)(2,1)S(1)}, u32[]{:S(2)}, u32[]{:S(2)}) collective-permute-start(bf16[2,16,24,128]{3,2,1,0:T(8,128)(2,1)S(1)} %collective-permute-done.30.refs_1_.refs_4_), channel_id=1, source_target_pairs={{0,1},{1,0},{2,3},{3,2},{4,5},{5,4},{6,7},{7,6},{8,9},{9,8},{10,11... | collective-permute-start | bytes 589832 | tf_op jit(solution)/shard_map/ppermute | solution.py:451
